TPU v7x, 128 devices: a whole 4x4x4 slice. The times are simulated.
128 devices in a mesh: fsdp: 8 (over x, z_lo), ctx: 2 (over z_hi), tp: 8 (over y, core).
Axes of the slice: x: 4, y: 4, z: 4 (z_hi: 2, z_lo: 2; z = z_hi * 2 + z_lo), core: 2. Of those that a mesh axis runs over, the one named last changes fastest.
Arguments:
- tokens: float32 [6144, 1024], P(('fsdp', 'ctx')), may hold values from -30 to 30
- cotangent: float32 [6144, 1024], P(('fsdp', 'ctx')), may hold values from -6 to 6
- segments: int32 [8, 768], P('fsdp'), may hold values from 0 to 3, never falling along the last dimension, each value on 1 to 384 neighbouring positions
- attention_norm_weight: float32 [2, 1024], replicated, may hold values from 0.25 to 1.75
- query_gain: float32 [2, 128], replicated, may hold values from 0.25 to 1.75
- key_gain: float32 [2, 128], replicated, may hold values from 0.25 to 1.75
- feedforward_gain: float32 [2, 1024], replicated, may hold values from 0.25 to 1.75
- query_weight: bfloat16 [2, 1024, 2048], P(None, ('fsdp', 'ctx'), 'tp'), may hold values from -0.1875 to 0.1875
- key_projection_matrix: bfloat16 [2, 1024, 1024], P(None, ('fsdp', 'ctx'), 'tp'), may hold values from -0.1875 to 0.1875
- value_projection_matrix: bfloat16 [2, 1024, 1024], P(None, ('fsdp', 'ctx'), 'tp'), may hold values from -0.1875 to 0.1875
- output_weight: bfloat16 [2, 1024, 2048], P(None, ('fsdp', 'ctx'), 'tp'), may hold values from -0.75 to 0.75
- gate_weight: bfloat16 [2, 1024, 3072], P(None, ('fsdp', 'ctx'), 'tp'), may hold values from -0.1875 to 0.1875
- up_weight: bfloat16 [2, 1024, 3072], P(None, ('fsdp', 'ctx'), 'tp'), may hold values from -0.1875 to 0.1875
- down_weight: bfloat16 [2, 1024, 3072], P(None, ('fsdp', 'ctx'), 'tp'), may hold values from -0.15625 to 0.15625
Outputs:
- block_output: float32 [6144, 1024], P(('fsdp', 'ctx'))
- token_grad: float32 [6144, 1024], P(('fsdp', 'ctx'))
- attention_gain_grad: float32 [2, 1024], replicated
- query_gain_grad: float32 [2, 128], replicated
- key_gain_grad: float32 [2, 128], replicated
- feedforward_gain_grad: float32 [2, 1024], replicated
- query_weight_grad: float32 [2, 1024, 2048], P(None, ('fsdp', 'ctx'), 'tp')
- key_weight_grad: float32 [2, 1024, 1024], P(None, ('fsdp', 'ctx'), 'tp')
- value_weight_grad: float32 [2, 1024, 1024], P(None, ('fsdp', 'ctx'), 'tp')
- output_weight_grad: float32 [2, 1024, 2048], P(None, ('fsdp', 'ctx'), 'tp')
- gate_weight_grad: float32 [2, 1024, 3072], P(None, ('fsdp', 'ctx'), 'tp')
- up_weight_grad: float32 [2, 1024, 3072], P(None, ('fsdp', 'ctx'), 'tp')
- down_weight_grad: float32 [2, 1024, 3072], P(None, ('fsdp', 'ctx'), 'tp')
Inputs may be any that keep to these rules, and one draw needn't show every extreme that they name: `segments`: within each sequence the numbers never fall; each of the 4 documents has 1 to 384 tokens, one exactly 384.
All inputs are finite; a program needn't handle non-finite values.
Results may differ from a plain program's by a relative error of at most 0.04.
Values may be sent and summed in bfloat16 or wider, within the bound.
No kernel may reach another device: no remote copies, remote signals or barrier semaphores. Data moves between devices by JAX's collectives and lax.ppermute only.
A program may use at most 128 MiB of HBM per device.

v0:
```python
import jax
import jax.numpy as jnp
from jax import lax
from jax.sharding import PartitionSpec as P

eps = 1e-06
rope_base = 1000000.0


def contract_last(left_side, right_side):
    return lax.dot_general(
        left_side, right_side, (((1,), (1,)), ((), ())), preferred_element_type=jnp.float32
    )


def contract_first(left_side, right_side):
    return lax.dot_general(
        left_side, right_side, (((0,), (0,)), ((), ())), preferred_element_type=jnp.float32
    )


def row_scale(source):
    return lax.rsqrt(jnp.mean(source * source, axis=-1, keepdims=True) + eps)


def norm_back(grad_out, normalized, scaling, norm_gain):
    weighted = grad_out * norm_gain
    return scaling * (
        weighted - normalized * jnp.mean(weighted * normalized, axis=-1, keepdims=True)
    )


def rotary_tables(positions, head_size):
    halfway = head_size // 2
    frequency = rope_base ** (-2.0 * jnp.arange(halfway, dtype=jnp.float32) / head_size)
    angles = positions.astype(jnp.float32)[:, None] * frequency[None, :]
    return (jnp.cos(angles)[:, None, :], jnp.sin(angles)[:, None, :])


def rotate(source, cosine_table, sine_table):
    halfway = source.shape[-1] // 2
    leading = source[..., :halfway]
    trailing = source[..., halfway:]
    return jnp.concatenate(
        [
            leading * cosine_table - trailing * sine_table,
            trailing * cosine_table + leading * sine_table,
        ],
        axis=-1,
    )


def per_device(
    tokens,
    cotangent,
    segments,
    attention_norm_weight,
    query_gain,
    key_gain,
    feedforward_gain,
    query_weight,
    key_projection_matrix,
    value_projection_matrix,
    output_weight,
    gate_weight,
    up_weight,
    down_weight,
):
    row_count = tokens.shape[0]
    model_width = tokens.shape[1]
    head_size = query_gain.shape[1]
    local_heads = query_weight.shape[2] // head_size
    local_groups = key_projection_matrix.shape[2] // head_size
    per_group = local_heads // local_groups
    layer_count = query_weight.shape[0]
    seq_length = segments.shape[1]
    row_start = lax.axis_index("ctx") * row_count
    column_width = model_width // lax.axis_size("tp")
    column_start = lax.axis_index("tp") * column_width
    score_scale = head_size ** (-0.5)
    positions = row_start + jnp.arange(row_count, dtype=jnp.int32)
    segment_row = segments[0]
    query_ids = lax.dynamic_slice_in_dim(segment_row, row_start, row_count)
    key_positions = jnp.arange(seq_length, dtype=jnp.int32)
    allowed = (query_ids[:, None] == segment_row[None, :]) & (
        key_positions[None, :] <= positions[:, None]
    )
    cosine_table, sine_table = rotary_tables(positions, head_size)

    def column_share(grad_rows, normalized):
        gradient_portion = lax.dynamic_slice_in_dim(grad_rows, column_start, column_width, 1)
        unit_slice = lax.dynamic_slice_in_dim(normalized, column_start, column_width, 1)
        part_sum = jnp.sum(gradient_portion * unit_slice, axis=0)
        return lax.dynamic_update_slice_in_dim(
            jnp.zeros((model_width,), jnp.float32), part_sum, column_start, 0
        )

    def attention_scores(query_groups, key_groups):
        return (
            jnp.einsum(
                "qgrd,kgd->grqk", query_groups, key_groups, preferred_element_type=jnp.float32
            )
            * score_scale
        )

    kept_weights = []
    stored_layers = []
    hidden = tokens
    for layer_index in range(layer_count):
        gathered = (
            lax.all_gather(query_weight[layer_index], ("fsdp", "ctx"), axis=0, tiled=True),
            lax.all_gather(key_projection_matrix[layer_index], ("fsdp", "ctx"), axis=0, tiled=True),
            lax.all_gather(
                value_projection_matrix[layer_index], ("fsdp", "ctx"), axis=0, tiled=True
            ),
            lax.all_gather(output_weight[layer_index], ("fsdp", "ctx"), axis=0, tiled=True),
            lax.all_gather(gate_weight[layer_index], ("fsdp", "ctx"), axis=0, tiled=True),
            lax.all_gather(up_weight[layer_index], ("fsdp", "ctx"), axis=0, tiled=True),
            lax.all_gather(down_weight[layer_index], ("fsdp", "ctx"), axis=0, tiled=True),
        )
        kept_weights.append(gathered)
        (
            forward_query_full,
            forward_key_full,
            forward_value_full,
            forward_output_full,
            forward_gate_full,
            forward_up_full,
            forward_down_full,
        ) = gathered
        forward_scale_one = row_scale(hidden)
        forward_normed = (hidden * forward_scale_one * attention_norm_weight[layer_index]).astype(
            jnp.bfloat16
        )
        query_raw = jnp.dot(
            forward_normed, forward_query_full, preferred_element_type=jnp.float32
        ).reshape(row_count, local_heads, head_size)
        key_raw = jnp.dot(
            forward_normed, forward_key_full, preferred_element_type=jnp.float32
        ).reshape(row_count, local_groups, head_size)
        values = jnp.dot(
            forward_normed, forward_value_full, preferred_element_type=jnp.float32
        ).astype(jnp.bfloat16)
        forward_query_scale = row_scale(query_raw)
        forward_query_unit = query_raw * forward_query_scale
        forward_key_scale = row_scale(key_raw)
        forward_key_unit = key_raw * forward_key_scale
        queries = rotate(
            forward_query_unit * query_gain[layer_index], cosine_table, sine_table
        ).astype(jnp.bfloat16)
        keys = rotate(forward_key_unit * key_gain[layer_index], cosine_table, sine_table).astype(
            jnp.bfloat16
        )
        keys = keys.reshape(row_count, local_groups * head_size)
        all_keys = lax.all_gather(keys, "ctx", axis=0, tiled=True)
        all_values = lax.all_gather(values, "ctx", axis=0, tiled=True)
        forward_query_groups = queries.reshape(row_count, local_groups, per_group, head_size)
        forward_key_groups = all_keys.reshape(seq_length, local_groups, head_size)
        forward_value_groups = all_values.reshape(seq_length, local_groups, head_size)
        forward_scores = attention_scores(forward_query_groups, forward_key_groups)
        exponent = jnp.where(allowed, jnp.exp(forward_scores), 0.0)
        forward_log_total = jnp.log(jnp.sum(exponent, axis=-1, keepdims=True))
        attention_probs = jnp.where(
            allowed, jnp.exp(forward_scores - forward_log_total), 0.0
        ).astype(jnp.bfloat16)
        forward_attended = jnp.einsum(
            "grqk,kgd->qgrd",
            attention_probs,
            forward_value_groups,
            preferred_element_type=jnp.float32,
        )
        forward_attended = forward_attended.astype(jnp.bfloat16).reshape(
            row_count, local_heads * head_size
        )
        forward_middle = hidden + lax.psum(
            contract_last(forward_attended, forward_output_full).astype(jnp.bfloat16), "tp"
        ).astype(jnp.float32)
        forward_scale_two = row_scale(forward_middle)
        forward_feed_normed = (
            forward_middle * forward_scale_two * feedforward_gain[layer_index]
        ).astype(jnp.bfloat16)
        forward_gate_linear = jnp.dot(
            forward_feed_normed, forward_gate_full, preferred_element_type=jnp.float32
        )
        forward_up_linear = jnp.dot(
            forward_feed_normed, forward_up_full, preferred_element_type=jnp.float32
        )
        forward_activated = (jax.nn.silu(forward_gate_linear) * forward_up_linear).astype(
            jnp.bfloat16
        )
        result = forward_middle + lax.psum(
            contract_last(forward_activated, forward_down_full).astype(jnp.bfloat16), "tp"
        ).astype(jnp.float32)
        forward_stored = (
            hidden,
            forward_scale_one,
            forward_normed,
            forward_query_unit,
            forward_query_scale,
            forward_key_unit,
            forward_key_scale,
            forward_query_groups,
            forward_key_groups,
            forward_value_groups,
            forward_log_total,
            forward_attended,
            forward_middle,
            forward_scale_two,
            forward_feed_normed,
            forward_gate_linear,
            forward_up_linear,
            forward_activated,
        )
        hidden = result
        stored_layers.append(forward_stored)
    grad_flow = cotangent
    weight_sums = [None] * layer_count
    gain_parts = [None] * layer_count
    for layer_index in reversed(range(layer_count)):
        gathered = (
            lax.all_gather(query_weight[layer_index], ("fsdp", "ctx"), axis=0, tiled=True),
            lax.all_gather(key_projection_matrix[layer_index], ("fsdp", "ctx"), axis=0, tiled=True),
            lax.all_gather(
                value_projection_matrix[layer_index], ("fsdp", "ctx"), axis=0, tiled=True
            ),
            lax.all_gather(output_weight[layer_index], ("fsdp", "ctx"), axis=0, tiled=True),
            lax.all_gather(gate_weight[layer_index], ("fsdp", "ctx"), axis=0, tiled=True),
            lax.all_gather(up_weight[layer_index], ("fsdp", "ctx"), axis=0, tiled=True),
            lax.all_gather(down_weight[layer_index], ("fsdp", "ctx"), axis=0, tiled=True),
        )
        backward_stored = stored_layers[layer_index]
        query_full, key_full, value_full, output_full, gate_full, up_full, down_full = gathered
        (
            source,
            scale_one,
            normed,
            query_unit,
            query_scale,
            key_unit,
            key_scale,
            backward_query_groups,
            backward_key_groups,
            value_groups,
            log_total,
            attended,
            middle,
            scale_two,
            feed_normed,
            gate_linear,
            up_linear,
            activated,
        ) = backward_stored
        grad_half = grad_flow.astype(jnp.bfloat16)
        down_grad = contract_first(grad_half, activated)
        act_grad = jnp.dot(grad_half, down_full, preferred_element_type=jnp.float32)
        sigmoid_gate = jax.nn.sigmoid(gate_linear)
        gate_grad = (
            act_grad * up_linear * sigmoid_gate * (1.0 + gate_linear * (1.0 - sigmoid_gate))
        ).astype(jnp.bfloat16)
        up_grad = (act_grad * jax.nn.silu(gate_linear)).astype(jnp.bfloat16)
        gate_weight_grad = contract_first(feed_normed, gate_grad)
        up_weight_grad = contract_first(feed_normed, up_grad)
        feed_part = contract_last(gate_grad, gate_full) + contract_last(up_grad, up_full)
        feed_grad = lax.psum(feed_part.astype(jnp.bfloat16), "tp").astype(jnp.float32)
        feed_unit = middle * scale_two
        feed_gain_grad = column_share(feed_grad, feed_unit)
        middle_grad = grad_flow + norm_back(
            feed_grad, feed_unit, scale_two, feedforward_gain[layer_index]
        )
        middle_half = middle_grad.astype(jnp.bfloat16)
        output_weight_grad = contract_first(middle_half, attended)
        attended_grad = jnp.dot(
            middle_half, output_full, preferred_element_type=jnp.float32
        ).astype(jnp.bfloat16)
        attended_grad = attended_grad.reshape(row_count, local_groups, per_group, head_size)
        scores = attention_scores(backward_query_groups, backward_key_groups)
        exact = jnp.where(allowed, jnp.exp(scores - log_total), 0.0)
        half_probs = exact.astype(jnp.bfloat16)
        value_grad = jnp.einsum(
            "grqk,qgrd->kgd", half_probs, attended_grad, preferred_element_type=jnp.float32
        )
        prob_grad = jnp.einsum(
            "qgrd,kgd->grqk", attended_grad, value_groups, preferred_element_type=jnp.float32
        )
        row_delta = jnp.sum(exact * prob_grad, axis=-1, keepdims=True)
        score_grad = (exact * (prob_grad - row_delta) * score_scale).astype(jnp.bfloat16)
        query_grad = jnp.einsum(
            "grqk,kgd->qgrd", score_grad, backward_key_groups, preferred_element_type=jnp.float32
        )
        query_grad = query_grad.reshape(row_count, local_heads, head_size)
        key_grad = jnp.einsum(
            "grqk,qgrd->kgd", score_grad, backward_query_groups, preferred_element_type=jnp.float32
        )
        key_own = lax.psum_scatter(
            key_grad.reshape(seq_length, local_groups * head_size).astype(jnp.bfloat16),
            "ctx",
            scatter_dimension=0,
            tiled=True,
        ).astype(jnp.float32)
        value_own = lax.psum_scatter(
            value_grad.reshape(seq_length, local_groups * head_size).astype(jnp.bfloat16),
            "ctx",
            scatter_dimension=0,
            tiled=True,
        )
        query_turned = rotate(query_grad, cosine_table, -sine_table)
        key_turned = rotate(
            key_own.reshape(row_count, local_groups, head_size), cosine_table, -sine_table
        )
        query_gain_grad = jnp.sum(query_turned * query_unit, axis=(0, 1))
        key_gain_grad = jnp.sum(key_turned * key_unit, axis=(0, 1))
        query_pre = norm_back(
            query_turned, query_unit, query_scale, query_gain[layer_index]
        ).astype(jnp.bfloat16)
        query_pre = query_pre.reshape(row_count, local_heads * head_size)
        key_pre = norm_back(key_turned, key_unit, key_scale, key_gain[layer_index]).astype(
            jnp.bfloat16
        )
        key_pre = key_pre.reshape(row_count, local_groups * head_size)
        query_weight_grad = contract_first(normed, query_pre)
        key_weight_grad = contract_first(normed, key_pre)
        value_weight_grad = contract_first(normed, value_own)
        attention_part = (
            contract_last(query_pre, query_full)
            + contract_last(key_pre, key_full)
            + contract_last(value_own, value_full)
        )
        normed_grad = lax.psum(attention_part.astype(jnp.bfloat16), "tp").astype(jnp.float32)
        source_unit = source * scale_one
        attention_gain_grad = column_share(normed_grad, source_unit)
        source_grad = middle_grad + norm_back(
            normed_grad, source_unit, scale_one, attention_norm_weight[layer_index]
        )
        weight_terms = (
            query_weight_grad,
            key_weight_grad,
            value_weight_grad,
            output_weight_grad,
            gate_weight_grad,
            up_weight_grad,
            down_grad,
        )
        gain_terms = (attention_gain_grad, query_gain_grad, key_gain_grad, feed_gain_grad)
        grad_flow, weight_terms, gain_terms = (source_grad, weight_terms, gain_terms)
        grad_query, grad_key, grad_value, grad_output, grad_gate, grad_up, grad_down = weight_terms
        weight_sums[layer_index] = (
            lax.psum_scatter(
                grad_query.astype(jnp.bfloat16), ("fsdp", "ctx"), scatter_dimension=0, tiled=True
            ).astype(jnp.float32),
            lax.psum_scatter(
                grad_key.astype(jnp.bfloat16), ("fsdp", "ctx"), scatter_dimension=0, tiled=True
            ).astype(jnp.float32),
            lax.psum_scatter(
                grad_value.astype(jnp.bfloat16), ("fsdp", "ctx"), scatter_dimension=0, tiled=True
            ).astype(jnp.float32),
            lax.psum_scatter(
                grad_output.astype(jnp.bfloat16), ("fsdp", "ctx"), scatter_dimension=0, tiled=True
            ).astype(jnp.float32),
            lax.psum_scatter(
                grad_gate.astype(jnp.bfloat16), ("fsdp", "ctx"), scatter_dimension=0, tiled=True
            ).astype(jnp.float32),
            lax.psum_scatter(
                grad_up.astype(jnp.bfloat16), ("fsdp", "ctx"), scatter_dimension=0, tiled=True
            ).astype(jnp.float32),
            lax.psum_scatter(
                grad_down.astype(jnp.bfloat16), ("fsdp", "ctx"), scatter_dimension=0, tiled=True
            ).astype(jnp.float32),
        )
        gain_parts[layer_index] = gain_terms
    gain_totals = lax.psum(
        (
            jnp.stack([member[0] for member in gain_parts]),
            jnp.stack([member[1] for member in gain_parts]),
            jnp.stack([member[2] for member in gain_parts]),
            jnp.stack([member[3] for member in gain_parts]),
        ),
        ("fsdp", "ctx", "tp"),
    )
    stacked = [jnp.stack([member[which] for member in weight_sums]) for which in range(7)]
    return (
        hidden,
        grad_flow,
        gain_totals[0],
        gain_totals[1],
        gain_totals[2],
        gain_totals[3],
        stacked[0],
        stacked[1],
        stacked[2],
        stacked[3],
        stacked[4],
        stacked[5],
        stacked[6],
    )


def solution(mesh):
    in_specs = (
        P(("fsdp", "ctx"), None),
        P(("fsdp", "ctx"), None),
        P("fsdp", None),
        P(),
        P(),
        P(),
        P(),
        P(None, ("fsdp", "ctx"), "tp"),
        P(None, ("fsdp", "ctx"), "tp"),
        P(None, ("fsdp", "ctx"), "tp"),
        P(None, ("fsdp", "ctx"), "tp"),
        P(None, ("fsdp", "ctx"), "tp"),
        P(None, ("fsdp", "ctx"), "tp"),
        P(None, ("fsdp", "ctx"), "tp"),
    )
    out_specs = (
        P(("fsdp", "ctx"), None),
        P(("fsdp", "ctx"), None),
        P(),
        P(),
        P(),
        P(),
        P(None, ("fsdp", "ctx"), "tp"),
        P(None, ("fsdp", "ctx"), "tp"),
        P(None, ("fsdp", "ctx"), "tp"),
        P(None, ("fsdp", "ctx"), "tp"),
        P(None, ("fsdp", "ctx"), "tp"),
        P(None, ("fsdp", "ctx"), "tp"),
        P(None, ("fsdp", "ctx"), "tp"),
    )
    return jax.shard_map(
        per_device, mesh=mesh, in_specs=in_specs, out_specs=out_specs, check_vma=False
    )
```

profile of v0, /device:TPU:0, one launch (start us, length us, event | category | flops | bytes accessed | tf_op | source)
XLA Modules:
  0.0 2159.9 jit_solution(3933166253589749794)
XLA Ops:
  14.9 42.0 %all-gather = bf16[1,1024,128]{2,1,0:T(8,128)(2,1)S(1)} all-gather(bf16[1,64,128]{2,1,0:T(8,128)(2,1)S(1)} %get-tuple-element.75), channel_id=2, replica_groups=mesh['fsdp'=8,'ctx'=2,'tp'=8] {'fsdp','ctx'}, dimensions={1}, use_global_device_ids=true | all-gather | bytes 278528 | tf_op jit(solution)/shard_map/all_gather | solution.py:113
  56.9 36.0 %all-gather.1 = bf16[1,1024,128]{2,1,0:T(8,128)(2,1)S(1)} all-gather(bf16[1,64,128]{2,1,0:T(8,128)(2,1)S(1)} %get-tuple-element.73), channel_id=3, replica_groups=mesh['fsdp'=8,'ctx'=2,'tp'=8] {'fsdp','ctx'}, dimensions={1}, use_global_device_ids=true | all-gather | bytes 278528 | tf_op jit(solution)/shard_map/all_gather | solution.py:112
  93.0 41.2 %all-gather.3 = bf16[1,1024,256]{2,1,0:T(8,128)(2,1)S(1)} all-gather(bf16[1,64,256]{2,1,0:T(8,128)(2,1)S(1)} %get-tuple-element.69), channel_id=5, replica_groups=mesh['fsdp'=8,'ctx'=2,'tp'=8] {'fsdp','ctx'}, dimensions={1}, use_global_device_ids=true | all-gather | bytes 557056 | tf_op jit(solution)/shard_map/all_gather | solution.py:116
  134.2 37.6 %all-gather.2 = bf16[1,1024,256]{2,1,0:T(8,128)(2,1)S(1)} all-gather(bf16[1,64,256]{2,1,0:T(8,128)(2,1)S(1)} %get-tuple-element.71), channel_id=4, replica_groups=mesh['fsdp'=8,'ctx'=2,'tp'=8] {'fsdp','ctx'}, dimensions={1}, use_global_device_ids=true | all-gather | bytes 557056 | tf_op jit(solution)/shard_map/all_gather | solution.py:111
  173.6 7.3 all_gather.69
  183.4 7.4 all_gather.71
  197.9 43.6 %all-gather.10 = bf16[1,1024,256]{2,1,0:T(8,128)(2,1)} all-gather(bf16[1,64,256]{2,1,0:T(8,128)(2,1)S(1)} %get-tuple-element.68), channel_id=12, replica_groups=mesh['fsdp'=8,'ctx'=2,'tp'=8] {'fsdp','ctx'}, dimensions={1}, use_global_device_ids=true | all-gather | bytes 557056 | tf_op jit(solution)/shard_map/all_gather | solution.py:116
  241.4 40.1 %all-gather.9 = bf16[1,1024,256]{2,1,0:T(8,128)(2,1)} all-gather(bf16[1,64,256]{2,1,0:T(8,128)(2,1)S(1)} %get-tuple-element.70), channel_id=11, replica_groups=mesh['fsdp'=8,'ctx'=2,'tp'=8] {'fsdp','ctx'}, dimensions={1}, use_global_device_ids=true | all-gather | bytes 557056 | tf_op jit(solution)/shard_map/all_gather | solution.py:111
  281.6 45.1 %all-gather.6 = bf16[1,1024,384]{2,1,0:T(8,128)(2,1)} all-gather(bf16[1,64,384]{2,1,0:T(8,128)(2,1)S(1)} %get-tuple-element.63), channel_id=8, replica_groups=mesh['fsdp'=8,'ctx'=2,'tp'=8] {'fsdp','ctx'}, dimensions={1}, use_global_device_ids=true | all-gather | bytes 835584 | tf_op jit(solution)/shard_map/all_gather | solution.py:119
  326.6 42.6 %all-gather.5 = bf16[1,1024,384]{2,1,0:T(8,128)(2,1)} all-gather(bf16[1,64,384]{2,1,0:T(8,128)(2,1)S(1)} %get-tuple-element.67), channel_id=7, replica_groups=mesh['fsdp'=8,'ctx'=2,'tp'=8] {'fsdp','ctx'}, dimensions={1}, use_global_device_ids=true | all-gather | bytes 835584 | tf_op jit(solution)/shard_map/all_gather | solution.py:118
  369.2 40.5 %all-gather.7 = bf16[1,1024,128]{2,1,0:T(8,128)(2,1)} all-gather(bf16[1,64,128]{2,1,0:T(8,128)(2,1)S(1)} %copy-done.113), channel_id=9, replica_groups=mesh['fsdp'=8,'ctx'=2,'tp'=8] {'fsdp','ctx'}, dimensions={1}, use_global_device_ids=true | all-gather | bytes 278528 | tf_op jit(solution)/shard_map/all_gather | solution.py:113
  409.8 40.2 %all-gather.4 = bf16[1,1024,384]{2,1,0:T(8,128)(2,1)S(1)} all-gather(bf16[1,64,384]{2,1,0:T(8,128)(2,1)S(1)} %get-tuple-element.65), channel_id=6, replica_groups=mesh['fsdp'=8,'ctx'=2,'tp'=8] {'fsdp','ctx'}, dimensions={1}, use_global_device_ids=true | all-gather | bytes 835584 | tf_op jit(solution)/shard_map/all_gather | solution.py:117
  458.3 41.1 %all-gather.8 = bf16[1,1024,128]{2,1,0:T(8,128)(2,1)} all-gather(bf16[1,64,128]{2,1,0:T(8,128)(2,1)S(1)} %copy-done.112), channel_id=10, replica_groups=mesh['fsdp'=8,'ctx'=2,'tp'=8] {'fsdp','ctx'}, dimensions={1}, use_global_device_ids=true | all-gather | bytes 278528 | tf_op jit(solution)/shard_map/all_gather | solution.py:112
  499.4 41.3 %all-gather.13 = bf16[1,1024,384]{2,1,0:T(8,128)(2,1)} all-gather(bf16[1,64,384]{2,1,0:T(8,128)(2,1)S(1)} %copy-done.106), channel_id=15, replica_groups=mesh['fsdp'=8,'ctx'=2,'tp'=8] {'fsdp','ctx'}, dimensions={1}, use_global_device_ids=true | all-gather | bytes 835584 | tf_op jit(solution)/shard_map/all_gather | solution.py:119
  540.8 1.8 multiply_reduce_fusion.5
  544.4 7.1 all_gather.78
  553.1 7.6 all_gather.80
  562.5 1.9 copy.103
  570.3 42.8 %all-gather.12 = bf16[1,1024,384]{2,1,0:T(8,128)(2,1)S(1)} all-gather(bf16[1,64,384]{2,1,0:T(8,128)(2,1)S(1)} %get-tuple-element.66), channel_id=14, replica_groups=mesh['fsdp'=8,'ctx'=2,'tp'=8] {'fsdp','ctx'}, dimensions={1}, use_global_device_ids=true | all-gather | bytes 835584 | tf_op jit(solution)/shard_map/all_gather | solution.py:118
  613.1 41.5 %all-gather.11 = bf16[1,1024,384]{2,1,0:T(8,128)(2,1)} all-gather(bf16[1,64,384]{2,1,0:T(8,128)(2,1)S(1)} %get-tuple-element.64), channel_id=13, replica_groups=mesh['fsdp'=8,'ctx'=2,'tp'=8] {'fsdp','ctx'}, dimensions={1}, use_global_device_ids=true | all-gather | bytes 835584 | tf_op jit(solution)/shard_map/all_gather | solution.py:117
  664.3 60.0 %all-reduce.16.cloned.1.call-done = bf16[384,1024]{1,0:T(8,128)(2,1)} async-done(((bf16[384,1024]{1,0:T(8,128)(2,1)}), bf16[384,1024]{1,0:T(8,128)(2,1)}) %all-reduce.16.cloned.1.call-update) | async-done | bytes 786448 | tf_op jit(solution)/shard_map/psum | solution.py:264
  724.3 2.0 multiply_reduce_fusion.3
  726.6 2.0 multiply_add_fusion.3
  739.2 1.9 copy.111
  741.2 1.8 fusion.71
  745.6 5.2 reduce-scatter.55.cloned.1.call-done
  754.8 13.2 reduce-scatter.57.cloned.1.call-done
  768.0 3.2 add_convert_fusion.2
  771.3 60.9 %all-reduce.18.cloned.1.call-done = bf16[384,1024]{1,0:T(8,128)(2,1)} async-done(((bf16[384,1024]{1,0:T(8,128)(2,1)}), bf16[384,1024]{1,0:T(8,128)(2,1)}) %all-reduce.18.cloned.1.call-update) | async-done | bytes 786448 | tf_op jit(solution)/shard_map/psum | solution.py:328
  832.2 2.0 multiply_reduce_fusion.2
  834.5 2.0 multiply_add_fusion.2
  840.7 61.0 %all-reduce.20.cloned.1.call-done = bf16[384,1024]{1,0:T(8,128)(2,1)} async-done(((bf16[384,1024]{1,0:T(8,128)(2,1)}), bf16[384,1024]{1,0:T(8,128)(2,1)}) %all-reduce.20.cloned.1.call-update) | async-done | bytes 786448 | tf_op jit(solution)/shard_map/psum | solution.py:264
  901.6 2.0 multiply_reduce_fusion.1
  903.9 2.0 multiply_add_fusion.1
  908.7 2.3 fusion
  911.9 3.2 fusion.22
  918.8 7.5 reduce-scatter.61.cloned.1.call-done
  926.4 2.0 convolution_convert_fusion.15
  929.6 13.9 reduce-scatter.59.cloned.1.call-done
  950.5 2.7 convolution_convert_fusion.10
  953.3 2.7 convolution_convert_fusion.11
  958.3 2.0 convolution_bitcast_fusion.2
  965.0 2.8 convolution_convert_fusion.8
  970.5 3.2 fusion.16
  975.5 2.8 convolution_convert_fusion.4
  978.4 2.6 convolution_convert_fusion.5
  988.5 33.2 %reduce-scatter.37.cloned.1.call-done = bf16[64,128]{1,0:T(8,128)(2,1)} async-done(((bf16[1024,128]{1,0:T(8,128)(2,1)}), bf16[64,128]{1,0:T(8,128)(2,1)}) %reduce-scatter.37.cloned.1.call-update) | async-done | bytes 16400 | tf_op jit(solution)/shard_map/reduce_scatter | solution.py:353
  1021.7 75.9 %reduce-scatter.35.cloned.1.call-done = bf16[64,128]{1,0:T(8,128)(2,1)} async-done(((bf16[1024,128]{1,0:T(8,128)(2,1)}), bf16[64,128]{1,0:T(8,128)(2,1)}) %reduce-scatter.35.cloned.1.call-update) | async-done | bytes 16400 | tf_op jit(solution)/shard_map/reduce_scatter | solution.py:353
  1099.0 74.6 %reduce-scatter.33.cloned.1.call-done = bf16[64,128]{1,0:T(8,128)(2,1)} async-done(((bf16[1024,128]{1,0:T(8,128)(2,1)}), bf16[64,128]{1,0:T(8,128)(2,1)}) %reduce-scatter.33.cloned.1.call-update) | async-done | bytes 16400 | tf_op jit(solution)/shard_map/reduce_scatter | solution.py:350
  1173.6 76.0 %reduce-scatter.31.cloned.1.call-done = bf16[64,128]{1,0:T(8,128)(2,1)} async-done(((bf16[1024,128]{1,0:T(8,128)(2,1)}), bf16[64,128]{1,0:T(8,128)(2,1)}) %reduce-scatter.31.cloned.1.call-update) | async-done | bytes 16400 | tf_op jit(solution)/shard_map/reduce_scatter | solution.py:350
  1250.9 74.9 %reduce-scatter.41.cloned.1.call-done = bf16[64,256]{1,0:T(8,128)(2,1)} async-done(((bf16[1024,256]{1,0:T(8,128)(2,1)}), bf16[64,256]{1,0:T(8,128)(2,1)}) %reduce-scatter.41.cloned.1.call-update) | async-done | bytes 32784 | tf_op jit(solution)/shard_map/reduce_scatter | solution.py:356
  1325.8 76.4 %reduce-scatter.39.cloned.1.call-done = bf16[64,256]{1,0:T(8,128)(2,1)} async-done(((bf16[1024,256]{1,0:T(8,128)(2,1)}), bf16[64,256]{1,0:T(8,128)(2,1)}) %reduce-scatter.39.cloned.1.call-update) | async-done | bytes 32784 | tf_op jit(solution)/shard_map/reduce_scatter | solution.py:356
  1403.7 75.0 %reduce-scatter.29.cloned.1.call-done = bf16[64,256]{1,0:T(8,128)(2,1)} async-done(((bf16[1024,256]{1,0:T(8,128)(2,1)}), bf16[64,256]{1,0:T(8,128)(2,1)}) %reduce-scatter.29.cloned.1.call-update) | async-done | bytes 32784 | tf_op jit(solution)/shard_map/reduce_scatter | solution.py:347
  1478.7 76.6 %reduce-scatter.27.cloned.1.call-done = bf16[64,256]{1,0:T(8,128)(2,1)} async-done(((bf16[1024,256]{1,0:T(8,128)(2,1)}), bf16[64,256]{1,0:T(8,128)(2,1)}) %reduce-scatter.27.cloned.1.call-update) | async-done | bytes 32784 | tf_op jit(solution)/shard_map/reduce_scatter | solution.py:347
  1556.7 62.1 %all-reduce.22.cloned.1.call-done = (bf16[384,1024]{1,0:T(8,128)(2,1)}, bf16[384,1024]{1,0:T(8,128)(2,1)}) async-done(((bf16[384,1024]{1,0:T(8,128)(2,1)}, bf16[384,1024]{1,0:T(8,128)(2,1)}), (bf16[384,1024]{1,0:T(8,128)(2,1)}, bf16[384,1024]{1,0:T(8,128)(2,1)})) %all-reduce.22.cloned.1.call-update) | async-done | bytes 1572880 | tf_op jit(solution)/shard_map/psum | solution.py:191
  1621.2 77.3 %reduce-scatter.53.cloned.1.call-done = bf16[64,384]{1,0:T(8,128)(2,1)} async-done(((bf16[1024,384]{1,0:T(8,128)(2,1)}), bf16[64,384]{1,0:T(8,128)(2,1)}) %reduce-scatter.53.cloned.1.call-update) | async-done | bytes 49168 | tf_op jit(solution)/shard_map/reduce_scatter | solution.py:365
  1698.4 77.2 %reduce-scatter.51.cloned.1.call-done = bf16[64,384]{1,0:T(8,128)(2,1)} async-done(((bf16[1024,384]{1,0:T(8,128)(2,1)}), bf16[64,384]{1,0:T(8,128)(2,1)}) %reduce-scatter.51.cloned.1.call-update) | async-done | bytes 49168 | tf_op jit(solution)/shard_map/reduce_scatter | solution.py:365
  1777.2 75.6 %reduce-scatter.49.cloned.1.call-done = bf16[64,384]{1,0:T(8,128)(2,1)} async-done(((bf16[1024,384]{1,0:T(8,128)(2,1)}), bf16[64,384]{1,0:T(8,128)(2,1)}) %reduce-scatter.49.cloned.1.call-update) | async-done | bytes 49168 | tf_op jit(solution)/shard_map/reduce_scatter | solution.py:362
  1852.7 77.2 %reduce-scatter.47.cloned.1.call-done = bf16[64,384]{1,0:T(8,128)(2,1)} async-done(((bf16[1024,384]{1,0:T(8,128)(2,1)}), bf16[64,384]{1,0:T(8,128)(2,1)}) %reduce-scatter.47.cloned.1.call-update) | async-done | bytes 49168 | tf_op jit(solution)/shard_map/reduce_scatter | solution.py:362
  1931.4 1.9 multiply_reduce_fusion
  1933.3 73.5 %reduce-scatter.45.cloned.1.call-done = bf16[64,384]{1,0:T(8,128)(2,1)} async-done(((bf16[1024,384]{1,0:T(8,128)(2,1)}), bf16[64,384]{1,0:T(8,128)(2,1)}) %reduce-scatter.45.cloned.1.call-update) | async-done | bytes 49168 | tf_op jit(solution)/shard_map/reduce_scatter | solution.py:359
  2006.8 77.1 %reduce-scatter.43.cloned.1.call-done = bf16[64,384]{1,0:T(8,128)(2,1)} async-done(((bf16[1024,384]{1,0:T(8,128)(2,1)}), bf16[64,384]{1,0:T(8,128)(2,1)}) %reduce-scatter.43.cloned.1.call-update) | async-done | bytes 49168 | tf_op jit(solution)/shard_map/reduce_scatter | solution.py:359
  2085.5 63.3 %all-reduce = (f32[2,1024]{1,0:T(2,128)}, f32[2,128]{1,0:T(2,128)}, f32[2,128]{1,0:T(2,128)}, f32[2,1024]{1,0:T(2,128)}) all-reduce(f32[2,1024]{1,0:T(2,128)S(1)} %get-tuple-element.107, f32[2,128]{1,0:T(2,128)S(1)} %get-tuple-element.109, ...), channel_id=1, replica_groups=mesh['fsdp'=8,'ctx'=2,'tp'=8] {'fsdp','ctx','tp'}, use_global_device_ids=true, to_apply=%region_34.35 | all-reduce | flops 4608 | bytes 36864 | tf_op jit(solution)/shard_map/psum | solution.py:370
  2148.8 4.1 multiply_add_fusion
  (501 shorter events, 115.9 us)
Async XLA Ops:
  7.2 7.0 copy-start.124
  7.2 7.6 copy-start.110
  7.2 7.6 copy-start.111
  7.2 442.8 %all-reduce.10.cloned.1.call-start = ((), (), s32[]{:S(2)}) async-start(), calls=%async_computation.18 | async-start | bytes 1572864 | tf_op jit(solution)/shard_map/psum | solution.py:175
  7.3 175.6 %copy-start.135 = (f32[64]{0:T(128)}, f32[64]{0:T(128)S(1)}, u32[]{:S(2)}) copy-start(f32[64]{0:T(128)S(1)} %multiply_power_fusion) | copy-start | bytes 772
  8.6 183.5 %copy-start.143 = (f32[128]{0:T(128)}, f32[128]{0:T(128)S(1)}, u32[]{:S(2)}) copy-start(f32[128]{0:T(128)S(1)} %get-tuple-element.84) | copy-start | bytes 1540
  9.9 173.0 %copy-start.138 = (f32[128]{0:T(128)}, f32[128]{0:T(128)S(1)}, u32[]{:S(2)}) copy-start(f32[128]{0:T(128)S(1)} %get-tuple-element.86) | copy-start | bytes 1540
  11.3 160.5 %copy-start = (f32[384,1024]{1,0:T(8,128)S(1)}, f32[384,1024]{1,0:T(8,128)}, u32[]{:S(2)}) copy-start(f32[384,1024]{1,0:T(8,128)} %param.14) | copy-start | bytes 4718596
  13.0 160.2 %copy-start.131 = (f32[384]{0:T(512)}, f32[384]{0:T(512)S(1)}, u32[]{:S(2)}) copy-start(f32[384]{0:T(512)S(1)} %add_rsqrt_fusion.7) | copy-start | bytes 4612
  56.9 116.2 %copy-start.59 = (bf16[1,1024,128]{2,1,0:T(8,128)(2,1)}, bf16[1,1024,128]{2,1,0:T(8,128)(2,1)S(1)}, u32[]{:S(2)}) copy-start(bf16[1,1024,128]{2,1,0:T(8,128)(2,1)S(1)} %all-gather) | copy-start | bytes 786436
  93.0 87.9 %copy-start.63 = (bf16[1,1024,128]{2,1,0:T(8,128)(2,1)}, bf16[1,1024,128]{2,1,0:T(8,128)(2,1)S(1)}, u32[]{:S(2)}) copy-start(bf16[1,1024,128]{2,1,0:T(8,128)(2,1)S(1)} %all-gather.1) | copy-start | bytes 786436
  134.2 61.6 %copy-start.34 = (bf16[1,1024,256]{2,1,0:T(8,128)(2,1)}, bf16[1,1024,256]{2,1,0:T(8,128)(2,1)S(1)}, u32[]{:S(2)}) copy-start(bf16[1,1024,256]{2,1,0:T(8,128)(2,1)S(1)} %all-gather.3) | copy-start | bytes 1572868
  171.8 19.0 copy-start.38
  173.2 17.7 copy-start.1
  181.3 10.0 copy-start.53
  181.3 10.0 copy-start.119
  182.8 9.5 copy-start.30
  195.7 45.7 %copy-start.91 = (bf16[128,2,384]{2,0,1:T(8,128)(2,1)}, bf16[128,2,384]{2,0,1:T(8,128)(2,1)S(1)}, u32[]{:S(2)}) copy-start(bf16[128,2,384]{2,0,1:T(8,128)(2,1)S(1)} %convolution_convert_fusion.21) | copy-start | bytes 589828
  197.1 343.7 %all-reduce.12.cloned.1.call-start = ((), (), s32[]{:S(2)}) async-start(), calls=%async_computation.19 | async-start | bytes 1572864 | tf_op jit(solution)/shard_map/psum | solution.py:191
  197.2 172.0 %copy-start.113 = (bf16[1,64,128]{2,1,0:T(8,128)(2,1)S(1)}, bf16[1,64,128]{2,1,0:T(8,128)(2,1)}, u32[]{:S(2)}) copy-start(bf16[1,64,128]{2,1,0:T(8,128)(2,1)} %get-tuple-element.74) | copy-start | bytes 49156
  456.0 43.4 %copy-start.106 = (bf16[1,64,384]{2,1,0:T(8,128)(2,1)S(1)}, bf16[1,64,384]{2,1,0:T(8,128)(2,1)}, u32[]{:S(2)}) copy-start(bf16[1,64,384]{2,1,0:T(8,128)(2,1)} %get-tuple-element.62) | copy-start | bytes 147460
  458.3 196.3 %all-reduce.14.cloned.1.call-start = ((), (), s32[]{:S(2)}) async-start(), calls=%async_computation.20 | async-start | bytes 1572864 | tf_op jit(solution)/shard_map/psum | solution.py:175
  544.0 7.5 copy-start.65
  544.0 8.5 copy-start.139
  544.0 8.6 copy-start.136
  544.4 16.3 copy-start.40
  551.9 10.0 copy-start.55
  570.3 154.0 %all-reduce.16.cloned.1.call-start = ((), (), s32[]{:S(2)}) async-start(), calls=%async_computation.21 | async-start | bytes 1572864 | tf_op jit(solution)/shard_map/psum | solution.py:264
  664.3 86.6 %reduce-scatter.55.cloned.1.call-start = ((), (), s32[]{:S(2)}) async-start(), calls=%async_computation.38 | async-start | bytes 294912
  736.3 31.7 %reduce-scatter.57.cloned.1.call-start = ((), (), s32[]{:S(2)}) async-start(), calls=%async_computation.39 | async-start | bytes 294912
  743.0 8.9 copy-start.137
  743.7 8.7 copy-start.56
  743.7 8.7 copy-start.122
  743.7 8.7 copy-start.140
  745.3 7.8 copy-start.66
  745.4 86.8 %all-reduce.18.cloned.1.call-start = ((), (), s32[]{:S(2)}) async-start(), calls=%async_computation.22 | async-start | bytes 1572864 | tf_op jit(solution)/shard_map/psum | solution.py:328
  751.9 16.1 copy-start.62
  754.8 77.4 %copy-start.115 = (f32[1,1024]{1,0:T(1,128)S(1)}, f32[1,1024]{1,0:T(1,128)}, u32[]{:S(2)}) copy-start(f32[1,1024]{1,0:T(1,128)} %get-tuple-element.76) | copy-start | bytes 12292
  771.2 63.0 %copy-start.134 = (f32[384]{0:T(512)S(1)}, f32[384]{0:T(512)}, u32[]{:S(2)}) copy-start(f32[384]{0:T(512)} %copy-done.133) | copy-start | bytes 4612
  771.2 130.4 %all-reduce.20.cloned.1.call-start = ((), (), s32[]{:S(2)}) async-start(), calls=%async_computation.23 | async-start | bytes 1572864 | tf_op jit(solution)/shard_map/psum | solution.py:264
  840.6 63.1 %copy-start.130 = (f32[384]{0:T(512)S(1)}, f32[384]{0:T(512)}, u32[]{:S(2)}) copy-start(f32[384]{0:T(512)} %copy-done.129) | copy-start | bytes 4612
  840.6 85.8 %reduce-scatter.61.cloned.1.call-start = ((), (), s32[]{:S(2)}) async-start(), calls=%async_computation.41 | async-start | bytes 294912
  911.8 31.7 %reduce-scatter.59.cloned.1.call-start = ((), (), s32[]{:S(2)}) async-start(), calls=%async_computation.40 | async-start | bytes 294912
  916.1 10.3 copy-start.2
  917.5 104.2 %reduce-scatter.37.cloned.1.call-start = ((), (), s32[]{:S(2)}) async-start(), calls=%async_computation.29 | async-start | bytes 278528 | tf_op jit(solution)/shard_map/reduce_scatter | solution.py:353
  918.8 27.8 %copy-start.54 = (f32[384,128]{0,1:T(8,128)S(1)}, f32[384,128]{0,1:T(8,128)}, u32[]{:S(2)}) copy-start(f32[384,128]{0,1:T(8,128)} %copy-done.53) | copy-start | bytes 589828
  918.8 27.8 %copy-start.120 = (f32[384]{0:T(512)S(1)}, f32[384]{0:T(512)}, u32[]{:S(2)}) copy-start(f32[384]{0:T(512)} %copy-done.119) | copy-start | bytes 4612
  918.8 178.8 %reduce-scatter.35.cloned.1.call-start = ((), (), s32[]{:S(2)}) async-start(), calls=%async_computation.28 | async-start | bytes 278528 | tf_op jit(solution)/shard_map/reduce_scatter | solution.py:353
  928.4 245.2 %reduce-scatter.33.cloned.1.call-start = ((), (), s32[]{:S(2)}) async-start(), calls=%async_computation.27 | async-start | bytes 278528 | tf_op jit(solution)/shard_map/reduce_scatter | solution.py:350
  929.6 20.9 copy-start.94
  929.6 319.9 %reduce-scatter.31.cloned.1.call-start = ((), (), s32[]{:S(2)}) async-start(), calls=%async_computation.26 | async-start | bytes 278528 | tf_op jit(solution)/shard_map/reduce_scatter | solution.py:350
  950.4 375.4 %reduce-scatter.41.cloned.1.call-start = ((), (), s32[]{:S(2)}) async-start(), calls=%async_computation.31 | async-start | bytes 557056 | tf_op jit(solution)/shard_map/reduce_scatter | solution.py:356
  953.2 449.0 %reduce-scatter.39.cloned.1.call-start = ((), (), s32[]{:S(2)}) async-start(), calls=%async_computation.30 | async-start | bytes 557056 | tf_op jit(solution)/shard_map/reduce_scatter | solution.py:356
  956.0 522.7 %reduce-scatter.29.cloned.1.call-start = ((), (), s32[]{:S(2)}) async-start(), calls=%async_computation.25 | async-start | bytes 557056 | tf_op jit(solution)/shard_map/reduce_scatter | solution.py:347
  958.0 597.3 %reduce-scatter.27.cloned.1.call-start = ((), (), s32[]{:S(2)}) async-start(), calls=%async_computation.24 | async-start | bytes 557056 | tf_op jit(solution)/shard_map/reduce_scatter | solution.py:347
  964.9 653.9 %all-reduce.22.cloned.1.call-start = ((), (), s32[]{:S(2)}) async-start(), calls=%async_computation.42 | async-start | bytes 3145728 | tf_op jit(solution)/shard_map/psum | solution.py:191
  970.4 728.0 %reduce-scatter.53.cloned.1.call-start = ((), (), s32[]{:S(2)}) async-start(), calls=%async_computation.37 | async-start | bytes 835584 | tf_op jit(solution)/shard_map/reduce_scatter | solution.py:365
  973.7 801.9 %reduce-scatter.51.cloned.1.call-start = ((), (), s32[]{:S(2)}) async-start(), calls=%async_computation.36 | async-start | bytes 835584 | tf_op jit(solution)/shard_map/reduce_scatter | solution.py:365
  975.4 877.3 %reduce-scatter.49.cloned.1.call-start = ((), (), s32[]{:S(2)}) async-start(), calls=%async_computation.35 | async-start | bytes 835584 | tf_op jit(solution)/shard_map/reduce_scatter | solution.py:362
  978.4 951.6 %reduce-scatter.47.cloned.1.call-start = ((), (), s32[]{:S(2)}) async-start(), calls=%async_computation.34 | async-start | bytes 835584 | tf_op jit(solution)/shard_map/reduce_scatter | solution.py:362
  981.1 1025.7 %reduce-scatter.45.cloned.1.call-start = ((), (), s32[]{:S(2)}) async-start(), calls=%async_computation.33 | async-start | bytes 835584 | tf_op jit(solution)/shard_map/reduce_scatter | solution.py:359
  982.9 1101.0 %reduce-scatter.43.cloned.1.call-start = ((), (), s32[]{:S(2)}) async-start(), calls=%async_computation.32 | async-start | bytes 835584 | tf_op jit(solution)/shard_map/reduce_scatter | solution.py:359
  1777.2 371.6 %copy-start.6 = (f32[384,1024]{1,0:T(8,128)S(1)}, f32[384,1024]{1,0:T(8,128)}, u32[]{:S(2)}) copy-start(f32[384,1024]{1,0:T(8,128)} %copy-done.5) | copy-start | bytes 4718596
  1777.2 371.6 %copy-start.132 = (f32[384]{0:T(512)S(1)}, f32[384]{0:T(512)}, u32[]{:S(2)}) copy-start(f32[384]{0:T(512)} %copy-done.131) | copy-start | bytes 4612
  (111 other events, 220.6 us)
Sparse Core Ops, SparseCore 0:
  197.2 61.7 all-reduce.9
  458.4 61.7 all-reduce.11
  570.4 61.3 all-reduce.13
  664.4 59.8 all-reduce.15
  736.5 14.3 reduce-scatter.54
  753.6 14.3 reduce-scatter.56
  771.3 60.7 all-reduce.17
  840.7 60.8 all-reduce.19
  912.0 14.3 reduce-scatter.60
  929.1 14.3 reduce-scatter.58
  945.9 75.7 reduce-scatter.36
  1024.0 73.5 reduce-scatter.34
  1100.0 73.5 reduce-scatter.32
  1175.9 73.6 reduce-scatter.30
  1251.7 74.0 reduce-scatter.40
  1328.1 74.0 reduce-scatter.38
  1404.5 74.2 reduce-scatter.28
  1481.0 74.2 reduce-scatter.26
  1557.7 61.0 all-reduce.21
  1621.1 77.3 reduce-scatter.52
  1700.9 74.6 reduce-scatter.50
  1778.0 74.6 reduce-scatter.48
  1855.2 74.6 reduce-scatter.46
  1932.1 74.6 reduce-scatter.44
  2009.3 74.5 reduce-scatter.42
where the time goes:
time: 2170 us; the launch traced here: 2160 us
  waiting for transfers between devices  1300 us (60%)
  blocking collectives  668 us (31%)
  matrix products  68.7 us (3%)
  other arithmetic  67.4 us (3%)
  local copies, waits for them, and re-layouts  32.9 us (2%)
    reduce_scatter x2, waiting for transfers between devices, per_device(): lax.psum_scatter(grad_down.astype(jnp.bfloat16), ('fsdp', 'ctx'), scatter...  154 us
    reduce_scatter x2, waiting for transfers between devices, per_device(): lax.psum_scatter(grad_up.astype(jnp.bfloat16), ('fsdp', 'ctx'), scatter_d...  153 us
    reduce_scatter x2, waiting for transfers between devices, per_device(): lax.psum_scatter(grad_query.astype(jnp.bfloat16), ('fsdp', 'ctx'), scatte...  152 us
    reduce_scatter x2, waiting for transfers between devices, per_device(): lax.psum_scatter(grad_output.astype(jnp.bfloat16), ('fsdp', 'ctx'), scatt...  151 us
    reduce_scatter x2, waiting for transfers between devices, per_device(): lax.psum_scatter(grad_gate.astype(jnp.bfloat16), ('fsdp', 'ctx'), scatter...  151 us
    reduce_scatter x2, waiting for transfers between devices, per_device(): lax.psum_scatter(grad_key.astype(jnp.bfloat16), ('fsdp', 'ctx'), scatter_...  151 us
    psum x2, waiting for transfers between devices, per_device(): lax.psum(feed_part.astype(jnp.bfloat16), 'tp').astype(jnp.float32)  121 us
    reduce_scatter x2, waiting for transfers between devices, per_device(): lax.psum_scatter(grad_value.astype(jnp.bfloat16), ('fsdp', 'ctx'), scatte...  109 us
  transfers between devices with their start and end apart: 25, of which 22 were waited for; matrix products, arithmetic and copies ran while one was open for 4% of the time, Pallas kernels for 0%

commit v1 on v0

--- a/solution.py
+++ b/solution.py
@@ -103,21 +103,37 @@
             * score_scale
         )
 
+    weight_shards = (
+        query_weight,
+        key_projection_matrix,
+        value_projection_matrix,
+        output_weight,
+        gate_weight,
+        up_weight,
+        down_weight,
+    )
+    widths = [member.shape[2] for member in weight_shards]
+    edges = [0]
+    for width in widths:
+        edges.append(edges[-1] + width)
+
+    def gather_layer(layer_index):
+        joined = jnp.concatenate([member[layer_index] for member in weight_shards], axis=1)
+        full = lax.all_gather(joined, ("fsdp", "ctx"), axis=0, tiled=True)
+        return tuple(full[:, edges[k] : edges[k + 1]] for k in range(len(widths)))
+
+    def scatter_layer(terms):
+        joined = jnp.concatenate([term.astype(jnp.bfloat16) for term in terms], axis=1)
+        owned = lax.psum_scatter(joined, ("fsdp", "ctx"), scatter_dimension=0, tiled=True)
+        return tuple(
+            owned[:, edges[k] : edges[k + 1]].astype(jnp.float32) for k in range(len(widths))
+        )
+
     kept_weights = []
     stored_layers = []
     hidden = tokens
     for layer_index in range(layer_count):
-        gathered = (
-            lax.all_gather(query_weight[layer_index], ("fsdp", "ctx"), axis=0, tiled=True),
-            lax.all_gather(key_projection_matrix[layer_index], ("fsdp", "ctx"), axis=0, tiled=True),
-            lax.all_gather(
-                value_projection_matrix[layer_index], ("fsdp", "ctx"), axis=0, tiled=True
-            ),
-            lax.all_gather(output_weight[layer_index], ("fsdp", "ctx"), axis=0, tiled=True),
-            lax.all_gather(gate_weight[layer_index], ("fsdp", "ctx"), axis=0, tiled=True),
-            lax.all_gather(up_weight[layer_index], ("fsdp", "ctx"), axis=0, tiled=True),
-            lax.all_gather(down_weight[layer_index], ("fsdp", "ctx"), axis=0, tiled=True),
-        )
+        gathered = gather_layer(layer_index)
         kept_weights.append(gathered)
         (
             forward_query_full,
@@ -217,17 +233,7 @@
     weight_sums = [None] * layer_count
     gain_parts = [None] * layer_count
     for layer_index in reversed(range(layer_count)):
-        gathered = (
-            lax.all_gather(query_weight[layer_index], ("fsdp", "ctx"), axis=0, tiled=True),
-            lax.all_gather(key_projection_matrix[layer_index], ("fsdp", "ctx"), axis=0, tiled=True),
-            lax.all_gather(
-                value_projection_matrix[layer_index], ("fsdp", "ctx"), axis=0, tiled=True
-            ),
-            lax.all_gather(output_weight[layer_index], ("fsdp", "ctx"), axis=0, tiled=True),
-            lax.all_gather(gate_weight[layer_index], ("fsdp", "ctx"), axis=0, tiled=True),
-            lax.all_gather(up_weight[layer_index], ("fsdp", "ctx"), axis=0, tiled=True),
-            lax.all_gather(down_weight[layer_index], ("fsdp", "ctx"), axis=0, tiled=True),
-        )
+        gathered = kept_weights[layer_index]
         backward_stored = stored_layers[layer_index]
         query_full, key_full, value_full, output_full, gate_full, up_full, down_full = gathered
         (
@@ -343,29 +349,7 @@
         gain_terms = (attention_gain_grad, query_gain_grad, key_gain_grad, feed_gain_grad)
         grad_flow, weight_terms, gain_terms = (source_grad, weight_terms, gain_terms)
         grad_query, grad_key, grad_value, grad_output, grad_gate, grad_up, grad_down = weight_terms
-        weight_sums[layer_index] = (
-            lax.psum_scatter(
-                grad_query.astype(jnp.bfloat16), ("fsdp", "ctx"), scatter_dimension=0, tiled=True
-            ).astype(jnp.float32),
-            lax.psum_scatter(
-                grad_key.astype(jnp.bfloat16), ("fsdp", "ctx"), scatter_dimension=0, tiled=True
-            ).astype(jnp.float32),
-            lax.psum_scatter(
-                grad_value.astype(jnp.bfloat16), ("fsdp", "ctx"), scatter_dimension=0, tiled=True
-            ).astype(jnp.float32),
-            lax.psum_scatter(
-                grad_output.astype(jnp.bfloat16), ("fsdp", "ctx"), scatter_dimension=0, tiled=True
-            ).astype(jnp.float32),
-            lax.psum_scatter(
-                grad_gate.astype(jnp.bfloat16), ("fsdp", "ctx"), scatter_dimension=0, tiled=True
-            ).astype(jnp.float32),
-            lax.psum_scatter(
-                grad_up.astype(jnp.bfloat16), ("fsdp", "ctx"), scatter_dimension=0, tiled=True
-            ).astype(jnp.float32),
-            lax.psum_scatter(
-                grad_down.astype(jnp.bfloat16), ("fsdp", "ctx"), scatter_dimension=0, tiled=True
-            ).astype(jnp.float32),
-        )
+        weight_sums[layer_index] = scatter_layer(weight_terms)
         gain_parts[layer_index] = gain_terms
     gain_totals = lax.psum(
         (

time: 2170 us -> 1070 us (0.49)
  waiting for transfers between devices: 1300 us -> 596 us
  blocking collectives: 668 us -> 245 us
  local copies, waits for them, and re-layouts: 32.9 us -> 62 us
    reduce_scatter x14 -> x0, waiting for transfers between devices: 1020 us -> none  [the longest x2 154 us: per_device(): lax.psum_scatter(grad_down.astype(jnp.bfloat16), ('fsdp', 'ctx'), scatter...]
    all_gather x14 -> x0, blocking collectives: 576 us -> none  [the longest x2 86.4 us: per_device(): lax.all_gather(down_weight[layer_index], ('fsdp', 'ctx'), axis=0, tiled=T...]
    all_gather x0 -> x2, waiting for transfers between devices: none -> 186 us  [gather_layer(): full = lax.all_gather(joined, ('fsdp', 'ctx'), axis=0, tiled=True)]
    psum x1, blocking collectives: 63.3 us -> 217 us  [per_device(): lax.psum((jnp.stack([member[0] for member in gain_parts]), jnp.stack([mem...]
    psum x2, waiting for transfers between devices: 0.01 us -> 119 us  [per_device(): lax.psum(contract_last(forward_attended, forward_output_full).astype(jnp....]
    unnamed x306 -> x259, local copies, waits for them, and re-layouts: 21.3 us -> 49.8 us
    psum x2, waiting for transfers between devices: 62.1 us -> 89.4 us  [per_device(): lax.psum(contract_last(forward_activated, forward_down_full).astype(jnp.b...]
  transfers between devices with their start and end apart: 25 -> 15, of which waited for: 22 -> 13; matrix products, arithmetic and copies ran while one was open for 4% -> 9% of each run, Pallas kernels for 0% -> 0%
where the time goes in v1:
time: 1070 us; the launch traced here: 1060 us
  waiting for transfers between devices  596 us (56%)
  blocking collectives  245 us (23%)
  matrix products  86 us (8%)
  local copies, waits for them, and re-layouts  62 us (6%)
  other arithmetic  54.6 us (5%)
  between operations  15.9 us (1%)
    psum x1, blocking collectives, per_device(): lax.psum((jnp.stack([member[0] for member in gain_parts]), jnp.stack([mem...  217 us
    all_gather x2, waiting for transfers between devices, gather_layer(): full = lax.all_gather(joined, ('fsdp', 'ctx'), axis=0, tiled=True)  186 us
    psum x2, waiting for transfers between devices, per_device(): lax.psum(contract_last(forward_attended, forward_output_full).astype(jnp....  119 us
    psum x2, waiting for transfers between devices, per_device(): lax.psum(feed_part.astype(jnp.bfloat16), 'tp').astype(jnp.float32)  114 us
    psum x2, waiting for transfers between devices, per_device(): lax.psum(contract_last(forward_activated, forward_down_full).astype(jnp.b...  89.4 us
    psum x1, waiting for transfers between devices, per_device(): lax.psum(attention_part.astype(jnp.bfloat16), 'tp').astype(jnp.float32)  57.3 us
    unnamed x259, local copies, waits for them, and re-layouts  49.8 us
    unnamed x21, waiting for transfers between devices  30.6 us
  transfers between devices with their start and end apart: 15, of which 13 were waited for; matrix products, arithmetic and copies ran while one was open for 9% of the time, Pallas kernels for 0%

profile of v1, /device:TPU:0, one launch (start us, length us, event | category | flops | bytes accessed | tf_op | source)
XLA Modules:
  0.0 1061.2 jit_solution(11207653772478920009)
XLA Ops:
  15.2 1.6 multiply_reduce_fusion.7
  20.0 92.1 %all-gather.3.cloned.1.call-done = bf16[1024,1920]{1,0:T(8,128)(2,1)} async-done(((bf16[64,1920]{1,0:T(8,128)(2,1)}), bf16[1024,1920]{1,0:T(8,128)(2,1)}) %all-gather.3.cloned.1.call-update) | async-done | bytes 3932176 | tf_op jit(solution)/shard_map/all_gather | solution.py:122
  113.5 7.1 all_gather.19
  122.5 6.9 all_gather.20
  129.4 2.3 multiply_reduce_fusion.11
  136.3 2.4 convolution_convert_fusion.1
  138.8 59.5 %all-reduce.10.cloned.1.call-done = bf16[384,1024]{1,0:T(8,128)(2,1)} async-done(((bf16[384,1024]{1,0:T(8,128)(2,1)}), bf16[384,1024]{1,0:T(8,128)(2,1)}) %all-reduce.10.cloned.1.call-update) | async-done | bytes 786448 | tf_op jit(solution)/shard_map/psum | solution.py:191
  201.3 1.5 copy-done.30
  207.1 60.4 %all-reduce.12.cloned.1.call-done = bf16[384,1024]{1,0:T(8,128)(2,1)} async-done(((bf16[384,1024]{1,0:T(8,128)(2,1)}), bf16[384,1024]{1,0:T(8,128)(2,1)}) %all-reduce.12.cloned.1.call-update) | async-done | bytes 786448 | tf_op jit(solution)/shard_map/psum | solution.py:207
  267.5 1.8 multiply_reduce_fusion.5
  270.6 93.4 %all-gather.5.cloned.1.call-done = bf16[1024,1920]{1,0:T(8,128)(2,1)} async-done(((bf16[64,1920]{1,0:T(8,128)(2,1)}), bf16[1024,1920]{1,0:T(8,128)(2,1)}) %all-gather.5.cloned.1.call-update) | async-done | bytes 3932176 | tf_op jit(solution)/shard_map/all_gather | solution.py:122
  365.4 6.9 all_gather.22
  374.3 7.1 all_gather.23
  381.4 1.6 multiply_reduce_fusion.10
  387.2 2.4 convolution_convert_fusion
  389.7 59.8 %all-reduce.14.cloned.1.call-done = bf16[384,1024]{1,0:T(8,128)(2,1)} async-done(((bf16[384,1024]{1,0:T(8,128)(2,1)}), bf16[384,1024]{1,0:T(8,128)(2,1)}) %all-reduce.14.cloned.1.call-update) | async-done | bytes 786448 | tf_op jit(solution)/shard_map/psum | solution.py:191
  451.3 2.6 copy-done.32
  460.9 2.7 convolution_convert_fusion.8
  463.6 57.6 %all-reduce.16.cloned.1.call-done = bf16[384,1024]{1,0:T(8,128)(2,1)} async-done(((bf16[384,1024]{1,0:T(8,128)(2,1)}), bf16[384,1024]{1,0:T(8,128)(2,1)}) %all-reduce.16.cloned.1.call-update) | async-done | bytes 786448 | tf_op jit(solution)/shard_map/psum | solution.py:270
  521.3 1.6 multiply_reduce_fusion.3
  523.2 2.0 multiply_add_fusion.3
  525.2 1.5 convolution_convert_fusion.19
  532.6 1.7 copy.177
  534.4 1.7 copy.175
  538.7 1.9 copy.133
  540.9 1.8 fusion.84
  543.4 2.7 fusion.69
  546.1 4.6 reduce-scatter.19.cloned.1.call-done
  552.8 1.6 multiply_reduce_fusion.14
  555.4 2.5 fusion.93
  557.9 9.4 reduce-scatter.21.cloned.1.call-done
  567.4 3.3 add_convert_fusion.2
  570.8 2.6 fusion.25
  574.3 57.3 %all-reduce.18.cloned.1.call-done = bf16[384,1024]{1,0:T(8,128)(2,1)} async-done(((bf16[384,1024]{1,0:T(8,128)(2,1)}), bf16[384,1024]{1,0:T(8,128)(2,1)}) %all-reduce.18.cloned.1.call-update) | async-done | bytes 786448 | tf_op jit(solution)/shard_map/psum | solution.py:334
  631.7 2.0 multiply_reduce_fusion.2
  634.4 2.2 copy-done.31
  640.1 2.2 fusion.29
  642.2 2.2 fusion.26
  644.4 56.6 %all-reduce.20.cloned.1.call-done = bf16[384,1024]{1,0:T(8,128)(2,1)} async-done(((bf16[384,1024]{1,0:T(8,128)(2,1)}), bf16[384,1024]{1,0:T(8,128)(2,1)}) %all-reduce.20.cloned.1.call-update) | async-done | bytes 786448 | tf_op jit(solution)/shard_map/psum | solution.py:270
  701.0 2.0 multiply_reduce_fusion.1
  703.4 2.0 multiply_add_fusion.1
  705.3 1.5 convolution_convert_fusion.18
  712.9 1.8 copy.181
  714.6 1.7 copy.179
  716.4 2.2 multiply_subtract_fusion
  718.6 2.9 multiply_reduce_fusion.8
  721.5 1.9 copy.141
  724.5 1.7 fusion.82
  726.9 2.7 fusion.75
  729.6 3.5 reduce-scatter.23.cloned.1.call-done
  734.9 2.5 fusion.99
  737.4 12.3 %reduce-scatter.25.cloned.1.call-done = bf16[384,128]{1,0:T(8,128)(2,1)} async-done(((bf16[768,128]{1,0:T(8,128)(2,1)}), bf16[384,128]{1,0:T(8,128)(2,1)}) %reduce-scatter.25.cloned.1.call-update) | async-done | bytes 98320
  749.7 3.3 add_convert_fusion
  753.1 2.8 fusion.17
  755.9 2.7 fusion.16
  758.6 1.5 fusion.22
  760.1 6.3 copy.185
  766.6 2.6 fusion.23
  777.0 6.3 copy.183
  787.5 29.0 %all-reduce.22.cloned.1.call-done = (bf16[384,1024]{1,0:T(8,128)(2,1)}, bf16[384,1024]{1,0:T(8,128)(2,1)}) async-done(((bf16[384,1024]{1,0:T(8,128)(2,1)}, bf16[384,1024]{1,0:T(8,128)(2,1)}), (bf16[384,1024]{1,0:T(8,128)(2,1)}, bf16[384,1024]{1,0:T(8,128)(2,1)})) %all-reduce.22.cloned.1.call-update) | async-done | bytes 1572880 | tf_op jit(solution)/shard_map/psum | solution.py:207
  818.9 217.3 %all-reduce = (f32[2,1024]{1,0:T(2,128)}, f32[2,128]{1,0:T(2,128)}, f32[2,128]{1,0:T(2,128)}, f32[2,1024]{1,0:T(2,128)}) all-reduce(f32[2,1024]{1,0:T(2,128)S(1)} %pad_maximum_fusion.12, f32[2,128]{1,0:T(2,128)S(1)} %get-tuple-element.173, ...), channel_id=1, replica_groups=mesh['fsdp'=8,'ctx'=2,'tp'=8] {'fsdp','ctx','tp'}, use_global_device_ids=true, to_apply=%region_34.35 | all-reduce | flops 4608 | bytes 36864 | tf_op jit(solution)/shard_map/psum | solution.py:354
  1036.2 2.0 multiply_reduce_fusion
  1038.2 1.6 convert_add_fusion
  1040.4 1.5 multiply_add_fusion
  (411 shorter events, 98.2 us)
Async XLA Ops:
  7.2 9.6 copy-start.105
  7.2 9.6 copy-start.106
  7.2 9.7 copy-start.100
  7.2 104.9 %all-gather.3.cloned.1.call-start = ((), (), s32[]{:S(2)}) async-start(), calls=%async_computation.6 | async-start | bytes 4177920 | tf_op jit(solution)/shard_map/all_gather | solution.py:122
  11.2 7.5 copy-start
  13.0 5.7 copy-start.71
  13.7 184.7 %all-reduce.10.cloned.1.call-start = ((), (), s32[]{:S(2)}) async-start(), calls=%async_computation.7 | async-start | bytes 1572864 | tf_op jit(solution)/shard_map/psum | solution.py:191
  15.2 358.6 %copy-start.95 = (f32[64]{0:T(128)}, f32[64]{0:T(128)S(1)}, u32[]{:S(2)}) copy-start(f32[64]{0:T(128)S(1)} %multiply_power_fusion) | copy-start | bytes 772
  16.8 443.5 %copy-start.102 = (f32[128]{0:T(128)}, f32[128]{0:T(128)S(1)}, u32[]{:S(2)}) copy-start(f32[128]{0:T(128)S(1)} %get-tuple-element.150) | copy-start | bytes 1540
  16.8 105.1 %copy-start.97 = (f32[128]{0:T(128)}, f32[128]{0:T(128)S(1)}, u32[]{:S(2)}) copy-start(f32[128]{0:T(128)S(1)} %get-tuple-element.152) | copy-start | bytes 1540
  16.9 356.8 %copy-start.99 = (f32[128]{0:T(128)}, f32[128]{0:T(128)S(1)}, u32[]{:S(2)}) copy-start(f32[128]{0:T(128)S(1)} %get-tuple-element.151) | copy-start | bytes 1540
  16.9 3.1 copy-start.91
  18.6 114.5 %copy-start.27 = (f32[384,64]{1,0:T(8,128)}, f32[384,64]{1,0:T(8,128)S(1)}, u32[]{:S(2)}) copy-start(f32[384,64]{1,0:T(8,128)S(1)} %get-tuple-element.148) | copy-start | bytes 294916
  18.6 114.5 %copy-start.39 = (f32[384,64]{1,0:T(8,128)}, f32[384,64]{1,0:T(8,128)S(1)}, u32[]{:S(2)}) copy-start(f32[384,64]{1,0:T(8,128)S(1)} %get-tuple-element.147) | copy-start | bytes 294916
  20.0 109.4 %copy-start.7 = (bf16[384,1024]{1,0:T(8,128)(2,1)}, bf16[384,1024]{1,0:T(8,128)(2,1)S(1)}, u32[]{:S(2)}) copy-start(bf16[384,1024]{1,0:T(8,128)(2,1)S(1)} %get-tuple-element.87) | copy-start | bytes 2359300
  121.9 11.0 %copy-start.36 = (f32[384,128]{0,1:T(8,128)}, f32[384,128]{0,1:T(8,128)S(1)}, u32[]{:S(2)}) copy-start(f32[384,128]{0,1:T(8,128)S(1)} %get-tuple-element.154) | copy-start | bytes 589828
  121.9 9.8 copy-start.84
  138.8 128.7 %all-reduce.12.cloned.1.call-start = ((), (), s32[]{:S(2)}) async-start(), calls=%async_computation.8 | async-start | bytes 1572864 | tf_op jit(solution)/shard_map/psum | solution.py:207
  199.9 3.0 copy-start.30
  201.3 3.6 copy-start.48
  206.5 157.6 %all-gather.5.cloned.1.call-start = ((), (), s32[]{:S(2)}) async-start(), calls=%async_computation.9 | async-start | bytes 4177920 | tf_op jit(solution)/shard_map/all_gather | solution.py:122
  207.0 242.5 %all-reduce.14.cloned.1.call-start = ((), (), s32[]{:S(2)}) async-start(), calls=%async_computation.10 | async-start | bytes 1572864 | tf_op jit(solution)/shard_map/psum | solution.py:191
  270.6 110.7 %copy-start.9 = (bf16[384,1024]{1,0:T(8,128)(2,1)}, bf16[384,1024]{1,0:T(8,128)(2,1)S(1)}, u32[]{:S(2)}) copy-start(bf16[384,1024]{1,0:T(8,128)(2,1)S(1)} %get-tuple-element.81) | copy-start | bytes 2359300
  373.6 9.3 copy-start.86
  387.2 63.8 %copy-start.66 = (bf16[128,2,384]{2,0,1:T(8,128)(2,1)}, bf16[128,2,384]{2,0,1:T(8,128)(2,1)S(1)}, u32[]{:S(2)}) copy-start(bf16[128,2,384]{2,0,1:T(8,128)(2,1)S(1)} %convolution_convert_fusion.20) | copy-start | bytes 589828
  389.6 131.6 %all-reduce.16.cloned.1.call-start = ((), (), s32[]{:S(2)}) async-start(), calls=%async_computation.11 | async-start | bytes 1572864 | tf_op jit(solution)/shard_map/psum | solution.py:270
  451.0 3.0 copy-start.32
  451.3 3.8 copy-start.50
  451.3 70.0 %copy-start.4 = (f32[384,1024]{1,0:T(8,128)}, f32[384,1024]{1,0:T(8,128)S(1)}, u32[]{:S(2)}) copy-start(f32[384,1024]{1,0:T(8,128)S(1)} %get-tuple-element.80) | copy-start | bytes 4718596
  460.3 90.4 %reduce-scatter.19.cloned.1.call-start = ((), (), s32[]{:S(2)}) async-start(), calls=%async_computation.14 | async-start | bytes 294912
  523.2 3.5 copy-start.14
  536.1 31.2 %reduce-scatter.21.cloned.1.call-start = ((), (), s32[]{:S(2)}) async-start(), calls=%async_computation.15 | async-start | bytes 294912
  540.6 91.0 %all-reduce.18.cloned.1.call-start = ((), (), s32[]{:S(2)}) async-start(), calls=%async_computation.12 | async-start | bytes 1572864 | tf_op jit(solution)/shard_map/psum | solution.py:334
  570.7 130.3 %all-reduce.20.cloned.1.call-start = ((), (), s32[]{:S(2)}) async-start(), calls=%async_computation.13 | async-start | bytes 1572864 | tf_op jit(solution)/shard_map/psum | solution.py:270
  570.8 2.6 copy-start.10
  574.3 59.4 %copy-start.94 = (f32[384]{0:T(512)S(1)}, f32[384]{0:T(512)}, u32[]{:S(2)}) copy-start(f32[384]{0:T(512)} %copy-done.93) | copy-start | bytes 4612
  634.0 2.7 copy-start.31
  634.0 2.8 copy-start.110
  634.0 3.0 copy-start.111
  634.4 3.3 copy-start.5
  640.0 93.1 %reduce-scatter.23.cloned.1.call-start = ((), (), s32[]{:S(2)}) async-start(), calls=%async_computation.16 | async-start | bytes 294912
  644.4 58.7 %copy-start.90 = (f32[384]{0:T(512)S(1)}, f32[384]{0:T(512)}, u32[]{:S(2)}) copy-start(f32[384]{0:T(512)} %copy-done.89) | copy-start | bytes 4612
  703.4 3.5 copy-start.12
  711.5 4.9 copy-start.29
  711.5 4.9 copy-start.41
  712.9 5.8 copy-start.83
  712.9 5.8 copy-start.103
  718.6 5.9 copy-start.42
  718.6 31.1 %reduce-scatter.25.cloned.1.call-start = ((), (), s32[]{:S(2)}) async-start(), calls=%async_computation.17 | async-start | bytes 294912
  724.2 92.3 %all-reduce.22.cloned.1.call-start = ((), (), s32[]{:S(2)}) async-start(), calls=%async_computation.20 | async-start | bytes 3145728 | tf_op jit(solution)/shard_map/psum | solution.py:207
  726.2 7.9 copy-start.96
  726.9 7.7 copy-start.37
  726.9 7.7 copy-start.85
  726.9 7.7 copy-start.98
  753.0 289.0 %reduce-scatter.29.cloned.1.call-start = ((), (), s32[]{:S(2)}) async-start(), calls=%async_computation.19 | async-start | bytes 4177920
  753.0 5.6 copy-start.26
  753.0 5.6 copy-start.75
  766.5 3.7 copy-start.70
  766.5 4.7 copy-start.65
  766.5 278.7 %reduce-scatter.27.cloned.1.call-start = ((), (), s32[]{:S(2)}) async-start(), calls=%async_computation.18 | async-start | bytes 4177920
  766.6 2.6 copy-start.8
  771.3 2.7 copy-start.79
  772.5 3.0 copy-start.6
  772.5 3.0 copy-start.74
  (63 other events, 97.8 us)
Sparse Core Ops, SparseCore 0:
  13.8 98.2 all-gather.2
  138.9 59.4 all-reduce.9
  206.6 60.8 all-reduce.11
  269.0 95.0 all-gather.4
  389.8 59.6 all-reduce.13
  460.4 60.8 all-reduce.15
  536.3 14.3 reduce-scatter.18
  553.0 14.3 reduce-scatter.20
  570.8 60.7 all-reduce.17
  640.2 60.8 all-reduce.19
  718.7 14.3 reduce-scatter.22
  735.3 14.3 reduce-scatter.24
  753.1 63.3 all-reduce.21
  818.8 97.0 reduce-scatter.28
  918.4 94.0 reduce-scatter.26

commit v2 on v1

--- a/solution.py
+++ b/solution.py
@@ -48,6 +48,36 @@
         ],
         axis=-1,
     )
+
+
+def tp_sum(term):
+    tp_count = lax.axis_size("tp")
+    tp_index = lax.axis_index("tp")
+    current = term.astype(jnp.bfloat16)
+    bits = []
+    step = 1
+    while step < tp_count:
+        bits.append(step)
+        step *= 2
+    for step in bits:
+        half = current.shape[0] // 2
+        upper = (tp_index // step) % 2
+        kept = lax.dynamic_slice_in_dim(current, upper * half, half, 0)
+        sent = lax.dynamic_slice_in_dim(current, (1 - upper) * half, half, 0)
+        pairs = [(device, device ^ step) for device in range(tp_count)]
+        received = lax.ppermute(sent.astype(jnp.bfloat16), "tp", pairs)
+        current = kept.astype(jnp.float32) + received.astype(jnp.float32)
+    current = current.astype(jnp.bfloat16)
+    for step in reversed(bits):
+        upper = (tp_index // step) % 2
+        pairs = [(device, device ^ step) for device in range(tp_count)]
+        received = lax.ppermute(current, "tp", pairs)
+        current = jnp.where(
+            upper == 0,
+            jnp.concatenate([current, received], axis=0),
+            jnp.concatenate([received, current], axis=0),
+        )
+    return current.astype(jnp.float32)
 
 
 def per_device(
@@ -188,9 +218,7 @@
         forward_attended = forward_attended.astype(jnp.bfloat16).reshape(
             row_count, local_heads * head_size
         )
-        forward_middle = hidden + lax.psum(
-            contract_last(forward_attended, forward_output_full).astype(jnp.bfloat16), "tp"
-        ).astype(jnp.float32)
+        forward_middle = hidden + tp_sum(contract_last(forward_attended, forward_output_full))
         forward_scale_two = row_scale(forward_middle)
         forward_feed_normed = (
             forward_middle * forward_scale_two * feedforward_gain[layer_index]
@@ -204,9 +232,7 @@
         forward_activated = (jax.nn.silu(forward_gate_linear) * forward_up_linear).astype(
             jnp.bfloat16
         )
-        result = forward_middle + lax.psum(
-            contract_last(forward_activated, forward_down_full).astype(jnp.bfloat16), "tp"
-        ).astype(jnp.float32)
+        result = forward_middle + tp_sum(contract_last(forward_activated, forward_down_full))
         forward_stored = (
             hidden,
             forward_scale_one,
@@ -267,7 +293,7 @@
         gate_weight_grad = contract_first(feed_normed, gate_grad)
         up_weight_grad = contract_first(feed_normed, up_grad)
         feed_part = contract_last(gate_grad, gate_full) + contract_last(up_grad, up_full)
-        feed_grad = lax.psum(feed_part.astype(jnp.bfloat16), "tp").astype(jnp.float32)
+        feed_grad = tp_sum(feed_part)
         feed_unit = middle * scale_two
         feed_gain_grad = column_share(feed_grad, feed_unit)
         middle_grad = grad_flow + norm_back(
@@ -331,7 +357,7 @@
             + contract_last(key_pre, key_full)
             + contract_last(value_own, value_full)
         )
-        normed_grad = lax.psum(attention_part.astype(jnp.bfloat16), "tp").astype(jnp.float32)
+        normed_grad = tp_sum(attention_part)
         source_unit = source * scale_one
         attention_gain_grad = column_share(normed_grad, source_unit)
         source_grad = middle_grad + norm_back(

time: 1070 us -> 729 us (0.68)
  waiting for transfers between devices: 596 us -> 282 us
  blocking collectives: 245 us -> 169 us
  starting transfers between devices: 1.08 us -> 73.1 us
  matrix products: 86 us -> 69 us
  other arithmetic: 54.6 us -> 43.8 us
    psum x7 -> x0, waiting for transfers between devices: 380 us -> none  [the longest x2 119 us: per_device(): lax.psum(contract_last(forward_attended, forward_output_full).astype(jnp....]
    ppermute x0 -> x48, waiting for transfers between devices: none -> 150 us  [the longest x24 80.6 us: tp_sum(): received = lax.ppermute(sent.astype(jnp.bfloat16), 'tp', pairs)]
    psum x1, blocking collectives: 217 us -> 141 us  [per_device(): lax.psum((jnp.stack([member[0] for member in gain_parts]), jnp.stack([mem...]
    ppermute x0 -> x48, starting transfers between devices: none -> 72.7 us  [the longest x24 38.1 us: tp_sum(): received = lax.ppermute(sent.astype(jnp.bfloat16), 'tp', pairs)]
    all_gather x2, waiting for transfers between devices: 186 us -> 117 us  [gather_layer(): full = lax.all_gather(joined, ('fsdp', 'ctx'), axis=0, tiled=True)]
    unnamed x21 -> x14, waiting for transfers between devices: 30.6 us -> 14.4 us
    dot_general x14, matrix products: 30.2 us -> 18.8 us  [contract_last(): lax.dot_general(left_side, right_side, (((1,), (1,)), ((), ())), preferre...]
    unnamed x259 -> x283, local copies, waits for them, and re-layouts: 49.8 us -> 50.5 us
  transfers between devices with their start and end apart: 15 -> 56, of which waited for: 13 -> 49; matrix products, arithmetic and copies ran while one was open for 9% -> 14% of each run, Pallas kernels for 0% -> 0%
where the time goes in v2:
time: 729 us; the launch traced here: 718 us
  waiting for transfers between devices  282 us (39%)
  blocking collectives  169 us (23%)
  starting transfers between devices  73.1 us (10%)
  matrix products  69 us (9%)
  local copies, waits for them, and re-layouts  64.1 us (9%)
  other arithmetic  43.8 us (6%)
  between operations  17.1 us (2%)
    psum x1, blocking collectives, per_device(): lax.psum((jnp.stack([member[0] for member in gain_parts]), jnp.stack([mem...  141 us
    all_gather x2, waiting for transfers between devices, gather_layer(): full = lax.all_gather(joined, ('fsdp', 'ctx'), axis=0, tiled=True)  117 us
    ppermute x24, waiting for transfers between devices, tp_sum(): received = lax.ppermute(sent.astype(jnp.bfloat16), 'tp', pairs)  80.6 us
    ppermute x24, waiting for transfers between devices, tp_sum(): received = lax.ppermute(current, 'tp', pairs)  69.8 us
    unnamed x283, local copies, waits for them, and re-layouts  50.5 us
    ppermute x24, starting transfers between devices, tp_sum(): received = lax.ppermute(sent.astype(jnp.bfloat16), 'tp', pairs)  38.1 us
    ppermute x24, starting transfers between devices, tp_sum(): received = lax.ppermute(current, 'tp', pairs)  34.7 us
    dot_general x14, matrix products, contract_first(): lax.dot_general(left_side, right_side, (((0,), (0,)), ((), ())), preferre...  21 us
  transfers between devices with their start and end apart: 56, of which 49 were waited for; matrix products, arithmetic and copies ran while one was open for 14% of the time, Pallas kernels for 0%

profile of v2, /device:TPU:0, one launch (start us, length us, event | category | flops | bytes accessed | tf_op | source)
XLA Modules:
  0.0 717.6 jit_solution(1211582188195193987)
XLA Ops:
  24.3 92.1 %all-gather.3.cloned.1.call-done = bf16[1024,1920]{1,0:T(8,128)(2,1)} async-done(((bf16[64,1920]{1,0:T(8,128)(2,1)}), bf16[1024,1920]{1,0:T(8,128)(2,1)}) %all-gather.3.cloned.1.call-update) | async-done | bytes 3932176 | tf_op jit(solution)/shard_map/all_gather | solution.py:152
  117.7 7.1 all_gather.19
  126.7 6.9 all_gather.20
  145.9 6.2 collective-permute-done.1
  152.2 2.4 collective-permute-start.2
  154.6 3.8 collective-permute-done.2
  158.4 2.4 collective-permute-start.3
  160.8 3.8 collective-permute-done.3
  165.5 4.9 collective-permute-done.4
  181.9 6.2 collective-permute-done.7
  188.2 2.3 collective-permute-start.8
  190.5 3.9 collective-permute-done.8
  196.8 3.9 collective-permute-done.9
  201.4 5.0 collective-permute-done.10
  210.6 25.1 %all-gather.5.cloned.1.call-done = bf16[1024,1920]{1,0:T(8,128)(2,1)} async-done(((bf16[64,1920]{1,0:T(8,128)(2,1)}), bf16[1024,1920]{1,0:T(8,128)(2,1)}) %all-gather.5.cloned.1.call-update) | async-done | bytes 3932176 | tf_op jit(solution)/shard_map/all_gather | solution.py:152
  237.1 6.9 all_gather.22
  245.9 6.9 all_gather.23
  261.7 5.7 collective-permute-done.13
  267.4 2.9 collective-permute-start.14
  270.3 3.3 collective-permute-done.14
  273.6 2.9 collective-permute-start.15
  276.6 3.3 collective-permute-done.15
  281.2 4.4 collective-permute-done.16
  295.2 5.7 collective-permute-done.25
  301.0 3.3 collective-permute-start.26
  304.2 2.9 collective-permute-done.26
  307.2 3.3 collective-permute-start.27
  310.5 2.9 collective-permute-done.27
  314.8 4.4 collective-permute-done.28
  339.1 2.6 fusion.73
  341.7 5.1 reduce-scatter.19.cloned.1.call-done
  351.6 2.6 fusion.97
  354.2 9.1 %reduce-scatter.21.cloned.1.call-done = bf16[384,128]{1,0:T(8,128)(2,1)} async-done(((bf16[768,128]{1,0:T(8,128)(2,1)}), bf16[384,128]{1,0:T(8,128)(2,1)}) %reduce-scatter.21.cloned.1.call-update) | async-done | bytes 98320
  363.3 2.4 add_convert_fusion.2
  369.3 5.5 collective-permute-done.31
  374.8 3.1 collective-permute-start.32
  377.9 3.1 collective-permute-done.32
  381.0 3.1 collective-permute-start.33
  384.1 3.1 collective-permute-done.33
  388.9 4.2 collective-permute-done.34
  404.2 5.5 collective-permute-done.37
  409.7 3.4 collective-permute-start.38
  413.1 2.8 collective-permute-done.38
  415.9 3.4 collective-permute-start.39
  419.8 2.4 collective-permute-done.39
  424.1 3.9 collective-permute-done.40
  438.8 2.7 fusion.17
  441.5 3.1 fusion.42
  446.5 2.8 fusion.16
  450.9 6.1 copy.185
  467.4 2.4 fusion.23
  482.2 6.3 copy.183
  491.4 5.3 collective-permute-done.19
  496.8 4.1 collective-permute-start.20
  500.8 2.6 collective-permute-done.20
  503.5 3.6 collective-permute-start.21
  507.1 2.6 collective-permute-done.21
  510.9 4.7 collective-permute-done.22
  526.0 5.8 collective-permute-done.43
  531.9 4.1 collective-permute-start.44
  536.0 2.6 collective-permute-done.44
  538.6 3.6 collective-permute-start.45
  545.8 5.3 collective-permute-done.46
  553.8 140.7 %all-reduce = (f32[2,1024]{1,0:T(2,128)}, f32[2,128]{1,0:T(2,128)}, f32[2,128]{1,0:T(2,128)}, f32[2,1024]{1,0:T(2,128)}) all-reduce(f32[2,1024]{1,0:T(2,128)S(1)} %get-tuple-element.169, f32[2,128]{1,0:T(2,128)S(1)} %get-tuple-element.171, ...), channel_id=1, replica_groups=mesh['fsdp'=8,'ctx'=2,'tp'=8] {'fsdp','ctx','tp'}, use_global_device_ids=true, to_apply=%region_26.27 | all-reduce | flops 4608 | bytes 36864 | tf_op jit(solution)/shard_map/psum | solution.py:380
  (574 shorter events, 192.3 us)
Async XLA Ops:
  7.2 109.2 %all-gather.3.cloned.1.call-start = ((), (), s32[]{:S(2)}) async-start(), calls=%async_computation.6 | async-start | bytes 4177920 | tf_op jit(solution)/shard_map/all_gather | solution.py:152
  17.9 217.8 %all-gather.5.cloned.1.call-start = ((), (), s32[]{:S(2)}) async-start(), calls=%async_computation.7 | async-start | bytes 4177920 | tf_op jit(solution)/shard_map/all_gather | solution.py:152
  19.4 226.0 %copy-start.106 = (f32[64]{0:T(128)}, f32[64]{0:T(128)S(1)}, u32[]{:S(2)}) copy-start(f32[64]{0:T(128)S(1)} %multiply_power_fusion) | copy-start | bytes 772
  21.1 116.1 %copy-start.113 = (f32[128]{0:T(128)}, f32[128]{0:T(128)S(1)}, u32[]{:S(2)}) copy-start(f32[128]{0:T(128)S(1)} %get-tuple-element.148) | copy-start | bytes 1540
  21.1 105.1 %copy-start.108 = (f32[128]{0:T(128)}, f32[128]{0:T(128)S(1)}, u32[]{:S(2)}) copy-start(f32[128]{0:T(128)S(1)} %get-tuple-element.150) | copy-start | bytes 1540
  21.1 224.2 %copy-start.110 = (f32[128]{0:T(128)}, f32[128]{0:T(128)S(1)}, u32[]{:S(2)}) copy-start(f32[128]{0:T(128)S(1)} %get-tuple-element.149) | copy-start | bytes 1540
  22.9 114.4 %copy-start.30 = (f32[384,64]{1,0:T(8,128)}, f32[384,64]{1,0:T(8,128)S(1)}, u32[]{:S(2)}) copy-start(f32[384,64]{1,0:T(8,128)S(1)} %get-tuple-element.146) | copy-start | bytes 294916
  22.9 114.4 %copy-start.55 = (f32[384,64]{1,0:T(8,128)}, f32[384,64]{1,0:T(8,128)S(1)}, u32[]{:S(2)}) copy-start(f32[384,64]{1,0:T(8,128)S(1)} %get-tuple-element.145) | copy-start | bytes 294916
  24.3 109.4 %copy-start.9 = (bf16[384,1024]{1,0:T(8,128)(2,1)}, bf16[384,1024]{1,0:T(8,128)(2,1)S(1)}, u32[]{:S(2)}) copy-start(bf16[384,1024]{1,0:T(8,128)(2,1)S(1)} %get-tuple-element.85) | copy-start | bytes 2359300
  142.0 1.9 collective-permute-start
  142.2 204.6 %reduce-scatter.19.cloned.1.call-start = ((), (), s32[]{:S(2)}) async-start(), calls=%async_computation.8 | async-start | bytes 294912
  145.1 7.0 collective-permute-start.1
  152.2 6.2 collective-permute-start.2
  158.4 6.2 collective-permute-start.3
  164.7 5.7 collective-permute-start.4
  170.5 1.8 collective-permute-start.5
  179.1 1.8 collective-permute-start.6
  181.1 7.0 collective-permute-start.7
  188.2 6.2 collective-permute-start.8
  194.4 6.2 collective-permute-start.9
  200.7 5.7 collective-permute-start.10
  206.5 2.0 collective-permute-start.11
  258.3 1.8 collective-permute-start.12
  260.3 7.0 collective-permute-start.13
  267.4 6.2 collective-permute-start.14
  273.6 6.2 collective-permute-start.15
  279.9 5.7 collective-permute-start.16
  285.7 1.8 collective-permute-start.17
  291.9 1.8 collective-permute-start.24
  293.9 7.0 collective-permute-start.25
  301.0 6.2 collective-permute-start.26
  307.2 6.2 collective-permute-start.27
  313.4 5.7 collective-permute-start.28
  319.3 2.2 collective-permute-start.29
  332.0 31.3 %reduce-scatter.21.cloned.1.call-start = ((), (), s32[]{:S(2)}) async-start(), calls=%async_computation.9 | async-start | bytes 294912
  336.5 133.3 %reduce-scatter.23.cloned.1.call-start = ((), (), s32[]{:S(2)}) async-start(), calls=%async_computation.10 | async-start | bytes 294912
  365.8 1.8 collective-permute-start.30
  367.7 7.0 collective-permute-start.31
  374.8 6.2 collective-permute-start.32
  381.0 6.2 collective-permute-start.33
  387.3 5.7 collective-permute-start.34
  393.1 1.8 collective-permute-start.35
  400.5 1.8 collective-permute-start.36
  402.4 7.2 %collective-permute-start.37 = (bf16[96,1024]{1,0:T(8,128)(2,1)S(1)}, bf16[96,1024]{1,0:T(8,128)(2,1)S(1)}, u32[]{:S(2)}, u32[]{:S(2)}) collective-permute-start(bf16[96,1024]{1,0:T(8,128)(2,1)S(1)} %dynamic-slice_convert_fusion.1), channel_id=1, source_target_pairs={{0,2},{1,3},{2,0},{3,1},{4,6},{5,7},{6,4},{7,5},{8,10},{9,11},{10,... | collective-permute-start | bytes 589832 | tf_op jit(solution)/shard_map/ppermute | solution.py:68
  409.7 6.2 collective-permute-start.38
  415.9 6.2 collective-permute-start.39
  422.2 5.7 collective-permute-start.40
  428.0 1.8 collective-permute-start.41
  438.7 34.4 %reduce-scatter.25.cloned.1.call-start = ((), (), s32[]{:S(2)}) async-start(), calls=%async_computation.11 | async-start | bytes 294912
  446.5 251.5 %reduce-scatter.29.cloned.1.call-start = ((), (), s32[]{:S(2)}) async-start(), calls=%async_computation.13 | async-start | bytes 4177920
  457.0 244.3 %reduce-scatter.27.cloned.1.call-start = ((), (), s32[]{:S(2)}) async-start(), calls=%async_computation.12 | async-start | bytes 4177920
  460.3 28.2 %collective-permute-start.18 = (bf16[192,1024]{1,0:T(8,128)(2,1)}, bf16[192,1024]{1,0:T(8,128)(2,1)}, u32[]{:S(2)}, u32[]{:S(2)}) collective-permute-start(bf16[192,1024]{1,0:T(8,128)(2,1)} %constant_dynamic-slice_fusion.4), channel_id=1, source_target_pairs={{0,1},{1,0},{2,3},{3,2},{4,5},{5,4},{6,7},{7,6},{8,9},{9,8},{10,11... | collective-permute-start | bytes 1179656 | tf_op jit(solution)/shard_map/ppermute | solution.py:68
  489.8 6.9 collective-permute-start.19
  496.8 6.6 collective-permute-start.20
  503.5 6.2 collective-permute-start.21
  509.7 5.9 collective-permute-start.22
  516.7 6.3 collective-permute-start.23
  521.2 3.5 collective-permute-start.42
  524.9 6.9 collective-permute-start.43
  531.9 6.7 collective-permute-start.44
  538.6 6.7 collective-permute-start.45
  545.3 5.7 collective-permute-start.46
  551.2 1.8 collective-permute-start.47
  553.2 143.1 %copy-start.101 = (f32[384]{0:T(512)S(1)}, f32[384]{0:T(512)}, u32[]{:S(2)}) copy-start(f32[384]{0:T(512)} %copy-done.100) | copy-start | bytes 4612
  (116 other events, 669.8 us)
Sparse Core Ops, SparseCore 0:
  18.1 98.2 all-gather.2
  142.3 93.4 all-gather.4
  332.1 14.5 reduce-scatter.18
  348.9 14.3 reduce-scatter.20
  438.8 15.3 reduce-scatter.22
  456.4 14.3 reduce-scatter.24
  473.2 96.4 reduce-scatter.28
  572.3 94.6 reduce-scatter.26

commit v3 on v2

--- a/solution.py
+++ b/solution.py
@@ -78,6 +78,39 @@
             jnp.concatenate([received, current], axis=0),
         )
     return current.astype(jnp.float32)
+
+
+def swap_halves(local, axis_name):
+    return lax.ppermute(local, axis_name, [(0, 1), (1, 0)])
+
+
+def ctx_gather(local):
+    other = swap_halves(local, "ctx")
+    first = lax.axis_index("ctx") == 0
+    return jnp.where(
+        first, jnp.concatenate([local, other], axis=0), jnp.concatenate([other, local], axis=0)
+    )
+
+
+def ctx_scatter(full):
+    rows = full.shape[0] // 2
+    place = lax.axis_index("ctx")
+    kept = lax.dynamic_slice_in_dim(full, place * rows, rows, 0)
+    sent = lax.dynamic_slice_in_dim(full, (1 - place) * rows, rows, 0)
+    received = swap_halves(sent.astype(jnp.bfloat16), "ctx")
+    return kept.astype(jnp.bfloat16).astype(jnp.float32) + received.astype(jnp.float32)
+
+
+def all_sum(value):
+    total = value
+    for axis_name in ("tp", "ctx", "fsdp"):
+        count = lax.axis_size(axis_name)
+        step = 1
+        while step < count:
+            pairs = [(device, device ^ step) for device in range(count)]
+            total = total + lax.ppermute(total, axis_name, pairs)
+            step *= 2
+    return total
 
 
 def per_device(
@@ -152,12 +185,18 @@
         full = lax.all_gather(joined, ("fsdp", "ctx"), axis=0, tiled=True)
         return tuple(full[:, edges[k] : edges[k + 1]] for k in range(len(widths)))
 
-    def scatter_layer(terms):
+    def scatter_terms(terms):
         joined = jnp.concatenate([term.astype(jnp.bfloat16) for term in terms], axis=1)
         owned = lax.psum_scatter(joined, ("fsdp", "ctx"), scatter_dimension=0, tiled=True)
-        return tuple(
-            owned[:, edges[k] : edges[k + 1]].astype(jnp.float32) for k in range(len(widths))
-        )
+        pieces = []
+        start = 0
+        for term in terms:
+            pieces.append(owned[:, start : start + term.shape[1]].astype(jnp.float32))
+            start += term.shape[1]
+        return pieces
+
+    def scatter_layer(terms):
+        return tuple(scatter_terms(terms[:4]) + scatter_terms(terms[4:]))
 
     kept_weights = []
     stored_layers = []
@@ -198,8 +237,8 @@
             jnp.bfloat16
         )
         keys = keys.reshape(row_count, local_groups * head_size)
-        all_keys = lax.all_gather(keys, "ctx", axis=0, tiled=True)
-        all_values = lax.all_gather(values, "ctx", axis=0, tiled=True)
+        all_keys = ctx_gather(keys)
+        all_values = ctx_gather(values)
         forward_query_groups = queries.reshape(row_count, local_groups, per_group, head_size)
         forward_key_groups = all_keys.reshape(seq_length, local_groups, head_size)
         forward_value_groups = all_values.reshape(seq_length, local_groups, head_size)
@@ -323,17 +362,9 @@
         key_grad = jnp.einsum(
             "grqk,qgrd->kgd", score_grad, backward_query_groups, preferred_element_type=jnp.float32
         )
-        key_own = lax.psum_scatter(
-            key_grad.reshape(seq_length, local_groups * head_size).astype(jnp.bfloat16),
-            "ctx",
-            scatter_dimension=0,
-            tiled=True,
-        ).astype(jnp.float32)
-        value_own = lax.psum_scatter(
-            value_grad.reshape(seq_length, local_groups * head_size).astype(jnp.bfloat16),
-            "ctx",
-            scatter_dimension=0,
-            tiled=True,
+        key_own = ctx_scatter(key_grad.reshape(seq_length, local_groups * head_size))
+        value_own = ctx_scatter(value_grad.reshape(seq_length, local_groups * head_size)).astype(
+            jnp.bfloat16
         )
         query_turned = rotate(query_grad, cosine_table, -sine_table)
         key_turned = rotate(
@@ -377,15 +408,16 @@
         grad_query, grad_key, grad_value, grad_output, grad_gate, grad_up, grad_down = weight_terms
         weight_sums[layer_index] = scatter_layer(weight_terms)
         gain_parts[layer_index] = gain_terms
-    gain_totals = lax.psum(
-        (
-            jnp.stack([member[0] for member in gain_parts]),
-            jnp.stack([member[1] for member in gain_parts]),
-            jnp.stack([member[2] for member in gain_parts]),
-            jnp.stack([member[3] for member in gain_parts]),
-        ),
-        ("fsdp", "ctx", "tp"),
-    )
+    gain_stacks = [
+        jnp.stack([member[which] for member in gain_parts]) for which in range(4)
+    ]
+    gain_edges = [0]
+    for member in gain_stacks:
+        gain_edges.append(gain_edges[-1] + member.shape[1])
+    gain_joined = all_sum(jnp.concatenate(gain_stacks, axis=1))
+    gain_totals = [
+        gain_joined[:, gain_edges[which] : gain_edges[which + 1]] for which in range(4)
+    ]
     stacked = [jnp.stack([member[which] for member in weight_sums]) for which in range(7)]
     return (
         hidden,

time: 729 us -> 724 us (level)
  blocking collectives: 169 us -> 0 us
  waiting for transfers between devices: 282 us -> 406 us
  other arithmetic: 43.8 us -> 79 us
  starting transfers between devices: 73.1 us -> 81.7 us
    psum x1 -> x0, blocking collectives: 141 us -> none  [per_device(): lax.psum((jnp.stack([member[0] for member in gain_parts]), jnp.stack([mem...]
    unnamed x14 -> x10, waiting for transfers between devices: 14.4 us -> 151 us
    all_gather x4 -> x0, blocking collectives: 27.8 us -> none  [the longest x2 14 us: per_device(): all_values = lax.all_gather(values, 'ctx', axis=0, tiled=True)]
    ppermute x0 -> x15, starting transfers between devices: none -> 19.5 us  [the longest x8 14.7 us: swap_halves(): return lax.ppermute(local, axis_name, [(0, 1), (1, 0)])]
    ppermute x24, waiting for transfers between devices: 80.6 us -> 67.1 us  [tp_sum(): received = lax.ppermute(sent.astype(jnp.bfloat16), 'tp', pairs)]
    ppermute x0 -> x15, waiting for transfers between devices: none -> 12.4 us  [the longest x7 12.4 us: all_sum(): total = total + lax.ppermute(total, axis_name, pairs)]
    ppermute x24, waiting for transfers between devices: 69.8 us -> 58.1 us  [tp_sum(): received = lax.ppermute(current, 'tp', pairs)]
    dot_general x14, matrix products: 21 us -> 10.4 us  [contract_first(): lax.dot_general(left_side, right_side, (((0,), (0,)), ((), ())), preferre...]
  transfers between devices with their start and end apart: 56 -> 69, of which waited for: 49 -> 46; matrix products, arithmetic and copies ran while one was open for 14% -> 23% of each run, Pallas kernels for 0% -> 0%
where the time goes in v3:
time: 724 us; the launch traced here: 712 us
  waiting for transfers between devices  406 us (56%)
  starting transfers between devices  81.7 us (11%)
  other arithmetic  79 us (11%)
  local copies, waits for them, and re-layouts  65.8 us (9%)
  matrix products  62.4 us (9%)
  between operations  17.2 us (2%)
    unnamed x10, waiting for transfers between devices  151 us
    all_gather x2, waiting for transfers between devices, gather_layer(): full = lax.all_gather(joined, ('fsdp', 'ctx'), axis=0, tiled=True)  118 us
    ppermute x24, waiting for transfers between devices, tp_sum(): received = lax.ppermute(sent.astype(jnp.bfloat16), 'tp', pairs)  67.1 us
    ppermute x24, waiting for transfers between devices, tp_sum(): received = lax.ppermute(current, 'tp', pairs)  58.1 us
    unnamed x335, local copies, waits for them, and re-layouts  44 us
    ppermute x24, starting transfers between devices, tp_sum(): received = lax.ppermute(sent.astype(jnp.bfloat16), 'tp', pairs)  33 us
    ppermute x24, starting transfers between devices, tp_sum(): received = lax.ppermute(current, 'tp', pairs)  28.9 us
    dot_general x14, matrix products, contract_last(): lax.dot_general(left_side, right_side, (((1,), (1,)), ((), ())), preferre...  15.3 us
  transfers between devices with their start and end apart: 69, of which 46 were waited for; matrix products, arithmetic and copies ran while one was open for 23% of the time, Pallas kernels for 0%

profile of v3, /device:TPU:0, one launch (start us, length us, event | category | flops | bytes accessed | tf_op | source)
XLA Modules:
  0.0 712.2 jit_solution(14336069141420871795)
XLA Ops:
  21.1 91.1 %all-gather.3.cloned.1.call-done = bf16[1024,1920]{1,0:T(8,128)(2,1)} async-done(((bf16[64,1920]{1,0:T(8,128)(2,1)}), bf16[1024,1920]{1,0:T(8,128)(2,1)}) %all-gather.3.cloned.1.call-update) | async-done | bytes 3932176 | tf_op jit(solution)/shard_map/all_gather | solution.py:185
  118.9 3.0 collective-permute-start.1
  121.9 2.3 multiply_reduce_fusion.11
  128.3 2.2 convolution_convert_fusion.21
  136.2 6.0 collective-permute-done.3
  142.3 2.6 collective-permute-start.4
  144.9 3.6 collective-permute-done.4
  148.6 2.6 collective-permute-start.5
  151.1 3.6 collective-permute-done.5
  155.8 4.7 collective-permute-done.6
  171.8 6.0 collective-permute-done.9
  177.9 2.5 collective-permute-start.10
  180.4 3.7 collective-permute-done.10
  184.1 2.5 collective-permute-start.11
  186.6 3.7 collective-permute-done.11
  191.3 4.8 collective-permute-done.12
  200.1 26.7 %all-gather.5.cloned.1.call-done = bf16[1024,1920]{1,0:T(8,128)(2,1)} async-done(((bf16[64,1920]{1,0:T(8,128)(2,1)}), bf16[1024,1920]{1,0:T(8,128)(2,1)}) %all-gather.5.cloned.1.call-update) | async-done | bytes 3932176 | tf_op jit(solution)/shard_map/all_gather | solution.py:185
  232.9 3.1 collective-permute-start.15
  241.5 2.4 convolution_convert_fusion.20
  248.4 5.6 collective-permute-done.17
  254.1 2.9 collective-permute-start.18
  257.1 3.3 collective-permute-done.18
  260.4 2.9 collective-permute-start.19
  263.3 3.3 collective-permute-done.19
  268.0 4.3 collective-permute-done.20
  282.6 5.6 collective-permute-done.29
  288.2 3.3 collective-permute-start.30
  291.5 2.9 collective-permute-done.30
  294.5 3.3 collective-permute-start.31
  297.7 2.9 collective-permute-done.31
  302.7 4.7 collective-permute-done.32
  316.9 2.8 collective-permute-start.35
  346.0 4.2 collective-permute-done.37
  350.3 3.3 collective-permute-start.38
  354.0 2.5 collective-permute-done.38
  356.5 3.3 collective-permute-start.39
  360.2 2.5 collective-permute-done.39
  364.5 4.0 collective-permute-done.40
  371.9 2.6 copy.207
  374.6 2.3 multiply_reduce_fusion.2
  386.9 5.4 collective-permute-done.23
  392.4 3.7 collective-permute-done.43
  396.1 3.9 collective-permute-start.44
  400.1 2.9 collective-permute-done.44
  403.1 4.1 collective-permute-start.45
  411.3 3.1 collective-permute-done.25
  415.1 2.7 collective-permute-done.46
  420.3 4.3 copy.211
  427.5 2.9 fusion.24
  437.4 3.0 collective-permute-start.49
  458.9 2.6 copy.205
  472.3 5.0 collective-permute-done.51
  477.9 2.6 collective-permute-start.52
  482.1 4.3 copy.209
  491.1 2.5 collective-permute-done.53
  494.1 5.4 collective-permute-done.54
  505.1 3.1 convert_add_fusion
  510.2 2.7 collective-permute-done.57
  519.6 2.3 collective-permute-start.59
  521.9 17.4 %reduce-scatter.19.cloned.1.call-done = bf16[64,1152]{1,0:T(8,128)(2,1)} async-done(((bf16[1024,1152]{1,0:T(8,128)(2,1)}), bf16[64,1152]{1,0:T(8,128)(2,1)}) %reduce-scatter.19.cloned.1.call-update) | async-done | bytes 147472
  550.2 3.7 collective-permute-done.61
  555.7 3.6 collective-permute-done.62
  560.5 57.4 %reduce-scatter.13.cloned.1.call-done = bf16[64,768]{1,0:T(8,128)(2,1)} async-done(((bf16[1024,768]{1,0:T(8,128)(2,1)}), bf16[64,768]{1,0:T(8,128)(2,1)}) %reduce-scatter.13.cloned.1.call-update) | async-done | bytes 98320
  625.5 75.8 %reduce-scatter.17.cloned.1.call-done = bf16[64,1152]{1,0:T(8,128)(2,1)} async-done(((bf16[1024,1152]{1,0:T(8,128)(2,1)}), bf16[64,1152]{1,0:T(8,128)(2,1)}) %reduce-scatter.17.cloned.1.call-update) | async-done | bytes 147472
  (663 shorter events, 221.1 us)
Async XLA Ops:
  7.2 104.9 %all-gather.3.cloned.1.call-start = ((), (), s32[]{:S(2)}) async-start(), calls=%async_computation.4 | async-start | bytes 4177920 | tf_op jit(solution)/shard_map/all_gather | solution.py:185
  13.7 213.0 %all-gather.5.cloned.1.call-start = ((), (), s32[]{:S(2)}) async-start(), calls=%async_computation.5 | async-start | bytes 4177920 | tf_op jit(solution)/shard_map/all_gather | solution.py:185
  114.1 14.2 %collective-permute-start = (bf16[384,128]{1,0:T(8,128)(2,1)}, bf16[384,128]{1,0:T(8,128)(2,1)}, u32[]{:S(2)}, u32[]{:S(2)}) collective-permute-start(bf16[384,128]{1,0:T(8,128)(2,1)} %convolution_convert_fusion.23), channel_id=1, source_target_pairs={{0,8},{8,0},{1,9},{9,1},{2,10},{10,2},{3,11},{11,3},{4,12},{12,4},... | collective-permute-start | bytes 294920 | tf_op jit(solution)/shard_map/ppermute | solution.py:84
  118.9 6.9 collective-permute-start.1
  132.2 1.9 collective-permute-start.2
  132.3 377.1 %reduce-scatter.15.cloned.1.call-start = ((), (), s32[]{:S(2)}) async-start(), calls=%async_computation.7 | async-start | bytes 1671168
  135.2 7.0 collective-permute-start.3
  142.3 6.2 collective-permute-start.4
  148.6 6.2 collective-permute-start.5
  154.8 5.7 collective-permute-start.6
  170.5 7.3 %collective-permute-start.9 = (bf16[96,1024]{1,0:T(8,128)(2,1)S(1)}, bf16[96,1024]{1,0:T(8,128)(2,1)S(1)}, u32[]{:S(2)}, u32[]{:S(2)}) collective-permute-start(bf16[96,1024]{1,0:T(8,128)(2,1)S(1)} %dynamic-slice_convert_fusion.6), channel_id=1, source_target_pairs={{0,2},{1,3},{2,0},{3,1},{4,6},{5,7},{6,4},{7,5},{8,10},{9,11},{10,... | collective-permute-start | bytes 589832 | tf_op jit(solution)/shard_map/ppermute | solution.py:68
  177.9 6.2 collective-permute-start.10
  184.1 6.2 collective-permute-start.11
  190.3 5.7 collective-permute-start.12
  228.7 12.8 %collective-permute-start.14 = (bf16[384,128]{1,0:T(8,128)(2,1)}, bf16[384,128]{1,0:T(8,128)(2,1)}, u32[]{:S(2)}, u32[]{:S(2)}) collective-permute-start(bf16[384,128]{1,0:T(8,128)(2,1)} %convolution_convert_fusion.22), channel_id=1, source_target_pairs={{0,8},{8,0},{1,9},{9,1},{2,10},{10,2},{3,11},{11,3},{4,12},{12,4},... | collective-permute-start | bytes 294920 | tf_op jit(solution)/shard_map/ppermute | solution.py:84
  232.9 6.6 collective-permute-start.15
  247.0 7.0 collective-permute-start.17
  254.1 6.2 collective-permute-start.18
  260.4 6.2 collective-permute-start.19
  266.6 5.7 collective-permute-start.20
  272.5 2.3 collective-permute-start.21
  281.2 7.0 collective-permute-start.29
  288.2 6.2 collective-permute-start.30
  294.5 6.2 collective-permute-start.31
  301.4 6.0 collective-permute-start.32
  308.7 2.5 collective-permute-start.33
  316.9 21.4 %collective-permute-start.35 = (bf16[384,128]{0,1:T(8,128)(2,1)}, bf16[384,128]{0,1:T(8,128)(2,1)}, u32[]{:S(2)}, u32[]{:S(2)}) collective-permute-start(bf16[384,128]{0,1:T(8,128)(2,1)} %fusion.137), channel_id=1, source_target_pairs={{0,8},{8,0},{1,9},{9,1},{2,10},{10,2},{3,11},{11,3},{4,12},{12,4},... | collective-permute-start | bytes 294920 | tf_op jit(solution)/shard_map/ppermute | solution.py:84
  324.5 9.7 %collective-permute-start.34 = (bf16[384,128]{1,0:T(8,128)(2,1)}, bf16[384,128]{1,0:T(8,128)(2,1)}, u32[]{:S(2)}, u32[]{:S(2)}) collective-permute-start(bf16[384,128]{1,0:T(8,128)(2,1)} %fusion.135), channel_id=1, source_target_pairs={{0,8},{8,0},{1,9},{9,1},{2,10},{10,2},{3,11},{11,3},{4,12},{12,4},... | collective-permute-start | bytes 294920 | tf_op jit(solution)/shard_map/ppermute | solution.py:84
  339.8 3.2 collective-permute-start.36
  342.5 40.7 %collective-permute-start.22 = (bf16[192,1024]{1,0:T(8,128)(2,1)}, bf16[192,1024]{1,0:T(8,128)(2,1)}, u32[]{:S(2)}, u32[]{:S(2)}) collective-permute-start(bf16[192,1024]{1,0:T(8,128)(2,1)} %constant_dynamic-slice_fusion.4), channel_id=1, source_target_pairs={{0,1},{1,0},{2,3},{3,2},{4,5},{5,4},{6,7},{7,6},{8,9},{9,8},{10,11... | collective-permute-start | bytes 1179656 | tf_op jit(solution)/shard_map/ppermute | solution.py:68
  343.1 7.1 collective-permute-start.37
  350.3 6.2 collective-permute-start.38
  356.5 6.2 collective-permute-start.39
  362.8 5.7 collective-permute-start.40
  369.4 5.2 collective-permute-start.41
  374.5 164.9 %reduce-scatter.19.cloned.1.call-start = ((), (), s32[]{:S(2)}) async-start(), calls=%async_computation.9 | async-start | bytes 2506752
  381.9 4.0 collective-permute-start.42
  384.3 8.0 %collective-permute-start.23 = (bf16[96,1024]{1,0:T(8,128)(2,1)S(1)}, bf16[96,1024]{1,0:T(8,128)(2,1)S(1)}, u32[]{:S(2)}, u32[]{:S(2)}) collective-permute-start(bf16[96,1024]{1,0:T(8,128)(2,1)S(1)} %dynamic-slice_convert_fusion.4), channel_id=1, source_target_pairs={{0,2},{1,3},{2,0},{3,1},{4,6},{5,7},{6,4},{7,5},{8,10},{9,11},{10,... | collective-permute-start | bytes 589832 | tf_op jit(solution)/shard_map/ppermute | solution.py:68
  386.1 10.0 %collective-permute-start.43 = (bf16[96,1024]{1,0:T(8,128)(2,1)S(1)}, bf16[96,1024]{1,0:T(8,128)(2,1)S(1)}, u32[]{:S(2)}, u32[]{:S(2)}) collective-permute-start(bf16[96,1024]{1,0:T(8,128)(2,1)S(1)} %dynamic-slice_convert_fusion.1), channel_id=1, source_target_pairs={{0,2},{1,3},{2,0},{3,1},{4,6},{5,7},{6,4},{7,5},{8,10},{9,11},{10,... | collective-permute-start | bytes 589832 | tf_op jit(solution)/shard_map/ppermute | solution.py:68
  396.1 6.9 collective-permute-start.44
  400.0 7.1 collective-permute-start.24
  403.1 7.3 %collective-permute-start.45 = (bf16[48,1024]{1,0:T(8,128)(2,1)S(1)}, bf16[48,1024]{1,0:T(8,128)(2,1)S(1)}, u32[]{:S(2)}, u32[]{:S(2)}) collective-permute-start(bf16[48,1024]{1,0:T(8,128)(2,1)S(1)} %add_convert_fusion.7), channel_id=1, source_target_pairs={{0,4},{1,5},{2,6},{3,7},{4,0},{5,1},{6,2},{7,3},{8,12},{9,13},{10,... | collective-permute-start | bytes 294920 | tf_op jit(solution)/shard_map/ppermute | solution.py:74
  407.2 7.2 %collective-permute-start.25 = (bf16[48,1024]{1,0:T(8,128)(2,1)S(1)}, bf16[48,1024]{1,0:T(8,128)(2,1)S(1)}, u32[]{:S(2)}, u32[]{:S(2)}) collective-permute-start(bf16[48,1024]{1,0:T(8,128)(2,1)S(1)} %add_convert_fusion.10), channel_id=1, source_target_pairs={{0,4},{1,5},{2,6},{3,7},{4,0},{5,1},{6,2},{7,3},{8,12},{9,13},{10,... | collective-permute-start | bytes 294920 | tf_op jit(solution)/shard_map/ppermute | solution.py:74
  410.4 7.5 %collective-permute-start.46 = (bf16[96,1024]{1,0:T(8,128)(2,1)S(1)}, bf16[96,1024]{1,0:T(8,128)(2,1)S(1)}, u32[]{:S(2)}, u32[]{:S(2)}) collective-permute-start(bf16[96,1024]{1,0:T(8,128)(2,1)S(1)} %maximum_select_fusion.26), channel_id=1, source_target_pairs={{0,2},{1,3},{2,0},{3,1},{4,6},{5,7},{6,4},{7,5},{8,10},{9,11},{10,... | collective-permute-start | bytes 589832 | tf_op jit(solution)/shard_map/ppermute | solution.py:74
  415.1 9.6 %collective-permute-start.26 = (bf16[96,1024]{1,0:T(8,128)(2,1)}, bf16[96,1024]{1,0:T(8,128)(2,1)}, u32[]{:S(2)}, u32[]{:S(2)}) collective-permute-start(bf16[96,1024]{1,0:T(8,128)(2,1)} %maximum_select_fusion.23), channel_id=1, source_target_pairs={{0,2},{1,3},{2,0},{3,1},{4,6},{5,7},{6,4},{7,5},{8,10},{9,11},{10,... | collective-permute-start | bytes 589832 | tf_op jit(solution)/shard_map/ppermute | solution.py:74
  418.7 11.7 %collective-permute-start.47 = (bf16[192,1024]{1,0:T(8,128)(2,1)}, bf16[192,1024]{1,0:T(8,128)(2,1)}, u32[]{:S(2)}, u32[]{:S(2)}) collective-permute-start(bf16[192,1024]{1,0:T(8,128)(2,1)} %maximum_select_fusion.14), channel_id=1, source_target_pairs={{0,1},{1,0},{2,3},{3,2},{4,5},{5,4},{6,7},{7,6},{8,9},{9,8},{10,11... | collective-permute-start | bytes 1179656 | tf_op jit(solution)/shard_map/ppermute | solution.py:74
  424.7 193.3 %reduce-scatter.13.cloned.1.call-start = ((), (), s32[]{:S(2)}) async-start(), calls=%async_computation.6 | async-start | bytes 1671168
  427.0 78.1 %collective-permute-start.27 = (bf16[192,1024]{1,0:T(8,128)(2,1)}, bf16[192,1024]{1,0:T(8,128)(2,1)}, u32[]{:S(2)}, u32[]{:S(2)}) collective-permute-start(bf16[192,1024]{1,0:T(8,128)(2,1)} %maximum_select_fusion.11), channel_id=1, source_target_pairs={{0,1},{1,0},{2,3},{3,2},{4,5},{5,4},{6,7},{7,6},{8,9},{9,8},{10,11... | collective-permute-start | bytes 1179656 | tf_op jit(solution)/shard_map/ppermute | solution.py:74
  437.4 19.0 %collective-permute-start.49 = (bf16[384,128]{0,1:T(8,128)(2,1)}, bf16[384,128]{0,1:T(8,128)(2,1)}, u32[]{:S(2)}, u32[]{:S(2)}) collective-permute-start(bf16[384,128]{0,1:T(8,128)(2,1)} %fusion.141), channel_id=1, source_target_pairs={{0,8},{8,0},{1,9},{9,1},{2,10},{10,2},{3,11},{11,3},{4,12},{12,4},... | collective-permute-start | bytes 294920 | tf_op jit(solution)/shard_map/ppermute | solution.py:84
  445.2 8.1 %collective-permute-start.48 = (bf16[384,128]{1,0:T(8,128)(2,1)}, bf16[384,128]{1,0:T(8,128)(2,1)}, u32[]{:S(2)}, u32[]{:S(2)}) collective-permute-start(bf16[384,128]{1,0:T(8,128)(2,1)} %fusion.139), channel_id=1, source_target_pairs={{0,8},{8,0},{1,9},{9,1},{2,10},{10,2},{3,11},{11,3},{4,12},{12,4},... | collective-permute-start | bytes 294920 | tf_op jit(solution)/shard_map/ppermute | solution.py:84
  461.5 239.8 %reduce-scatter.17.cloned.1.call-start = ((), (), s32[]{:S(2)}) async-start(), calls=%async_computation.8 | async-start | bytes 2506752
  468.3 2.0 collective-permute-start.50
  470.4 6.8 collective-permute-start.51
  477.9 8.6 %collective-permute-start.52 = (bf16[48,1024]{1,0:T(8,128)(2,1)}, bf16[48,1024]{1,0:T(8,128)(2,1)}, u32[]{:S(2)}, u32[]{:S(2)}) collective-permute-start(bf16[48,1024]{1,0:T(8,128)(2,1)} %dynamic-slice_convert_fusion.8), channel_id=1, source_target_pairs={{0,4},{1,5},{2,6},{3,7},{4,0},{5,1},{6,2},{7,3},{8,12},{9,13},{10,... | collective-permute-start | bytes 294920 | tf_op jit(solution)/shard_map/ppermute | solution.py:68
  487.4 6.2 collective-permute-start.53
  493.7 5.7 collective-permute-start.54
  499.5 2.9 collective-permute-start.55
  504.5 3.7 collective-permute-start.56
  508.8 4.0 collective-permute-start.57
  513.6 5.3 collective-permute-start.58
  519.6 25.9 %collective-permute-start.59 = (f32[2,2304]{1,0:T(2,128)}, f32[2,2304]{1,0:T(2,128)}, u32[]{:S(2)}, u32[]{:S(2)}) collective-permute-start(f32[2,2304]{1,0:T(2,128)} %add.496), channel_id=1, source_target_pairs={{0,8},{8,0},{1,9},{9,1},{2,10},{10,2},{3,11},{11,3},{4,12},{12,4},... | collective-permute-start | bytes 55304 | tf_op jit(solution)/shard_map/ppermute | solution.py:111
  546.3 3.8 collective-permute-start.60
  550.1 3.8 collective-permute-start.61
  554.0 5.3 collective-permute-start.62
  (157 other events, 1643.8 us)
Sparse Core Ops, SparseCore 0:
  13.8 98.2 all-gather.2
  132.4 94.2 all-gather.4
  374.6 80.6 reduce-scatter.14
  457.7 81.5 reduce-scatter.18
  541.7 76.1 reduce-scatter.12
  620.2 81.0 reduce-scatter.16

commit v4 on v3

--- a/solution.py
+++ b/solution.py
@@ -111,6 +111,32 @@
             total = total + lax.ppermute(total, axis_name, pairs)
             step *= 2
     return total
+
+
+def shard_scatter(full):
+    fsdp_count = lax.axis_size("fsdp")
+    ctx_count = lax.axis_size("ctx")
+    fsdp_bits = []
+    step = 1
+    while step < fsdp_count:
+        fsdp_bits.append(step)
+        step *= 2
+    rows = full.shape[0] // (fsdp_count * ctx_count)
+    current = full.astype(jnp.bfloat16).reshape((2,) * len(fsdp_bits) + (ctx_count, rows, -1))
+    order = [("fsdp", 1), ("fsdp", 2), ("ctx", 1)] + [("fsdp", bit) for bit in fsdp_bits[2:]]
+    for axis_name, bit in order:
+        if axis_name == "fsdp":
+            dim = len(fsdp_bits) - 1 - fsdp_bits.index(bit)
+        else:
+            dim = len(fsdp_bits)
+        upper = (lax.axis_index(axis_name) // bit) % 2
+        kept = lax.dynamic_slice_in_dim(current, upper, 1, dim)
+        sent = lax.dynamic_slice_in_dim(current, 1 - upper, 1, dim)
+        count = fsdp_count if axis_name == "fsdp" else ctx_count
+        pairs = [(device, device ^ bit) for device in range(count)]
+        received = lax.ppermute(sent.astype(jnp.bfloat16), axis_name, pairs)
+        current = kept.astype(jnp.float32) + received.astype(jnp.float32)
+    return current.reshape(rows, -1)
 
 
 def per_device(
@@ -195,8 +221,19 @@
             start += term.shape[1]
         return pieces
 
-    def scatter_layer(terms):
-        return tuple(scatter_terms(terms[:4]) + scatter_terms(terms[4:]))
+    def scatter_layer(terms, layer_index):
+        if layer_index > 0:
+            return tuple(scatter_terms(terms))
+        early = scatter_terms(terms[3:])
+        joined = shard_scatter(
+            jnp.concatenate([term.astype(jnp.bfloat16) for term in terms[:3]], axis=1)
+        )
+        late = []
+        start = 0
+        for term in terms[:3]:
+            late.append(joined[:, start : start + term.shape[1]])
+            start += term.shape[1]
+        return tuple(late + early)
 
     kept_weights = []
     stored_layers = []
@@ -406,7 +443,7 @@
         gain_terms = (attention_gain_grad, query_gain_grad, key_gain_grad, feed_gain_grad)
         grad_flow, weight_terms, gain_terms = (source_grad, weight_terms, gain_terms)
         grad_query, grad_key, grad_value, grad_output, grad_gate, grad_up, grad_down = weight_terms
-        weight_sums[layer_index] = scatter_layer(weight_terms)
+        weight_sums[layer_index] = scatter_layer(weight_terms, layer_index)
         gain_parts[layer_index] = gain_terms
     gain_stacks = [
         jnp.stack([member[which] for member in gain_parts]) for which in range(4)

time: 724 us -> 615 us (0.85)
  waiting for transfers between devices: 406 us -> 321 us
  other arithmetic: 79 us -> 55.1 us
  local copies, waits for them, and re-layouts: 65.8 us -> 56.1 us
  matrix products: 62.4 us -> 69.9 us
    unnamed x10 -> x5, waiting for transfers between devices: 151 us -> 43.7 us
    ppermute x0 -> x4, waiting for transfers between devices: none -> 20.1 us  [shard_scatter(): received = lax.ppermute(sent.astype(jnp.bfloat16), axis_name, pairs)]
    unnamed x335 -> x362, local copies, waits for them, and re-layouts: 44 us -> 33.5 us
    ppermute x24, waiting for transfers between devices: 67.1 us -> 57.6 us  [tp_sum(): received = lax.ppermute(sent.astype(jnp.bfloat16), 'tp', pairs)]
    ppermute x8, waiting for transfers between devices: 0.02 us -> 8.01 us  [swap_halves(): return lax.ppermute(local, axis_name, [(0, 1), (1, 0)])]
    dot_general x14, matrix products: 10.4 us -> 18.1 us  [contract_first(): lax.dot_general(left_side, right_side, (((0,), (0,)), ((), ())), preferre...]
  transfers between devices with their start and end apart: 69 -> 71, of which waited for: 46 -> 50; matrix products, arithmetic and copies ran while one was open for 23% -> 23% of each run, Pallas kernels for 0% -> 0%
where the time goes in v4:
time: 615 us; the launch traced here: 604 us
  waiting for transfers between devices  321 us (52%)
  starting transfers between devices  85 us (14%)
  matrix products  69.9 us (11%)
  local copies, waits for them, and re-layouts  56.1 us (9%)
  other arithmetic  55.1 us (9%)
  between operations  17.3 us (3%)
    all_gather x2, waiting for transfers between devices, gather_layer(): full = lax.all_gather(joined, ('fsdp', 'ctx'), axis=0, tiled=True)  118 us
    ppermute x24, waiting for transfers between devices, tp_sum(): received = lax.ppermute(current, 'tp', pairs)  60.8 us
    ppermute x24, waiting for transfers between devices, tp_sum(): received = lax.ppermute(sent.astype(jnp.bfloat16), 'tp', pairs)  57.6 us
    unnamed x5, waiting for transfers between devices  43.7 us
    unnamed x362, local copies, waits for them, and re-layouts  33.5 us
    ppermute x24, starting transfers between devices, tp_sum(): received = lax.ppermute(sent.astype(jnp.bfloat16), 'tp', pairs)  29 us
    ppermute x24, starting transfers between devices, tp_sum(): received = lax.ppermute(current, 'tp', pairs)  26.1 us
    ppermute x4, waiting for transfers between devices, shard_scatter(): received = lax.ppermute(sent.astype(jnp.bfloat16), axis_name, pairs)  20.1 us
  transfers between devices with their start and end apart: 71, of which 50 were waited for; matrix products, arithmetic and copies ran while one was open for 23% of the time, Pallas kernels for 0%

profile of v4, /device:TPU:0, one launch (start us, length us, event | category | flops | bytes accessed | tf_op | source)
XLA Modules:
  0.0 604.2 jit_solution(14245352992242869367)
XLA Ops:
  21.0 91.1 %all-gather.3.cloned.1.call-done = bf16[1024,1920]{1,0:T(8,128)(2,1)} async-done(((bf16[64,1920]{1,0:T(8,128)(2,1)}), bf16[1024,1920]{1,0:T(8,128)(2,1)}) %all-gather.3.cloned.1.call-update) | async-done | bytes 3932176 | tf_op jit(solution)/shard_map/all_gather | solution.py:211
  119.1 3.0 collective-permute-start.1
  122.1 2.3 multiply_reduce_fusion.11
  128.5 2.2 convolution_convert_fusion.21
  136.5 6.0 collective-permute-done.3
  142.6 2.6 collective-permute-start.4
  145.1 3.6 collective-permute-done.4
  148.8 2.6 collective-permute-start.5
  151.4 3.6 collective-permute-done.5
  156.0 4.8 collective-permute-done.6
  171.9 6.1 %collective-permute-done.9 = bf16[96,1024]{1,0:T(8,128)(2,1)S(1)} collective-permute-done((bf16[96,1024]{1,0:T(8,128)(2,1)S(1)}, bf16[96,1024]{1,0:T(8,128)(2,1)S(1)}, u32[]{:S(2)}, u32[]{:S(2)}) %collective-permute-start.9) | collective-permute-done | bytes 196640 | tf_op jit(solution)/shard_map/ppermute | solution.py:68
  178.0 2.6 collective-permute-start.10
  180.6 3.6 collective-permute-done.10
  184.3 2.6 collective-permute-start.11
  186.8 3.6 collective-permute-done.11
  191.5 4.7 collective-permute-done.12
  200.3 26.7 %all-gather.5.cloned.1.call-done = bf16[1024,1920]{1,0:T(8,128)(2,1)} async-done(((bf16[64,1920]{1,0:T(8,128)(2,1)}), bf16[1024,1920]{1,0:T(8,128)(2,1)}) %all-gather.5.cloned.1.call-update) | async-done | bytes 3932176 | tf_op jit(solution)/shard_map/all_gather | solution.py:211
  233.3 3.0 collective-permute-start.15
  241.7 2.4 convolution_convert_fusion.20
  248.8 5.5 collective-permute-done.17
  254.4 3.1 collective-permute-start.18
  257.4 3.1 collective-permute-done.18
  260.6 3.1 collective-permute-start.19
  263.7 3.1 collective-permute-done.19
  268.4 4.2 collective-permute-done.20
  286.8 4.5 collective-permute-done.29
  291.4 3.4 collective-permute-start.30
  294.9 4.5 collective-permute-done.30
  303.1 3.5 collective-permute-done.31
  312.5 2.4 collective-permute-done.25
  315.8 4.9 collective-permute-done.26
  351.1 3.1 convert_add_fusion
  356.6 5.2 collective-permute-done.37
  363.4 4.6 collective-permute-done.38
  370.2 4.0 collective-permute-done.39
  375.8 4.3 collective-permute-done.40
  384.8 2.2 copy-done.40
  396.8 6.3 %copy.212 = bf16[1024,1920]{1,0:T(8,128)(2,1)} copy(bf16[1024,1920]{0,1:T(8,128)(2,1)} %fusion.19) | data formatting | bytes 7864320
  404.5 2.4 collective-permute-start.44
  406.9 2.5 convolution_convert_fusion.3
  410.8 2.4 collective-permute-start.45
  413.5 3.5 collective-permute-done.45
  420.3 2.5 collective-permute-done.46
  432.4 2.4 collective-permute-start.48
  441.5 2.7 fusion.64
  449.2 7.5 %collective-permute-done.49 = bf16[384,128]{0,1:T(8,128)(2,1)S(1)} collective-permute-done((bf16[384,128]{0,1:T(8,128)(2,1)S(1)}, bf16[384,128]{0,1:T(8,128)(2,1)S(1)}, u32[]{:S(2)}, u32[]{:S(2)}) %collective-permute-start.49) | collective-permute-done | bytes 98336 | tf_op jit(solution)/shard_map/ppermute | solution.py:84
  458.4 2.4 copy.175
  467.6 4.6 copy.214
  475.4 14.9 %collective-permute-done.63 = bf16[2,2,1,2,64,512]{5,4,3,2,1,0:T(8,128)(2,1)S(1)} collective-permute-done((bf16[2,2,1,2,64,512]{5,4,3,2,1,0:T(8,128)(2,1)}, bf16[2,2,1,2,64,512]{5,4,3,2,1,0:T(8,128)(2,1)S(1)}, u32[]{:S(2)}, u32[]{:S(2)}) %collective-permute-start.63) | collective-permute-done | bytes 524320 | tf_op jit(solution)/shard_map/ppermute | solution.py:137
  490.6 2.1 collective-permute-start.52
  494.3 2.5 collective-permute-done.52
  496.8 2.1 collective-permute-start.53
  500.2 2.8 collective-permute-done.53
  505.3 3.5 collective-permute-done.54
  509.1 2.1 collective-permute-done.65
  514.8 3.1 collective-permute-done.66
  517.9 2.2 collective-permute-start.58
  520.1 3.1 collective-permute-done.58
  523.3 2.4 collective-permute-start.59
  525.7 3.7 collective-permute-done.59
  529.9 3.4 collective-permute-done.60
  533.2 2.2 collective-permute-start.61
  537.2 2.9 collective-permute-start.62
  548.0 43.6 %reduce-scatter.9.cloned.1.call-done = bf16[64,1408]{1,0:T(8,128)(2,1)} async-done(((bf16[1024,1408]{1,0:T(8,128)(2,1)}), bf16[64,1408]{1,0:T(8,128)(2,1)}) %reduce-scatter.9.cloned.1.call-update) | async-done | bytes 180240
  (699 shorter events, 205.4 us)
Async XLA Ops:
  7.2 104.9 %all-gather.3.cloned.1.call-start = ((), (), s32[]{:S(2)}) async-start(), calls=%async_computation.2 | async-start | bytes 4177920 | tf_op jit(solution)/shard_map/all_gather | solution.py:211
  13.7 213.2 %all-gather.5.cloned.1.call-start = ((), (), s32[]{:S(2)}) async-start(), calls=%async_computation.3 | async-start | bytes 4177920 | tf_op jit(solution)/shard_map/all_gather | solution.py:211
  114.1 14.4 %collective-permute-start = (bf16[384,128]{1,0:T(8,128)(2,1)}, bf16[384,128]{1,0:T(8,128)(2,1)}, u32[]{:S(2)}, u32[]{:S(2)}) collective-permute-start(bf16[384,128]{1,0:T(8,128)(2,1)} %convolution_convert_fusion.23), channel_id=1, source_target_pairs={{0,8},{8,0},{1,9},{9,1},{2,10},{10,2},{3,11},{11,3},{4,12},{12,4},... | collective-permute-start | bytes 294920 | tf_op jit(solution)/shard_map/ppermute | solution.py:84
  119.1 7.0 %collective-permute-start.1 = (bf16[384,128]{1,0:T(8,128)(2,1)}, bf16[384,128]{1,0:T(8,128)(2,1)}, u32[]{:S(2)}, u32[]{:S(2)}) collective-permute-start(bf16[384,128]{1,0:T(8,128)(2,1)} %pad_maximum_fusion.9), channel_id=1, source_target_pairs={{0,8},{8,0},{1,9},{9,1},{2,10},{10,2},{3,11},{11,3},{4,12},{12,4},... | collective-permute-start | bytes 294920 | tf_op jit(solution)/shard_map/ppermute | solution.py:84
  132.5 411.2 %reduce-scatter.7.cloned.1.call-start = ((), (), s32[]{:S(2)}) async-start(), calls=%async_computation.4 | async-start | bytes 4177920 | tf_op jit(solution)/shard_map/reduce_scatter | solution.py:216
  135.5 7.0 %collective-permute-start.3 = (bf16[96,1024]{1,0:T(8,128)(2,1)S(1)}, bf16[96,1024]{1,0:T(8,128)(2,1)S(1)}, u32[]{:S(2)}, u32[]{:S(2)}) collective-permute-start(bf16[96,1024]{1,0:T(8,128)(2,1)S(1)} %dynamic-slice_convert_fusion.8), channel_id=1, source_target_pairs={{0,2},{1,3},{2,0},{3,1},{4,6},{5,7},{6,4},{7,5},{8,10},{9,11},{10,... | collective-permute-start | bytes 589832 | tf_op jit(solution)/shard_map/ppermute | solution.py:68
  142.6 6.2 %collective-permute-start.4 = (bf16[48,1024]{1,0:T(8,128)(2,1)S(1)}, bf16[48,1024]{1,0:T(8,128)(2,1)S(1)}, u32[]{:S(2)}, u32[]{:S(2)}) collective-permute-start(bf16[48,1024]{1,0:T(8,128)(2,1)S(1)} %dynamic-slice_convert_fusion.25), channel_id=1, source_target_pairs={{0,4},{1,5},{2,6},{3,7},{4,0},{5,1},{6,2},{7,3},{8,12},{9,13},{10,... | collective-permute-start | bytes 294920 | tf_op jit(solution)/shard_map/ppermute | solution.py:68
  148.8 6.2 %collective-permute-start.5 = (bf16[48,1024]{1,0:T(8,128)(2,1)S(1)}, bf16[48,1024]{1,0:T(8,128)(2,1)S(1)}, u32[]{:S(2)}, u32[]{:S(2)}) collective-permute-start(bf16[48,1024]{1,0:T(8,128)(2,1)S(1)} %add_convert_fusion.13), channel_id=1, source_target_pairs={{0,4},{1,5},{2,6},{3,7},{4,0},{5,1},{6,2},{7,3},{8,12},{9,13},{10,... | collective-permute-start | bytes 294920 | tf_op jit(solution)/shard_map/ppermute | solution.py:74
  155.0 5.7 collective-permute-start.6
  170.7 7.2 %collective-permute-start.9 = (bf16[96,1024]{1,0:T(8,128)(2,1)S(1)}, bf16[96,1024]{1,0:T(8,128)(2,1)S(1)}, u32[]{:S(2)}, u32[]{:S(2)}) collective-permute-start(bf16[96,1024]{1,0:T(8,128)(2,1)S(1)} %dynamic-slice_convert_fusion.7), channel_id=1, source_target_pairs={{0,2},{1,3},{2,0},{3,1},{4,6},{5,7},{6,4},{7,5},{8,10},{9,11},{10,... | collective-permute-start | bytes 589832 | tf_op jit(solution)/shard_map/ppermute | solution.py:68
  178.0 6.2 %collective-permute-start.10 = (bf16[48,1024]{1,0:T(8,128)(2,1)S(1)}, bf16[48,1024]{1,0:T(8,128)(2,1)S(1)}, u32[]{:S(2)}, u32[]{:S(2)}) collective-permute-start(bf16[48,1024]{1,0:T(8,128)(2,1)S(1)} %dynamic-slice_convert_fusion.24), channel_id=1, source_target_pairs={{0,4},{1,5},{2,6},{3,7},{4,0},{5,1},{6,2},{7,3},{8,12},{9,13},{10,... | collective-permute-start | bytes 294920 | tf_op jit(solution)/shard_map/ppermute | solution.py:68
  184.3 6.2 %collective-permute-start.11 = (bf16[48,1024]{1,0:T(8,128)(2,1)S(1)}, bf16[48,1024]{1,0:T(8,128)(2,1)S(1)}, u32[]{:S(2)}, u32[]{:S(2)}) collective-permute-start(bf16[48,1024]{1,0:T(8,128)(2,1)S(1)} %add_convert_fusion.12), channel_id=1, source_target_pairs={{0,4},{1,5},{2,6},{3,7},{4,0},{5,1},{6,2},{7,3},{8,12},{9,13},{10,... | collective-permute-start | bytes 294920 | tf_op jit(solution)/shard_map/ppermute | solution.py:74
  190.5 5.7 collective-permute-start.12
  228.9 12.8 %collective-permute-start.14 = (bf16[384,128]{1,0:T(8,128)(2,1)}, bf16[384,128]{1,0:T(8,128)(2,1)}, u32[]{:S(2)}, u32[]{:S(2)}) collective-permute-start(bf16[384,128]{1,0:T(8,128)(2,1)} %convolution_convert_fusion.22), channel_id=1, source_target_pairs={{0,8},{8,0},{1,9},{9,1},{2,10},{10,2},{3,11},{11,3},{4,12},{12,4},... | collective-permute-start | bytes 294920 | tf_op jit(solution)/shard_map/ppermute | solution.py:84
  233.3 6.4 %collective-permute-start.15 = (bf16[384,128]{1,0:T(8,128)(2,1)}, bf16[384,128]{1,0:T(8,128)(2,1)}, u32[]{:S(2)}, u32[]{:S(2)}) collective-permute-start(bf16[384,128]{1,0:T(8,128)(2,1)} %pad_maximum_fusion.10), channel_id=1, source_target_pairs={{0,8},{8,0},{1,9},{9,1},{2,10},{10,2},{3,11},{11,3},{4,12},{12,4},... | collective-permute-start | bytes 294920 | tf_op jit(solution)/shard_map/ppermute | solution.py:84
  247.3 7.0 %collective-permute-start.17 = (bf16[96,1024]{1,0:T(8,128)(2,1)S(1)}, bf16[96,1024]{1,0:T(8,128)(2,1)S(1)}, u32[]{:S(2)}, u32[]{:S(2)}) collective-permute-start(bf16[96,1024]{1,0:T(8,128)(2,1)S(1)} %dynamic-slice_convert_fusion.6), channel_id=1, source_target_pairs={{0,2},{1,3},{2,0},{3,1},{4,6},{5,7},{6,4},{7,5},{8,10},{9,11},{10,... | collective-permute-start | bytes 589832 | tf_op jit(solution)/shard_map/ppermute | solution.py:68
  254.4 6.2 %collective-permute-start.18 = (bf16[48,1024]{1,0:T(8,128)(2,1)S(1)}, bf16[48,1024]{1,0:T(8,128)(2,1)S(1)}, u32[]{:S(2)}, u32[]{:S(2)}) collective-permute-start(bf16[48,1024]{1,0:T(8,128)(2,1)S(1)} %dynamic-slice_convert_fusion.23), channel_id=1, source_target_pairs={{0,4},{1,5},{2,6},{3,7},{4,0},{5,1},{6,2},{7,3},{8,12},{9,13},{10,... | collective-permute-start | bytes 294920 | tf_op jit(solution)/shard_map/ppermute | solution.py:68
  260.6 6.2 %collective-permute-start.19 = (bf16[48,1024]{1,0:T(8,128)(2,1)S(1)}, bf16[48,1024]{1,0:T(8,128)(2,1)S(1)}, u32[]{:S(2)}, u32[]{:S(2)}) collective-permute-start(bf16[48,1024]{1,0:T(8,128)(2,1)S(1)} %add_convert_fusion.11), channel_id=1, source_target_pairs={{0,4},{1,5},{2,6},{3,7},{4,0},{5,1},{6,2},{7,3},{8,12},{9,13},{10,... | collective-permute-start | bytes 294920 | tf_op jit(solution)/shard_map/ppermute | solution.py:74
  266.8 5.7 collective-permute-start.20
  272.7 2.2 collective-permute-start.21
  279.6 2.6 collective-permute-start.28
  281.2 3.8 collective-permute-start.22
  283.5 7.8 %collective-permute-start.29 = (bf16[96,1024]{1,0:T(8,128)(2,1)S(1)}, bf16[96,1024]{1,0:T(8,128)(2,1)S(1)}, u32[]{:S(2)}, u32[]{:S(2)}) collective-permute-start(bf16[96,1024]{1,0:T(8,128)(2,1)S(1)} %dynamic-slice_convert_fusion.4), channel_id=1, source_target_pairs={{0,2},{1,3},{2,0},{3,1},{4,6},{5,7},{6,4},{7,5},{8,10},{9,11},{10,... | collective-permute-start | bytes 589832 | tf_op jit(solution)/shard_map/ppermute | solution.py:68
  286.2 8.7 %collective-permute-start.23 = (bf16[96,1024]{1,0:T(8,128)(2,1)S(1)}, bf16[96,1024]{1,0:T(8,128)(2,1)S(1)}, u32[]{:S(2)}, u32[]{:S(2)}) collective-permute-start(bf16[96,1024]{1,0:T(8,128)(2,1)S(1)} %dynamic-slice_convert_fusion.5), channel_id=1, source_target_pairs={{0,2},{1,3},{2,0},{3,1},{4,6},{5,7},{6,4},{7,5},{8,10},{9,11},{10,... | collective-permute-start | bytes 589832 | tf_op jit(solution)/shard_map/ppermute | solution.py:68
  291.4 8.0 %collective-permute-start.30 = (bf16[48,1024]{1,0:T(8,128)(2,1)S(1)}, bf16[48,1024]{1,0:T(8,128)(2,1)S(1)}, u32[]{:S(2)}, u32[]{:S(2)}) collective-permute-start(bf16[48,1024]{1,0:T(8,128)(2,1)S(1)} %dynamic-slice_convert_fusion.21), channel_id=1, source_target_pairs={{0,4},{1,5},{2,6},{3,7},{4,0},{5,1},{6,2},{7,3},{8,12},{9,13},{10,... | collective-permute-start | bytes 294920 | tf_op jit(solution)/shard_map/ppermute | solution.py:68
  299.4 7.2 %collective-permute-start.31 = (bf16[48,1024]{1,0:T(8,128)(2,1)S(1)}, bf16[48,1024]{1,0:T(8,128)(2,1)S(1)}, u32[]{:S(2)}, u32[]{:S(2)}) collective-permute-start(bf16[48,1024]{1,0:T(8,128)(2,1)S(1)} %add_convert_fusion.9), channel_id=1, source_target_pairs={{0,4},{1,5},{2,6},{3,7},{4,0},{5,1},{6,2},{7,3},{8,12},{9,13},{10,... | collective-permute-start | bytes 294920 | tf_op jit(solution)/shard_map/ppermute | solution.py:74
  301.0 7.6 %collective-permute-start.24 = (bf16[48,1024]{1,0:T(8,128)(2,1)S(1)}, bf16[48,1024]{1,0:T(8,128)(2,1)S(1)}, u32[]{:S(2)}, u32[]{:S(2)}) collective-permute-start(bf16[48,1024]{1,0:T(8,128)(2,1)S(1)} %dynamic-slice_convert_fusion.22), channel_id=1, source_target_pairs={{0,4},{1,5},{2,6},{3,7},{4,0},{5,1},{6,2},{7,3},{8,12},{9,13},{10,... | collective-permute-start | bytes 294920 | tf_op jit(solution)/shard_map/ppermute | solution.py:68
  306.6 5.7 collective-permute-start.32
  308.7 6.2 %collective-permute-start.25 = (bf16[48,1024]{1,0:T(8,128)(2,1)S(1)}, bf16[48,1024]{1,0:T(8,128)(2,1)S(1)}, u32[]{:S(2)}, u32[]{:S(2)}) collective-permute-start(bf16[48,1024]{1,0:T(8,128)(2,1)S(1)} %add_convert_fusion.10), channel_id=1, source_target_pairs={{0,4},{1,5},{2,6},{3,7},{4,0},{5,1},{6,2},{7,3},{8,12},{9,13},{10,... | collective-permute-start | bytes 294920 | tf_op jit(solution)/shard_map/ppermute | solution.py:74
  312.4 9.1 %collective-permute-start.33 = (bf16[192,1024]{1,0:T(8,128)(2,1)S(1)}, bf16[192,1024]{1,0:T(8,128)(2,1)S(1)}, u32[]{:S(2)}, u32[]{:S(2)}) collective-permute-start(bf16[192,1024]{1,0:T(8,128)(2,1)S(1)} %maximum_select_fusion.12), channel_id=1, source_target_pairs={{0,1},{1,0},{2,3},{3,2},{4,5},{5,4},{6,7},{7,6},{8,9},{9,8},{10,11... | collective-permute-start | bytes 1179656 | tf_op jit(solution)/shard_map/ppermute | solution.py:74
  314.9 5.7 collective-permute-start.26
  321.5 29.5 %collective-permute-start.27 = (bf16[192,1024]{1,0:T(8,128)(2,1)}, bf16[192,1024]{1,0:T(8,128)(2,1)}, u32[]{:S(2)}, u32[]{:S(2)}) collective-permute-start(bf16[192,1024]{1,0:T(8,128)(2,1)} %maximum_select_fusion.11), channel_id=1, source_target_pairs={{0,1},{1,0},{2,3},{3,2},{4,5},{5,4},{6,7},{7,6},{8,9},{9,8},{10,11... | collective-permute-start | bytes 1179656 | tf_op jit(solution)/shard_map/ppermute | solution.py:74
  327.1 21.0 %collective-permute-start.35 = (bf16[384,128]{0,1:T(8,128)(2,1)}, bf16[384,128]{0,1:T(8,128)(2,1)}, u32[]{:S(2)}, u32[]{:S(2)}) collective-permute-start(bf16[384,128]{0,1:T(8,128)(2,1)} %fusion.144), channel_id=1, source_target_pairs={{0,8},{8,0},{1,9},{9,1},{2,10},{10,2},{3,11},{11,3},{4,12},{12,4},... | collective-permute-start | bytes 294920 | tf_op jit(solution)/shard_map/ppermute | solution.py:84
  333.9 10.1 %collective-permute-start.34 = (bf16[384,128]{1,0:T(8,128)(2,1)}, bf16[384,128]{1,0:T(8,128)(2,1)}, u32[]{:S(2)}, u32[]{:S(2)}) collective-permute-start(bf16[384,128]{1,0:T(8,128)(2,1)} %fusion.142), channel_id=1, source_target_pairs={{0,8},{8,0},{1,9},{9,1},{2,10},{10,2},{3,11},{11,3},{4,12},{12,4},... | collective-permute-start | bytes 294920 | tf_op jit(solution)/shard_map/ppermute | solution.py:84
  349.7 4.5 collective-permute-start.36
  354.4 7.4 %collective-permute-start.37 = (bf16[96,1024]{1,0:T(8,128)(2,1)S(1)}, bf16[96,1024]{1,0:T(8,128)(2,1)S(1)}, u32[]{:S(2)}, u32[]{:S(2)}) collective-permute-start(bf16[96,1024]{1,0:T(8,128)(2,1)S(1)} %dynamic-slice_convert_fusion.3), channel_id=1, source_target_pairs={{0,2},{1,3},{2,0},{3,1},{4,6},{5,7},{6,4},{7,5},{8,10},{9,11},{10,... | collective-permute-start | bytes 589832 | tf_op jit(solution)/shard_map/ppermute | solution.py:68
  361.8 6.2 %collective-permute-start.38 = (bf16[48,1024]{1,0:T(8,128)(2,1)S(1)}, bf16[48,1024]{1,0:T(8,128)(2,1)S(1)}, u32[]{:S(2)}, u32[]{:S(2)}) collective-permute-start(bf16[48,1024]{1,0:T(8,128)(2,1)S(1)} %dynamic-slice_convert_fusion.16), channel_id=1, source_target_pairs={{0,4},{1,5},{2,6},{3,7},{4,0},{5,1},{6,2},{7,3},{8,12},{9,13},{10,... | collective-permute-start | bytes 294920 | tf_op jit(solution)/shard_map/ppermute | solution.py:68
  368.0 6.2 %collective-permute-start.39 = (bf16[48,1024]{1,0:T(8,128)(2,1)S(1)}, bf16[48,1024]{1,0:T(8,128)(2,1)S(1)}, u32[]{:S(2)}, u32[]{:S(2)}) collective-permute-start(bf16[48,1024]{1,0:T(8,128)(2,1)S(1)} %add_convert_fusion.8), channel_id=1, source_target_pairs={{0,4},{1,5},{2,6},{3,7},{4,0},{5,1},{6,2},{7,3},{8,12},{9,13},{10,... | collective-permute-start | bytes 294920 | tf_op jit(solution)/shard_map/ppermute | solution.py:74
  374.3 5.7 collective-permute-start.40
  380.1 3.5 collective-permute-start.41
  389.4 3.6 collective-permute-start.42
  394.7 8.5 %collective-permute-start.43 = (bf16[96,1024]{1,0:T(8,128)(2,1)}, bf16[96,1024]{1,0:T(8,128)(2,1)}, u32[]{:S(2)}, u32[]{:S(2)}) collective-permute-start(bf16[96,1024]{1,0:T(8,128)(2,1)} %dynamic-slice_convert_fusion.2), channel_id=1, source_target_pairs={{0,2},{1,3},{2,0},{3,1},{4,6},{5,7},{6,4},{7,5},{8,10},{9,11},{10,... | collective-permute-start | bytes 589832 | tf_op jit(solution)/shard_map/ppermute | solution.py:68
  403.2 188.4 %reduce-scatter.9.cloned.1.call-start = ((), (), s32[]{:S(2)}) async-start(), calls=%async_computation.5 | async-start | bytes 3063808
  404.5 6.3 %collective-permute-start.44 = (bf16[48,1024]{1,0:T(8,128)(2,1)S(1)}, bf16[48,1024]{1,0:T(8,128)(2,1)S(1)}, u32[]{:S(2)}, u32[]{:S(2)}) collective-permute-start(bf16[48,1024]{1,0:T(8,128)(2,1)S(1)} %dynamic-slice_convert_fusion.15), channel_id=1, source_target_pairs={{0,4},{1,5},{2,6},{3,7},{4,0},{5,1},{6,2},{7,3},{8,12},{9,13},{10,... | collective-permute-start | bytes 294920 | tf_op jit(solution)/shard_map/ppermute | solution.py:68
  410.8 6.2 %collective-permute-start.45 = (bf16[48,1024]{1,0:T(8,128)(2,1)S(1)}, bf16[48,1024]{1,0:T(8,128)(2,1)S(1)}, u32[]{:S(2)}, u32[]{:S(2)}) collective-permute-start(bf16[48,1024]{1,0:T(8,128)(2,1)S(1)} %add_convert_fusion.7), channel_id=1, source_target_pairs={{0,4},{1,5},{2,6},{3,7},{4,0},{5,1},{6,2},{7,3},{8,12},{9,13},{10,... | collective-permute-start | bytes 294920 | tf_op jit(solution)/shard_map/ppermute | solution.py:74
  417.1 5.7 collective-permute-start.46
  432.4 14.1 %collective-permute-start.48 = (bf16[384,128]{1,0:T(8,128)(2,1)}, bf16[384,128]{1,0:T(8,128)(2,1)}, u32[]{:S(2)}, u32[]{:S(2)}) collective-permute-start(bf16[384,128]{1,0:T(8,128)(2,1)} %fusion.146), channel_id=1, source_target_pairs={{0,8},{8,0},{1,9},{9,1},{2,10},{10,2},{3,11},{11,3},{4,12},{12,4},... | collective-permute-start | bytes 294920 | tf_op jit(solution)/shard_map/ppermute | solution.py:84
  445.0 11.7 %collective-permute-start.49 = (bf16[384,128]{0,1:T(8,128)(2,1)S(1)}, bf16[384,128]{0,1:T(8,128)(2,1)S(1)}, u32[]{:S(2)}, u32[]{:S(2)}) collective-permute-start(bf16[384,128]{0,1:T(8,128)(2,1)S(1)} %fusion.148), channel_id=1, source_target_pairs={{0,8},{8,0},{1,9},{9,1},{2,10},{10,2},{3,11},{11,3},{4,12},{12,4},... | collective-permute-start | bytes 294920 | tf_op jit(solution)/shard_map/ppermute | solution.py:84
  464.6 7.6 %collective-permute-start.50 = (bf16[192,1024]{1,0:T(8,128)(2,1)}, bf16[192,1024]{1,0:T(8,128)(2,1)}, u32[]{:S(2)}, u32[]{:S(2)}) collective-permute-start(bf16[192,1024]{1,0:T(8,128)(2,1)} %constant_dynamic-slice_fusion.1), channel_id=1, source_target_pairs={{0,1},{1,0},{2,3},{3,2},{4,5},{5,4},{6,7},{7,6},{8,9},{9,8},{10,11... | collective-permute-start | bytes 1179656 | tf_op jit(solution)/shard_map/ppermute | solution.py:68
  465.5 24.9 %collective-permute-start.63 = (bf16[2,2,1,2,64,512]{5,4,3,2,1,0:T(8,128)(2,1)}, bf16[2,2,1,2,64,512]{5,4,3,2,1,0:T(8,128)(2,1)S(1)}, u32[]{:S(2)}, u32[]{:S(2)}) collective-permute-start(bf16[2,2,1,2,64,512]{5,4,3,2,1,0:T(8,128)(2,1)} %constant_dynamic-slice_fusion), channel_id=1, source_target_pairs={{0,16},{16,0},{32,48},{48,32},{64,80},{80,64},{96,112},{112,96},{1... | collective-permute-start | bytes 1572872 | tf_op jit(solution)/shard_map/ppermute | solution.py:137
  474.4 16.1 %collective-permute-start.51 = (bf16[96,1024]{1,0:T(8,128)(2,1)S(1)}, bf16[96,1024]{1,0:T(8,128)(2,1)S(1)}, u32[]{:S(2)}, u32[]{:S(2)}) collective-permute-start(bf16[96,1024]{1,0:T(8,128)(2,1)S(1)} %dynamic-slice_convert_fusion.1), channel_id=1, source_target_pairs={{0,2},{1,3},{2,0},{3,1},{4,6},{5,7},{6,4},{7,5},{8,10},{9,11},{10,... | collective-permute-start | bytes 589832 | tf_op jit(solution)/shard_map/ppermute | solution.py:68
  490.6 6.2 %collective-permute-start.52 = (bf16[48,1024]{1,0:T(8,128)(2,1)S(1)}, bf16[48,1024]{1,0:T(8,128)(2,1)S(1)}, u32[]{:S(2)}, u32[]{:S(2)}) collective-permute-start(bf16[48,1024]{1,0:T(8,128)(2,1)S(1)} %dynamic-slice_convert_fusion.10), channel_id=1, source_target_pairs={{0,4},{1,5},{2,6},{3,7},{4,0},{5,1},{6,2},{7,3},{8,12},{9,13},{10,... | collective-permute-start | bytes 294920 | tf_op jit(solution)/shard_map/ppermute | solution.py:68
  492.8 11.8 %collective-permute-start.64 = (bf16[2,1,1,2,64,512]{5,4,3,2,1,0:T(8,128)(2,1)S(1)}, bf16[2,1,1,2,64,512]{5,4,3,2,1,0:T(8,128)(2,1)S(1)}, u32[]{:S(2)}, u32[]{:S(2)}) collective-permute-start(bf16[2,1,1,2,64,512]{5,4,3,2,1,0:T(8,128)(2,1)S(1)} %dynamic-slice_convert_fusion), channel_id=1, source_target_pairs={{0,32},{16,48},{32,0},{48,16},{64,96},{80,112},{96,64},{112,80},{1... | collective-permute-start | bytes 786440 | tf_op jit(solution)/shard_map/ppermute | solution.py:137
  496.8 6.2 %collective-permute-start.53 = (bf16[48,1024]{1,0:T(8,128)(2,1)S(1)}, bf16[48,1024]{1,0:T(8,128)(2,1)S(1)}, u32[]{:S(2)}, u32[]{:S(2)}) collective-permute-start(bf16[48,1024]{1,0:T(8,128)(2,1)S(1)} %add_convert_fusion.6), channel_id=1, source_target_pairs={{0,4},{1,5},{2,6},{3,7},{4,0},{5,1},{6,2},{7,3},{8,12},{9,13},{10,... | collective-permute-start | bytes 294920 | tf_op jit(solution)/shard_map/ppermute | solution.py:74
  503.1 5.7 collective-permute-start.54
  504.7 6.6 %collective-permute-start.65 = (bf16[2,1,1,1,64,512]{5,4,3,2,1,0:T(8,128)(2,1)S(1)}, bf16[2,1,1,1,64,512]{5,4,3,2,1,0:T(8,128)(2,1)S(1)}, u32[]{:S(2)}, u32[]{:S(2)}) collective-permute-start(bf16[2,1,1,1,64,512]{5,4,3,2,1,0:T(8,128)(2,1)S(1)} %dynamic-slice_convert_fusion.9), channel_id=1, source_target_pairs={{0,8},{8,0},{1,9},{9,1},{2,10},{10,2},{3,11},{11,3},{4,12},{12,4},... | collective-permute-start | bytes 393224 | tf_op jit(solution)/shard_map/ppermute | solution.py:137
  508.9 2.3 collective-permute-start.55
  511.8 6.1 %collective-permute-start.66 = (bf16[1,1,1,1,64,512]{5,4,3,2,1,0:T(8,128)(2,1)S(1)}, bf16[1,1,1,1,64,512]{5,4,3,2,1,0:T(8,128)(2,1)S(1)}, u32[]{:S(2)}, u32[]{:S(2)}) collective-permute-start(bf16[1,1,1,1,64,512]{5,4,3,2,1,0:T(8,128)(2,1)S(1)} %dynamic-slice_convert_fusion.26), channel_id=1, source_target_pairs={{0,64},{16,80},{32,96},{48,112},{64,0},{80,16},{96,32},{112,48},{1... | collective-permute-start | bytes 196616 | tf_op jit(solution)/shard_map/ppermute | solution.py:137
  513.7 4.2 collective-permute-start.57
  517.9 5.3 collective-permute-start.58
  523.3 6.1 %collective-permute-start.59 = (f32[2,2304]{1,0:T(2,128)S(1)}, f32[2,2304]{1,0:T(2,128)S(1)}, u32[]{:S(2)}, u32[]{:S(2)}) collective-permute-start(f32[2,2304]{1,0:T(2,128)S(1)} %add.548), channel_id=1, source_target_pairs={{0,8},{8,0},{1,9},{9,1},{2,10},{10,2},{3,11},{11,3},{4,12},{12,4},... | collective-permute-start | bytes 55304 | tf_op jit(solution)/shard_map/ppermute | solution.py:111
  529.4 3.8 collective-permute-start.60
  533.2 4.0 collective-permute-start.61
  537.2 5.3 collective-permute-start.62
  (178 other events, 1218.7 us)
Sparse Core Ops, SparseCore 0:
  13.8 98.2 all-gather.2
  132.6 94.2 all-gather.4
  403.3 99.0 reduce-scatter.6
  504.7 86.8 reduce-scatter.8

commit v5 on v4

--- a/solution.py
+++ b/solution.py
@@ -54,30 +54,28 @@
     tp_count = lax.axis_size("tp")
     tp_index = lax.axis_index("tp")
     current = term.astype(jnp.bfloat16)
-    bits = []
-    step = 1
+    half = current.shape[0] // 2
+    upper = tp_index % 2
+    core_pairs = [(device, device ^ 1) for device in range(tp_count)]
+    kept = lax.dynamic_slice_in_dim(current, upper * half, half, 0)
+    sent = lax.dynamic_slice_in_dim(current, (1 - upper) * half, half, 0)
+    received = lax.ppermute(sent, "tp", core_pairs)
+    total = kept.astype(jnp.float32) + received.astype(jnp.float32)
+    step = 2
     while step < tp_count:
-        bits.append(step)
+        mine = total.astype(jnp.bfloat16)
+        pairs = [(device, device ^ step) for device in range(tp_count)]
+        received = lax.ppermute(mine, "tp", pairs)
+        total = mine.astype(jnp.float32) + received.astype(jnp.float32)
         step *= 2
-    for step in bits:
-        half = current.shape[0] // 2
-        upper = (tp_index // step) % 2
-        kept = lax.dynamic_slice_in_dim(current, upper * half, half, 0)
-        sent = lax.dynamic_slice_in_dim(current, (1 - upper) * half, half, 0)
-        pairs = [(device, device ^ step) for device in range(tp_count)]
-        received = lax.ppermute(sent.astype(jnp.bfloat16), "tp", pairs)
-        current = kept.astype(jnp.float32) + received.astype(jnp.float32)
-    current = current.astype(jnp.bfloat16)
-    for step in reversed(bits):
-        upper = (tp_index // step) % 2
-        pairs = [(device, device ^ step) for device in range(tp_count)]
-        received = lax.ppermute(current, "tp", pairs)
-        current = jnp.where(
-            upper == 0,
-            jnp.concatenate([current, received], axis=0),
-            jnp.concatenate([received, current], axis=0),
-        )
-    return current.astype(jnp.float32)
+    mine = total.astype(jnp.bfloat16)
+    other = lax.ppermute(mine, "tp", core_pairs)
+    joined = jnp.where(
+        upper == 0,
+        jnp.concatenate([mine, other], axis=0),
+        jnp.concatenate([other, mine], axis=0),
+    )
+    return joined.astype(jnp.float32)
 
 
 def swap_halves(local, axis_name):

time: 615 us -> 584 us (0.950)
  starting transfers between devices: 85 us -> 62.5 us
  waiting for transfers between devices: 321 us -> 312 us
    ppermute x48 -> x32, starting transfers between devices: 55.1 us -> 35.6 us  [the longest x16 32.6 us: tp_sum(): received = lax.ppermute(mine, 'tp', pairs)]
    all_gather x2, waiting for transfers between devices: 118 us -> 98.4 us  [gather_layer(): full = lax.all_gather(joined, ('fsdp', 'ctx'), axis=0, tiled=True)]
    convert_element_type x12 -> x28, other arithmetic: 1.07 us -> 12 us  [the longest x24 11.1 us: tp_sum(): mine = total.astype(jnp.bfloat16)]
    add x16 -> x0, other arithmetic: 6.53 us -> none  [tp_sum(): current = kept.astype(jnp.float32) + received.astype(jnp.float32)]
    ppermute x48 -> x32, waiting for transfers between devices: 118 us -> 115 us  [the longest x16 104 us: tp_sum(): received = lax.ppermute(mine, 'tp', pairs)]
    unnamed x362 -> x326, local copies, waits for them, and re-layouts: 33.5 us -> 31.6 us
  transfers between devices with their start and end apart: 71 -> 55, of which waited for: 50 -> 36; matrix products, arithmetic and copies ran while one was open for 23% -> 25% of each run, Pallas kernels for 0% -> 0%
where the time goes in v5:
time: 584 us; the launch traced here: 573 us
  waiting for transfers between devices  312 us (53%)
  matrix products  70.4 us (12%)
  starting transfers between devices  62.5 us (11%)
  other arithmetic  57.5 us (10%)
  local copies, waits for them, and re-layouts  53.9 us (9%)
  between operations  16.9 us (3%)
    ppermute x16, waiting for transfers between devices, tp_sum(): received = lax.ppermute(mine, 'tp', pairs)  104 us
    all_gather x2, waiting for transfers between devices, gather_layer(): full = lax.all_gather(joined, ('fsdp', 'ctx'), axis=0, tiled=True)  98.4 us
    unnamed x5, waiting for transfers between devices  47.6 us
    ppermute x16, starting transfers between devices, tp_sum(): received = lax.ppermute(mine, 'tp', pairs)  32.6 us
    unnamed x326, local copies, waits for them, and re-layouts  31.6 us
    ppermute x4, waiting for transfers between devices, shard_scatter(): received = lax.ppermute(sent.astype(jnp.bfloat16), axis_name, pairs)  25.7 us
    dot_general x14, matrix products, contract_first(): lax.dot_general(left_side, right_side, (((0,), (0,)), ((), ())), preferre...  18.1 us
    dot_general x14, matrix products, contract_last(): lax.dot_general(left_side, right_side, (((1,), (1,)), ((), ())), preferre...  15.2 us
  transfers between devices with their start and end apart: 55, of which 36 were waited for; matrix products, arithmetic and copies ran while one was open for 25% of the time, Pallas kernels for 0%

profile of v5, /device:TPU:0, one launch (start us, length us, event | category | flops | bytes accessed | tf_op | source)
XLA Modules:
  0.0 572.7 jit_solution(11321792100885516832)
XLA Ops:
  21.3 90.8 %all-gather.3.cloned.1.call-done = bf16[1024,1920]{1,0:T(8,128)(2,1)} async-done(((bf16[64,1920]{1,0:T(8,128)(2,1)}), bf16[1024,1920]{1,0:T(8,128)(2,1)}) %all-gather.3.cloned.1.call-update) | async-done | bytes 3932176 | tf_op jit(solution)/shard_map/all_gather | solution.py:209
  112.1 2.0 convolution_convert_fusion.23
  119.1 3.0 collective-permute-start.1
  122.1 2.3 multiply_reduce_fusion.11
  126.0 3.2 collective-permute-done.1
  129.2 1.8 fusion.13
  131.1 2.2 convolution_convert_fusion.21
  135.7 1.9 collective-permute-done.2
  139.3 9.7 %collective-permute-done.3 = bf16[192,1024]{1,0:T(8,128)(2,1)S(1)} collective-permute-done((bf16[192,1024]{1,0:T(8,128)(2,1)S(1)}, bf16[192,1024]{1,0:T(8,128)(2,1)S(1)}, u32[]{:S(2)}, u32[]{:S(2)}) %collective-permute-start.3) | collective-permute-done | bytes 393248 | tf_op jit(solution)/shard_map/ppermute | solution.py:68
  149.2 3.0 collective-permute-start.4
  152.2 9.0 %collective-permute-done.4 = bf16[192,1024]{1,0:T(8,128)(2,1)S(1)} collective-permute-done((bf16[192,1024]{1,0:T(8,128)(2,1)S(1)}, bf16[192,1024]{1,0:T(8,128)(2,1)S(1)}, u32[]{:S(2)}, u32[]{:S(2)}) %collective-permute-start.4) | collective-permute-done | bytes 393248 | tf_op jit(solution)/shard_map/ppermute | solution.py:68
  172.7 9.8 %collective-permute-done.7 = bf16[192,1024]{1,0:T(8,128)(2,1)S(1)} collective-permute-done((bf16[192,1024]{1,0:T(8,128)(2,1)S(1)}, bf16[192,1024]{1,0:T(8,128)(2,1)S(1)}, u32[]{:S(2)}, u32[]{:S(2)}) %collective-permute-start.7) | collective-permute-done | bytes 393248 | tf_op jit(solution)/shard_map/ppermute | solution.py:68
  182.6 3.0 collective-permute-start.8
  185.6 9.0 %collective-permute-done.8 = bf16[192,1024]{1,0:T(8,128)(2,1)S(1)} collective-permute-done((bf16[192,1024]{1,0:T(8,128)(2,1)S(1)}, bf16[192,1024]{1,0:T(8,128)(2,1)S(1)}, u32[]{:S(2)}, u32[]{:S(2)}) %collective-permute-start.8) | collective-permute-done | bytes 393248 | tf_op jit(solution)/shard_map/ppermute | solution.py:68
  198.9 7.6 %all-gather.5.cloned.1.call-done = bf16[1024,1920]{1,0:T(8,128)(2,1)} async-done(((bf16[64,1920]{1,0:T(8,128)(2,1)}), bf16[1024,1920]{1,0:T(8,128)(2,1)}) %all-gather.5.cloned.1.call-update) | async-done | bytes 3932176 | tf_op jit(solution)/shard_map/all_gather | solution.py:209
  206.5 2.0 convolution_convert_fusion.22
  213.5 2.4 collective-permute-start.11
  219.9 1.8 fusion.9
  221.9 2.4 convolution_convert_fusion.20
  229.2 9.5 %collective-permute-done.13 = bf16[192,1024]{1,0:T(8,128)(2,1)S(1)} collective-permute-done((bf16[192,1024]{1,0:T(8,128)(2,1)S(1)}, bf16[192,1024]{1,0:T(8,128)(2,1)S(1)}, u32[]{:S(2)}, u32[]{:S(2)}) %collective-permute-start.13) | collective-permute-done | bytes 393248 | tf_op jit(solution)/shard_map/ppermute | solution.py:68
  238.8 3.4 collective-permute-start.14
  242.2 8.6 %collective-permute-done.14 = bf16[192,1024]{1,0:T(8,128)(2,1)S(1)} collective-permute-done((bf16[192,1024]{1,0:T(8,128)(2,1)S(1)}, bf16[192,1024]{1,0:T(8,128)(2,1)S(1)}, u32[]{:S(2)}, u32[]{:S(2)}) %collective-permute-start.14) | collective-permute-done | bytes 393248 | tf_op jit(solution)/shard_map/ppermute | solution.py:68
  258.9 1.9 collective-permute-done.20
  263.8 1.8 convolution_convert_fusion.8
  266.2 7.2 %collective-permute-done.21 = bf16[192,1024]{1,0:T(8,128)(2,1)S(1)} collective-permute-done((bf16[192,1024]{1,0:T(8,128)(2,1)S(1)}, bf16[192,1024]{1,0:T(8,128)(2,1)S(1)}, u32[]{:S(2)}, u32[]{:S(2)}) %collective-permute-start.21) | collective-permute-done | bytes 393248 | tf_op jit(solution)/shard_map/ppermute | solution.py:68
  273.5 3.3 collective-permute-start.22
  278.2 8.9 %collective-permute-done.22 = bf16[192,1024]{1,0:T(8,128)(2,1)S(1)} collective-permute-done((bf16[192,1024]{1,0:T(8,128)(2,1)S(1)}, bf16[192,1024]{1,0:T(8,128)(2,1)S(1)}, u32[]{:S(2)}, u32[]{:S(2)}) %collective-permute-start.22) | collective-permute-done | bytes 393248 | tf_op jit(solution)/shard_map/ppermute | solution.py:68
  288.0 6.2 %collective-permute-done.17 = bf16[192,1024]{1,0:T(8,128)(2,1)S(1)} collective-permute-done((bf16[192,1024]{1,0:T(8,128)(2,1)S(1)}, bf16[192,1024]{1,0:T(8,128)(2,1)S(1)}, u32[]{:S(2)}, u32[]{:S(2)}) %collective-permute-start.17) | collective-permute-done | bytes 393248 | tf_op jit(solution)/shard_map/ppermute | solution.py:68
  295.0 1.9 collective-permute-start.18
  297.4 2.0 multiply_add_fusion.3
  302.5 2.4 collective-permute-start.25
  304.8 1.9 fusion.4
  314.3 1.9 copy.158
  331.3 8.2 %collective-permute-done.27 = bf16[192,1024]{1,0:T(8,128)(2,1)S(1)} collective-permute-done((bf16[192,1024]{1,0:T(8,128)(2,1)S(1)}, bf16[192,1024]{1,0:T(8,128)(2,1)S(1)}, u32[]{:S(2)}, u32[]{:S(2)}) %collective-permute-start.27) | collective-permute-done | bytes 393248 | tf_op jit(solution)/shard_map/ppermute | solution.py:68
  339.6 2.0 collective-permute-start.28
  343.3 8.2 %collective-permute-done.28 = bf16[192,1024]{1,0:T(8,128)(2,1)S(1)} collective-permute-done((bf16[192,1024]{1,0:T(8,128)(2,1)S(1)}, bf16[192,1024]{1,0:T(8,128)(2,1)S(1)}, u32[]{:S(2)}, u32[]{:S(2)}) %collective-permute-start.28) | collective-permute-done | bytes 393248 | tf_op jit(solution)/shard_map/ppermute | solution.py:68
  351.8 2.1 fusion.24
  356.3 2.2 copy-done.35
  367.6 6.3 %copy.212 = bf16[1024,1920]{1,0:T(8,128)(2,1)} copy(bf16[1024,1920]{0,1:T(8,128)(2,1)} %fusion.19) | data formatting | bytes 7864320
  375.0 2.5 convolution_convert_fusion.3
  378.7 3.2 collective-permute-start.32
  383.7 7.6 %collective-permute-done.32 = bf16[192,1024]{1,0:T(8,128)(2,1)S(1)} collective-permute-done((bf16[192,1024]{1,0:T(8,128)(2,1)S(1)}, bf16[192,1024]{1,0:T(8,128)(2,1)S(1)}, u32[]{:S(2)}, u32[]{:S(2)}) %collective-permute-start.32) | collective-permute-done | bytes 393248 | tf_op jit(solution)/shard_map/ppermute | solution.py:68
  396.3 2.0 fusion
  401.2 2.4 collective-permute-start.34
  406.6 1.9 copy.169
  418.8 6.5 %collective-permute-done.35 = bf16[384,128]{0,1:T(8,128)(2,1)S(1)} collective-permute-done((bf16[384,128]{0,1:T(8,128)(2,1)S(1)}, bf16[384,128]{0,1:T(8,128)(2,1)S(1)}, u32[]{:S(2)}, u32[]{:S(2)}) %collective-permute-start.35) | collective-permute-done | bytes 98336 | tf_op jit(solution)/shard_map/ppermute | solution.py:82
  431.7 2.0 add_convert_fusion.6
  434.4 2.8 pad_maximum_fusion
  437.2 4.6 copy.214
  441.8 15.3 %collective-permute-done.47 = bf16[2,2,1,2,64,512]{5,4,3,2,1,0:T(8,128)(2,1)} collective-permute-done((bf16[2,2,1,2,64,512]{5,4,3,2,1,0:T(8,128)(2,1)}, bf16[2,2,1,2,64,512]{5,4,3,2,1,0:T(8,128)(2,1)}, u32[]{:S(2)}, u32[]{:S(2)}) %collective-permute-start.47) | collective-permute-done | bytes 524320 | tf_op jit(solution)/shard_map/ppermute | solution.py:135
  459.8 4.0 collective-permute-start.38
  465.1 4.8 collective-permute-done.48
  470.1 2.5 collective-permute-done.38
  472.9 3.7 collective-permute-done.49
  477.2 2.2 collective-permute-start.50
  479.4 1.9 collective-permute-start.41
  481.3 1.9 collective-permute-done.50
  483.3 3.0 collective-permute-start.42
  486.3 2.3 collective-permute-done.42
  490.2 4.2 collective-permute-done.43
  494.9 3.5 collective-permute-done.44
  498.9 3.6 collective-permute-done.45
  502.5 3.1 collective-permute-start.46
  513.2 46.9 %reduce-scatter.9.cloned.1.call-done = bf16[64,1408]{1,0:T(8,128)(2,1)} async-done(((bf16[1024,1408]{1,0:T(8,128)(2,1)}), bf16[64,1408]{1,0:T(8,128)(2,1)}) %reduce-scatter.9.cloned.1.call-update) | async-done | bytes 180240
  (599 shorter events, 160.3 us)
Async XLA Ops:
  7.2 104.9 %all-gather.3.cloned.1.call-start = ((), (), s32[]{:S(2)}) async-start(), calls=%async_computation.2 | async-start | bytes 4177920 | tf_op jit(solution)/shard_map/all_gather | solution.py:209
  13.7 192.8 %all-gather.5.cloned.1.call-start = ((), (), s32[]{:S(2)}) async-start(), calls=%async_computation.3 | async-start | bytes 4177920 | tf_op jit(solution)/shard_map/all_gather | solution.py:209
  14.4 494.6 %reduce-scatter.7.cloned.1.call-start = ((), (), s32[]{:S(2)}) async-start(), calls=%async_computation.4 | async-start | bytes 4177920 | tf_op jit(solution)/shard_map/reduce_scatter | solution.py:214
  17.2 98.9 %copy-start.138 = (f32[128]{0:T(128)}, f32[128]{0:T(128)S(1)}, u32[]{:S(2)}) copy-start(f32[128]{0:T(128)S(1)} %get-tuple-element.148) | copy-start | bytes 1540
  19.6 106.1 %copy-start.30 = (f32[384,64]{1,0:T(8,128)}, f32[384,64]{1,0:T(8,128)S(1)}, u32[]{:S(2)}) copy-start(f32[384,64]{1,0:T(8,128)S(1)} %get-tuple-element.144) | copy-start | bytes 294916
  19.6 106.1 %copy-start.59 = (f32[384,64]{1,0:T(8,128)}, f32[384,64]{1,0:T(8,128)S(1)}, u32[]{:S(2)}) copy-start(f32[384,64]{1,0:T(8,128)S(1)} %get-tuple-element.143) | copy-start | bytes 294916
  21.0 101.1 %copy-start.1 = (bf16[384,1024]{1,0:T(8,128)(2,1)}, bf16[384,1024]{1,0:T(8,128)(2,1)S(1)}, u32[]{:S(2)}) copy-start(bf16[384,1024]{1,0:T(8,128)(2,1)S(1)} %get-tuple-element.81) | copy-start | bytes 2359300
  114.1 17.1 %collective-permute-start = (bf16[384,128]{1,0:T(8,128)(2,1)}, bf16[384,128]{1,0:T(8,128)(2,1)}, u32[]{:S(2)}, u32[]{:S(2)}) collective-permute-start(bf16[384,128]{1,0:T(8,128)(2,1)} %convolution_convert_fusion.23), channel_id=1, source_target_pairs={{0,8},{8,0},{1,9},{9,1},{2,10},{10,2},{3,11},{11,3},{4,12},{12,4},... | collective-permute-start | bytes 294920 | tf_op jit(solution)/shard_map/ppermute | solution.py:82
  119.1 10.1 %collective-permute-start.1 = (bf16[384,128]{1,0:T(8,128)(2,1)}, bf16[384,128]{1,0:T(8,128)(2,1)}, u32[]{:S(2)}, u32[]{:S(2)}) collective-permute-start(bf16[384,128]{1,0:T(8,128)(2,1)} %pad_maximum_fusion.9), channel_id=1, source_target_pairs={{0,8},{8,0},{1,9},{9,1},{2,10},{10,2},{3,11},{11,3},{4,12},{12,4},... | collective-permute-start | bytes 294920 | tf_op jit(solution)/shard_map/ppermute | solution.py:82
  135.7 1.9 collective-permute-start.2
  137.8 11.2 %collective-permute-start.3 = (bf16[192,1024]{1,0:T(8,128)(2,1)S(1)}, bf16[192,1024]{1,0:T(8,128)(2,1)S(1)}, u32[]{:S(2)}, u32[]{:S(2)}) collective-permute-start(bf16[192,1024]{1,0:T(8,128)(2,1)S(1)} %add_convert_fusion.27), channel_id=1, source_target_pairs={{0,2},{1,3},{2,0},{3,1},{4,6},{5,7},{6,4},{7,5},{8,10},{9,11},{10,... | collective-permute-start | bytes 1179656 | tf_op jit(solution)/shard_map/ppermute | solution.py:68
  149.2 12.0 %collective-permute-start.4 = (bf16[192,1024]{1,0:T(8,128)(2,1)S(1)}, bf16[192,1024]{1,0:T(8,128)(2,1)S(1)}, u32[]{:S(2)}, u32[]{:S(2)}) collective-permute-start(bf16[192,1024]{1,0:T(8,128)(2,1)S(1)} %add_convert_fusion.26), channel_id=1, source_target_pairs={{0,4},{1,5},{2,6},{3,7},{4,0},{5,1},{6,2},{7,3},{8,12},{9,13},{10,... | collective-permute-start | bytes 1179656 | tf_op jit(solution)/shard_map/ppermute | solution.py:68
  161.4 1.8 collective-permute-start.5
  169.2 27.6 %copy-start.28 = (bf16[192,1024]{1,0:T(8,128)(2,1)S(1)}, bf16[192,1024]{1,0:T(8,128)(2,1)}, u32[]{:S(2)}) copy-start(bf16[192,1024]{1,0:T(8,128)(2,1)} %copy-done.27) | copy-start | bytes 1179652
  169.2 27.6 %copy-start.49 = (bf16[192,1024]{1,0:T(8,128)(2,1)S(1)}, bf16[192,1024]{1,0:T(8,128)(2,1)}, u32[]{:S(2)}) copy-start(bf16[192,1024]{1,0:T(8,128)(2,1)} %copy-done.48) | copy-start | bytes 1179652
  169.2 1.8 collective-permute-start.6
  171.2 11.3 %collective-permute-start.7 = (bf16[192,1024]{1,0:T(8,128)(2,1)S(1)}, bf16[192,1024]{1,0:T(8,128)(2,1)S(1)}, u32[]{:S(2)}, u32[]{:S(2)}) collective-permute-start(bf16[192,1024]{1,0:T(8,128)(2,1)S(1)} %add_convert_fusion.24), channel_id=1, source_target_pairs={{0,2},{1,3},{2,0},{3,1},{4,6},{5,7},{6,4},{7,5},{8,10},{9,11},{10,... | collective-permute-start | bytes 1179656 | tf_op jit(solution)/shard_map/ppermute | solution.py:68
  182.6 12.1 %collective-permute-start.8 = (bf16[192,1024]{1,0:T(8,128)(2,1)S(1)}, bf16[192,1024]{1,0:T(8,128)(2,1)S(1)}, u32[]{:S(2)}, u32[]{:S(2)}) collective-permute-start(bf16[192,1024]{1,0:T(8,128)(2,1)S(1)} %add_convert_fusion.23), channel_id=1, source_target_pairs={{0,4},{1,5},{2,6},{3,7},{4,0},{5,1},{6,2},{7,3},{8,12},{9,13},{10,... | collective-permute-start | bytes 1179656 | tf_op jit(solution)/shard_map/ppermute | solution.py:68
  194.8 2.0 collective-permute-start.9
  208.5 13.4 %collective-permute-start.10 = (bf16[384,128]{1,0:T(8,128)(2,1)}, bf16[384,128]{1,0:T(8,128)(2,1)}, u32[]{:S(2)}, u32[]{:S(2)}) collective-permute-start(bf16[384,128]{1,0:T(8,128)(2,1)} %convolution_convert_fusion.22), channel_id=1, source_target_pairs={{0,8},{8,0},{1,9},{9,1},{2,10},{10,2},{3,11},{11,3},{4,12},{12,4},... | collective-permute-start | bytes 294920 | tf_op jit(solution)/shard_map/ppermute | solution.py:82
  213.5 6.4 %collective-permute-start.11 = (bf16[384,128]{1,0:T(8,128)(2,1)}, bf16[384,128]{1,0:T(8,128)(2,1)}, u32[]{:S(2)}, u32[]{:S(2)}) collective-permute-start(bf16[384,128]{1,0:T(8,128)(2,1)} %pad_maximum_fusion.10), channel_id=1, source_target_pairs={{0,8},{8,0},{1,9},{9,1},{2,10},{10,2},{3,11},{11,3},{4,12},{12,4},... | collective-permute-start | bytes 294920 | tf_op jit(solution)/shard_map/ppermute | solution.py:82
  225.4 25.6 %copy-start.7 = (f32[384,1024]{1,0:T(8,128)S(1)}, f32[384,1024]{1,0:T(8,128)}, u32[]{:S(2)}) copy-start(f32[384,1024]{1,0:T(8,128)} %param.15) | copy-start | bytes 4718596
  225.5 1.8 collective-permute-start.12
  227.4 11.2 %collective-permute-start.13 = (bf16[192,1024]{1,0:T(8,128)(2,1)S(1)}, bf16[192,1024]{1,0:T(8,128)(2,1)S(1)}, u32[]{:S(2)}, u32[]{:S(2)}) collective-permute-start(bf16[192,1024]{1,0:T(8,128)(2,1)S(1)} %add_convert_fusion.21), channel_id=1, source_target_pairs={{0,2},{1,3},{2,0},{3,1},{4,6},{5,7},{6,4},{7,5},{8,10},{9,11},{10,... | collective-permute-start | bytes 1179656 | tf_op jit(solution)/shard_map/ppermute | solution.py:68
  238.8 12.0 %collective-permute-start.14 = (bf16[192,1024]{1,0:T(8,128)(2,1)S(1)}, bf16[192,1024]{1,0:T(8,128)(2,1)S(1)}, u32[]{:S(2)}, u32[]{:S(2)}) collective-permute-start(bf16[192,1024]{1,0:T(8,128)(2,1)S(1)} %add_convert_fusion.20), channel_id=1, source_target_pairs={{0,4},{1,5},{2,6},{3,7},{4,0},{5,1},{6,2},{7,3},{8,12},{9,13},{10,... | collective-permute-start | bytes 1179656 | tf_op jit(solution)/shard_map/ppermute | solution.py:68
  251.0 1.8 collective-permute-start.15
  253.8 43.1 %copy-start.6 = (f32[384,1024]{1,0:T(8,128)}, f32[384,1024]{1,0:T(8,128)S(1)}, u32[]{:S(2)}) copy-start(f32[384,1024]{1,0:T(8,128)S(1)} %get-tuple-element.74) | copy-start | bytes 4718596
  258.8 2.1 collective-permute-start.20
  262.1 11.2 %collective-permute-start.21 = (bf16[192,1024]{1,0:T(8,128)(2,1)S(1)}, bf16[192,1024]{1,0:T(8,128)(2,1)S(1)}, u32[]{:S(2)}, u32[]{:S(2)}) collective-permute-start(bf16[192,1024]{1,0:T(8,128)(2,1)S(1)} %add_convert_fusion.15), channel_id=1, source_target_pairs={{0,2},{1,3},{2,0},{3,1},{4,6},{5,7},{6,4},{7,5},{8,10},{9,11},{10,... | collective-permute-start | bytes 1179656 | tf_op jit(solution)/shard_map/ppermute | solution.py:68
  265.7 11.7 %collective-permute-start.16 = (bf16[192,1024]{1,0:T(8,128)(2,1)S(1)}, bf16[192,1024]{1,0:T(8,128)(2,1)S(1)}, u32[]{:S(2)}, u32[]{:S(2)}) collective-permute-start(bf16[192,1024]{1,0:T(8,128)(2,1)S(1)} %constant_dynamic-slice_fusion.5), channel_id=1, source_target_pairs={{0,1},{1,0},{2,3},{3,2},{4,5},{5,4},{6,7},{7,6},{8,9},{9,8},{10,11... | collective-permute-start | bytes 1179656 | tf_op jit(solution)/shard_map/ppermute | solution.py:62
  273.5 13.6 %collective-permute-start.22 = (bf16[192,1024]{1,0:T(8,128)(2,1)S(1)}, bf16[192,1024]{1,0:T(8,128)(2,1)S(1)}, u32[]{:S(2)}, u32[]{:S(2)}) collective-permute-start(bf16[192,1024]{1,0:T(8,128)(2,1)S(1)} %add_convert_fusion.14), channel_id=1, source_target_pairs={{0,4},{1,5},{2,6},{3,7},{4,0},{5,1},{6,2},{7,3},{8,12},{9,13},{10,... | collective-permute-start | bytes 1179656 | tf_op jit(solution)/shard_map/ppermute | solution.py:68
  277.5 16.6 %collective-permute-start.17 = (bf16[192,1024]{1,0:T(8,128)(2,1)S(1)}, bf16[192,1024]{1,0:T(8,128)(2,1)S(1)}, u32[]{:S(2)}, u32[]{:S(2)}) collective-permute-start(bf16[192,1024]{1,0:T(8,128)(2,1)S(1)} %add_convert_fusion.18), channel_id=1, source_target_pairs={{0,2},{1,3},{2,0},{3,1},{4,6},{5,7},{6,4},{7,5},{8,10},{9,11},{10,... | collective-permute-start | bytes 1179656 | tf_op jit(solution)/shard_map/ppermute | solution.py:68
  287.3 9.6 %collective-permute-start.23 = (bf16[192,1024]{1,0:T(8,128)(2,1)S(1)}, bf16[192,1024]{1,0:T(8,128)(2,1)S(1)}, u32[]{:S(2)}, u32[]{:S(2)}) collective-permute-start(bf16[192,1024]{1,0:T(8,128)(2,1)S(1)} %add_convert_fusion.13), channel_id=1, source_target_pairs={{0,1},{1,0},{2,3},{3,2},{4,5},{5,4},{6,7},{7,6},{8,9},{9,8},{10,11... | collective-permute-start | bytes 1179656 | tf_op jit(solution)/shard_map/ppermute | solution.py:72
  295.0 29.8 %collective-permute-start.18 = (bf16[192,1024]{1,0:T(8,128)(2,1)}, bf16[192,1024]{1,0:T(8,128)(2,1)}, u32[]{:S(2)}, u32[]{:S(2)}) collective-permute-start(bf16[192,1024]{1,0:T(8,128)(2,1)} %add_convert_fusion.17), channel_id=1, source_target_pairs={{0,4},{1,5},{2,6},{3,7},{4,0},{5,1},{6,2},{7,3},{8,12},{9,13},{10,... | collective-permute-start | bytes 1179656 | tf_op jit(solution)/shard_map/ppermute | solution.py:68
  302.5 20.8 %collective-permute-start.25 = (bf16[384,128]{0,1:T(8,128)(2,1)}, bf16[384,128]{0,1:T(8,128)(2,1)}, u32[]{:S(2)}, u32[]{:S(2)}) collective-permute-start(bf16[384,128]{0,1:T(8,128)(2,1)} %fusion.144), channel_id=1, source_target_pairs={{0,8},{8,0},{1,9},{9,1},{2,10},{10,2},{3,11},{11,3},{4,12},{12,4},... | collective-permute-start | bytes 294920 | tf_op jit(solution)/shard_map/ppermute | solution.py:82
  309.6 9.5 %collective-permute-start.24 = (bf16[384,128]{1,0:T(8,128)(2,1)}, bf16[384,128]{1,0:T(8,128)(2,1)}, u32[]{:S(2)}, u32[]{:S(2)}) collective-permute-start(bf16[384,128]{1,0:T(8,128)(2,1)} %fusion.142), channel_id=1, source_target_pairs={{0,8},{8,0},{1,9},{9,1},{2,10},{10,2},{3,11},{11,3},{4,12},{12,4},... | collective-permute-start | bytes 294920 | tf_op jit(solution)/shard_map/ppermute | solution.py:82
  324.8 3.2 collective-permute-start.26
  326.2 3.4 collective-permute-start.19
  328.1 11.4 %collective-permute-start.27 = (bf16[192,1024]{1,0:T(8,128)(2,1)S(1)}, bf16[192,1024]{1,0:T(8,128)(2,1)S(1)}, u32[]{:S(2)}, u32[]{:S(2)}) collective-permute-start(bf16[192,1024]{1,0:T(8,128)(2,1)S(1)} %add_convert_fusion.12), channel_id=1, source_target_pairs={{0,2},{1,3},{2,0},{3,1},{4,6},{5,7},{6,4},{7,5},{8,10},{9,11},{10,... | collective-permute-start | bytes 1179656 | tf_op jit(solution)/shard_map/ppermute | solution.py:68
  339.6 11.9 %collective-permute-start.28 = (bf16[192,1024]{1,0:T(8,128)(2,1)S(1)}, bf16[192,1024]{1,0:T(8,128)(2,1)S(1)}, u32[]{:S(2)}, u32[]{:S(2)}) collective-permute-start(bf16[192,1024]{1,0:T(8,128)(2,1)S(1)} %add_convert_fusion.11), channel_id=1, source_target_pairs={{0,4},{1,5},{2,6},{3,7},{4,0},{5,1},{6,2},{7,3},{8,12},{9,13},{10,... | collective-permute-start | bytes 1179656 | tf_op jit(solution)/shard_map/ppermute | solution.py:68
  351.7 3.4 collective-permute-start.29
  360.9 3.6 collective-permute-start.30
  365.4 12.0 %collective-permute-start.31 = (bf16[192,1024]{1,0:T(8,128)(2,1)}, bf16[192,1024]{1,0:T(8,128)(2,1)}, u32[]{:S(2)}, u32[]{:S(2)}) collective-permute-start(bf16[192,1024]{1,0:T(8,128)(2,1)} %add_convert_fusion.9), channel_id=1, source_target_pairs={{0,2},{1,3},{2,0},{3,1},{4,6},{5,7},{6,4},{7,5},{8,10},{9,11},{10,... | collective-permute-start | bytes 1179656 | tf_op jit(solution)/shard_map/ppermute | solution.py:68
  373.9 186.2 %reduce-scatter.9.cloned.1.call-start = ((), (), s32[]{:S(2)}) async-start(), calls=%async_computation.5 | async-start | bytes 3063808
  378.7 12.6 %collective-permute-start.32 = (bf16[192,1024]{1,0:T(8,128)(2,1)S(1)}, bf16[192,1024]{1,0:T(8,128)(2,1)S(1)}, u32[]{:S(2)}, u32[]{:S(2)}) collective-permute-start(bf16[192,1024]{1,0:T(8,128)(2,1)S(1)} %add_convert_fusion.8), channel_id=1, source_target_pairs={{0,4},{1,5},{2,6},{3,7},{4,0},{5,1},{6,2},{7,3},{8,12},{9,13},{10,... | collective-permute-start | bytes 1179656 | tf_op jit(solution)/shard_map/ppermute | solution.py:68
  391.5 2.0 collective-permute-start.33
  401.2 14.0 %collective-permute-start.34 = (bf16[384,128]{1,0:T(8,128)(2,1)}, bf16[384,128]{1,0:T(8,128)(2,1)}, u32[]{:S(2)}, u32[]{:S(2)}) collective-permute-start(bf16[384,128]{1,0:T(8,128)(2,1)} %fusion.146), channel_id=1, source_target_pairs={{0,8},{8,0},{1,9},{9,1},{2,10},{10,2},{3,11},{11,3},{4,12},{12,4},... | collective-permute-start | bytes 294920 | tf_op jit(solution)/shard_map/ppermute | solution.py:82
  414.0 11.3 %collective-permute-start.35 = (bf16[384,128]{0,1:T(8,128)(2,1)S(1)}, bf16[384,128]{0,1:T(8,128)(2,1)S(1)}, u32[]{:S(2)}, u32[]{:S(2)}) collective-permute-start(bf16[384,128]{0,1:T(8,128)(2,1)S(1)} %fusion.148), channel_id=1, source_target_pairs={{0,8},{8,0},{1,9},{9,1},{2,10},{10,2},{3,11},{11,3},{4,12},{12,4},... | collective-permute-start | bytes 294920 | tf_op jit(solution)/shard_map/ppermute | solution.py:82
  427.5 4.2 collective-permute-start.36
  431.6 25.5 %collective-permute-start.47 = (bf16[2,2,1,2,64,512]{5,4,3,2,1,0:T(8,128)(2,1)}, bf16[2,2,1,2,64,512]{5,4,3,2,1,0:T(8,128)(2,1)}, u32[]{:S(2)}, u32[]{:S(2)}) collective-permute-start(bf16[2,2,1,2,64,512]{5,4,3,2,1,0:T(8,128)(2,1)} %constant_dynamic-slice_fusion), channel_id=1, source_target_pairs={{0,16},{16,0},{32,48},{48,32},{64,80},{80,64},{96,112},{112,96},{1... | collective-permute-start | bytes 1572872 | tf_op jit(solution)/shard_map/ppermute | solution.py:135
  433.7 24.9 %collective-permute-start.37 = (bf16[192,1024]{1,0:T(8,128)(2,1)}, bf16[192,1024]{1,0:T(8,128)(2,1)}, u32[]{:S(2)}, u32[]{:S(2)}) collective-permute-start(bf16[192,1024]{1,0:T(8,128)(2,1)} %add_convert_fusion.6), channel_id=1, source_target_pairs={{0,2},{1,3},{2,0},{3,1},{4,6},{5,7},{6,4},{7,5},{8,10},{9,11},{10,... | collective-permute-start | bytes 1179656 | tf_op jit(solution)/shard_map/ppermute | solution.py:68
  458.3 11.5 %collective-permute-start.48 = (bf16[2,1,1,2,64,512]{5,4,3,2,1,0:T(8,128)(2,1)S(1)}, bf16[2,1,1,2,64,512]{5,4,3,2,1,0:T(8,128)(2,1)S(1)}, u32[]{:S(2)}, u32[]{:S(2)}) collective-permute-start(bf16[2,1,1,2,64,512]{5,4,3,2,1,0:T(8,128)(2,1)S(1)} %dynamic-slice_convert_fusion), channel_id=1, source_target_pairs={{0,32},{16,48},{32,0},{48,16},{64,96},{80,112},{96,64},{112,80},{1... | collective-permute-start | bytes 786440 | tf_op jit(solution)/shard_map/ppermute | solution.py:135
  459.8 12.8 %collective-permute-start.38 = (bf16[192,1024]{1,0:T(8,128)(2,1)S(1)}, bf16[192,1024]{1,0:T(8,128)(2,1)S(1)}, u32[]{:S(2)}, u32[]{:S(2)}) collective-permute-start(bf16[192,1024]{1,0:T(8,128)(2,1)S(1)} %add_convert_fusion.5), channel_id=1, source_target_pairs={{0,4},{1,5},{2,6},{3,7},{4,0},{5,1},{6,2},{7,3},{8,12},{9,13},{10,... | collective-permute-start | bytes 1179656 | tf_op jit(solution)/shard_map/ppermute | solution.py:68
  470.0 6.6 %collective-permute-start.49 = (bf16[2,1,1,1,64,512]{5,4,3,2,1,0:T(8,128)(2,1)S(1)}, bf16[2,1,1,1,64,512]{5,4,3,2,1,0:T(8,128)(2,1)S(1)}, u32[]{:S(2)}, u32[]{:S(2)}) collective-permute-start(bf16[2,1,1,1,64,512]{5,4,3,2,1,0:T(8,128)(2,1)S(1)} %dynamic-slice_convert_fusion.1), channel_id=1, source_target_pairs={{0,8},{8,0},{1,9},{9,1},{2,10},{10,2},{3,11},{11,3},{4,12},{12,4},... | collective-permute-start | bytes 393224 | tf_op jit(solution)/shard_map/ppermute | solution.py:135
  472.8 3.9 collective-permute-start.39
  477.1 2.3 collective-permute-start.40
  477.2 6.1 %collective-permute-start.50 = (bf16[1,1,1,1,64,512]{5,4,3,2,1,0:T(8,128)(2,1)S(1)}, bf16[1,1,1,1,64,512]{5,4,3,2,1,0:T(8,128)(2,1)S(1)}, u32[]{:S(2)}, u32[]{:S(2)}) collective-permute-start(bf16[1,1,1,1,64,512]{5,4,3,2,1,0:T(8,128)(2,1)S(1)} %dynamic-slice_convert_fusion.10), channel_id=1, source_target_pairs={{0,64},{16,80},{32,96},{48,112},{64,0},{80,16},{96,32},{112,48},{1... | collective-permute-start | bytes 196616 | tf_op jit(solution)/shard_map/ppermute | solution.py:135
  479.4 26.1 %copy-start.126 = (f32[384]{0:T(512)S(1)}, f32[384]{0:T(512)}, u32[]{:S(2)}) copy-start(f32[384]{0:T(512)} %copy-done.125) | copy-start | bytes 4612
  479.4 3.9 collective-permute-start.41
  483.3 5.3 collective-permute-start.42
  488.7 5.7 collective-permute-start.43
  494.4 4.0 collective-permute-start.44
  498.4 4.1 collective-permute-start.45
  502.5 5.3 collective-permute-start.46
  (144 other events, 546.9 us)
Sparse Core Ops, SparseCore 0:
  13.8 98.2 all-gather.2
  113.8 92.6 all-gather.4
  374.0 99.1 reduce-scatter.6
  475.6 84.4 reduce-scatter.8

commit v6 on v5

--- a/solution.py
+++ b/solution.py
@@ -135,6 +135,33 @@
         received = lax.ppermute(sent.astype(jnp.bfloat16), axis_name, pairs)
         current = kept.astype(jnp.float32) + received.astype(jnp.float32)
     return current.reshape(rows, -1)
+
+
+def shard_gather(local):
+    fsdp_count = lax.axis_size("fsdp")
+    ctx_count = lax.axis_size("ctx")
+    fsdp_bits = []
+    step = 1
+    while step < fsdp_count:
+        fsdp_bits.append(step)
+        step *= 2
+    current = local.reshape((1,) * (len(fsdp_bits) + 1) + local.shape)
+    order = [("ctx", 1)] + [("fsdp", bit) for bit in fsdp_bits[2:]] + [("fsdp", 1), ("fsdp", 2)]
+    for axis_name, bit in order:
+        if axis_name == "fsdp":
+            dim = len(fsdp_bits) - 1 - fsdp_bits.index(bit)
+        else:
+            dim = len(fsdp_bits)
+        count = fsdp_count if axis_name == "fsdp" else ctx_count
+        pairs = [(device, device ^ bit) for device in range(count)]
+        received = lax.ppermute(current, axis_name, pairs)
+        upper = (lax.axis_index(axis_name) // bit) % 2
+        current = jnp.where(
+            upper == 0,
+            jnp.concatenate([current, received], axis=dim),
+            jnp.concatenate([received, current], axis=dim),
+        )
+    return current.reshape(-1, local.shape[1])
 
 
 def per_device(
@@ -205,9 +232,17 @@
         edges.append(edges[-1] + width)
 
     def gather_layer(layer_index):
-        joined = jnp.concatenate([member[layer_index] for member in weight_shards], axis=1)
-        full = lax.all_gather(joined, ("fsdp", "ctx"), axis=0, tiled=True)
-        return tuple(full[:, edges[k] : edges[k + 1]] for k in range(len(widths)))
+        early = jnp.concatenate([member[layer_index] for member in weight_shards[:3]], axis=1)
+        early_full = shard_gather(early)
+        late = jnp.concatenate([member[layer_index] for member in weight_shards[3:]], axis=1)
+        late_full = lax.all_gather(late, ("fsdp", "ctx"), axis=0, tiled=True)
+        pieces = []
+        for k in range(len(widths)):
+            if k < 3:
+                pieces.append(early_full[:, edges[k] : edges[k + 1]])
+            else:
+                pieces.append(late_full[:, edges[k] - edges[3] : edges[k + 1] - edges[3]])
+        return tuple(pieces)
 
     def scatter_terms(terms):
         joined = jnp.concatenate([term.astype(jnp.bfloat16) for term in terms], axis=1)

time: 584 us -> 582 us (level)
  matrix products: 70.4 us -> 59.1 us
    ppermute x0 -> x8, waiting for transfers between devices: none -> 68.6 us  [shard_gather(): received = lax.ppermute(current, axis_name, pairs)]
    all_gather x2, waiting for transfers between devices: 98.4 us -> 38.5 us  [gather_layer(): late_full = lax.all_gather(late, ('fsdp', 'ctx'), axis=0, tiled=True)]
    ppermute x16, waiting for transfers between devices: 104 us -> 86.1 us  [tp_sum(): received = lax.ppermute(mine, 'tp', pairs)]
    ppermute x8, waiting for transfers between devices: 10.7 us -> 21.6 us  [swap_halves(): return lax.ppermute(local, axis_name, [(0, 1), (1, 0)])]
    ppermute x0 -> x8, starting transfers between devices: none -> 10.4 us  [shard_gather(): received = lax.ppermute(current, axis_name, pairs)]
    squeeze x0 -> x5, local copies, waits for them, and re-layouts: none -> 7.24 us  [gather_layer(): member[layer_index]]
    unnamed x326 -> x344, local copies, waits for them, and re-layouts: 31.6 us -> 25 us
  transfers between devices with their start and end apart: 55 -> 63, of which waited for: 36 -> 45; matrix products, arithmetic and copies ran while one was open for 25% -> 24% of each run, Pallas kernels for 0% -> 0%
where the time goes in v6:
time: 582 us; the launch traced here: 571 us
  waiting for transfers between devices  317 us (54%)
  starting transfers between devices  67.7 us (12%)
  matrix products  59.1 us (10%)
  other arithmetic  56.9 us (10%)
  local copies, waits for them, and re-layouts  53.4 us (9%)
  between operations  17.1 us (3%)
    ppermute x16, waiting for transfers between devices, tp_sum(): received = lax.ppermute(mine, 'tp', pairs)  86.1 us
    ppermute x8, waiting for transfers between devices, shard_gather(): received = lax.ppermute(current, axis_name, pairs)  68.6 us
    unnamed x5, waiting for transfers between devices  46.5 us
    all_gather x2, waiting for transfers between devices, gather_layer(): late_full = lax.all_gather(late, ('fsdp', 'ctx'), axis=0, tiled=True)  38.5 us
    ppermute x16, starting transfers between devices, tp_sum(): received = lax.ppermute(mine, 'tp', pairs)  32.4 us
    ppermute x4, waiting for transfers between devices, shard_scatter(): received = lax.ppermute(sent.astype(jnp.bfloat16), axis_name, pairs)  28.4 us
    unnamed x344, local copies, waits for them, and re-layouts  25 us
    ppermute x8, waiting for transfers between devices, swap_halves(): return lax.ppermute(local, axis_name, [(0, 1), (1, 0)])  21.6 us
  transfers between devices with their start and end apart: 63, of which 45 were waited for; matrix products, arithmetic and copies ran while one was open for 24% of the time, Pallas kernels for 0%

profile of v6, /device:TPU:0, one launch (start us, length us, event | category | flops | bytes accessed | tf_op | source)
XLA Modules:
  0.0 571.3 jit_solution(13635335609320551730)
XLA Ops:
  10.2 4.0 collective-permute-start
  21.4 3.1 collective-permute-start.1
  24.6 3.4 collective-permute-done.1
  29.7 10.6 %collective-permute-done.2 = bf16[2,1,1,2,64,512]{5,4,3,2,1,0:T(8,128)(2,1)S(1)} collective-permute-done((bf16[2,1,1,2,64,512]{5,4,3,2,1,0:T(8,128)(2,1)S(1)}, bf16[2,1,1,2,64,512]{5,4,3,2,1,0:T(8,128)(2,1)S(1)}, u32[]{:S(2)}, u32[]{:S(2)}) %collective-permute-start.2) | collective-permute-done | bytes 262176 | tf_op jit(solution)/shard_map/ppermute | solution.py:157
  44.2 18.1 %collective-permute-done.3 = bf16[2,1,2,2,64,512]{5,4,3,2,1,0:T(8,128)(2,1)S(1)} collective-permute-done((bf16[2,1,2,2,64,512]{5,4,3,2,1,0:T(8,128)(2,1)S(1)}, bf16[2,1,2,2,64,512]{5,4,3,2,1,0:T(8,128)(2,1)S(1)}, u32[]{:S(2)}, u32[]{:S(2)}) %collective-permute-start.3) | collective-permute-done | bytes 524320 | tf_op jit(solution)/shard_map/ppermute | solution.py:157
  66.5 2.1 multiply_reduce_fusion.21
  71.5 3.6 collective-permute-start.5
  75.6 6.0 %collective-permute-done.5 = bf16[384,128]{1,0:T(8,128)(2,1)S(1)} collective-permute-done((bf16[384,128]{1,0:T(8,128)(2,1)S(1)}, bf16[384,128]{1,0:T(8,128)(2,1)S(1)}, u32[]{:S(2)}, u32[]{:S(2)}) %collective-permute-start.5) | collective-permute-done | bytes 98336 | tf_op jit(solution)/shard_map/ppermute | solution.py:82
  85.8 18.5 %all-gather.3.cloned.1.call-done = bf16[1024,1408]{1,0:T(8,128)(2,1)} async-done(((bf16[64,1408]{1,0:T(8,128)(2,1)}), bf16[1024,1408]{1,0:T(8,128)(2,1)}) %all-gather.3.cloned.1.call-update) | async-done | bytes 2883600 | tf_op jit(solution)/shard_map/all_gather | solution.py:238
  106.6 1.9 collective-permute-done.6
  108.6 2.5 collective-permute-start.7
  111.1 9.4 %collective-permute-done.7 = bf16[192,1024]{1,0:T(8,128)(2,1)S(1)} collective-permute-done((bf16[192,1024]{1,0:T(8,128)(2,1)S(1)}, bf16[192,1024]{1,0:T(8,128)(2,1)S(1)}, u32[]{:S(2)}, u32[]{:S(2)}) %collective-permute-start.7) | collective-permute-done | bytes 393248 | tf_op jit(solution)/shard_map/ppermute | solution.py:68
  120.7 2.0 collective-permute-start.8
  122.7 10.2 %collective-permute-done.8 = bf16[192,1024]{1,0:T(8,128)(2,1)S(1)} collective-permute-done((bf16[192,1024]{1,0:T(8,128)(2,1)S(1)}, bf16[192,1024]{1,0:T(8,128)(2,1)S(1)}, u32[]{:S(2)}, u32[]{:S(2)}) %collective-permute-start.8) | collective-permute-done | bytes 393248 | tf_op jit(solution)/shard_map/ppermute | solution.py:68
  144.8 2.0 collective-permute-done.14
  146.9 6.4 %collective-permute-done.15 = bf16[1,1,1,2,64,512]{5,4,3,2,1,0:T(8,128)(2,1)S(1)} collective-permute-done((bf16[1,1,1,2,64,512]{5,4,3,2,1,0:T(8,128)(2,1)S(1)}, bf16[1,1,1,2,64,512]{5,4,3,2,1,0:T(8,128)(2,1)S(1)}, u32[]{:S(2)}, u32[]{:S(2)}) %collective-permute-start.15) | collective-permute-done | bytes 131104 | tf_op jit(solution)/shard_map/ppermute | solution.py:157
  155.6 8.9 %collective-permute-done.16 = bf16[2,1,1,2,64,512]{5,4,3,2,1,0:T(8,128)(2,1)S(1)} collective-permute-done((bf16[2,1,1,2,64,512]{5,4,3,2,1,0:T(8,128)(2,1)S(1)}, bf16[2,1,1,2,64,512]{5,4,3,2,1,0:T(8,128)(2,1)S(1)}, u32[]{:S(2)}, u32[]{:S(2)}) %collective-permute-start.16) | collective-permute-done | bytes 262176 | tf_op jit(solution)/shard_map/ppermute | solution.py:157
  166.0 19.1 %collective-permute-done.17 = bf16[2,1,2,2,64,512]{5,4,3,2,1,0:T(8,128)(2,1)S(1)} collective-permute-done((bf16[2,1,2,2,64,512]{5,4,3,2,1,0:T(8,128)(2,1)S(1)}, bf16[2,1,2,2,64,512]{5,4,3,2,1,0:T(8,128)(2,1)S(1)}, u32[]{:S(2)}, u32[]{:S(2)}) %collective-permute-start.17) | collective-permute-done | bytes 524320 | tf_op jit(solution)/shard_map/ppermute | solution.py:157
  193.3 3.6 collective-permute-start.19
  198.1 5.0 collective-permute-done.19
  207.3 20.0 %all-gather.5.cloned.1.call-done = bf16[1024,1408]{1,0:T(8,128)(2,1)} async-done(((bf16[64,1408]{1,0:T(8,128)(2,1)}), bf16[1024,1408]{1,0:T(8,128)(2,1)}) %all-gather.5.cloned.1.call-update) | async-done | bytes 2883600 | tf_op jit(solution)/shard_map/all_gather | solution.py:238
  230.9 2.4 collective-permute-start.21
  233.4 9.4 %collective-permute-done.21 = bf16[192,1024]{1,0:T(8,128)(2,1)S(1)} collective-permute-done((bf16[192,1024]{1,0:T(8,128)(2,1)S(1)}, bf16[192,1024]{1,0:T(8,128)(2,1)S(1)}, u32[]{:S(2)}, u32[]{:S(2)}) %collective-permute-start.21) | collective-permute-done | bytes 393248 | tf_op jit(solution)/shard_map/ppermute | solution.py:68
  242.9 4.2 collective-permute-start.22
  247.1 8.6 %collective-permute-done.22 = bf16[192,1024]{1,0:T(8,128)(2,1)S(1)} collective-permute-done((bf16[192,1024]{1,0:T(8,128)(2,1)S(1)}, bf16[192,1024]{1,0:T(8,128)(2,1)S(1)}, u32[]{:S(2)}, u32[]{:S(2)}) %collective-permute-start.22) | collective-permute-done | bytes 393248 | tf_op jit(solution)/shard_map/ppermute | solution.py:68
  265.9 8.8 %collective-permute-done.29 = bf16[192,1024]{1,0:T(8,128)(2,1)S(1)} collective-permute-done((bf16[192,1024]{1,0:T(8,128)(2,1)S(1)}, bf16[192,1024]{1,0:T(8,128)(2,1)S(1)}, u32[]{:S(2)}, u32[]{:S(2)}) %collective-permute-start.29) | collective-permute-done | bytes 393248 | tf_op jit(solution)/shard_map/ppermute | solution.py:68
  275.6 3.2 collective-permute-start.30
  280.2 9.3 %collective-permute-done.30 = bf16[192,1024]{1,0:T(8,128)(2,1)} collective-permute-done((bf16[192,1024]{1,0:T(8,128)(2,1)}, bf16[192,1024]{1,0:T(8,128)(2,1)}, u32[]{:S(2)}, u32[]{:S(2)}) %collective-permute-start.30) | collective-permute-done | bytes 393248 | tf_op jit(solution)/shard_map/ppermute | solution.py:68
  292.1 3.5 collective-permute-done.25
  296.4 2.3 collective-permute-start.26
  299.2 2.0 multiply_add_fusion.3
  311.0 1.9 copy.170
  318.1 2.2 collective-permute-start.33
  320.3 2.5 collective-permute-done.32
  332.2 7.9 %collective-permute-done.35 = bf16[192,1024]{1,0:T(8,128)(2,1)S(1)} collective-permute-done((bf16[192,1024]{1,0:T(8,128)(2,1)S(1)}, bf16[192,1024]{1,0:T(8,128)(2,1)S(1)}, u32[]{:S(2)}, u32[]{:S(2)}) %collective-permute-start.35) | collective-permute-done | bytes 393248 | tf_op jit(solution)/shard_map/ppermute | solution.py:68
  340.2 2.8 collective-permute-start.36
  344.6 7.5 %collective-permute-done.36 = bf16[192,1024]{1,0:T(8,128)(2,1)S(1)} collective-permute-done((bf16[192,1024]{1,0:T(8,128)(2,1)S(1)}, bf16[192,1024]{1,0:T(8,128)(2,1)S(1)}, u32[]{:S(2)}, u32[]{:S(2)}) %collective-permute-start.36) | collective-permute-done | bytes 393248 | tf_op jit(solution)/shard_map/ppermute | solution.py:68
  366.9 6.3 %copy.224 = bf16[1024,1920]{1,0:T(8,128)(2,1)} copy(bf16[1024,1920]{0,1:T(8,128)(2,1)} %fusion.19) | data formatting | bytes 7864320
  374.3 2.5 convolution_convert_fusion.3
  378.1 3.9 collective-permute-start.40
  383.9 7.4 %collective-permute-done.40 = bf16[192,1024]{1,0:T(8,128)(2,1)S(1)} collective-permute-done((bf16[192,1024]{1,0:T(8,128)(2,1)S(1)}, bf16[192,1024]{1,0:T(8,128)(2,1)S(1)}, u32[]{:S(2)}, u32[]{:S(2)}) %collective-permute-start.40) | collective-permute-done | bytes 393248 | tf_op jit(solution)/shard_map/ppermute | solution.py:68
  396.4 2.0 fusion
  404.0 2.0 convolution_bitcast_fusion.1
  411.0 2.1 collective-permute-start.43
  413.0 5.0 collective-permute-done.42
  419.8 3.0 collective-permute-done.43
  425.8 2.3 copy.187
  428.1 2.0 constant_dynamic-slice_fusion
  430.2 2.0 add_convert_fusion.6
  432.8 2.8 pad_maximum_fusion
  435.6 4.6 copy.226
  440.2 15.4 %collective-permute-done.55 = bf16[2,2,1,2,64,512]{5,4,3,2,1,0:T(8,128)(2,1)} collective-permute-done((bf16[2,2,1,2,64,512]{5,4,3,2,1,0:T(8,128)(2,1)}, bf16[2,2,1,2,64,512]{5,4,3,2,1,0:T(8,128)(2,1)}, u32[]{:S(2)}, u32[]{:S(2)}) %collective-permute-start.55) | collective-permute-done | bytes 524320 | tf_op jit(solution)/shard_map/ppermute | solution.py:135
  458.4 3.1 collective-permute-start.46
  461.7 6.1 %collective-permute-done.56 = bf16[2,1,1,2,64,512]{5,4,3,2,1,0:T(8,128)(2,1)S(1)} collective-permute-done((bf16[2,1,1,2,64,512]{5,4,3,2,1,0:T(8,128)(2,1)S(1)}, bf16[2,1,1,2,64,512]{5,4,3,2,1,0:T(8,128)(2,1)S(1)}, u32[]{:S(2)}, u32[]{:S(2)}) %collective-permute-start.56) | collective-permute-done | bytes 262176 | tf_op jit(solution)/shard_map/ppermute | solution.py:135
  468.0 2.8 collective-permute-done.46
  471.1 3.5 collective-permute-done.57
  477.9 3.4 collective-permute-done.58
  481.3 2.8 collective-permute-start.50
  484.1 2.6 collective-permute-done.50
  487.6 5.3 collective-permute-done.51
  493.4 3.6 collective-permute-done.52
  497.1 3.7 collective-permute-done.53
  503.6 2.6 collective-permute-done.54
  512.2 46.5 %reduce-scatter.9.cloned.1.call-done = bf16[64,1408]{1,0:T(8,128)(2,1)} async-done(((bf16[1024,1408]{1,0:T(8,128)(2,1)}), bf16[64,1408]{1,0:T(8,128)(2,1)}) %reduce-scatter.9.cloned.1.call-update) | async-done | bytes 180240
  (653 shorter events, 165.6 us)
Async XLA Ops:
  7.2 97.1 %all-gather.3.cloned.1.call-start = ((), (), s32[]{:S(2)}) async-start(), calls=%async_computation.2 | async-start | bytes 3063808 | tf_op jit(solution)/shard_map/all_gather | solution.py:238
  10.2 11.2 %collective-permute-start = (bf16[1,1,1,1,64,512]{5,4,3,2,1,0:T(8,128)(2,1)S(1)}, bf16[1,1,1,1,64,512]{5,4,3,2,1,0:T(8,128)(2,1)S(1)}, u32[]{:S(2)}, u32[]{:S(2)}) collective-permute-start(bf16[1,1,1,1,64,512]{5,4,3,2,1,0:T(8,128)(2,1)S(1)} %get-tuple-element.139), channel_id=1, source_target_pairs={{0,8},{8,0},{1,9},{9,1},{2,10},{10,2},{3,11},{11,3},{4,12},{12,4},... | collective-permute-start | bytes 196616 | tf_op jit(solution)/shard_map/ppermute | solution.py:157
  19.3 208.0 %all-gather.5.cloned.1.call-start = ((), (), s32[]{:S(2)}) async-start(), calls=%async_computation.3 | async-start | bytes 3063808 | tf_op jit(solution)/shard_map/all_gather | solution.py:238
  21.2 54.2 %copy-start.65 = (f32[384,64]{1,0:T(8,128)}, f32[384,64]{1,0:T(8,128)S(1)}, u32[]{:S(2)}) copy-start(f32[384,64]{1,0:T(8,128)S(1)} %get-tuple-element.153) | copy-start | bytes 294916
  21.4 6.6 %collective-permute-start.1 = (bf16[1,1,1,2,64,512]{5,4,3,2,1,0:T(8,128)(2,1)S(1)}, bf16[1,1,1,2,64,512]{5,4,3,2,1,0:T(8,128)(2,1)S(1)}, u32[]{:S(2)}, u32[]{:S(2)}) collective-permute-start(bf16[1,1,1,2,64,512]{5,4,3,2,1,0:T(8,128)(2,1)S(1)} %maximum_select_fusion.21), channel_id=1, source_target_pairs={{0,64},{16,80},{32,96},{48,112},{64,0},{80,16},{96,32},{112,48},{1... | collective-permute-start | bytes 393224 | tf_op jit(solution)/shard_map/ppermute | solution.py:157
  28.0 12.4 %collective-permute-start.2 = (bf16[2,1,1,2,64,512]{5,4,3,2,1,0:T(8,128)(2,1)S(1)}, bf16[2,1,1,2,64,512]{5,4,3,2,1,0:T(8,128)(2,1)S(1)}, u32[]{:S(2)}, u32[]{:S(2)}) collective-permute-start(bf16[2,1,1,2,64,512]{5,4,3,2,1,0:T(8,128)(2,1)S(1)} %maximum_select_fusion.13), channel_id=1, source_target_pairs={{0,16},{16,0},{32,48},{48,32},{64,80},{80,64},{96,112},{112,96},{1... | collective-permute-start | bytes 786440 | tf_op jit(solution)/shard_map/ppermute | solution.py:157
  40.4 21.9 %collective-permute-start.3 = (bf16[2,1,2,2,64,512]{5,4,3,2,1,0:T(8,128)(2,1)S(1)}, bf16[2,1,2,2,64,512]{5,4,3,2,1,0:T(8,128)(2,1)S(1)}, u32[]{:S(2)}, u32[]{:S(2)}) collective-permute-start(bf16[2,1,2,2,64,512]{5,4,3,2,1,0:T(8,128)(2,1)S(1)} %maximum_select_fusion.10), channel_id=1, source_target_pairs={{0,32},{16,48},{32,0},{48,16},{64,96},{80,112},{96,64},{112,80},{1... | collective-permute-start | bytes 1572872 | tf_op jit(solution)/shard_map/ppermute | solution.py:157
  63.5 19.1 %collective-permute-start.4 = (bf16[384,128]{1,0:T(8,128)(2,1)}, bf16[384,128]{1,0:T(8,128)(2,1)}, u32[]{:S(2)}, u32[]{:S(2)}) collective-permute-start(bf16[384,128]{1,0:T(8,128)(2,1)} %convolution_convert_fusion.23), channel_id=1, source_target_pairs={{0,8},{8,0},{1,9},{9,1},{2,10},{10,2},{3,11},{11,3},{4,12},{12,4},... | collective-permute-start | bytes 294920 | tf_op jit(solution)/shard_map/ppermute | solution.py:82
  71.5 10.1 %collective-permute-start.5 = (bf16[384,128]{1,0:T(8,128)(2,1)S(1)}, bf16[384,128]{1,0:T(8,128)(2,1)S(1)}, u32[]{:S(2)}, u32[]{:S(2)}) collective-permute-start(bf16[384,128]{1,0:T(8,128)(2,1)S(1)} %pad_maximum_fusion.12), channel_id=1, source_target_pairs={{0,8},{8,0},{1,9},{9,1},{2,10},{10,2},{3,11},{11,3},{4,12},{12,4},... | collective-permute-start | bytes 294920 | tf_op jit(solution)/shard_map/ppermute | solution.py:82
  106.6 1.9 collective-permute-start.6
  108.6 11.9 %collective-permute-start.7 = (bf16[192,1024]{1,0:T(8,128)(2,1)S(1)}, bf16[192,1024]{1,0:T(8,128)(2,1)S(1)}, u32[]{:S(2)}, u32[]{:S(2)}) collective-permute-start(bf16[192,1024]{1,0:T(8,128)(2,1)S(1)} %add_convert_fusion.27), channel_id=1, source_target_pairs={{0,2},{1,3},{2,0},{3,1},{4,6},{5,7},{6,4},{7,5},{8,10},{9,11},{10,... | collective-permute-start | bytes 1179656 | tf_op jit(solution)/shard_map/ppermute | solution.py:68
  120.7 12.2 %collective-permute-start.8 = (bf16[192,1024]{1,0:T(8,128)(2,1)S(1)}, bf16[192,1024]{1,0:T(8,128)(2,1)S(1)}, u32[]{:S(2)}, u32[]{:S(2)}) collective-permute-start(bf16[192,1024]{1,0:T(8,128)(2,1)S(1)} %add_convert_fusion.26), channel_id=1, source_target_pairs={{0,4},{1,5},{2,6},{3,7},{4,0},{5,1},{6,2},{7,3},{8,12},{9,13},{10,... | collective-permute-start | bytes 1179656 | tf_op jit(solution)/shard_map/ppermute | solution.py:68
  133.1 2.0 collective-permute-start.9
  140.5 1.8 collective-permute-start.10
  140.8 6.0 %collective-permute-start.14 = (bf16[1,1,1,1,64,512]{5,4,3,2,1,0:T(8,128)(2,1)S(1)}, bf16[1,1,1,1,64,512]{5,4,3,2,1,0:T(8,128)(2,1)S(1)}, u32[]{:S(2)}, u32[]{:S(2)}) collective-permute-start(bf16[1,1,1,1,64,512]{5,4,3,2,1,0:T(8,128)(2,1)S(1)} %get-tuple-element.134), channel_id=1, source_target_pairs={{0,8},{8,0},{1,9},{9,1},{2,10},{10,2},{3,11},{11,3},{4,12},{12,4},... | collective-permute-start | bytes 196616 | tf_op jit(solution)/shard_map/ppermute | solution.py:157
  142.5 11.2 %collective-permute-start.11 = (bf16[192,1024]{1,0:T(8,128)(2,1)S(1)}, bf16[192,1024]{1,0:T(8,128)(2,1)S(1)}, u32[]{:S(2)}, u32[]{:S(2)}) collective-permute-start(bf16[192,1024]{1,0:T(8,128)(2,1)S(1)} %add_convert_fusion.24), channel_id=1, source_target_pairs={{0,2},{1,3},{2,0},{3,1},{4,6},{5,7},{6,4},{7,5},{8,10},{9,11},{10,... | collective-permute-start | bytes 1179656 | tf_op jit(solution)/shard_map/ppermute | solution.py:68
  144.7 362.6 %reduce-scatter.7.cloned.1.call-start = ((), (), s32[]{:S(2)}) async-start(), calls=%async_computation.4 | async-start | bytes 4177920 | tf_op jit(solution)/shard_map/reduce_scatter | solution.py:249
  146.8 6.6 %collective-permute-start.15 = (bf16[1,1,1,2,64,512]{5,4,3,2,1,0:T(8,128)(2,1)S(1)}, bf16[1,1,1,2,64,512]{5,4,3,2,1,0:T(8,128)(2,1)S(1)}, u32[]{:S(2)}, u32[]{:S(2)}) collective-permute-start(bf16[1,1,1,2,64,512]{5,4,3,2,1,0:T(8,128)(2,1)S(1)} %maximum_select_fusion.23), channel_id=1, source_target_pairs={{0,64},{16,80},{32,96},{48,112},{64,0},{80,16},{96,32},{112,48},{1... | collective-permute-start | bytes 393224 | tf_op jit(solution)/shard_map/ppermute | solution.py:157
  153.3 11.2 %collective-permute-start.16 = (bf16[2,1,1,2,64,512]{5,4,3,2,1,0:T(8,128)(2,1)S(1)}, bf16[2,1,1,2,64,512]{5,4,3,2,1,0:T(8,128)(2,1)S(1)}, u32[]{:S(2)}, u32[]{:S(2)}) collective-permute-start(bf16[2,1,1,2,64,512]{5,4,3,2,1,0:T(8,128)(2,1)S(1)} %maximum_select_fusion.15), channel_id=1, source_target_pairs={{0,16},{16,0},{32,48},{48,32},{64,80},{80,64},{96,112},{112,96},{1... | collective-permute-start | bytes 786440 | tf_op jit(solution)/shard_map/ppermute | solution.py:157
  153.9 11.9 %collective-permute-start.12 = (bf16[192,1024]{1,0:T(8,128)(2,1)S(1)}, bf16[192,1024]{1,0:T(8,128)(2,1)S(1)}, u32[]{:S(2)}, u32[]{:S(2)}) collective-permute-start(bf16[192,1024]{1,0:T(8,128)(2,1)S(1)} %add_convert_fusion.23), channel_id=1, source_target_pairs={{0,4},{1,5},{2,6},{3,7},{4,0},{5,1},{6,2},{7,3},{8,12},{9,13},{10,... | collective-permute-start | bytes 1179656 | tf_op jit(solution)/shard_map/ppermute | solution.py:68
  164.7 20.4 %collective-permute-start.17 = (bf16[2,1,2,2,64,512]{5,4,3,2,1,0:T(8,128)(2,1)S(1)}, bf16[2,1,2,2,64,512]{5,4,3,2,1,0:T(8,128)(2,1)S(1)}, u32[]{:S(2)}, u32[]{:S(2)}) collective-permute-start(bf16[2,1,2,2,64,512]{5,4,3,2,1,0:T(8,128)(2,1)S(1)} %maximum_select_fusion.11), channel_id=1, source_target_pairs={{0,32},{16,48},{32,0},{48,16},{64,96},{80,112},{96,64},{112,80},{1... | collective-permute-start | bytes 1572872 | tf_op jit(solution)/shard_map/ppermute | solution.py:157
  165.9 19.3 %collective-permute-start.13 = (bf16[192,1024]{1,0:T(8,128)(2,1)S(1)}, bf16[192,1024]{1,0:T(8,128)(2,1)S(1)}, u32[]{:S(2)}, u32[]{:S(2)}) collective-permute-start(bf16[192,1024]{1,0:T(8,128)(2,1)S(1)} %add_convert_fusion.22), channel_id=1, source_target_pairs={{0,1},{1,0},{2,3},{3,2},{4,5},{5,4},{6,7},{7,6},{8,9},{9,8},{10,11... | collective-permute-start | bytes 1179656 | tf_op jit(solution)/shard_map/ppermute | solution.py:72
  188.4 15.7 %collective-permute-start.18 = (bf16[384,128]{1,0:T(8,128)(2,1)}, bf16[384,128]{1,0:T(8,128)(2,1)}, u32[]{:S(2)}, u32[]{:S(2)}) collective-permute-start(bf16[384,128]{1,0:T(8,128)(2,1)} %convolution_convert_fusion.22), channel_id=1, source_target_pairs={{0,8},{8,0},{1,9},{9,1},{2,10},{10,2},{3,11},{11,3},{4,12},{12,4},... | collective-permute-start | bytes 294920 | tf_op jit(solution)/shard_map/ppermute | solution.py:82
  193.3 9.8 %collective-permute-start.19 = (bf16[384,128]{1,0:T(8,128)(2,1)S(1)}, bf16[384,128]{1,0:T(8,128)(2,1)S(1)}, u32[]{:S(2)}, u32[]{:S(2)}) collective-permute-start(bf16[384,128]{1,0:T(8,128)(2,1)S(1)} %pad_maximum_fusion.13), channel_id=1, source_target_pairs={{0,8},{8,0},{1,9},{9,1},{2,10},{10,2},{3,11},{11,3},{4,12},{12,4},... | collective-permute-start | bytes 294920 | tf_op jit(solution)/shard_map/ppermute | solution.py:82
  229.0 1.8 collective-permute-start.20
  230.9 11.9 %collective-permute-start.21 = (bf16[192,1024]{1,0:T(8,128)(2,1)S(1)}, bf16[192,1024]{1,0:T(8,128)(2,1)S(1)}, u32[]{:S(2)}, u32[]{:S(2)}) collective-permute-start(bf16[192,1024]{1,0:T(8,128)(2,1)S(1)} %add_convert_fusion.21), channel_id=1, source_target_pairs={{0,2},{1,3},{2,0},{3,1},{4,6},{5,7},{6,4},{7,5},{8,10},{9,11},{10,... | collective-permute-start | bytes 1179656 | tf_op jit(solution)/shard_map/ppermute | solution.py:68
  242.9 12.8 %collective-permute-start.22 = (bf16[192,1024]{1,0:T(8,128)(2,1)S(1)}, bf16[192,1024]{1,0:T(8,128)(2,1)S(1)}, u32[]{:S(2)}, u32[]{:S(2)}) collective-permute-start(bf16[192,1024]{1,0:T(8,128)(2,1)S(1)} %add_convert_fusion.20), channel_id=1, source_target_pairs={{0,4},{1,5},{2,6},{3,7},{4,0},{5,1},{6,2},{7,3},{8,12},{9,13},{10,... | collective-permute-start | bytes 1179656 | tf_op jit(solution)/shard_map/ppermute | solution.py:68
  255.9 1.8 collective-permute-start.23
  261.5 1.8 collective-permute-start.28
  263.4 11.2 %collective-permute-start.29 = (bf16[192,1024]{1,0:T(8,128)(2,1)S(1)}, bf16[192,1024]{1,0:T(8,128)(2,1)S(1)}, u32[]{:S(2)}, u32[]{:S(2)}) collective-permute-start(bf16[192,1024]{1,0:T(8,128)(2,1)S(1)} %add_convert_fusion.15), channel_id=1, source_target_pairs={{0,2},{1,3},{2,0},{3,1},{4,6},{5,7},{6,4},{7,5},{8,10},{9,11},{10,... | collective-permute-start | bytes 1179656 | tf_op jit(solution)/shard_map/ppermute | solution.py:68
  265.9 12.9 %collective-permute-start.24 = (bf16[192,1024]{1,0:T(8,128)(2,1)}, bf16[192,1024]{1,0:T(8,128)(2,1)}, u32[]{:S(2)}, u32[]{:S(2)}) collective-permute-start(bf16[192,1024]{1,0:T(8,128)(2,1)} %constant_dynamic-slice_fusion.5), channel_id=1, source_target_pairs={{0,1},{1,0},{2,3},{3,2},{4,5},{5,4},{6,7},{7,6},{8,9},{9,8},{10,11... | collective-permute-start | bytes 1179656 | tf_op jit(solution)/shard_map/ppermute | solution.py:62
  275.6 13.9 %collective-permute-start.30 = (bf16[192,1024]{1,0:T(8,128)(2,1)}, bf16[192,1024]{1,0:T(8,128)(2,1)}, u32[]{:S(2)}, u32[]{:S(2)}) collective-permute-start(bf16[192,1024]{1,0:T(8,128)(2,1)} %add_convert_fusion.14), channel_id=1, source_target_pairs={{0,4},{1,5},{2,6},{3,7},{4,0},{5,1},{6,2},{7,3},{8,12},{9,13},{10,... | collective-permute-start | bytes 1179656 | tf_op jit(solution)/shard_map/ppermute | solution.py:68
  280.1 15.5 %collective-permute-start.25 = (bf16[192,1024]{1,0:T(8,128)(2,1)S(1)}, bf16[192,1024]{1,0:T(8,128)(2,1)S(1)}, u32[]{:S(2)}, u32[]{:S(2)}) collective-permute-start(bf16[192,1024]{1,0:T(8,128)(2,1)S(1)} %add_convert_fusion.18), channel_id=1, source_target_pairs={{0,2},{1,3},{2,0},{3,1},{4,6},{5,7},{6,4},{7,5},{8,10},{9,11},{10,... | collective-permute-start | bytes 1179656 | tf_op jit(solution)/shard_map/ppermute | solution.py:68
  290.7 8.1 %collective-permute-start.31 = (bf16[192,1024]{1,0:T(8,128)(2,1)S(1)}, bf16[192,1024]{1,0:T(8,128)(2,1)S(1)}, u32[]{:S(2)}, u32[]{:S(2)}) collective-permute-start(bf16[192,1024]{1,0:T(8,128)(2,1)S(1)} %add_convert_fusion.13), channel_id=1, source_target_pairs={{0,1},{1,0},{2,3},{3,2},{4,5},{5,4},{6,7},{7,6},{8,9},{9,8},{10,11... | collective-permute-start | bytes 1179656 | tf_op jit(solution)/shard_map/ppermute | solution.py:72
  296.4 29.2 %collective-permute-start.26 = (bf16[192,1024]{1,0:T(8,128)(2,1)}, bf16[192,1024]{1,0:T(8,128)(2,1)}, u32[]{:S(2)}, u32[]{:S(2)}) collective-permute-start(bf16[192,1024]{1,0:T(8,128)(2,1)} %add_convert_fusion.17), channel_id=1, source_target_pairs={{0,4},{1,5},{2,6},{3,7},{4,0},{5,1},{6,2},{7,3},{8,12},{9,13},{10,... | collective-permute-start | bytes 1179656 | tf_op jit(solution)/shard_map/ppermute | solution.py:68
  316.6 6.2 %collective-permute-start.32 = (bf16[384,128]{1,0:T(8,128)(2,1)S(1)}, bf16[384,128]{1,0:T(8,128)(2,1)S(1)}, u32[]{:S(2)}, u32[]{:S(2)}) collective-permute-start(bf16[384,128]{1,0:T(8,128)(2,1)S(1)} %fusion.143), channel_id=1, source_target_pairs={{0,8},{8,0},{1,9},{9,1},{2,10},{10,2},{3,11},{11,3},{4,12},{12,4},... | collective-permute-start | bytes 294920 | tf_op jit(solution)/shard_map/ppermute | solution.py:82
  318.1 6.9 %collective-permute-start.33 = (bf16[384,128]{0,1:T(8,128)(2,1)S(1)}, bf16[384,128]{0,1:T(8,128)(2,1)S(1)}, u32[]{:S(2)}, u32[]{:S(2)}) collective-permute-start(bf16[384,128]{0,1:T(8,128)(2,1)S(1)} %fusion.145), channel_id=1, source_target_pairs={{0,8},{8,0},{1,9},{9,1},{2,10},{10,2},{3,11},{11,3},{4,12},{12,4},... | collective-permute-start | bytes 294920 | tf_op jit(solution)/shard_map/ppermute | solution.py:82
  325.5 3.2 collective-permute-start.34
  327.0 3.6 collective-permute-start.27
  328.9 11.2 %collective-permute-start.35 = (bf16[192,1024]{1,0:T(8,128)(2,1)S(1)}, bf16[192,1024]{1,0:T(8,128)(2,1)S(1)}, u32[]{:S(2)}, u32[]{:S(2)}) collective-permute-start(bf16[192,1024]{1,0:T(8,128)(2,1)S(1)} %add_convert_fusion.12), channel_id=1, source_target_pairs={{0,2},{1,3},{2,0},{3,1},{4,6},{5,7},{6,4},{7,5},{8,10},{9,11},{10,... | collective-permute-start | bytes 1179656 | tf_op jit(solution)/shard_map/ppermute | solution.py:68
  340.2 11.9 %collective-permute-start.36 = (bf16[192,1024]{1,0:T(8,128)(2,1)S(1)}, bf16[192,1024]{1,0:T(8,128)(2,1)S(1)}, u32[]{:S(2)}, u32[]{:S(2)}) collective-permute-start(bf16[192,1024]{1,0:T(8,128)(2,1)S(1)} %add_convert_fusion.11), channel_id=1, source_target_pairs={{0,4},{1,5},{2,6},{3,7},{4,0},{5,1},{6,2},{7,3},{8,12},{9,13},{10,... | collective-permute-start | bytes 1179656 | tf_op jit(solution)/shard_map/ppermute | solution.py:68
  352.2 2.6 collective-permute-start.37
  360.2 3.7 collective-permute-start.38
  364.7 12.1 %collective-permute-start.39 = (bf16[192,1024]{1,0:T(8,128)(2,1)}, bf16[192,1024]{1,0:T(8,128)(2,1)}, u32[]{:S(2)}, u32[]{:S(2)}) collective-permute-start(bf16[192,1024]{1,0:T(8,128)(2,1)} %add_convert_fusion.9), channel_id=1, source_target_pairs={{0,2},{1,3},{2,0},{3,1},{4,6},{5,7},{6,4},{7,5},{8,10},{9,11},{10,... | collective-permute-start | bytes 1179656 | tf_op jit(solution)/shard_map/ppermute | solution.py:68
  373.2 185.5 %reduce-scatter.9.cloned.1.call-start = ((), (), s32[]{:S(2)}) async-start(), calls=%async_computation.5 | async-start | bytes 3063808
  378.1 13.3 %collective-permute-start.40 = (bf16[192,1024]{1,0:T(8,128)(2,1)S(1)}, bf16[192,1024]{1,0:T(8,128)(2,1)S(1)}, u32[]{:S(2)}, u32[]{:S(2)}) collective-permute-start(bf16[192,1024]{1,0:T(8,128)(2,1)S(1)} %add_convert_fusion.8), channel_id=1, source_target_pairs={{0,4},{1,5},{2,6},{3,7},{4,0},{5,1},{6,2},{7,3},{8,12},{9,13},{10,... | collective-permute-start | bytes 1179656 | tf_op jit(solution)/shard_map/ppermute | solution.py:68
  391.6 2.0 collective-permute-start.41
  406.1 11.9 %collective-permute-start.42 = (bf16[384,128]{1,0:T(8,128)(2,1)S(1)}, bf16[384,128]{1,0:T(8,128)(2,1)S(1)}, u32[]{:S(2)}, u32[]{:S(2)}) collective-permute-start(bf16[384,128]{1,0:T(8,128)(2,1)S(1)} %fusion.147), channel_id=1, source_target_pairs={{0,8},{8,0},{1,9},{9,1},{2,10},{10,2},{3,11},{11,3},{4,12},{12,4},... | collective-permute-start | bytes 294920 | tf_op jit(solution)/shard_map/ppermute | solution.py:82
  411.0 11.9 %collective-permute-start.43 = (bf16[384,128]{0,1:T(8,128)(2,1)S(1)}, bf16[384,128]{0,1:T(8,128)(2,1)S(1)}, u32[]{:S(2)}, u32[]{:S(2)}) collective-permute-start(bf16[384,128]{0,1:T(8,128)(2,1)S(1)} %fusion.149), channel_id=1, source_target_pairs={{0,8},{8,0},{1,9},{9,1},{2,10},{10,2},{3,11},{11,3},{4,12},{12,4},... | collective-permute-start | bytes 294920 | tf_op jit(solution)/shard_map/ppermute | solution.py:82
  424.1 6.1 %collective-permute-start.44 = (bf16[192,1024]{1,0:T(8,128)(2,1)}, bf16[192,1024]{1,0:T(8,128)(2,1)}, u32[]{:S(2)}, u32[]{:S(2)}) collective-permute-start(bf16[192,1024]{1,0:T(8,128)(2,1)} %constant_dynamic-slice_fusion.1), channel_id=1, source_target_pairs={{0,1},{1,0},{2,3},{3,2},{4,5},{5,4},{6,7},{7,6},{8,9},{9,8},{10,11... | collective-permute-start | bytes 1179656 | tf_op jit(solution)/shard_map/ppermute | solution.py:62
  430.1 25.4 %collective-permute-start.55 = (bf16[2,2,1,2,64,512]{5,4,3,2,1,0:T(8,128)(2,1)}, bf16[2,2,1,2,64,512]{5,4,3,2,1,0:T(8,128)(2,1)}, u32[]{:S(2)}, u32[]{:S(2)}) collective-permute-start(bf16[2,2,1,2,64,512]{5,4,3,2,1,0:T(8,128)(2,1)} %constant_dynamic-slice_fusion), channel_id=1, source_target_pairs={{0,16},{16,0},{32,48},{48,32},{64,80},{80,64},{96,112},{112,96},{1... | collective-permute-start | bytes 1572872 | tf_op jit(solution)/shard_map/ppermute | solution.py:135
  432.2 24.9 %collective-permute-start.45 = (bf16[192,1024]{1,0:T(8,128)(2,1)}, bf16[192,1024]{1,0:T(8,128)(2,1)}, u32[]{:S(2)}, u32[]{:S(2)}) collective-permute-start(bf16[192,1024]{1,0:T(8,128)(2,1)} %add_convert_fusion.6), channel_id=1, source_target_pairs={{0,2},{1,3},{2,0},{3,1},{4,6},{5,7},{6,4},{7,5},{8,10},{9,11},{10,... | collective-permute-start | bytes 1179656 | tf_op jit(solution)/shard_map/ppermute | solution.py:68
  457.0 10.8 %collective-permute-start.56 = (bf16[2,1,1,2,64,512]{5,4,3,2,1,0:T(8,128)(2,1)S(1)}, bf16[2,1,1,2,64,512]{5,4,3,2,1,0:T(8,128)(2,1)S(1)}, u32[]{:S(2)}, u32[]{:S(2)}) collective-permute-start(bf16[2,1,1,2,64,512]{5,4,3,2,1,0:T(8,128)(2,1)S(1)} %dynamic-slice_convert_fusion), channel_id=1, source_target_pairs={{0,32},{16,48},{32,0},{48,16},{64,96},{80,112},{96,64},{112,80},{1... | collective-permute-start | bytes 786440 | tf_op jit(solution)/shard_map/ppermute | solution.py:135
  458.4 12.4 %collective-permute-start.46 = (bf16[192,1024]{1,0:T(8,128)(2,1)S(1)}, bf16[192,1024]{1,0:T(8,128)(2,1)S(1)}, u32[]{:S(2)}, u32[]{:S(2)}) collective-permute-start(bf16[192,1024]{1,0:T(8,128)(2,1)S(1)} %add_convert_fusion.5), channel_id=1, source_target_pairs={{0,4},{1,5},{2,6},{3,7},{4,0},{5,1},{6,2},{7,3},{8,12},{9,13},{10,... | collective-permute-start | bytes 1179656 | tf_op jit(solution)/shard_map/ppermute | solution.py:68
  467.9 6.7 %collective-permute-start.57 = (bf16[2,1,1,1,64,512]{5,4,3,2,1,0:T(8,128)(2,1)S(1)}, bf16[2,1,1,1,64,512]{5,4,3,2,1,0:T(8,128)(2,1)S(1)}, u32[]{:S(2)}, u32[]{:S(2)}) collective-permute-start(bf16[2,1,1,1,64,512]{5,4,3,2,1,0:T(8,128)(2,1)S(1)} %dynamic-slice_convert_fusion.1), channel_id=1, source_target_pairs={{0,8},{8,0},{1,9},{9,1},{2,10},{10,2},{3,11},{11,3},{4,12},{12,4},... | collective-permute-start | bytes 393224 | tf_op jit(solution)/shard_map/ppermute | solution.py:135
  471.0 3.7 collective-permute-start.47
  475.1 1.3 collective-permute-start.48
  475.2 6.1 %collective-permute-start.58 = (bf16[1,1,1,1,64,512]{5,4,3,2,1,0:T(8,128)(2,1)S(1)}, bf16[1,1,1,1,64,512]{5,4,3,2,1,0:T(8,128)(2,1)S(1)}, u32[]{:S(2)}, u32[]{:S(2)}) collective-permute-start(bf16[1,1,1,1,64,512]{5,4,3,2,1,0:T(8,128)(2,1)S(1)} %dynamic-slice_convert_fusion.10), channel_id=1, source_target_pairs={{0,64},{16,80},{32,96},{48,112},{64,0},{80,16},{96,32},{112,48},{1... | collective-permute-start | bytes 196616 | tf_op jit(solution)/shard_map/ppermute | solution.py:135
  476.4 4.9 collective-permute-start.49
  481.3 5.3 collective-permute-start.50
  486.7 6.2 %collective-permute-start.51 = (f32[2,2304]{1,0:T(2,128)S(1)}, f32[2,2304]{1,0:T(2,128)S(1)}, u32[]{:S(2)}, u32[]{:S(2)}) collective-permute-start(f32[2,2304]{1,0:T(2,128)S(1)} %add.467), channel_id=1, source_target_pairs={{0,8},{8,0},{1,9},{9,1},{2,10},{10,2},{3,11},{11,3},{4,12},{12,4},... | collective-permute-start | bytes 55304 | tf_op jit(solution)/shard_map/ppermute | solution.py:109
  492.9 4.0 collective-permute-start.52
  497.0 3.8 collective-permute-start.53
  500.8 5.3 collective-permute-start.54
  (164 other events, 998.5 us)
Sparse Core Ops, SparseCore 0:
  19.4 84.8 all-gather.2
  144.8 82.3 all-gather.4
  373.3 99.2 reduce-scatter.6
  475.0 83.6 reduce-scatter.8

commit v7 on v6

--- a/solution.py
+++ b/solution.py
@@ -232,6 +232,10 @@
         edges.append(edges[-1] + width)
 
     def gather_layer(layer_index):
+        if layer_index > 0:
+            joined = jnp.concatenate([member[layer_index] for member in weight_shards], axis=1)
+            full = lax.all_gather(joined, ("fsdp", "ctx"), axis=0, tiled=True)
+            return tuple(full[:, edges[k] : edges[k + 1]] for k in range(len(widths)))
         early = jnp.concatenate([member[layer_index] for member in weight_shards[:3]], axis=1)
         early_full = shard_gather(early)
         late = jnp.concatenate([member[layer_index] for member in weight_shards[3:]], axis=1)

time: 582 us -> 573 us (0.985)
  waiting for transfers between devices: 317 us -> 307 us
    ppermute x8 -> x4, waiting for transfers between devices: 68.6 us -> 29.2 us  [shard_gather(): received = lax.ppermute(current, axis_name, pairs)]
    all_gather x0 -> x1, waiting for transfers between devices: none -> 33.2 us  [gather_layer(): full = lax.all_gather(joined, ('fsdp', 'ctx'), axis=0, tiled=True)]
    ppermute x16, waiting for transfers between devices: 86.1 us -> 107 us  [tp_sum(): received = lax.ppermute(mine, 'tp', pairs)]
    all_gather x2 -> x1, waiting for transfers between devices: 38.5 us -> 20.1 us  [gather_layer(): late_full = lax.all_gather(late, ('fsdp', 'ctx'), axis=0, tiled=True)]
    ppermute x8, waiting for transfers between devices: 21.6 us -> 13.3 us  [swap_halves(): return lax.ppermute(local, axis_name, [(0, 1), (1, 0)])]
    unnamed x344 -> x342, local copies, waits for them, and re-layouts: 25 us -> 31.8 us
  transfers between devices with their start and end apart: 63 -> 59, of which waited for: 45 -> 38; matrix products, arithmetic and copies ran while one was open for 24% -> 24% of each run, Pallas kernels for 0% -> 0%
where the time goes in v7:
time: 573 us; the launch traced here: 564 us
  waiting for transfers between devices  307 us (54%)
  starting transfers between devices  65.7 us (11%)
  matrix products  61.2 us (11%)
  other arithmetic  58.3 us (10%)
  local copies, waits for them, and re-layouts  53.9 us (9%)
  between operations  17 us (3%)
    ppermute x16, waiting for transfers between devices, tp_sum(): received = lax.ppermute(mine, 'tp', pairs)  107 us
    unnamed x5, waiting for transfers between devices  47.9 us
    all_gather x1, waiting for transfers between devices, gather_layer(): full = lax.all_gather(joined, ('fsdp', 'ctx'), axis=0, tiled=True)  33.2 us
    unnamed x342, local copies, waits for them, and re-layouts  31.8 us
    ppermute x4, waiting for transfers between devices, shard_gather(): received = lax.ppermute(current, axis_name, pairs)  29.2 us
    ppermute x4, waiting for transfers between devices, shard_scatter(): received = lax.ppermute(sent.astype(jnp.bfloat16), axis_name, pairs)  28.7 us
    ppermute x16, starting transfers between devices, tp_sum(): received = lax.ppermute(mine, 'tp', pairs)  28.3 us
    all_gather x1, waiting for transfers between devices, gather_layer(): late_full = lax.all_gather(late, ('fsdp', 'ctx'), axis=0, tiled=True)  20.1 us
  transfers between devices with their start and end apart: 59, of which 38 were waited for; matrix products, arithmetic and copies ran while one was open for 24% of the time, Pallas kernels for 0%

profile of v7, /device:TPU:0, one launch (start us, length us, event | category | flops | bytes accessed | tf_op | source)
XLA Modules:
  0.0 563.5 jit_solution(2816852113762419063)
XLA Ops:
  12.1 4.0 collective-permute-start
  23.6 3.1 collective-permute-start.1
  26.7 3.4 collective-permute-done.1
  31.9 8.8 %collective-permute-done.2 = bf16[2,1,1,2,64,512]{5,4,3,2,1,0:T(8,128)(2,1)S(1)} collective-permute-done((bf16[2,1,1,2,64,512]{5,4,3,2,1,0:T(8,128)(2,1)S(1)}, bf16[2,1,1,2,64,512]{5,4,3,2,1,0:T(8,128)(2,1)S(1)}, u32[]{:S(2)}, u32[]{:S(2)}) %collective-permute-start.2) | collective-permute-done | bytes 262176 | tf_op jit(solution)/shard_map/ppermute | solution.py:157
  40.7 2.2 collective-permute-start.3
  44.8 17.1 %collective-permute-done.3 = bf16[2,1,2,2,64,512]{5,4,3,2,1,0:T(8,128)(2,1)S(1)} collective-permute-done((bf16[2,1,2,2,64,512]{5,4,3,2,1,0:T(8,128)(2,1)S(1)}, bf16[2,1,2,2,64,512]{5,4,3,2,1,0:T(8,128)(2,1)S(1)}, u32[]{:S(2)}, u32[]{:S(2)}) %collective-permute-start.3) | collective-permute-done | bytes 524320 | tf_op jit(solution)/shard_map/ppermute | solution.py:157
  65.1 3.6 collective-permute-start.5
  70.7 5.5 collective-permute-done.5
  76.2 1.8 fusion.13
  80.2 20.1 %all-gather.3.cloned.1.call-done = bf16[1024,1408]{1,0:T(8,128)(2,1)} async-done(((bf16[64,1408]{1,0:T(8,128)(2,1)}), bf16[1024,1408]{1,0:T(8,128)(2,1)}) %all-gather.3.cloned.1.call-update) | async-done | bytes 2883600 | tf_op jit(solution)/shard_map/all_gather | solution.py:242
  102.6 1.9 collective-permute-done.6
  105.4 10.5 %collective-permute-done.7 = bf16[192,1024]{1,0:T(8,128)(2,1)S(1)} collective-permute-done((bf16[192,1024]{1,0:T(8,128)(2,1)S(1)}, bf16[192,1024]{1,0:T(8,128)(2,1)S(1)}, u32[]{:S(2)}, u32[]{:S(2)}) %collective-permute-start.7) | collective-permute-done | bytes 393248 | tf_op jit(solution)/shard_map/ppermute | solution.py:68
  116.0 3.7 collective-permute-start.8
  119.7 8.7 %collective-permute-done.8 = bf16[192,1024]{1,0:T(8,128)(2,1)S(1)} collective-permute-done((bf16[192,1024]{1,0:T(8,128)(2,1)S(1)}, bf16[192,1024]{1,0:T(8,128)(2,1)S(1)}, u32[]{:S(2)}, u32[]{:S(2)}) %collective-permute-start.8) | collective-permute-done | bytes 393248 | tf_op jit(solution)/shard_map/ppermute | solution.py:68
  138.2 11.0 %collective-permute-done.11 = bf16[192,1024]{1,0:T(8,128)(2,1)S(1)} collective-permute-done((bf16[192,1024]{1,0:T(8,128)(2,1)S(1)}, bf16[192,1024]{1,0:T(8,128)(2,1)S(1)}, u32[]{:S(2)}, u32[]{:S(2)}) %collective-permute-start.11) | collective-permute-done | bytes 393248 | tf_op jit(solution)/shard_map/ppermute | solution.py:68
  149.4 3.3 collective-permute-start.12
  152.7 8.7 %collective-permute-done.12 = bf16[192,1024]{1,0:T(8,128)(2,1)S(1)} collective-permute-done((bf16[192,1024]{1,0:T(8,128)(2,1)S(1)}, bf16[192,1024]{1,0:T(8,128)(2,1)S(1)}, u32[]{:S(2)}, u32[]{:S(2)}) %collective-permute-start.12) | collective-permute-done | bytes 393248 | tf_op jit(solution)/shard_map/ppermute | solution.py:68
  165.4 33.2 %all-gather.5.cloned.1.call-done = bf16[1024,1920]{1,0:T(8,128)(2,1)} async-done(((bf16[64,1920]{1,0:T(8,128)(2,1)}), bf16[1024,1920]{1,0:T(8,128)(2,1)}) %all-gather.5.cloned.1.call-update) | async-done | bytes 3932176 | tf_op jit(solution)/shard_map/all_gather | solution.py:237
  198.6 2.0 convolution_convert_fusion.22
  204.4 3.1 collective-permute-start.15
  211.0 1.9 fusion.9
  213.1 2.4 convolution_convert_fusion.20
  220.0 9.9 %collective-permute-done.17 = bf16[192,1024]{1,0:T(8,128)(2,1)S(1)} collective-permute-done((bf16[192,1024]{1,0:T(8,128)(2,1)S(1)}, bf16[192,1024]{1,0:T(8,128)(2,1)S(1)}, u32[]{:S(2)}, u32[]{:S(2)}) %collective-permute-start.17) | collective-permute-done | bytes 393248 | tf_op jit(solution)/shard_map/ppermute | solution.py:68
  230.0 2.9 collective-permute-start.18
  232.9 9.0 %collective-permute-done.18 = bf16[192,1024]{1,0:T(8,128)(2,1)S(1)} collective-permute-done((bf16[192,1024]{1,0:T(8,128)(2,1)S(1)}, bf16[192,1024]{1,0:T(8,128)(2,1)S(1)}, u32[]{:S(2)}, u32[]{:S(2)}) %collective-permute-start.18) | collective-permute-done | bytes 393248 | tf_op jit(solution)/shard_map/ppermute | solution.py:68
  250.4 1.9 collective-permute-done.24
  255.0 1.8 convolution_convert_fusion.8
  256.9 7.9 %collective-permute-done.25 = bf16[192,1024]{1,0:T(8,128)(2,1)S(1)} collective-permute-done((bf16[192,1024]{1,0:T(8,128)(2,1)S(1)}, bf16[192,1024]{1,0:T(8,128)(2,1)S(1)}, u32[]{:S(2)}, u32[]{:S(2)}) %collective-permute-start.25) | collective-permute-done | bytes 393248 | tf_op jit(solution)/shard_map/ppermute | solution.py:68
  265.0 2.9 collective-permute-start.26
  269.2 9.4 %collective-permute-done.26 = bf16[192,1024]{1,0:T(8,128)(2,1)S(1)} collective-permute-done((bf16[192,1024]{1,0:T(8,128)(2,1)S(1)}, bf16[192,1024]{1,0:T(8,128)(2,1)S(1)}, u32[]{:S(2)}, u32[]{:S(2)}) %collective-permute-start.26) | collective-permute-done | bytes 393248 | tf_op jit(solution)/shard_map/ppermute | solution.py:68
  279.4 5.7 %collective-permute-done.21 = bf16[192,1024]{1,0:T(8,128)(2,1)S(1)} collective-permute-done((bf16[192,1024]{1,0:T(8,128)(2,1)S(1)}, bf16[192,1024]{1,0:T(8,128)(2,1)S(1)}, u32[]{:S(2)}, u32[]{:S(2)}) %collective-permute-start.21) | collective-permute-done | bytes 393248 | tf_op jit(solution)/shard_map/ppermute | solution.py:68
  286.1 2.0 collective-permute-start.22
  288.5 2.0 multiply_add_fusion.3
  293.7 2.5 collective-permute-start.29
  296.1 1.9 fusion.4
  305.7 2.0 copy.158
  322.5 8.2 %collective-permute-done.31 = bf16[192,1024]{1,0:T(8,128)(2,1)S(1)} collective-permute-done((bf16[192,1024]{1,0:T(8,128)(2,1)S(1)}, bf16[192,1024]{1,0:T(8,128)(2,1)S(1)}, u32[]{:S(2)}, u32[]{:S(2)}) %collective-permute-start.31) | collective-permute-done | bytes 393248 | tf_op jit(solution)/shard_map/ppermute | solution.py:68
  330.8 1.9 collective-permute-start.32
  334.3 8.4 %collective-permute-done.32 = bf16[192,1024]{1,0:T(8,128)(2,1)S(1)} collective-permute-done((bf16[192,1024]{1,0:T(8,128)(2,1)S(1)}, bf16[192,1024]{1,0:T(8,128)(2,1)S(1)}, u32[]{:S(2)}, u32[]{:S(2)}) %collective-permute-start.32) | collective-permute-done | bytes 393248 | tf_op jit(solution)/shard_map/ppermute | solution.py:68
  342.9 2.1 fusion.24
  347.5 1.9 copy-done.59
  358.5 6.3 %copy.212 = bf16[1024,1920]{1,0:T(8,128)(2,1)} copy(bf16[1024,1920]{0,1:T(8,128)(2,1)} %fusion.19) | data formatting | bytes 7864320
  365.9 2.5 convolution_convert_fusion.3
  369.7 3.1 collective-permute-start.36
  374.6 7.7 %collective-permute-done.36 = bf16[192,1024]{1,0:T(8,128)(2,1)S(1)} collective-permute-done((bf16[192,1024]{1,0:T(8,128)(2,1)S(1)}, bf16[192,1024]{1,0:T(8,128)(2,1)S(1)}, u32[]{:S(2)}, u32[]{:S(2)}) %collective-permute-start.36) | collective-permute-done | bytes 393248 | tf_op jit(solution)/shard_map/ppermute | solution.py:68
  391.0 2.5 collective-permute-start.38
  396.5 1.9 copy.169
  407.4 7.7 %collective-permute-done.39 = bf16[384,128]{0,1:T(8,128)(2,1)S(1)} collective-permute-done((bf16[384,128]{0,1:T(8,128)(2,1)S(1)}, bf16[384,128]{0,1:T(8,128)(2,1)S(1)}, u32[]{:S(2)}, u32[]{:S(2)}) %collective-permute-start.39) | collective-permute-done | bytes 98336 | tf_op jit(solution)/shard_map/ppermute | solution.py:82
  420.5 2.0 add_convert_fusion.6
  422.9 2.8 pad_maximum_fusion
  425.6 4.6 copy.214
  430.3 15.2 %collective-permute-done.51 = bf16[2,2,1,2,64,512]{5,4,3,2,1,0:T(8,128)(2,1)} collective-permute-done((bf16[2,2,1,2,64,512]{5,4,3,2,1,0:T(8,128)(2,1)}, bf16[2,2,1,2,64,512]{5,4,3,2,1,0:T(8,128)(2,1)}, u32[]{:S(2)}, u32[]{:S(2)}) %collective-permute-start.51) | collective-permute-done | bytes 524320 | tf_op jit(solution)/shard_map/ppermute | solution.py:135
  448.6 3.0 collective-permute-start.42
  452.8 6.0 %collective-permute-done.52 = bf16[2,1,1,2,64,512]{5,4,3,2,1,0:T(8,128)(2,1)S(1)} collective-permute-done((bf16[2,1,1,2,64,512]{5,4,3,2,1,0:T(8,128)(2,1)S(1)}, bf16[2,1,1,2,64,512]{5,4,3,2,1,0:T(8,128)(2,1)S(1)}, u32[]{:S(2)}, u32[]{:S(2)}) %collective-permute-start.52) | collective-permute-done | bytes 262176 | tf_op jit(solution)/shard_map/ppermute | solution.py:135
  460.9 5.0 collective-permute-done.53
  468.0 1.9 collective-permute-start.45
  469.9 2.5 collective-permute-done.54
  472.5 2.7 collective-permute-start.46
  475.3 2.6 collective-permute-done.46
  478.5 5.3 collective-permute-done.47
  484.3 3.5 collective-permute-done.48
  487.9 3.9 collective-permute-done.49
  494.9 2.2 collective-permute-done.50
  503.1 47.8 %reduce-scatter.9.cloned.1.call-done = bf16[64,1408]{1,0:T(8,128)(2,1)} async-done(((bf16[1024,1408]{1,0:T(8,128)(2,1)}), bf16[64,1408]{1,0:T(8,128)(2,1)}) %reduce-scatter.9.cloned.1.call-update) | async-done | bytes 180240
  (637 shorter events, 159.7 us)
Async XLA Ops:
  7.2 93.1 %all-gather.3.cloned.1.call-start = ((), (), s32[]{:S(2)}) async-start(), calls=%async_computation.2 | async-start | bytes 3063808 | tf_op jit(solution)/shard_map/all_gather | solution.py:242
  10.5 188.1 %all-gather.5.cloned.1.call-start = ((), (), s32[]{:S(2)}) async-start(), calls=%async_computation.3 | async-start | bytes 4177920 | tf_op jit(solution)/shard_map/all_gather | solution.py:237
  12.1 11.5 %collective-permute-start = (bf16[1,1,1,1,64,512]{5,4,3,2,1,0:T(8,128)(2,1)S(1)}, bf16[1,1,1,1,64,512]{5,4,3,2,1,0:T(8,128)(2,1)S(1)}, u32[]{:S(2)}, u32[]{:S(2)}) collective-permute-start(bf16[1,1,1,1,64,512]{5,4,3,2,1,0:T(8,128)(2,1)S(1)} %get-tuple-element.123), channel_id=1, source_target_pairs={{0,8},{8,0},{1,9},{9,1},{2,10},{10,2},{3,11},{11,3},{4,12},{12,4},... | collective-permute-start | bytes 196616 | tf_op jit(solution)/shard_map/ppermute | solution.py:157
  21.4 476.9 %reduce-scatter.7.cloned.1.call-start = ((), (), s32[]{:S(2)}) async-start(), calls=%async_computation.4 | async-start | bytes 4177920 | tf_op jit(solution)/shard_map/reduce_scatter | solution.py:253
  21.5 42.7 %copy-start.139 = (f32[64]{0:T(128)}, f32[64]{0:T(128)S(1)}, u32[]{:S(2)}) copy-start(f32[64]{0:T(128)S(1)} %multiply_power_fusion) | copy-start | bytes 772
  23.1 47.3 %copy-start.32 = (f32[384,64]{1,0:T(8,128)}, f32[384,64]{1,0:T(8,128)S(1)}, u32[]{:S(2)}) copy-start(f32[384,64]{1,0:T(8,128)S(1)} %get-tuple-element.134) | copy-start | bytes 294916
  23.1 47.3 %copy-start.61 = (f32[384,64]{1,0:T(8,128)}, f32[384,64]{1,0:T(8,128)S(1)}, u32[]{:S(2)}) copy-start(f32[384,64]{1,0:T(8,128)S(1)} %get-tuple-element.133) | copy-start | bytes 294916
  23.6 6.6 %collective-permute-start.1 = (bf16[1,1,1,2,64,512]{5,4,3,2,1,0:T(8,128)(2,1)S(1)}, bf16[1,1,1,2,64,512]{5,4,3,2,1,0:T(8,128)(2,1)S(1)}, u32[]{:S(2)}, u32[]{:S(2)}) collective-permute-start(bf16[1,1,1,2,64,512]{5,4,3,2,1,0:T(8,128)(2,1)S(1)} %maximum_select_fusion.17), channel_id=1, source_target_pairs={{0,64},{16,80},{32,96},{48,112},{64,0},{80,16},{96,32},{112,48},{1... | collective-permute-start | bytes 393224 | tf_op jit(solution)/shard_map/ppermute | solution.py:157
  30.2 10.4 %collective-permute-start.2 = (bf16[2,1,1,2,64,512]{5,4,3,2,1,0:T(8,128)(2,1)S(1)}, bf16[2,1,1,2,64,512]{5,4,3,2,1,0:T(8,128)(2,1)S(1)}, u32[]{:S(2)}, u32[]{:S(2)}) collective-permute-start(bf16[2,1,1,2,64,512]{5,4,3,2,1,0:T(8,128)(2,1)S(1)} %maximum_select_fusion.11), channel_id=1, source_target_pairs={{0,16},{16,0},{32,48},{48,32},{64,80},{80,64},{96,112},{112,96},{1... | collective-permute-start | bytes 786440 | tf_op jit(solution)/shard_map/ppermute | solution.py:157
  40.7 21.2 %collective-permute-start.3 = (bf16[2,1,2,2,64,512]{5,4,3,2,1,0:T(8,128)(2,1)S(1)}, bf16[2,1,2,2,64,512]{5,4,3,2,1,0:T(8,128)(2,1)S(1)}, u32[]{:S(2)}, u32[]{:S(2)}) collective-permute-start(bf16[2,1,2,2,64,512]{5,4,3,2,1,0:T(8,128)(2,1)S(1)} %maximum_select_fusion.9), channel_id=1, source_target_pairs={{0,32},{16,48},{32,0},{48,16},{64,96},{80,112},{96,64},{112,80},{1... | collective-permute-start | bytes 1572872 | tf_op jit(solution)/shard_map/ppermute | solution.py:157
  63.9 14.2 %collective-permute-start.4 = (bf16[384,128]{1,0:T(8,128)(2,1)S(1)}, bf16[384,128]{1,0:T(8,128)(2,1)S(1)}, u32[]{:S(2)}, u32[]{:S(2)}) collective-permute-start(bf16[384,128]{1,0:T(8,128)(2,1)S(1)} %convolution_convert_fusion.23), channel_id=1, source_target_pairs={{0,8},{8,0},{1,9},{9,1},{2,10},{10,2},{3,11},{11,3},{4,12},{12,4},... | collective-permute-start | bytes 294920 | tf_op jit(solution)/shard_map/ppermute | solution.py:82
  65.1 11.1 %collective-permute-start.5 = (bf16[384,128]{1,0:T(8,128)(2,1)S(1)}, bf16[384,128]{1,0:T(8,128)(2,1)}, u32[]{:S(2)}, u32[]{:S(2)}) collective-permute-start(bf16[384,128]{1,0:T(8,128)(2,1)S(1)} %pad_maximum_fusion.10), channel_id=1, source_target_pairs={{0,8},{8,0},{1,9},{9,1},{2,10},{10,2},{3,11},{11,3},{4,12},{12,4},... | collective-permute-start | bytes 294920 | tf_op jit(solution)/shard_map/ppermute | solution.py:82
  102.5 1.9 collective-permute-start.6
  104.6 11.2 %collective-permute-start.7 = (bf16[192,1024]{1,0:T(8,128)(2,1)S(1)}, bf16[192,1024]{1,0:T(8,128)(2,1)S(1)}, u32[]{:S(2)}, u32[]{:S(2)}) collective-permute-start(bf16[192,1024]{1,0:T(8,128)(2,1)S(1)} %add_convert_fusion.27), channel_id=1, source_target_pairs={{0,2},{1,3},{2,0},{3,1},{4,6},{5,7},{6,4},{7,5},{8,10},{9,11},{10,... | collective-permute-start | bytes 1179656 | tf_op jit(solution)/shard_map/ppermute | solution.py:68
  116.0 12.4 %collective-permute-start.8 = (bf16[192,1024]{1,0:T(8,128)(2,1)S(1)}, bf16[192,1024]{1,0:T(8,128)(2,1)S(1)}, u32[]{:S(2)}, u32[]{:S(2)}) collective-permute-start(bf16[192,1024]{1,0:T(8,128)(2,1)S(1)} %add_convert_fusion.26), channel_id=1, source_target_pairs={{0,4},{1,5},{2,6},{3,7},{4,0},{5,1},{6,2},{7,3},{8,12},{9,13},{10,... | collective-permute-start | bytes 1179656 | tf_op jit(solution)/shard_map/ppermute | solution.py:68
  128.5 2.0 collective-permute-start.9
  136.0 1.8 collective-permute-start.10
  138.0 11.2 %collective-permute-start.11 = (bf16[192,1024]{1,0:T(8,128)(2,1)S(1)}, bf16[192,1024]{1,0:T(8,128)(2,1)S(1)}, u32[]{:S(2)}, u32[]{:S(2)}) collective-permute-start(bf16[192,1024]{1,0:T(8,128)(2,1)S(1)} %add_convert_fusion.24), channel_id=1, source_target_pairs={{0,2},{1,3},{2,0},{3,1},{4,6},{5,7},{6,4},{7,5},{8,10},{9,11},{10,... | collective-permute-start | bytes 1179656 | tf_op jit(solution)/shard_map/ppermute | solution.py:68
  149.4 12.0 %collective-permute-start.12 = (bf16[192,1024]{1,0:T(8,128)(2,1)S(1)}, bf16[192,1024]{1,0:T(8,128)(2,1)S(1)}, u32[]{:S(2)}, u32[]{:S(2)}) collective-permute-start(bf16[192,1024]{1,0:T(8,128)(2,1)S(1)} %add_convert_fusion.23), channel_id=1, source_target_pairs={{0,4},{1,5},{2,6},{3,7},{4,0},{5,1},{6,2},{7,3},{8,12},{9,13},{10,... | collective-permute-start | bytes 1179656 | tf_op jit(solution)/shard_map/ppermute | solution.py:68
  161.5 1.8 collective-permute-start.13
  165.4 42.0 %copy-start.12 = (bf16[384,1024]{1,0:T(8,128)(2,1)}, bf16[384,1024]{1,0:T(8,128)(2,1)S(1)}, u32[]{:S(2)}) copy-start(bf16[384,1024]{1,0:T(8,128)(2,1)S(1)} %get-tuple-element.75) | copy-start | bytes 2359300
  200.6 12.4 %collective-permute-start.14 = (bf16[384,128]{1,0:T(8,128)(2,1)}, bf16[384,128]{1,0:T(8,128)(2,1)}, u32[]{:S(2)}, u32[]{:S(2)}) collective-permute-start(bf16[384,128]{1,0:T(8,128)(2,1)} %convolution_convert_fusion.22), channel_id=1, source_target_pairs={{0,8},{8,0},{1,9},{9,1},{2,10},{10,2},{3,11},{11,3},{4,12},{12,4},... | collective-permute-start | bytes 294920 | tf_op jit(solution)/shard_map/ppermute | solution.py:82
  204.4 6.6 %collective-permute-start.15 = (bf16[384,128]{1,0:T(8,128)(2,1)}, bf16[384,128]{1,0:T(8,128)(2,1)}, u32[]{:S(2)}, u32[]{:S(2)}) collective-permute-start(bf16[384,128]{1,0:T(8,128)(2,1)} %pad_maximum_fusion.11), channel_id=1, source_target_pairs={{0,8},{8,0},{1,9},{9,1},{2,10},{10,2},{3,11},{11,3},{4,12},{12,4},... | collective-permute-start | bytes 294920 | tf_op jit(solution)/shard_map/ppermute | solution.py:82
  216.7 1.8 collective-permute-start.16
  218.6 11.2 %collective-permute-start.17 = (bf16[192,1024]{1,0:T(8,128)(2,1)S(1)}, bf16[192,1024]{1,0:T(8,128)(2,1)S(1)}, u32[]{:S(2)}, u32[]{:S(2)}) collective-permute-start(bf16[192,1024]{1,0:T(8,128)(2,1)S(1)} %add_convert_fusion.21), channel_id=1, source_target_pairs={{0,2},{1,3},{2,0},{3,1},{4,6},{5,7},{6,4},{7,5},{8,10},{9,11},{10,... | collective-permute-start | bytes 1179656 | tf_op jit(solution)/shard_map/ppermute | solution.py:68
  230.0 11.9 %collective-permute-start.18 = (bf16[192,1024]{1,0:T(8,128)(2,1)S(1)}, bf16[192,1024]{1,0:T(8,128)(2,1)S(1)}, u32[]{:S(2)}, u32[]{:S(2)}) collective-permute-start(bf16[192,1024]{1,0:T(8,128)(2,1)S(1)} %add_convert_fusion.20), channel_id=1, source_target_pairs={{0,4},{1,5},{2,6},{3,7},{4,0},{5,1},{6,2},{7,3},{8,12},{9,13},{10,... | collective-permute-start | bytes 1179656 | tf_op jit(solution)/shard_map/ppermute | solution.py:68
  242.0 2.2 collective-permute-start.19
  245.3 42.8 %copy-start.6 = (f32[384,1024]{1,0:T(8,128)}, f32[384,1024]{1,0:T(8,128)S(1)}, u32[]{:S(2)}) copy-start(f32[384,1024]{1,0:T(8,128)S(1)} %get-tuple-element.74) | copy-start | bytes 4718596
  250.3 2.1 collective-permute-start.24
  253.6 11.2 %collective-permute-start.25 = (bf16[192,1024]{1,0:T(8,128)(2,1)S(1)}, bf16[192,1024]{1,0:T(8,128)(2,1)S(1)}, u32[]{:S(2)}, u32[]{:S(2)}) collective-permute-start(bf16[192,1024]{1,0:T(8,128)(2,1)S(1)} %add_convert_fusion.15), channel_id=1, source_target_pairs={{0,2},{1,3},{2,0},{3,1},{4,6},{5,7},{6,4},{7,5},{8,10},{9,11},{10,... | collective-permute-start | bytes 1179656 | tf_op jit(solution)/shard_map/ppermute | solution.py:68
  256.8 11.6 %collective-permute-start.20 = (bf16[192,1024]{1,0:T(8,128)(2,1)S(1)}, bf16[192,1024]{1,0:T(8,128)(2,1)S(1)}, u32[]{:S(2)}, u32[]{:S(2)}) collective-permute-start(bf16[192,1024]{1,0:T(8,128)(2,1)S(1)} %constant_dynamic-slice_fusion.5), channel_id=1, source_target_pairs={{0,1},{1,0},{2,3},{3,2},{4,5},{5,4},{6,7},{7,6},{8,9},{9,8},{10,11... | collective-permute-start | bytes 1179656 | tf_op jit(solution)/shard_map/ppermute | solution.py:62
  265.0 13.6 %collective-permute-start.26 = (bf16[192,1024]{1,0:T(8,128)(2,1)S(1)}, bf16[192,1024]{1,0:T(8,128)(2,1)S(1)}, u32[]{:S(2)}, u32[]{:S(2)}) collective-permute-start(bf16[192,1024]{1,0:T(8,128)(2,1)S(1)} %add_convert_fusion.14), channel_id=1, source_target_pairs={{0,4},{1,5},{2,6},{3,7},{4,0},{5,1},{6,2},{7,3},{8,12},{9,13},{10,... | collective-permute-start | bytes 1179656 | tf_op jit(solution)/shard_map/ppermute | solution.py:68
  268.6 16.6 %collective-permute-start.21 = (bf16[192,1024]{1,0:T(8,128)(2,1)S(1)}, bf16[192,1024]{1,0:T(8,128)(2,1)S(1)}, u32[]{:S(2)}, u32[]{:S(2)}) collective-permute-start(bf16[192,1024]{1,0:T(8,128)(2,1)S(1)} %add_convert_fusion.18), channel_id=1, source_target_pairs={{0,2},{1,3},{2,0},{3,1},{4,6},{5,7},{6,4},{7,5},{8,10},{9,11},{10,... | collective-permute-start | bytes 1179656 | tf_op jit(solution)/shard_map/ppermute | solution.py:68
  278.8 9.3 %collective-permute-start.27 = (bf16[192,1024]{1,0:T(8,128)(2,1)S(1)}, bf16[192,1024]{1,0:T(8,128)(2,1)S(1)}, u32[]{:S(2)}, u32[]{:S(2)}) collective-permute-start(bf16[192,1024]{1,0:T(8,128)(2,1)S(1)} %add_convert_fusion.13), channel_id=1, source_target_pairs={{0,1},{1,0},{2,3},{3,2},{4,5},{5,4},{6,7},{7,6},{8,9},{9,8},{10,11... | collective-permute-start | bytes 1179656 | tf_op jit(solution)/shard_map/ppermute | solution.py:72
  286.1 30.1 %collective-permute-start.22 = (bf16[192,1024]{1,0:T(8,128)(2,1)}, bf16[192,1024]{1,0:T(8,128)(2,1)}, u32[]{:S(2)}, u32[]{:S(2)}) collective-permute-start(bf16[192,1024]{1,0:T(8,128)(2,1)} %add_convert_fusion.17), channel_id=1, source_target_pairs={{0,4},{1,5},{2,6},{3,7},{4,0},{5,1},{6,2},{7,3},{8,12},{9,13},{10,... | collective-permute-start | bytes 1179656 | tf_op jit(solution)/shard_map/ppermute | solution.py:68
  293.7 21.0 %collective-permute-start.29 = (bf16[384,128]{0,1:T(8,128)(2,1)}, bf16[384,128]{0,1:T(8,128)(2,1)}, u32[]{:S(2)}, u32[]{:S(2)}) collective-permute-start(bf16[384,128]{0,1:T(8,128)(2,1)} %fusion.145), channel_id=1, source_target_pairs={{0,8},{8,0},{1,9},{9,1},{2,10},{10,2},{3,11},{11,3},{4,12},{12,4},... | collective-permute-start | bytes 294920 | tf_op jit(solution)/shard_map/ppermute | solution.py:82
  300.9 9.6 %collective-permute-start.28 = (bf16[384,128]{1,0:T(8,128)(2,1)}, bf16[384,128]{1,0:T(8,128)(2,1)}, u32[]{:S(2)}, u32[]{:S(2)}) collective-permute-start(bf16[384,128]{1,0:T(8,128)(2,1)} %fusion.143), channel_id=1, source_target_pairs={{0,8},{8,0},{1,9},{9,1},{2,10},{10,2},{3,11},{11,3},{4,12},{12,4},... | collective-permute-start | bytes 294920 | tf_op jit(solution)/shard_map/ppermute | solution.py:82
  316.1 3.2 collective-permute-start.30
  317.6 3.3 collective-permute-start.23
  319.5 11.2 %collective-permute-start.31 = (bf16[192,1024]{1,0:T(8,128)(2,1)S(1)}, bf16[192,1024]{1,0:T(8,128)(2,1)S(1)}, u32[]{:S(2)}, u32[]{:S(2)}) collective-permute-start(bf16[192,1024]{1,0:T(8,128)(2,1)S(1)} %add_convert_fusion.12), channel_id=1, source_target_pairs={{0,2},{1,3},{2,0},{3,1},{4,6},{5,7},{6,4},{7,5},{8,10},{9,11},{10,... | collective-permute-start | bytes 1179656 | tf_op jit(solution)/shard_map/ppermute | solution.py:68
  330.8 11.9 %collective-permute-start.32 = (bf16[192,1024]{1,0:T(8,128)(2,1)S(1)}, bf16[192,1024]{1,0:T(8,128)(2,1)S(1)}, u32[]{:S(2)}, u32[]{:S(2)}) collective-permute-start(bf16[192,1024]{1,0:T(8,128)(2,1)S(1)} %add_convert_fusion.11), channel_id=1, source_target_pairs={{0,4},{1,5},{2,6},{3,7},{4,0},{5,1},{6,2},{7,3},{8,12},{9,13},{10,... | collective-permute-start | bytes 1179656 | tf_op jit(solution)/shard_map/ppermute | solution.py:68
  342.9 3.5 collective-permute-start.33
  351.7 3.6 collective-permute-start.34
  356.2 12.2 %collective-permute-start.35 = (bf16[192,1024]{1,0:T(8,128)(2,1)}, bf16[192,1024]{1,0:T(8,128)(2,1)}, u32[]{:S(2)}, u32[]{:S(2)}) collective-permute-start(bf16[192,1024]{1,0:T(8,128)(2,1)} %add_convert_fusion.9), channel_id=1, source_target_pairs={{0,2},{1,3},{2,0},{3,1},{4,6},{5,7},{6,4},{7,5},{8,10},{9,11},{10,... | collective-permute-start | bytes 1179656 | tf_op jit(solution)/shard_map/ppermute | solution.py:68
  364.8 186.1 %reduce-scatter.9.cloned.1.call-start = ((), (), s32[]{:S(2)}) async-start(), calls=%async_computation.5 | async-start | bytes 3063808
  369.7 12.6 %collective-permute-start.36 = (bf16[192,1024]{1,0:T(8,128)(2,1)S(1)}, bf16[192,1024]{1,0:T(8,128)(2,1)S(1)}, u32[]{:S(2)}, u32[]{:S(2)}) collective-permute-start(bf16[192,1024]{1,0:T(8,128)(2,1)S(1)} %add_convert_fusion.8), channel_id=1, source_target_pairs={{0,4},{1,5},{2,6},{3,7},{4,0},{5,1},{6,2},{7,3},{8,12},{9,13},{10,... | collective-permute-start | bytes 1179656 | tf_op jit(solution)/shard_map/ppermute | solution.py:68
  382.5 1.8 collective-permute-start.37
  391.0 13.7 %collective-permute-start.38 = (bf16[384,128]{1,0:T(8,128)(2,1)}, bf16[384,128]{1,0:T(8,128)(2,1)}, u32[]{:S(2)}, u32[]{:S(2)}) collective-permute-start(bf16[384,128]{1,0:T(8,128)(2,1)} %fusion.147), channel_id=1, source_target_pairs={{0,8},{8,0},{1,9},{9,1},{2,10},{10,2},{3,11},{11,3},{4,12},{12,4},... | collective-permute-start | bytes 294920 | tf_op jit(solution)/shard_map/ppermute | solution.py:82
  403.3 11.8 %collective-permute-start.39 = (bf16[384,128]{0,1:T(8,128)(2,1)S(1)}, bf16[384,128]{0,1:T(8,128)(2,1)S(1)}, u32[]{:S(2)}, u32[]{:S(2)}) collective-permute-start(bf16[384,128]{0,1:T(8,128)(2,1)S(1)} %fusion.149), channel_id=1, source_target_pairs={{0,8},{8,0},{1,9},{9,1},{2,10},{10,2},{3,11},{11,3},{4,12},{12,4},... | collective-permute-start | bytes 294920 | tf_op jit(solution)/shard_map/ppermute | solution.py:82
  416.3 4.1 collective-permute-start.40
  420.5 25.0 %collective-permute-start.51 = (bf16[2,2,1,2,64,512]{5,4,3,2,1,0:T(8,128)(2,1)}, bf16[2,2,1,2,64,512]{5,4,3,2,1,0:T(8,128)(2,1)}, u32[]{:S(2)}, u32[]{:S(2)}) collective-permute-start(bf16[2,2,1,2,64,512]{5,4,3,2,1,0:T(8,128)(2,1)} %constant_dynamic-slice_fusion), channel_id=1, source_target_pairs={{0,16},{16,0},{32,48},{48,32},{64,80},{80,64},{96,112},{112,96},{1... | collective-permute-start | bytes 1572872 | tf_op jit(solution)/shard_map/ppermute | solution.py:135
  422.5 24.8 %collective-permute-start.41 = (bf16[192,1024]{1,0:T(8,128)(2,1)}, bf16[192,1024]{1,0:T(8,128)(2,1)}, u32[]{:S(2)}, u32[]{:S(2)}) collective-permute-start(bf16[192,1024]{1,0:T(8,128)(2,1)} %add_convert_fusion.6), channel_id=1, source_target_pairs={{0,2},{1,3},{2,0},{3,1},{4,6},{5,7},{6,4},{7,5},{8,10},{9,11},{10,... | collective-permute-start | bytes 1179656 | tf_op jit(solution)/shard_map/ppermute | solution.py:68
  446.7 12.1 %collective-permute-start.52 = (bf16[2,1,1,2,64,512]{5,4,3,2,1,0:T(8,128)(2,1)S(1)}, bf16[2,1,1,2,64,512]{5,4,3,2,1,0:T(8,128)(2,1)S(1)}, u32[]{:S(2)}, u32[]{:S(2)}) collective-permute-start(bf16[2,1,1,2,64,512]{5,4,3,2,1,0:T(8,128)(2,1)S(1)} %dynamic-slice_convert_fusion), channel_id=1, source_target_pairs={{0,32},{16,48},{32,0},{48,16},{64,96},{80,112},{96,64},{112,80},{1... | collective-permute-start | bytes 786440 | tf_op jit(solution)/shard_map/ppermute | solution.py:135
  448.6 12.0 %collective-permute-start.42 = (bf16[192,1024]{1,0:T(8,128)(2,1)S(1)}, bf16[192,1024]{1,0:T(8,128)(2,1)S(1)}, u32[]{:S(2)}, u32[]{:S(2)}) collective-permute-start(bf16[192,1024]{1,0:T(8,128)(2,1)S(1)} %add_convert_fusion.5), channel_id=1, source_target_pairs={{0,4},{1,5},{2,6},{3,7},{4,0},{5,1},{6,2},{7,3},{8,12},{9,13},{10,... | collective-permute-start | bytes 1179656 | tf_op jit(solution)/shard_map/ppermute | solution.py:68
  459.0 6.9 %collective-permute-start.53 = (bf16[2,1,1,1,64,512]{5,4,3,2,1,0:T(8,128)(2,1)S(1)}, bf16[2,1,1,1,64,512]{5,4,3,2,1,0:T(8,128)(2,1)S(1)}, u32[]{:S(2)}, u32[]{:S(2)}) collective-permute-start(bf16[2,1,1,1,64,512]{5,4,3,2,1,0:T(8,128)(2,1)S(1)} %dynamic-slice_convert_fusion.1), channel_id=1, source_target_pairs={{0,8},{8,0},{1,9},{9,1},{2,10},{10,2},{3,11},{11,3},{4,12},{12,4},... | collective-permute-start | bytes 393224 | tf_op jit(solution)/shard_map/ppermute | solution.py:135
  460.7 5.2 collective-permute-start.43
  466.3 1.7 collective-permute-start.44
  466.4 6.1 %collective-permute-start.54 = (bf16[1,1,1,1,64,512]{5,4,3,2,1,0:T(8,128)(2,1)S(1)}, bf16[1,1,1,1,64,512]{5,4,3,2,1,0:T(8,128)(2,1)S(1)}, u32[]{:S(2)}, u32[]{:S(2)}) collective-permute-start(bf16[1,1,1,1,64,512]{5,4,3,2,1,0:T(8,128)(2,1)S(1)} %dynamic-slice_convert_fusion.10), channel_id=1, source_target_pairs={{0,64},{16,80},{32,96},{48,112},{64,0},{80,16},{96,32},{112,48},{1... | collective-permute-start | bytes 196616 | tf_op jit(solution)/shard_map/ppermute | solution.py:135
  468.0 4.5 collective-permute-start.45
  472.5 5.3 collective-permute-start.46
  477.9 5.9 %collective-permute-start.47 = (f32[2,2304]{1,0:T(2,128)S(1)}, f32[2,2304]{1,0:T(2,128)S(1)}, u32[]{:S(2)}, u32[]{:S(2)}) collective-permute-start(f32[2,2304]{1,0:T(2,128)S(1)} %add.463), channel_id=1, source_target_pairs={{0,8},{8,0},{1,9},{9,1},{2,10},{10,2},{3,11},{11,3},{4,12},{12,4},... | collective-permute-start | bytes 55304 | tf_op jit(solution)/shard_map/ppermute | solution.py:109
  483.8 4.0 collective-permute-start.48
  487.8 4.0 collective-permute-start.49
  491.8 5.3 collective-permute-start.50
  (156 other events, 833.7 us)
Sparse Core Ops, SparseCore 0:
  10.6 89.6 all-gather.2
  101.9 96.6 all-gather.4
  364.9 100.0 reduce-scatter.6
  467.4 83.4 reduce-scatter.8

commit v8 on v7

--- a/solution.py
+++ b/solution.py
@@ -1,7 +1,9 @@
 import jax
 import jax.numpy as jnp
 from jax import lax
+from jax.experimental import pallas as pl
 from jax.sharding import PartitionSpec as P
+import functools
 
 eps = 1e-06
 rope_base = 1000000.0
@@ -47,6 +49,63 @@
             trailing * cosine_table + leading * sine_table,
         ],
         axis=-1,
+    )
+
+
+def attention_kernel(
+    query_ref, key_ref, value_ref, query_ids_ref, key_ids_ref, position_ref,
+    attended_ref, log_total_ref, *, groups, per_group, head_size, score_scale
+):
+    query_ids = query_ids_ref[...]
+    key_ids = key_ids_ref[...]
+    key_positions = lax.broadcasted_iota(jnp.int32, key_ids.shape, 1)
+    allowed = (query_ids == key_ids) & (key_positions <= position_ref[...])
+    for group in range(groups):
+        key_block = key_ref[:, group * head_size : (group + 1) * head_size]
+        value_block = value_ref[:, group * head_size : (group + 1) * head_size]
+        for member in range(per_group):
+            head = group * per_group + member
+            query_block = query_ref[:, head * head_size : (head + 1) * head_size]
+            scores = (
+                lax.dot_general(
+                    query_block, key_block, (((1,), (1,)), ((), ())),
+                    preferred_element_type=jnp.float32,
+                )
+                * score_scale
+            )
+            exponent = jnp.where(allowed, jnp.exp(scores), 0.0)
+            log_total = jnp.log(jnp.sum(exponent, axis=1, keepdims=True))
+            probs = jnp.where(allowed, jnp.exp(scores - log_total), 0.0).astype(jnp.bfloat16)
+            attended = jnp.dot(probs, value_block, preferred_element_type=jnp.float32)
+            attended_ref[:, head * head_size : (head + 1) * head_size] = attended.astype(
+                jnp.bfloat16
+            )
+            log_total_ref[head] = log_total
+
+
+def fused_attention(queries, keys, values, query_ids, key_ids, positions, per_group, head_size):
+    rows = queries.shape[0]
+    heads = queries.shape[1] // head_size
+    groups = heads // per_group
+    keys_count = keys.shape[0]
+    kernel = functools.partial(
+        attention_kernel, groups=groups, per_group=per_group, head_size=head_size,
+        score_scale=head_size ** (-0.5),
+    )
+    return pl.pallas_call(
+        kernel,
+        out_shape=(
+            jax.ShapeDtypeStruct((rows, heads * head_size), jnp.bfloat16),
+            jax.ShapeDtypeStruct((heads, rows, 1), jnp.float32),
+        ),
+        cost_estimate=pl.CostEstimate(
+            flops=4 * heads * rows * keys_count * head_size,
+            transcendentals=2 * heads * rows * keys_count,
+            bytes_accessed=2 * (2 * rows * heads * head_size + 2 * keys_count * groups * head_size),
+        ),
+    )(
+        queries, keys, values, query_ids.reshape(rows, 1), key_ids.reshape(1, keys_count),
+        positions.reshape(rows, 1),
     )
 
 
@@ -316,21 +375,17 @@
         forward_query_groups = queries.reshape(row_count, local_groups, per_group, head_size)
         forward_key_groups = all_keys.reshape(seq_length, local_groups, head_size)
         forward_value_groups = all_values.reshape(seq_length, local_groups, head_size)
-        forward_scores = attention_scores(forward_query_groups, forward_key_groups)
-        exponent = jnp.where(allowed, jnp.exp(forward_scores), 0.0)
-        forward_log_total = jnp.log(jnp.sum(exponent, axis=-1, keepdims=True))
-        attention_probs = jnp.where(
-            allowed, jnp.exp(forward_scores - forward_log_total), 0.0
-        ).astype(jnp.bfloat16)
-        forward_attended = jnp.einsum(
-            "grqk,kgd->qgrd",
-            attention_probs,
-            forward_value_groups,
-            preferred_element_type=jnp.float32,
-        )
-        forward_attended = forward_attended.astype(jnp.bfloat16).reshape(
-            row_count, local_heads * head_size
-        )
+        forward_attended, forward_log_total = fused_attention(
+            queries.reshape(row_count, local_heads * head_size),
+            all_keys,
+            all_values,
+            query_ids,
+            segment_row,
+            positions,
+            per_group,
+            head_size,
+        )
+        forward_log_total = forward_log_total.reshape(local_groups, per_group, row_count, 1)
         forward_middle = hidden + tp_sum(contract_last(forward_attended, forward_output_full))
         forward_scale_two = row_scale(forward_middle)
         forward_feed_normed = (

time: 573 us -> 574 us (level)
  waiting for transfers between devices: 307 us -> 289 us
  other arithmetic: 58.3 us -> 73.4 us
  Pallas kernels: 0 us -> 7.22 us
  matrix products: 61.2 us -> 54.3 us
    pallas_call x0 -> x2, Pallas kernels: none -> 7.22 us  [fused_attention(): pl.pallas_call(kernel, out_shape=(jax.ShapeDtypeStruct((rows, heads * hea...]
    unnamed x342 -> x296, local copies, waits for them, and re-layouts: 31.8 us -> 29.4 us
  transfers between devices with their start and end apart: 59 -> 59, of which waited for: 38 -> 39; matrix products, arithmetic and copies ran while one was open for 24% -> 26% of each run, Pallas kernels for 0% -> 1%
where the time goes in v8:
time: 574 us; the launch traced here: 564 us
  waiting for transfers between devices  289 us (50%)
  other arithmetic  73.4 us (13%)
  starting transfers between devices  69.9 us (12%)
  matrix products  54.3 us (9%)
  local copies, waits for them, and re-layouts  54.1 us (9%)
  between operations  16.6 us (3%)
  Pallas kernels  7.22 us (1%)
    ppermute x16, waiting for transfers between devices, tp_sum(): received = lax.ppermute(mine, 'tp', pairs)  104 us
    unnamed x5, waiting for transfers between devices  45.5 us
    all_gather x1, waiting for transfers between devices, gather_layer(): full = lax.all_gather(joined, ('fsdp', 'ctx'), axis=0, tiled=True)  32 us
    unnamed x296, local copies, waits for them, and re-layouts  29.4 us
    ppermute x16, starting transfers between devices, tp_sum(): received = lax.ppermute(mine, 'tp', pairs)  28.7 us
    ppermute x4, waiting for transfers between devices, shard_gather(): received = lax.ppermute(current, axis_name, pairs)  26.6 us
    ppermute x4, waiting for transfers between devices, shard_scatter(): received = lax.ppermute(sent.astype(jnp.bfloat16), axis_name, pairs)  23.7 us
    all_gather x1, waiting for transfers between devices, gather_layer(): late_full = lax.all_gather(late, ('fsdp', 'ctx'), axis=0, tiled=True)  20.2 us
  transfers between devices with their start and end apart: 59, of which 39 were waited for; matrix products, arithmetic and copies ran while one was open for 26% of the time, Pallas kernels for 1%

profile of v8, /device:TPU:0, one launch (start us, length us, event | category | flops | bytes accessed | tf_op | source)
XLA Modules:
  0.0 564.4 jit_solution(17013129102451712771)
XLA Ops:
  12.1 4.0 collective-permute-start
  23.3 3.1 collective-permute-start.1
  27.0 2.8 collective-permute-done.1
  33.1 7.3 %collective-permute-done.2 = bf16[2,1,1,2,64,512]{5,4,3,2,1,0:T(8,128)(2,1)S(1)} collective-permute-done((bf16[2,1,1,2,64,512]{5,4,3,2,1,0:T(8,128)(2,1)S(1)}, bf16[2,1,1,2,64,512]{5,4,3,2,1,0:T(8,128)(2,1)S(1)}, u32[]{:S(2)}, u32[]{:S(2)}) %collective-permute-start.2) | collective-permute-done | bytes 262176 | tf_op jit(solution)/shard_map/ppermute | solution.py:216
  40.4 2.7 collective-permute-start.3
  45.1 16.5 %collective-permute-done.3 = bf16[2,1,2,2,64,512]{5,4,3,2,1,0:T(8,128)(2,1)S(1)} collective-permute-done((bf16[2,1,2,2,64,512]{5,4,3,2,1,0:T(8,128)(2,1)S(1)}, bf16[2,1,2,2,64,512]{5,4,3,2,1,0:T(8,128)(2,1)S(1)}, u32[]{:S(2)}, u32[]{:S(2)}) %collective-permute-start.3) | collective-permute-done | bytes 524320 | tf_op jit(solution)/shard_map/ppermute | solution.py:216
  64.4 3.6 collective-permute-start.4
  69.5 4.2 collective-permute-done.5
  76.1 3.6 shard_map.237
  79.7 20.2 %all-gather.3.cloned.1.call-done = bf16[1024,1408]{1,0:T(8,128)(2,1)} async-done(((bf16[64,1408]{1,0:T(8,128)(2,1)}), bf16[1024,1408]{1,0:T(8,128)(2,1)}) %all-gather.3.cloned.1.call-update) | async-done | bytes 2883600 | tf_op jit(solution)/shard_map/all_gather | solution.py:301
  103.4 1.9 collective-permute-start.7
  105.3 9.4 %collective-permute-done.7 = bf16[192,1024]{1,0:T(8,128)(2,1)S(1)} collective-permute-done((bf16[192,1024]{1,0:T(8,128)(2,1)S(1)}, bf16[192,1024]{1,0:T(8,128)(2,1)S(1)}, u32[]{:S(2)}, u32[]{:S(2)}) %collective-permute-start.7) | collective-permute-done | bytes 393248 | tf_op jit(solution)/shard_map/ppermute | solution.py:127
  114.9 2.9 collective-permute-start.8
  117.8 9.2 %collective-permute-done.8 = bf16[192,1024]{1,0:T(8,128)(2,1)S(1)} collective-permute-done((bf16[192,1024]{1,0:T(8,128)(2,1)S(1)}, bf16[192,1024]{1,0:T(8,128)(2,1)S(1)}, u32[]{:S(2)}, u32[]{:S(2)}) %collective-permute-start.8) | collective-permute-done | bytes 393248 | tf_op jit(solution)/shard_map/ppermute | solution.py:127
  138.4 9.5 %collective-permute-done.11 = bf16[192,1024]{1,0:T(8,128)(2,1)S(1)} collective-permute-done((bf16[192,1024]{1,0:T(8,128)(2,1)S(1)}, bf16[192,1024]{1,0:T(8,128)(2,1)S(1)}, u32[]{:S(2)}, u32[]{:S(2)}) %collective-permute-start.11) | collective-permute-done | bytes 393248 | tf_op jit(solution)/shard_map/ppermute | solution.py:127
  148.0 2.8 collective-permute-start.12
  150.8 9.2 %collective-permute-done.12 = bf16[192,1024]{1,0:T(8,128)(2,1)S(1)} collective-permute-done((bf16[192,1024]{1,0:T(8,128)(2,1)S(1)}, bf16[192,1024]{1,0:T(8,128)(2,1)S(1)}, u32[]{:S(2)}, u32[]{:S(2)}) %collective-permute-start.12) | collective-permute-done | bytes 393248 | tf_op jit(solution)/shard_map/ppermute | solution.py:127
  164.1 32.0 %all-gather.5.cloned.1.call-done = bf16[1024,1920]{1,0:T(8,128)(2,1)} async-done(((bf16[64,1920]{1,0:T(8,128)(2,1)}), bf16[1024,1920]{1,0:T(8,128)(2,1)}) %all-gather.5.cloned.1.call-update) | async-done | bytes 3932176 | tf_op jit(solution)/shard_map/all_gather | solution.py:296
  196.1 2.0 convolution_convert_fusion.20
  201.9 3.0 collective-permute-start.14
  212.0 3.6 shard_map.238
  220.4 10.2 %collective-permute-done.17 = bf16[192,1024]{1,0:T(8,128)(2,1)S(1)} collective-permute-done((bf16[192,1024]{1,0:T(8,128)(2,1)S(1)}, bf16[192,1024]{1,0:T(8,128)(2,1)S(1)}, u32[]{:S(2)}, u32[]{:S(2)}) %collective-permute-start.17) | collective-permute-done | bytes 393248 | tf_op jit(solution)/shard_map/ppermute | solution.py:127
  230.7 2.6 collective-permute-start.18
  233.3 9.3 %collective-permute-done.18 = bf16[192,1024]{1,0:T(8,128)(2,1)S(1)} collective-permute-done((bf16[192,1024]{1,0:T(8,128)(2,1)S(1)}, bf16[192,1024]{1,0:T(8,128)(2,1)S(1)}, u32[]{:S(2)}, u32[]{:S(2)}) %collective-permute-start.18) | collective-permute-done | bytes 393248 | tf_op jit(solution)/shard_map/ppermute | solution.py:127
  258.5 8.3 %collective-permute-done.25 = bf16[192,1024]{1,0:T(8,128)(2,1)S(1)} collective-permute-done((bf16[192,1024]{1,0:T(8,128)(2,1)S(1)}, bf16[192,1024]{1,0:T(8,128)(2,1)S(1)}, u32[]{:S(2)}, u32[]{:S(2)}) %collective-permute-start.25) | collective-permute-done | bytes 393248 | tf_op jit(solution)/shard_map/ppermute | solution.py:127
  267.0 2.6 collective-permute-start.26
  271.5 9.1 %collective-permute-done.26 = bf16[192,1024]{1,0:T(8,128)(2,1)S(1)} collective-permute-done((bf16[192,1024]{1,0:T(8,128)(2,1)S(1)}, bf16[192,1024]{1,0:T(8,128)(2,1)S(1)}, u32[]{:S(2)}, u32[]{:S(2)}) %collective-permute-start.26) | collective-permute-done | bytes 393248 | tf_op jit(solution)/shard_map/ppermute | solution.py:127
  284.9 2.2 collective-permute-done.21
  287.1 2.0 add_convert_fusion.17
  289.1 2.1 collective-permute-start.22
  292.8 2.1 multiply_add_fusion.3
  303.2 2.6 collective-permute-start.28
  307.7 1.9 copy.152
  325.6 7.0 %collective-permute-done.31 = bf16[192,1024]{1,0:T(8,128)(2,1)S(1)} collective-permute-done((bf16[192,1024]{1,0:T(8,128)(2,1)S(1)}, bf16[192,1024]{1,0:T(8,128)(2,1)S(1)}, u32[]{:S(2)}, u32[]{:S(2)}) %collective-permute-start.31) | collective-permute-done | bytes 393248 | tf_op jit(solution)/shard_map/ppermute | solution.py:127
  332.8 1.9 collective-permute-start.32
  336.2 8.4 %collective-permute-done.32 = bf16[192,1024]{1,0:T(8,128)(2,1)S(1)} collective-permute-done((bf16[192,1024]{1,0:T(8,128)(2,1)S(1)}, bf16[192,1024]{1,0:T(8,128)(2,1)S(1)}, u32[]{:S(2)}, u32[]{:S(2)}) %collective-permute-start.32) | collective-permute-done | bytes 393248 | tf_op jit(solution)/shard_map/ppermute | solution.py:127
  344.9 2.0 fusion.18
  349.3 1.9 copy-done.57
  359.5 6.1 %copy.195 = bf16[1024,1920]{1,0:T(8,128)(2,1)} copy(bf16[1024,1920]{0,1:T(8,128)(2,1)} %fusion.15) | data formatting | bytes 7864320
  366.8 2.5 convolution_convert_fusion.3
  370.5 3.0 collective-permute-start.36
  375.4 7.9 %collective-permute-done.36 = bf16[192,1024]{1,0:T(8,128)(2,1)S(1)} collective-permute-done((bf16[192,1024]{1,0:T(8,128)(2,1)S(1)}, bf16[192,1024]{1,0:T(8,128)(2,1)S(1)}, u32[]{:S(2)}, u32[]{:S(2)}) %collective-permute-start.36) | collective-permute-done | bytes 393248 | tf_op jit(solution)/shard_map/ppermute | solution.py:127
  396.4 1.9 copy.162
  400.8 2.4 convolution_bitcast_fusion.3
  405.5 2.6 collective-permute-start.39
  410.8 7.6 %collective-permute-done.39 = bf16[384,128]{0,1:T(8,128)(2,1)S(1)} collective-permute-done((bf16[384,128]{0,1:T(8,128)(2,1)S(1)}, bf16[384,128]{0,1:T(8,128)(2,1)S(1)}, u32[]{:S(2)}, u32[]{:S(2)}) %collective-permute-start.39) | collective-permute-done | bytes 98336 | tf_op jit(solution)/shard_map/ppermute | solution.py:141
  421.7 2.3 copy.168
  424.0 2.0 constant_dynamic-slice_fusion
  426.0 2.0 add_convert_fusion.6
  429.1 2.8 pad_maximum_fusion
  431.9 4.6 copy.197
  436.5 14.8 %collective-permute-done.51 = bf16[2,2,1,2,64,512]{5,4,3,2,1,0:T(8,128)(2,1)} collective-permute-done((bf16[2,2,1,2,64,512]{5,4,3,2,1,0:T(8,128)(2,1)}, bf16[2,2,1,2,64,512]{5,4,3,2,1,0:T(8,128)(2,1)}, u32[]{:S(2)}, u32[]{:S(2)}) %collective-permute-start.51) | collective-permute-done | bytes 524320 | tf_op jit(solution)/shard_map/ppermute | solution.py:194
  454.1 2.7 collective-permute-start.42
  457.1 5.1 collective-permute-done.52
  462.5 4.1 collective-permute-done.42
  466.9 2.0 collective-permute-done.53
  469.5 2.8 collective-permute-start.54
  476.2 2.0 collective-permute-start.46
  478.2 3.4 collective-permute-done.46
  483.3 3.7 collective-permute-done.47
  487.4 3.4 collective-permute-done.48
  492.2 2.8 collective-permute-done.49
  495.0 2.4 collective-permute-start.50
  506.4 45.4 %reduce-scatter.9.cloned.1.call-done = bf16[64,1408]{1,0:T(8,128)(2,1)} async-done(((bf16[1024,1408]{1,0:T(8,128)(2,1)}), bf16[64,1408]{1,0:T(8,128)(2,1)}) %reduce-scatter.9.cloned.1.call-update) | async-done | bytes 180240
  (599 shorter events, 175.6 us)
Async XLA Ops:
  7.2 92.7 %all-gather.3.cloned.1.call-start = ((), (), s32[]{:S(2)}) async-start(), calls=%async_computation.2 | async-start | bytes 3063808 | tf_op jit(solution)/shard_map/all_gather | solution.py:301
  10.5 185.6 %all-gather.5.cloned.1.call-start = ((), (), s32[]{:S(2)}) async-start(), calls=%async_computation.3 | async-start | bytes 4177920 | tf_op jit(solution)/shard_map/all_gather | solution.py:296
  12.1 11.2 %collective-permute-start = (bf16[1,1,1,1,64,512]{5,4,3,2,1,0:T(8,128)(2,1)S(1)}, bf16[1,1,1,1,64,512]{5,4,3,2,1,0:T(8,128)(2,1)S(1)}, u32[]{:S(2)}, u32[]{:S(2)}) collective-permute-start(bf16[1,1,1,1,64,512]{5,4,3,2,1,0:T(8,128)(2,1)S(1)} %get-tuple-element.131), channel_id=1, source_target_pairs={{0,8},{8,0},{1,9},{9,1},{2,10},{10,2},{3,11},{11,3},{4,12},{12,4},... | collective-permute-start | bytes 196616 | tf_op jit(solution)/shard_map/ppermute | solution.py:216
  21.4 480.1 %reduce-scatter.7.cloned.1.call-start = ((), (), s32[]{:S(2)}) async-start(), calls=%async_computation.4 | async-start | bytes 4177920 | tf_op jit(solution)/shard_map/reduce_scatter | solution.py:312
  21.5 41.9 %copy-start.111 = (f32[64]{0:T(128)}, f32[64]{0:T(128)S(1)}, u32[]{:S(2)}) copy-start(f32[64]{0:T(128)S(1)} %multiply_power_fusion) | copy-start | bytes 772
  23.2 45.2 %copy-start.22 = (f32[384,64]{1,0:T(8,128)}, f32[384,64]{1,0:T(8,128)S(1)}, u32[]{:S(2)}) copy-start(f32[384,64]{1,0:T(8,128)S(1)} %get-tuple-element.144) | copy-start | bytes 294916
  23.2 45.2 %copy-start.61 = (f32[384,64]{1,0:T(8,128)}, f32[384,64]{1,0:T(8,128)S(1)}, u32[]{:S(2)}) copy-start(f32[384,64]{1,0:T(8,128)S(1)} %get-tuple-element.143) | copy-start | bytes 294916
  23.3 6.6 %collective-permute-start.1 = (bf16[1,1,1,2,64,512]{5,4,3,2,1,0:T(8,128)(2,1)S(1)}, bf16[1,1,1,2,64,512]{5,4,3,2,1,0:T(8,128)(2,1)S(1)}, u32[]{:S(2)}, u32[]{:S(2)}) collective-permute-start(bf16[1,1,1,2,64,512]{5,4,3,2,1,0:T(8,128)(2,1)S(1)} %maximum_select_fusion.17), channel_id=1, source_target_pairs={{0,64},{16,80},{32,96},{48,112},{64,0},{80,16},{96,32},{112,48},{1... | collective-permute-start | bytes 393224 | tf_op jit(solution)/shard_map/ppermute | solution.py:216
  27.0 41.2 %copy-start.126 = (f32[128]{0:T(128)}, f32[128]{0:T(128)S(1)}, u32[]{:S(2)}) copy-start(f32[128]{0:T(128)S(1)} %get-tuple-element.148) | copy-start | bytes 1540
  29.9 10.5 %collective-permute-start.2 = (bf16[2,1,1,2,64,512]{5,4,3,2,1,0:T(8,128)(2,1)S(1)}, bf16[2,1,1,2,64,512]{5,4,3,2,1,0:T(8,128)(2,1)S(1)}, u32[]{:S(2)}, u32[]{:S(2)}) collective-permute-start(bf16[2,1,1,2,64,512]{5,4,3,2,1,0:T(8,128)(2,1)S(1)} %maximum_select_fusion.11), channel_id=1, source_target_pairs={{0,16},{16,0},{32,48},{48,32},{64,80},{80,64},{96,112},{112,96},{1... | collective-permute-start | bytes 786440 | tf_op jit(solution)/shard_map/ppermute | solution.py:216
  40.4 21.2 %collective-permute-start.3 = (bf16[2,1,2,2,64,512]{5,4,3,2,1,0:T(8,128)(2,1)S(1)}, bf16[2,1,2,2,64,512]{5,4,3,2,1,0:T(8,128)(2,1)S(1)}, u32[]{:S(2)}, u32[]{:S(2)}) collective-permute-start(bf16[2,1,2,2,64,512]{5,4,3,2,1,0:T(8,128)(2,1)S(1)} %maximum_select_fusion.9), channel_id=1, source_target_pairs={{0,32},{16,48},{32,0},{48,16},{64,96},{80,112},{96,64},{112,80},{1... | collective-permute-start | bytes 1572872 | tf_op jit(solution)/shard_map/ppermute | solution.py:216
  63.1 10.6 %collective-permute-start.5 = (bf16[384,128]{1,0:T(8,128)(2,1)S(1)}, bf16[384,128]{1,0:T(8,128)(2,1)S(1)}, u32[]{:S(2)}, u32[]{:S(2)}) collective-permute-start(bf16[384,128]{1,0:T(8,128)(2,1)S(1)} %convolution_convert_fusion.21), channel_id=1, source_target_pairs={{0,8},{8,0},{1,9},{9,1},{2,10},{10,2},{3,11},{11,3},{4,12},{12,4},... | collective-permute-start | bytes 294920 | tf_op jit(solution)/shard_map/ppermute | solution.py:141
  64.4 10.8 %collective-permute-start.4 = (bf16[384,128]{1,0:T(8,128)(2,1)S(1)}, bf16[384,128]{1,0:T(8,128)(2,1)S(1)}, u32[]{:S(2)}, u32[]{:S(2)}) collective-permute-start(bf16[384,128]{1,0:T(8,128)(2,1)S(1)} %pad_maximum_fusion.8), channel_id=1, source_target_pairs={{0,8},{8,0},{1,9},{9,1},{2,10},{10,2},{3,11},{11,3},{4,12},{12,4},... | collective-permute-start | bytes 294920 | tf_op jit(solution)/shard_map/ppermute | solution.py:141
  101.5 1.8 collective-permute-start.6
  103.4 11.3 %collective-permute-start.7 = (bf16[192,1024]{1,0:T(8,128)(2,1)S(1)}, bf16[192,1024]{1,0:T(8,128)(2,1)S(1)}, u32[]{:S(2)}, u32[]{:S(2)}) collective-permute-start(bf16[192,1024]{1,0:T(8,128)(2,1)S(1)} %add_convert_fusion.27), channel_id=1, source_target_pairs={{0,2},{1,3},{2,0},{3,1},{4,6},{5,7},{6,4},{7,5},{8,10},{9,11},{10,... | collective-permute-start | bytes 1179656 | tf_op jit(solution)/shard_map/ppermute | solution.py:127
  114.9 12.1 %collective-permute-start.8 = (bf16[192,1024]{1,0:T(8,128)(2,1)S(1)}, bf16[192,1024]{1,0:T(8,128)(2,1)S(1)}, u32[]{:S(2)}, u32[]{:S(2)}) collective-permute-start(bf16[192,1024]{1,0:T(8,128)(2,1)S(1)} %add_convert_fusion.26), channel_id=1, source_target_pairs={{0,4},{1,5},{2,6},{3,7},{4,0},{5,1},{6,2},{7,3},{8,12},{9,13},{10,... | collective-permute-start | bytes 1179656 | tf_op jit(solution)/shard_map/ppermute | solution.py:127
  127.1 2.0 collective-permute-start.9
  134.7 1.8 collective-permute-start.10
  136.7 11.2 %collective-permute-start.11 = (bf16[192,1024]{1,0:T(8,128)(2,1)S(1)}, bf16[192,1024]{1,0:T(8,128)(2,1)S(1)}, u32[]{:S(2)}, u32[]{:S(2)}) collective-permute-start(bf16[192,1024]{1,0:T(8,128)(2,1)S(1)} %add_convert_fusion.24), channel_id=1, source_target_pairs={{0,2},{1,3},{2,0},{3,1},{4,6},{5,7},{6,4},{7,5},{8,10},{9,11},{10,... | collective-permute-start | bytes 1179656 | tf_op jit(solution)/shard_map/ppermute | solution.py:127
  148.0 12.0 %collective-permute-start.12 = (bf16[192,1024]{1,0:T(8,128)(2,1)S(1)}, bf16[192,1024]{1,0:T(8,128)(2,1)S(1)}, u32[]{:S(2)}, u32[]{:S(2)}) collective-permute-start(bf16[192,1024]{1,0:T(8,128)(2,1)S(1)} %add_convert_fusion.23), channel_id=1, source_target_pairs={{0,4},{1,5},{2,6},{3,7},{4,0},{5,1},{6,2},{7,3},{8,12},{9,13},{10,... | collective-permute-start | bytes 1179656 | tf_op jit(solution)/shard_map/ppermute | solution.py:127
  160.2 1.8 collective-permute-start.13
  198.1 10.4 %collective-permute-start.15 = (bf16[384,128]{1,0:T(8,128)(2,1)}, bf16[384,128]{1,0:T(8,128)(2,1)}, u32[]{:S(2)}, u32[]{:S(2)}) collective-permute-start(bf16[384,128]{1,0:T(8,128)(2,1)} %convolution_convert_fusion.20), channel_id=1, source_target_pairs={{0,8},{8,0},{1,9},{9,1},{2,10},{10,2},{3,11},{11,3},{4,12},{12,4},... | collective-permute-start | bytes 294920 | tf_op jit(solution)/shard_map/ppermute | solution.py:141
  201.9 8.4 %collective-permute-start.14 = (bf16[384,128]{1,0:T(8,128)(2,1)}, bf16[384,128]{1,0:T(8,128)(2,1)}, u32[]{:S(2)}, u32[]{:S(2)}) collective-permute-start(bf16[384,128]{1,0:T(8,128)(2,1)} %pad_maximum_fusion.9), channel_id=1, source_target_pairs={{0,8},{8,0},{1,9},{9,1},{2,10},{10,2},{3,11},{11,3},{4,12},{12,4},... | collective-permute-start | bytes 294920 | tf_op jit(solution)/shard_map/ppermute | solution.py:141
  217.4 1.8 collective-permute-start.16
  219.3 11.2 %collective-permute-start.17 = (bf16[192,1024]{1,0:T(8,128)(2,1)S(1)}, bf16[192,1024]{1,0:T(8,128)(2,1)S(1)}, u32[]{:S(2)}, u32[]{:S(2)}) collective-permute-start(bf16[192,1024]{1,0:T(8,128)(2,1)S(1)} %add_convert_fusion.21), channel_id=1, source_target_pairs={{0,2},{1,3},{2,0},{3,1},{4,6},{5,7},{6,4},{7,5},{8,10},{9,11},{10,... | collective-permute-start | bytes 1179656 | tf_op jit(solution)/shard_map/ppermute | solution.py:127
  230.7 11.9 %collective-permute-start.18 = (bf16[192,1024]{1,0:T(8,128)(2,1)S(1)}, bf16[192,1024]{1,0:T(8,128)(2,1)S(1)}, u32[]{:S(2)}, u32[]{:S(2)}) collective-permute-start(bf16[192,1024]{1,0:T(8,128)(2,1)S(1)} %add_convert_fusion.20), channel_id=1, source_target_pairs={{0,4},{1,5},{2,6},{3,7},{4,0},{5,1},{6,2},{7,3},{8,12},{9,13},{10,... | collective-permute-start | bytes 1179656 | tf_op jit(solution)/shard_map/ppermute | solution.py:127
  242.8 2.2 collective-permute-start.19
  246.0 45.3 %copy-start.7 = (f32[384,1024]{1,0:T(8,128)}, f32[384,1024]{1,0:T(8,128)S(1)}, u32[]{:S(2)}) copy-start(f32[384,1024]{1,0:T(8,128)S(1)} %get-tuple-element.82) | copy-start | bytes 4718596
  251.1 3.1 collective-permute-start.24
  255.3 11.5 %collective-permute-start.25 = (bf16[192,1024]{1,0:T(8,128)(2,1)S(1)}, bf16[192,1024]{1,0:T(8,128)(2,1)S(1)}, u32[]{:S(2)}, u32[]{:S(2)}) collective-permute-start(bf16[192,1024]{1,0:T(8,128)(2,1)S(1)} %add_convert_fusion.15), channel_id=1, source_target_pairs={{0,2},{1,3},{2,0},{3,1},{4,6},{5,7},{6,4},{7,5},{8,10},{9,11},{10,... | collective-permute-start | bytes 1179656 | tf_op jit(solution)/shard_map/ppermute | solution.py:127
  258.3 11.8 %collective-permute-start.20 = (bf16[192,1024]{1,0:T(8,128)(2,1)S(1)}, bf16[192,1024]{1,0:T(8,128)(2,1)S(1)}, u32[]{:S(2)}, u32[]{:S(2)}) collective-permute-start(bf16[192,1024]{1,0:T(8,128)(2,1)S(1)} %constant_dynamic-slice_fusion.5), channel_id=1, source_target_pairs={{0,1},{1,0},{2,3},{3,2},{4,5},{5,4},{6,7},{7,6},{8,9},{9,8},{10,11... | collective-permute-start | bytes 1179656 | tf_op jit(solution)/shard_map/ppermute | solution.py:121
  267.0 13.6 %collective-permute-start.26 = (bf16[192,1024]{1,0:T(8,128)(2,1)S(1)}, bf16[192,1024]{1,0:T(8,128)(2,1)S(1)}, u32[]{:S(2)}, u32[]{:S(2)}) collective-permute-start(bf16[192,1024]{1,0:T(8,128)(2,1)S(1)} %add_convert_fusion.14), channel_id=1, source_target_pairs={{0,4},{1,5},{2,6},{3,7},{4,0},{5,1},{6,2},{7,3},{8,12},{9,13},{10,... | collective-permute-start | bytes 1179656 | tf_op jit(solution)/shard_map/ppermute | solution.py:127
  271.0 16.1 %collective-permute-start.21 = (bf16[192,1024]{1,0:T(8,128)(2,1)}, bf16[192,1024]{1,0:T(8,128)(2,1)}, u32[]{:S(2)}, u32[]{:S(2)}) collective-permute-start(bf16[192,1024]{1,0:T(8,128)(2,1)} %add_convert_fusion.18), channel_id=1, source_target_pairs={{0,2},{1,3},{2,0},{3,1},{4,6},{5,7},{6,4},{7,5},{8,10},{9,11},{10,... | collective-permute-start | bytes 1179656 | tf_op jit(solution)/shard_map/ppermute | solution.py:127
  280.7 10.5 %collective-permute-start.27 = (bf16[192,1024]{1,0:T(8,128)(2,1)S(1)}, bf16[192,1024]{1,0:T(8,128)(2,1)}, u32[]{:S(2)}, u32[]{:S(2)}) collective-permute-start(bf16[192,1024]{1,0:T(8,128)(2,1)S(1)} %add_convert_fusion.13), channel_id=1, source_target_pairs={{0,1},{1,0},{2,3},{3,2},{4,5},{5,4},{6,7},{7,6},{8,9},{9,8},{10,11... | collective-permute-start | bytes 1179656 | tf_op jit(solution)/shard_map/ppermute | solution.py:131
  289.1 29.0 %collective-permute-start.22 = (bf16[192,1024]{1,0:T(8,128)(2,1)}, bf16[192,1024]{1,0:T(8,128)(2,1)}, u32[]{:S(2)}, u32[]{:S(2)}) collective-permute-start(bf16[192,1024]{1,0:T(8,128)(2,1)} %add_convert_fusion.17), channel_id=1, source_target_pairs={{0,4},{1,5},{2,6},{3,7},{4,0},{5,1},{6,2},{7,3},{8,12},{9,13},{10,... | collective-permute-start | bytes 1179656 | tf_op jit(solution)/shard_map/ppermute | solution.py:127
  302.1 14.5 %collective-permute-start.29 = (bf16[384,128]{0,1:T(8,128)(2,1)}, bf16[384,128]{0,1:T(8,128)(2,1)}, u32[]{:S(2)}, u32[]{:S(2)}) collective-permute-start(bf16[384,128]{0,1:T(8,128)(2,1)} %fusion.139), channel_id=1, source_target_pairs={{0,8},{8,0},{1,9},{9,1},{2,10},{10,2},{3,11},{11,3},{4,12},{12,4},... | collective-permute-start | bytes 294920 | tf_op jit(solution)/shard_map/ppermute | solution.py:141
  303.2 9.3 %collective-permute-start.28 = (bf16[384,128]{1,0:T(8,128)(2,1)}, bf16[384,128]{1,0:T(8,128)(2,1)}, u32[]{:S(2)}, u32[]{:S(2)}) collective-permute-start(bf16[384,128]{1,0:T(8,128)(2,1)} %fusion.137), channel_id=1, source_target_pairs={{0,8},{8,0},{1,9},{9,1},{2,10},{10,2},{3,11},{11,3},{4,12},{12,4},... | collective-permute-start | bytes 294920 | tf_op jit(solution)/shard_map/ppermute | solution.py:141
  318.1 3.2 collective-permute-start.30
  319.5 4.5 collective-permute-start.23
  321.4 11.2 %collective-permute-start.31 = (bf16[192,1024]{1,0:T(8,128)(2,1)S(1)}, bf16[192,1024]{1,0:T(8,128)(2,1)S(1)}, u32[]{:S(2)}, u32[]{:S(2)}) collective-permute-start(bf16[192,1024]{1,0:T(8,128)(2,1)S(1)} %add_convert_fusion.12), channel_id=1, source_target_pairs={{0,2},{1,3},{2,0},{3,1},{4,6},{5,7},{6,4},{7,5},{8,10},{9,11},{10,... | collective-permute-start | bytes 1179656 | tf_op jit(solution)/shard_map/ppermute | solution.py:127
  332.8 11.9 %collective-permute-start.32 = (bf16[192,1024]{1,0:T(8,128)(2,1)S(1)}, bf16[192,1024]{1,0:T(8,128)(2,1)S(1)}, u32[]{:S(2)}, u32[]{:S(2)}) collective-permute-start(bf16[192,1024]{1,0:T(8,128)(2,1)S(1)} %add_convert_fusion.11), channel_id=1, source_target_pairs={{0,4},{1,5},{2,6},{3,7},{4,0},{5,1},{6,2},{7,3},{8,12},{9,13},{10,... | collective-permute-start | bytes 1179656 | tf_op jit(solution)/shard_map/ppermute | solution.py:127
  344.8 3.4 collective-permute-start.33
  353.6 3.7 collective-permute-start.34
  357.4 11.9 %collective-permute-start.35 = (bf16[192,1024]{1,0:T(8,128)(2,1)S(1)}, bf16[192,1024]{1,0:T(8,128)(2,1)}, u32[]{:S(2)}, u32[]{:S(2)}) collective-permute-start(bf16[192,1024]{1,0:T(8,128)(2,1)S(1)} %add_convert_fusion.9), channel_id=1, source_target_pairs={{0,2},{1,3},{2,0},{3,1},{4,6},{5,7},{6,4},{7,5},{8,10},{9,11},{10,... | collective-permute-start | bytes 1179656 | tf_op jit(solution)/shard_map/ppermute | solution.py:127
  365.7 186.2 %reduce-scatter.9.cloned.1.call-start = ((), (), s32[]{:S(2)}) async-start(), calls=%async_computation.5 | async-start | bytes 3063808
  370.5 12.8 %collective-permute-start.36 = (bf16[192,1024]{1,0:T(8,128)(2,1)S(1)}, bf16[192,1024]{1,0:T(8,128)(2,1)S(1)}, u32[]{:S(2)}, u32[]{:S(2)}) collective-permute-start(bf16[192,1024]{1,0:T(8,128)(2,1)S(1)} %add_convert_fusion.8), channel_id=1, source_target_pairs={{0,4},{1,5},{2,6},{3,7},{4,0},{5,1},{6,2},{7,3},{8,12},{9,13},{10,... | collective-permute-start | bytes 1179656 | tf_op jit(solution)/shard_map/ppermute | solution.py:127
  383.4 1.8 collective-permute-start.37
  392.8 15.4 %collective-permute-start.38 = (bf16[384,128]{1,0:T(8,128)(2,1)}, bf16[384,128]{1,0:T(8,128)(2,1)}, u32[]{:S(2)}, u32[]{:S(2)}) collective-permute-start(bf16[384,128]{1,0:T(8,128)(2,1)} %fusion.141), channel_id=1, source_target_pairs={{0,8},{8,0},{1,9},{9,1},{2,10},{10,2},{3,11},{11,3},{4,12},{12,4},... | collective-permute-start | bytes 294920 | tf_op jit(solution)/shard_map/ppermute | solution.py:141
  405.5 12.9 %collective-permute-start.39 = (bf16[384,128]{0,1:T(8,128)(2,1)S(1)}, bf16[384,128]{0,1:T(8,128)(2,1)S(1)}, u32[]{:S(2)}, u32[]{:S(2)}) collective-permute-start(bf16[384,128]{0,1:T(8,128)(2,1)S(1)} %fusion.143), channel_id=1, source_target_pairs={{0,8},{8,0},{1,9},{9,1},{2,10},{10,2},{3,11},{11,3},{4,12},{12,4},... | collective-permute-start | bytes 294920 | tf_op jit(solution)/shard_map/ppermute | solution.py:141
  419.7 6.3 %collective-permute-start.40 = (bf16[192,1024]{1,0:T(8,128)(2,1)}, bf16[192,1024]{1,0:T(8,128)(2,1)}, u32[]{:S(2)}, u32[]{:S(2)}) collective-permute-start(bf16[192,1024]{1,0:T(8,128)(2,1)} %constant_dynamic-slice_fusion.1), channel_id=1, source_target_pairs={{0,1},{1,0},{2,3},{3,2},{4,5},{5,4},{6,7},{7,6},{8,9},{9,8},{10,11... | collective-permute-start | bytes 1179656 | tf_op jit(solution)/shard_map/ppermute | solution.py:121
  426.0 25.3 %collective-permute-start.51 = (bf16[2,2,1,2,64,512]{5,4,3,2,1,0:T(8,128)(2,1)}, bf16[2,2,1,2,64,512]{5,4,3,2,1,0:T(8,128)(2,1)}, u32[]{:S(2)}, u32[]{:S(2)}) collective-permute-start(bf16[2,2,1,2,64,512]{5,4,3,2,1,0:T(8,128)(2,1)} %constant_dynamic-slice_fusion), channel_id=1, source_target_pairs={{0,16},{16,0},{32,48},{48,32},{64,80},{80,64},{96,112},{112,96},{1... | collective-permute-start | bytes 1572872 | tf_op jit(solution)/shard_map/ppermute | solution.py:194
  428.0 24.9 %collective-permute-start.41 = (bf16[192,1024]{1,0:T(8,128)(2,1)}, bf16[192,1024]{1,0:T(8,128)(2,1)}, u32[]{:S(2)}, u32[]{:S(2)}) collective-permute-start(bf16[192,1024]{1,0:T(8,128)(2,1)} %add_convert_fusion.6), channel_id=1, source_target_pairs={{0,2},{1,3},{2,0},{3,1},{4,6},{5,7},{6,4},{7,5},{8,10},{9,11},{10,... | collective-permute-start | bytes 1179656 | tf_op jit(solution)/shard_map/ppermute | solution.py:127
  452.7 9.5 %collective-permute-start.52 = (bf16[2,1,1,2,64,512]{5,4,3,2,1,0:T(8,128)(2,1)S(1)}, bf16[2,1,1,2,64,512]{5,4,3,2,1,0:T(8,128)(2,1)S(1)}, u32[]{:S(2)}, u32[]{:S(2)}) collective-permute-start(bf16[2,1,1,2,64,512]{5,4,3,2,1,0:T(8,128)(2,1)S(1)} %dynamic-slice_convert_fusion), channel_id=1, source_target_pairs={{0,32},{16,48},{32,0},{48,16},{64,96},{80,112},{96,64},{112,80},{1... | collective-permute-start | bytes 786440 | tf_op jit(solution)/shard_map/ppermute | solution.py:194
  454.1 12.5 %collective-permute-start.42 = (bf16[192,1024]{1,0:T(8,128)(2,1)S(1)}, bf16[192,1024]{1,0:T(8,128)(2,1)S(1)}, u32[]{:S(2)}, u32[]{:S(2)}) collective-permute-start(bf16[192,1024]{1,0:T(8,128)(2,1)S(1)} %add_convert_fusion.5), channel_id=1, source_target_pairs={{0,4},{1,5},{2,6},{3,7},{4,0},{5,1},{6,2},{7,3},{8,12},{9,13},{10,... | collective-permute-start | bytes 1179656 | tf_op jit(solution)/shard_map/ppermute | solution.py:127
  462.4 6.6 %collective-permute-start.53 = (bf16[2,1,1,1,64,512]{5,4,3,2,1,0:T(8,128)(2,1)S(1)}, bf16[2,1,1,1,64,512]{5,4,3,2,1,0:T(8,128)(2,1)S(1)}, u32[]{:S(2)}, u32[]{:S(2)}) collective-permute-start(bf16[2,1,1,1,64,512]{5,4,3,2,1,0:T(8,128)(2,1)S(1)} %dynamic-slice_convert_fusion.1), channel_id=1, source_target_pairs={{0,8},{8,0},{1,9},{9,1},{2,10},{10,2},{3,11},{11,3},{4,12},{12,4},... | collective-permute-start | bytes 393224 | tf_op jit(solution)/shard_map/ppermute | solution.py:194
  466.8 2.2 collective-permute-start.43
  469.4 2.9 collective-permute-start.44
  469.5 6.1 %collective-permute-start.54 = (bf16[1,1,1,1,64,512]{5,4,3,2,1,0:T(8,128)(2,1)S(1)}, bf16[1,1,1,1,64,512]{5,4,3,2,1,0:T(8,128)(2,1)S(1)}, u32[]{:S(2)}, u32[]{:S(2)}) collective-permute-start(bf16[1,1,1,1,64,512]{5,4,3,2,1,0:T(8,128)(2,1)S(1)} %dynamic-slice_convert_fusion.10), channel_id=1, source_target_pairs={{0,64},{16,80},{32,96},{48,112},{64,0},{80,16},{96,32},{112,48},{1... | collective-permute-start | bytes 196616 | tf_op jit(solution)/shard_map/ppermute | solution.py:194
  472.3 3.8 collective-permute-start.45
  476.2 5.3 collective-permute-start.46
  481.6 5.3 collective-permute-start.47
  486.9 3.8 collective-permute-start.48
  490.8 4.2 collective-permute-start.49
  495.0 5.3 collective-permute-start.50
  (133 other events, 768.1 us)
Sparse Core Ops, SparseCore 0:
  10.6 89.2 all-gather.2
  101.5 94.5 all-gather.4
  365.8 99.0 reduce-scatter.6
  467.3 84.5 reduce-scatter.8

commit v9 on v8

--- a/solution.py
+++ b/solution.py
@@ -290,13 +290,11 @@
     for width in widths:
         edges.append(edges[-1] + width)
 
-    def gather_layer(layer_index):
-        if layer_index > 0:
-            joined = jnp.concatenate([member[layer_index] for member in weight_shards], axis=1)
-            full = lax.all_gather(joined, ("fsdp", "ctx"), axis=0, tiled=True)
-            return tuple(full[:, edges[k] : edges[k + 1]] for k in range(len(widths)))
+    def gather_early(layer_index):
         early = jnp.concatenate([member[layer_index] for member in weight_shards[:3]], axis=1)
-        early_full = shard_gather(early)
+        return shard_gather(early)
+
+    def gather_layer(layer_index, early_full):
         late = jnp.concatenate([member[layer_index] for member in weight_shards[3:]], axis=1)
         late_full = lax.all_gather(late, ("fsdp", "ctx"), axis=0, tiled=True)
         pieces = []
@@ -318,8 +316,6 @@
         return pieces
 
     def scatter_layer(terms, layer_index):
-        if layer_index > 0:
-            return tuple(scatter_terms(terms))
         early = scatter_terms(terms[3:])
         joined = shard_scatter(
             jnp.concatenate([term.astype(jnp.bfloat16) for term in terms[:3]], axis=1)
@@ -332,10 +328,11 @@
         return tuple(late + early)
 
     kept_weights = []
+    early_gathered = [gather_early(layer_index) for layer_index in range(layer_count)]
     stored_layers = []
     hidden = tokens
     for layer_index in range(layer_count):
-        gathered = gather_layer(layer_index)
+        gathered = gather_layer(layer_index, early_gathered[layer_index])
         kept_weights.append(gathered)
         (
             forward_query_full,
@@ -387,6 +384,10 @@
         )
         forward_log_total = forward_log_total.reshape(local_groups, per_group, row_count, 1)
         forward_middle = hidden + tp_sum(contract_last(forward_attended, forward_output_full))
+        if layer_index + 1 < layer_count:
+            forward_middle, early_gathered[layer_index + 1] = lax.optimization_barrier(
+                (forward_middle, early_gathered[layer_index + 1])
+            )
         forward_scale_two = row_scale(forward_middle)
         forward_feed_normed = (
             forward_middle * forward_scale_two * feedforward_gain[layer_index]

time: 574 us -> 589 us (1.026)
  local copies, waits for them, and re-layouts: 54.1 us -> 61.2 us
    ppermute x4 -> x8, waiting for transfers between devices: 23.7 us -> 72.9 us  [shard_scatter(): received = lax.ppermute(sent.astype(jnp.bfloat16), axis_name, pairs)]
    unnamed x5 -> x6, waiting for transfers between devices: 45.5 us -> 0.09 us
    all_gather x1 -> x2, waiting for transfers between devices: 20.2 us -> 56.9 us  [gather_layer(): late_full = lax.all_gather(late, ('fsdp', 'ctx'), axis=0, tiled=True)]
    all_gather x1 -> x0, waiting for transfers between devices: 32 us -> none  [gather_layer(): full = lax.all_gather(joined, ('fsdp', 'ctx'), axis=0, tiled=True)]
    ppermute x4 -> x8, waiting for transfers between devices: 26.6 us -> 47.4 us  [shard_gather(): received = lax.ppermute(current, axis_name, pairs)]
    ppermute x16, waiting for transfers between devices: 104 us -> 85.4 us  [tp_sum(): received = lax.ppermute(mine, 'tp', pairs)]
    ppermute x8, waiting for transfers between devices: 12.7 us -> 2.3 us  [swap_halves(): return lax.ppermute(local, axis_name, [(0, 1), (1, 0)])]
    unnamed x296 -> x246, local copies, waits for them, and re-layouts: 29.4 us -> 25.8 us
  transfers between devices with their start and end apart: 59 -> 67, of which waited for: 39 -> 46; matrix products, arithmetic and copies ran while one was open for 26% -> 27% of each run, Pallas kernels for 1% -> 1%
where the time goes in v9:
time: 589 us; the launch traced here: 578 us
  waiting for transfers between devices  289 us (49%)
  other arithmetic  77.6 us (13%)
  starting transfers between devices  72.6 us (12%)
  local copies, waits for them, and re-layouts  61.2 us (10%)
  matrix products  54.6 us (9%)
  between operations  16.2 us (3%)
  Pallas kernels  7.22 us (1%)
    ppermute x16, waiting for transfers between devices, tp_sum(): received = lax.ppermute(mine, 'tp', pairs)  85.4 us
    ppermute x8, waiting for transfers between devices, shard_scatter(): received = lax.ppermute(sent.astype(jnp.bfloat16), axis_name, pairs)  72.9 us
    all_gather x2, waiting for transfers between devices, gather_layer(): late_full = lax.all_gather(late, ('fsdp', 'ctx'), axis=0, tiled=True)  56.9 us
    ppermute x8, waiting for transfers between devices, shard_gather(): received = lax.ppermute(current, axis_name, pairs)  47.4 us
    ppermute x16, starting transfers between devices, tp_sum(): received = lax.ppermute(mine, 'tp', pairs)  30.1 us
    unnamed x246, local copies, waits for them, and re-layouts  25.8 us
    dot_general x14, matrix products, contract_last(): lax.dot_general(left_side, right_side, (((1,), (1,)), ((), ())), preferre...  16.5 us
    ppermute x7, waiting for transfers between devices, all_sum(): total = total + lax.ppermute(total, axis_name, pairs)  15.8 us
  transfers between devices with their start and end apart: 67, of which 46 were waited for; matrix products, arithmetic and copies ran while one was open for 27% of the time, Pallas kernels for 1%

profile of v9, /device:TPU:0, one launch (start us, length us, event | category | flops | bytes accessed | tf_op | source)
XLA Modules:
  0.0 578.2 jit_solution(6748202684474299487)
XLA Ops:
  8.9 4.0 collective-permute-start
  19.9 3.1 collective-permute-start.1
  23.6 2.9 collective-permute-done.1
  29.7 8.7 %collective-permute-done.2 = bf16[2,1,1,2,64,512]{5,4,3,2,1,0:T(8,128)(2,1)S(1)} collective-permute-done((bf16[2,1,1,2,64,512]{5,4,3,2,1,0:T(8,128)(2,1)S(1)}, bf16[2,1,1,2,64,512]{5,4,3,2,1,0:T(8,128)(2,1)S(1)}, u32[]{:S(2)}, u32[]{:S(2)}) %collective-permute-start.2) | collective-permute-done | bytes 262176 | tf_op jit(solution)/shard_map/ppermute | solution.py:216
  42.1 18.0 %collective-permute-done.3 = bf16[2,1,2,2,64,512]{5,4,3,2,1,0:T(8,128)(2,1)S(1)} collective-permute-done((bf16[2,1,2,2,64,512]{5,4,3,2,1,0:T(8,128)(2,1)S(1)}, bf16[2,1,2,2,64,512]{5,4,3,2,1,0:T(8,128)(2,1)S(1)}, u32[]{:S(2)}, u32[]{:S(2)}) %collective-permute-start.3) | collective-permute-done | bytes 524320 | tf_op jit(solution)/shard_map/ppermute | solution.py:216
  62.3 3.6 collective-permute-start.4
  69.8 3.6 shard_map.237
  73.4 30.5 %all-gather.3.cloned.1.call-done = bf16[1024,1408]{1,0:T(8,128)(2,1)} async-done(((bf16[64,1408]{1,0:T(8,128)(2,1)}), bf16[1024,1408]{1,0:T(8,128)(2,1)}) %all-gather.3.cloned.1.call-update) | async-done | bytes 2883600 | tf_op jit(solution)/shard_map/all_gather | solution.py:299
  107.4 2.2 collective-permute-start.7
  109.7 2.0 collective-permute-done.10
  111.8 6.6 %collective-permute-done.11 = bf16[1,1,1,2,64,512]{5,4,3,2,1,0:T(8,128)(2,1)S(1)} collective-permute-done((bf16[1,1,1,2,64,512]{5,4,3,2,1,0:T(8,128)(2,1)S(1)}, bf16[1,1,1,2,64,512]{5,4,3,2,1,0:T(8,128)(2,1)S(1)}, u32[]{:S(2)}, u32[]{:S(2)}) %collective-permute-start.11) | collective-permute-done | bytes 131104 | tf_op jit(solution)/shard_map/ppermute | solution.py:216
  121.2 4.3 collective-permute-done.12
  125.8 5.8 %collective-permute-done.8 = bf16[192,1024]{1,0:T(8,128)(2,1)S(1)} collective-permute-done((bf16[192,1024]{1,0:T(8,128)(2,1)S(1)}, bf16[192,1024]{1,0:T(8,128)(2,1)S(1)}, u32[]{:S(2)}, u32[]{:S(2)}) %collective-permute-start.8) | collective-permute-done | bytes 393248 | tf_op jit(solution)/shard_map/ppermute | solution.py:127
  132.7 4.8 collective-permute-done.13
  148.9 1.9 collective-permute-start.15
  150.8 9.4 %collective-permute-done.15 = bf16[192,1024]{1,0:T(8,128)(2,1)S(1)} collective-permute-done((bf16[192,1024]{1,0:T(8,128)(2,1)S(1)}, bf16[192,1024]{1,0:T(8,128)(2,1)S(1)}, u32[]{:S(2)}, u32[]{:S(2)}) %collective-permute-start.15) | collective-permute-done | bytes 393248 | tf_op jit(solution)/shard_map/ppermute | solution.py:127
  160.4 2.2 collective-permute-start.16
  162.6 9.9 %collective-permute-done.16 = bf16[192,1024]{1,0:T(8,128)(2,1)S(1)} collective-permute-done((bf16[192,1024]{1,0:T(8,128)(2,1)S(1)}, bf16[192,1024]{1,0:T(8,128)(2,1)S(1)}, u32[]{:S(2)}, u32[]{:S(2)}) %collective-permute-start.16) | collective-permute-done | bytes 393248 | tf_op jit(solution)/shard_map/ppermute | solution.py:127
  177.4 2.1 collective-permute-start.19
  189.0 2.9 multiply_reduce_fusion.10
  202.0 3.6 shard_map.238
  205.6 26.4 %all-gather.5.cloned.1.call-done = bf16[1024,1408]{1,0:T(8,128)(2,1)} async-done(((bf16[64,1408]{1,0:T(8,128)(2,1)}), bf16[1024,1408]{1,0:T(8,128)(2,1)}) %all-gather.5.cloned.1.call-update) | async-done | bytes 2883600 | tf_op jit(solution)/shard_map/all_gather | solution.py:299
  237.2 9.5 %collective-permute-done.21 = bf16[192,1024]{1,0:T(8,128)(2,1)S(1)} collective-permute-done((bf16[192,1024]{1,0:T(8,128)(2,1)S(1)}, bf16[192,1024]{1,0:T(8,128)(2,1)S(1)}, u32[]{:S(2)}, u32[]{:S(2)}) %collective-permute-start.21) | collective-permute-done | bytes 393248 | tf_op jit(solution)/shard_map/ppermute | solution.py:127
  247.6 2.9 collective-permute-start.22
  252.9 6.9 %collective-permute-done.22 = bf16[192,1024]{1,0:T(8,128)(2,1)} collective-permute-done((bf16[192,1024]{1,0:T(8,128)(2,1)}, bf16[192,1024]{1,0:T(8,128)(2,1)}, u32[]{:S(2)}, u32[]{:S(2)}) %collective-permute-start.22) | collective-permute-done | bytes 393248 | tf_op jit(solution)/shard_map/ppermute | solution.py:127
  259.8 2.0 add_convert_fusion.19
  265.1 3.0 convolution_bitcast_fusion
  269.9 2.2 multiply_reduce_fusion.4
  283.6 8.2 %collective-permute-done.29 = bf16[192,1024]{1,0:T(8,128)(2,1)S(1)} collective-permute-done((bf16[192,1024]{1,0:T(8,128)(2,1)S(1)}, bf16[192,1024]{1,0:T(8,128)(2,1)S(1)}, u32[]{:S(2)}, u32[]{:S(2)}) %collective-permute-start.29) | collective-permute-done | bytes 393248 | tf_op jit(solution)/shard_map/ppermute | solution.py:127
  291.9 2.9 collective-permute-start.30
  296.4 3.8 collective-permute-done.25
  300.4 2.9 collective-permute-start.26
  303.3 7.3 %collective-permute-done.30 = bf16[192,1024]{1,0:T(8,128)(2,1)S(1)} collective-permute-done((bf16[192,1024]{1,0:T(8,128)(2,1)S(1)}, bf16[192,1024]{1,0:T(8,128)(2,1)S(1)}, u32[]{:S(2)}, u32[]{:S(2)}) %collective-permute-start.30) | collective-permute-done | bytes 393248 | tf_op jit(solution)/shard_map/ppermute | solution.py:127
  312.4 6.1 %collective-permute-done.26 = bf16[192,1024]{1,0:T(8,128)(2,1)S(1)} collective-permute-done((bf16[192,1024]{1,0:T(8,128)(2,1)S(1)}, bf16[192,1024]{1,0:T(8,128)(2,1)S(1)}, u32[]{:S(2)}, u32[]{:S(2)}) %collective-permute-start.26) | collective-permute-done | bytes 393248 | tf_op jit(solution)/shard_map/ppermute | solution.py:127
  332.3 1.9 fusion.62
  339.0 4.6 copy.200
  347.2 2.0 collective-permute-start.33
  349.2 2.2 collective-permute-done.32
  360.3 2.4 copy.174
  364.3 3.0 convert_add_fusion
  369.1 17.1 %collective-permute-done.59 = bf16[2,2,1,2,64,512]{5,4,3,2,1,0:T(8,128)(2,1)S(1)} collective-permute-done((bf16[2,2,1,2,64,512]{5,4,3,2,1,0:T(8,128)(2,1)S(1)}, bf16[2,2,1,2,64,512]{5,4,3,2,1,0:T(8,128)(2,1)S(1)}, u32[]{:S(2)}, u32[]{:S(2)}) %collective-permute-start.59) | collective-permute-done | bytes 524320 | tf_op jit(solution)/shard_map/ppermute | solution.py:194
  388.7 9.8 %collective-permute-done.60 = bf16[2,1,1,2,64,512]{5,4,3,2,1,0:T(8,128)(2,1)S(1)} collective-permute-done((bf16[2,1,1,2,64,512]{5,4,3,2,1,0:T(8,128)(2,1)S(1)}, bf16[2,1,1,2,64,512]{5,4,3,2,1,0:T(8,128)(2,1)S(1)}, u32[]{:S(2)}, u32[]{:S(2)}) %collective-permute-start.60) | collective-permute-done | bytes 262176 | tf_op jit(solution)/shard_map/ppermute | solution.py:194
  400.0 8.1 %collective-permute-done.61 = bf16[2,1,1,1,64,512]{5,4,3,2,1,0:T(8,128)(2,1)S(1)} collective-permute-done((bf16[2,1,1,1,64,512]{5,4,3,2,1,0:T(8,128)(2,1)S(1)}, bf16[2,1,1,1,64,512]{5,4,3,2,1,0:T(8,128)(2,1)S(1)}, u32[]{:S(2)}, u32[]{:S(2)}) %collective-permute-start.61) | collective-permute-done | bytes 131104 | tf_op jit(solution)/shard_map/ppermute | solution.py:194
  418.3 8.6 %collective-permute-done.39 = bf16[192,1024]{1,0:T(8,128)(2,1)S(1)} collective-permute-done((bf16[192,1024]{1,0:T(8,128)(2,1)S(1)}, bf16[192,1024]{1,0:T(8,128)(2,1)S(1)}, u32[]{:S(2)}, u32[]{:S(2)}) %collective-permute-start.39) | collective-permute-done | bytes 393248 | tf_op jit(solution)/shard_map/ppermute | solution.py:127
  427.0 2.4 collective-permute-start.40
  430.4 8.7 %collective-permute-done.40 = bf16[192,1024]{1,0:T(8,128)(2,1)S(1)} collective-permute-done((bf16[192,1024]{1,0:T(8,128)(2,1)S(1)}, bf16[192,1024]{1,0:T(8,128)(2,1)S(1)}, u32[]{:S(2)}, u32[]{:S(2)}) %collective-permute-start.40) | collective-permute-done | bytes 393248 | tf_op jit(solution)/shard_map/ppermute | solution.py:127
  444.7 4.6 copy.198
  458.0 1.9 copy.167
  461.8 2.3 convolution_bitcast_fusion.3
  467.6 3.5 collective-permute-start.43
  474.8 2.5 fusion.91
  480.0 2.3 copy.173
  483.6 2.4 add_convert_fusion
  487.4 18.0 %collective-permute-done.55 = bf16[2,2,1,2,64,512]{5,4,3,2,1,0:T(8,128)(2,1)S(1)} collective-permute-done((bf16[2,2,1,2,64,512]{5,4,3,2,1,0:T(8,128)(2,1)S(1)}, bf16[2,2,1,2,64,512]{5,4,3,2,1,0:T(8,128)(2,1)S(1)}, u32[]{:S(2)}, u32[]{:S(2)}) %collective-permute-start.55) | collective-permute-done | bytes 524320 | tf_op jit(solution)/shard_map/ppermute | solution.py:194
  507.8 9.2 %collective-permute-done.56 = bf16[2,1,1,2,64,512]{5,4,3,2,1,0:T(8,128)(2,1)S(1)} collective-permute-done((bf16[2,1,1,2,64,512]{5,4,3,2,1,0:T(8,128)(2,1)S(1)}, bf16[2,1,1,2,64,512]{5,4,3,2,1,0:T(8,128)(2,1)S(1)}, u32[]{:S(2)}, u32[]{:S(2)}) %collective-permute-start.56) | collective-permute-done | bytes 262176 | tf_op jit(solution)/shard_map/ppermute | solution.py:194
  517.4 2.7 collective-permute-start.46
  520.2 6.9 %collective-permute-done.57 = bf16[2,1,1,1,64,512]{5,4,3,2,1,0:T(8,128)(2,1)S(1)} collective-permute-done((bf16[2,1,1,1,64,512]{5,4,3,2,1,0:T(8,128)(2,1)S(1)}, bf16[2,1,1,1,64,512]{5,4,3,2,1,0:T(8,128)(2,1)S(1)}, u32[]{:S(2)}, u32[]{:S(2)}) %collective-permute-start.57) | collective-permute-done | bytes 131104 | tf_op jit(solution)/shard_map/ppermute | solution.py:194
  527.1 2.0 collective-permute-start.58
  529.4 3.5 collective-permute-done.58
  538.6 3.4 collective-permute-start.50
  545.1 4.4 collective-permute-done.51
  550.3 3.0 collective-permute-done.52
  554.5 2.7 collective-permute-done.53
  557.2 2.0 collective-permute-start.54
  (584 shorter events, 197.3 us)
Async XLA Ops:
  7.2 96.7 %all-gather.3.cloned.1.call-start = ((), (), s32[]{:S(2)}) async-start(), calls=%async_computation.2 | async-start | bytes 3063808 | tf_op jit(solution)/shard_map/all_gather | solution.py:299
  8.9 10.9 %collective-permute-start = (bf16[1,1,1,1,64,512]{5,4,3,2,1,0:T(8,128)(2,1)S(1)}, bf16[1,1,1,1,64,512]{5,4,3,2,1,0:T(8,128)(2,1)S(1)}, u32[]{:S(2)}, u32[]{:S(2)}) collective-permute-start(bf16[1,1,1,1,64,512]{5,4,3,2,1,0:T(8,128)(2,1)S(1)} %get-tuple-element.149), channel_id=1, source_target_pairs={{0,8},{8,0},{1,9},{9,1},{2,10},{10,2},{3,11},{11,3},{4,12},{12,4},... | collective-permute-start | bytes 196616 | tf_op jit(solution)/shard_map/ppermute | solution.py:216
  18.1 213.9 %all-gather.5.cloned.1.call-start = ((), (), s32[]{:S(2)}) async-start(), calls=%async_computation.3 | async-start | bytes 3063808 | tf_op jit(solution)/shard_map/all_gather | solution.py:299
  19.9 6.6 %collective-permute-start.1 = (bf16[1,1,1,2,64,512]{5,4,3,2,1,0:T(8,128)(2,1)S(1)}, bf16[1,1,1,2,64,512]{5,4,3,2,1,0:T(8,128)(2,1)S(1)}, u32[]{:S(2)}, u32[]{:S(2)}) collective-permute-start(bf16[1,1,1,2,64,512]{5,4,3,2,1,0:T(8,128)(2,1)S(1)} %maximum_select_fusion.21), channel_id=1, source_target_pairs={{0,64},{16,80},{32,96},{48,112},{64,0},{80,16},{96,32},{112,48},{1... | collective-permute-start | bytes 393224 | tf_op jit(solution)/shard_map/ppermute | solution.py:216
  26.5 12.0 %collective-permute-start.2 = (bf16[2,1,1,2,64,512]{5,4,3,2,1,0:T(8,128)(2,1)S(1)}, bf16[2,1,1,2,64,512]{5,4,3,2,1,0:T(8,128)(2,1)S(1)}, u32[]{:S(2)}, u32[]{:S(2)}) collective-permute-start(bf16[2,1,1,2,64,512]{5,4,3,2,1,0:T(8,128)(2,1)S(1)} %maximum_select_fusion.13), channel_id=1, source_target_pairs={{0,16},{16,0},{32,48},{48,32},{64,80},{80,64},{96,112},{112,96},{1... | collective-permute-start | bytes 786440 | tf_op jit(solution)/shard_map/ppermute | solution.py:216
  38.5 21.5 %collective-permute-start.3 = (bf16[2,1,2,2,64,512]{5,4,3,2,1,0:T(8,128)(2,1)S(1)}, bf16[2,1,2,2,64,512]{5,4,3,2,1,0:T(8,128)(2,1)S(1)}, u32[]{:S(2)}, u32[]{:S(2)}) collective-permute-start(bf16[2,1,2,2,64,512]{5,4,3,2,1,0:T(8,128)(2,1)S(1)} %maximum_select_fusion.10), channel_id=1, source_target_pairs={{0,32},{16,48},{32,0},{48,16},{64,96},{80,112},{96,64},{112,80},{1... | collective-permute-start | bytes 1572872 | tf_op jit(solution)/shard_map/ppermute | solution.py:216
  60.6 7.4 %collective-permute-start.5 = (bf16[384,128]{1,0:T(8,128)(2,1)S(1)}, bf16[384,128]{1,0:T(8,128)(2,1)S(1)}, u32[]{:S(2)}, u32[]{:S(2)}) collective-permute-start(bf16[384,128]{1,0:T(8,128)(2,1)S(1)} %convolution_convert_fusion.21), channel_id=1, source_target_pairs={{0,8},{8,0},{1,9},{9,1},{2,10},{10,2},{3,11},{11,3},{4,12},{12,4},... | collective-permute-start | bytes 294920 | tf_op jit(solution)/shard_map/ppermute | solution.py:141
  62.3 6.6 %collective-permute-start.4 = (bf16[384,128]{1,0:T(8,128)(2,1)S(1)}, bf16[384,128]{1,0:T(8,128)(2,1)S(1)}, u32[]{:S(2)}, u32[]{:S(2)}) collective-permute-start(bf16[384,128]{1,0:T(8,128)(2,1)S(1)} %pad_maximum_fusion.12), channel_id=1, source_target_pairs={{0,8},{8,0},{1,9},{9,1},{2,10},{10,2},{3,11},{11,3},{4,12},{12,4},... | collective-permute-start | bytes 294920 | tf_op jit(solution)/shard_map/ppermute | solution.py:141
  105.6 6.1 %collective-permute-start.10 = (bf16[1,1,1,1,64,512]{5,4,3,2,1,0:T(8,128)(2,1)S(1)}, bf16[1,1,1,1,64,512]{5,4,3,2,1,0:T(8,128)(2,1)S(1)}, u32[]{:S(2)}, u32[]{:S(2)}) collective-permute-start(bf16[1,1,1,1,64,512]{5,4,3,2,1,0:T(8,128)(2,1)S(1)} %get-tuple-element.144), channel_id=1, source_target_pairs={{0,8},{8,0},{1,9},{9,1},{2,10},{10,2},{3,11},{11,3},{4,12},{12,4},... | collective-permute-start | bytes 196616 | tf_op jit(solution)/shard_map/ppermute | solution.py:216
  107.4 11.7 %collective-permute-start.7 = (bf16[192,1024]{1,0:T(8,128)(2,1)S(1)}, bf16[192,1024]{1,0:T(8,128)(2,1)S(1)}, u32[]{:S(2)}, u32[]{:S(2)}) collective-permute-start(bf16[192,1024]{1,0:T(8,128)(2,1)S(1)} %add_convert_fusion.27), channel_id=1, source_target_pairs={{0,2},{1,3},{2,0},{3,1},{4,6},{5,7},{6,4},{7,5},{8,10},{9,11},{10,... | collective-permute-start | bytes 1179656 | tf_op jit(solution)/shard_map/ppermute | solution.py:127
  111.7 6.7 %collective-permute-start.11 = (bf16[1,1,1,2,64,512]{5,4,3,2,1,0:T(8,128)(2,1)S(1)}, bf16[1,1,1,2,64,512]{5,4,3,2,1,0:T(8,128)(2,1)S(1)}, u32[]{:S(2)}, u32[]{:S(2)}) collective-permute-start(bf16[1,1,1,2,64,512]{5,4,3,2,1,0:T(8,128)(2,1)S(1)} %maximum_select_fusion.23), channel_id=1, source_target_pairs={{0,64},{16,80},{32,96},{48,112},{64,0},{80,16},{96,32},{112,48},{1... | collective-permute-start | bytes 393224 | tf_op jit(solution)/shard_map/ppermute | solution.py:216
  118.4 7.1 %collective-permute-start.12 = (bf16[2,1,1,2,64,512]{5,4,3,2,1,0:T(8,128)(2,1)S(1)}, bf16[2,1,1,2,64,512]{5,4,3,2,1,0:T(8,128)(2,1)S(1)}, u32[]{:S(2)}, u32[]{:S(2)}) collective-permute-start(bf16[2,1,1,2,64,512]{5,4,3,2,1,0:T(8,128)(2,1)S(1)} %maximum_select_fusion.15), channel_id=1, source_target_pairs={{0,16},{16,0},{32,48},{48,32},{64,80},{80,64},{96,112},{112,96},{1... | collective-permute-start | bytes 786440 | tf_op jit(solution)/shard_map/ppermute | solution.py:216
  119.3 12.3 %collective-permute-start.8 = (bf16[192,1024]{1,0:T(8,128)(2,1)S(1)}, bf16[192,1024]{1,0:T(8,128)(2,1)S(1)}, u32[]{:S(2)}, u32[]{:S(2)}) collective-permute-start(bf16[192,1024]{1,0:T(8,128)(2,1)S(1)} %add_convert_fusion.26), channel_id=1, source_target_pairs={{0,4},{1,5},{2,6},{3,7},{4,0},{5,1},{6,2},{7,3},{8,12},{9,13},{10,... | collective-permute-start | bytes 1179656 | tf_op jit(solution)/shard_map/ppermute | solution.py:127
  125.7 11.8 %collective-permute-start.13 = (bf16[2,1,2,2,64,512]{5,4,3,2,1,0:T(8,128)(2,1)S(1)}, bf16[2,1,2,2,64,512]{5,4,3,2,1,0:T(8,128)(2,1)S(1)}, u32[]{:S(2)}, u32[]{:S(2)}) collective-permute-start(bf16[2,1,2,2,64,512]{5,4,3,2,1,0:T(8,128)(2,1)S(1)} %maximum_select_fusion.11), channel_id=1, source_target_pairs={{0,32},{16,48},{32,0},{48,16},{64,96},{80,112},{96,64},{112,80},{1... | collective-permute-start | bytes 1572872 | tf_op jit(solution)/shard_map/ppermute | solution.py:216
  131.7 7.0 %collective-permute-start.9 = (bf16[192,1024]{1,0:T(8,128)(2,1)S(1)}, bf16[192,1024]{1,0:T(8,128)(2,1)}, u32[]{:S(2)}, u32[]{:S(2)}) collective-permute-start(bf16[192,1024]{1,0:T(8,128)(2,1)S(1)} %add_convert_fusion.25), channel_id=1, source_target_pairs={{0,1},{1,0},{2,3},{3,2},{4,5},{5,4},{6,7},{7,6},{8,9},{9,8},{10,11... | collective-permute-start | bytes 1179656 | tf_op jit(solution)/shard_map/ppermute | solution.py:131
  146.8 1.9 collective-permute-start.14
  147.5 416.2 %reduce-scatter.9.cloned.1.call-start = ((), (), s32[]{:S(2)}) async-start(), calls=%async_computation.5 | async-start | bytes 3063808
  148.9 11.4 %collective-permute-start.15 = (bf16[192,1024]{1,0:T(8,128)(2,1)S(1)}, bf16[192,1024]{1,0:T(8,128)(2,1)S(1)}, u32[]{:S(2)}, u32[]{:S(2)}) collective-permute-start(bf16[192,1024]{1,0:T(8,128)(2,1)S(1)} %add_convert_fusion.24), channel_id=1, source_target_pairs={{0,2},{1,3},{2,0},{3,1},{4,6},{5,7},{6,4},{7,5},{8,10},{9,11},{10,... | collective-permute-start | bytes 1179656 | tf_op jit(solution)/shard_map/ppermute | solution.py:127
  160.4 12.2 %collective-permute-start.16 = (bf16[192,1024]{1,0:T(8,128)(2,1)S(1)}, bf16[192,1024]{1,0:T(8,128)(2,1)S(1)}, u32[]{:S(2)}, u32[]{:S(2)}) collective-permute-start(bf16[192,1024]{1,0:T(8,128)(2,1)S(1)} %add_convert_fusion.23), channel_id=1, source_target_pairs={{0,4},{1,5},{2,6},{3,7},{4,0},{5,1},{6,2},{7,3},{8,12},{9,13},{10,... | collective-permute-start | bytes 1179656 | tf_op jit(solution)/shard_map/ppermute | solution.py:127
  172.7 1.8 collective-permute-start.17
  177.4 21.0 %collective-permute-start.19 = (bf16[384,128]{1,0:T(8,128)(2,1)}, bf16[384,128]{1,0:T(8,128)(2,1)}, u32[]{:S(2)}, u32[]{:S(2)}) collective-permute-start(bf16[384,128]{1,0:T(8,128)(2,1)} %convolution_convert_fusion.20), channel_id=1, source_target_pairs={{0,8},{8,0},{1,9},{9,1},{2,10},{10,2},{3,11},{11,3},{4,12},{12,4},... | collective-permute-start | bytes 294920 | tf_op jit(solution)/shard_map/ppermute | solution.py:141
  187.5 12.7 %collective-permute-start.18 = (bf16[384,128]{1,0:T(8,128)(2,1)}, bf16[384,128]{1,0:T(8,128)(2,1)}, u32[]{:S(2)}, u32[]{:S(2)}) collective-permute-start(bf16[384,128]{1,0:T(8,128)(2,1)} %pad_maximum_fusion.13), channel_id=1, source_target_pairs={{0,8},{8,0},{1,9},{9,1},{2,10},{10,2},{3,11},{11,3},{4,12},{12,4},... | collective-permute-start | bytes 294920 | tf_op jit(solution)/shard_map/ppermute | solution.py:141
  233.6 1.8 collective-permute-start.20
  235.5 11.2 %collective-permute-start.21 = (bf16[192,1024]{1,0:T(8,128)(2,1)S(1)}, bf16[192,1024]{1,0:T(8,128)(2,1)S(1)}, u32[]{:S(2)}, u32[]{:S(2)}) collective-permute-start(bf16[192,1024]{1,0:T(8,128)(2,1)S(1)} %add_convert_fusion.21), channel_id=1, source_target_pairs={{0,2},{1,3},{2,0},{3,1},{4,6},{5,7},{6,4},{7,5},{8,10},{9,11},{10,... | collective-permute-start | bytes 1179656 | tf_op jit(solution)/shard_map/ppermute | solution.py:127
  247.6 12.1 %collective-permute-start.22 = (bf16[192,1024]{1,0:T(8,128)(2,1)}, bf16[192,1024]{1,0:T(8,128)(2,1)}, u32[]{:S(2)}, u32[]{:S(2)}) collective-permute-start(bf16[192,1024]{1,0:T(8,128)(2,1)} %add_convert_fusion.20), channel_id=1, source_target_pairs={{0,4},{1,5},{2,6},{3,7},{4,0},{5,1},{6,2},{7,3},{8,12},{9,13},{10,... | collective-permute-start | bytes 1179656 | tf_op jit(solution)/shard_map/ppermute | solution.py:127
  261.8 8.1 %collective-permute-start.23 = (bf16[192,1024]{1,0:T(8,128)(2,1)}, bf16[192,1024]{1,0:T(8,128)(2,1)}, u32[]{:S(2)}, u32[]{:S(2)}) collective-permute-start(bf16[192,1024]{1,0:T(8,128)(2,1)} %add_convert_fusion.19), channel_id=1, source_target_pairs={{0,1},{1,0},{2,3},{3,2},{4,5},{5,4},{6,7},{7,6},{8,9},{9,8},{10,11... | collective-permute-start | bytes 1179656 | tf_op jit(solution)/shard_map/ppermute | solution.py:131
  277.7 1.9 collective-permute-start.28
  278.9 4.1 collective-permute-start.24
  279.8 12.0 %collective-permute-start.29 = (bf16[192,1024]{1,0:T(8,128)(2,1)S(1)}, bf16[192,1024]{1,0:T(8,128)(2,1)S(1)}, u32[]{:S(2)}, u32[]{:S(2)}) collective-permute-start(bf16[192,1024]{1,0:T(8,128)(2,1)S(1)} %add_convert_fusion.15), channel_id=1, source_target_pairs={{0,2},{1,3},{2,0},{3,1},{4,6},{5,7},{6,4},{7,5},{8,10},{9,11},{10,... | collective-permute-start | bytes 1179656 | tf_op jit(solution)/shard_map/ppermute | solution.py:127
  283.2 17.1 %collective-permute-start.25 = (bf16[192,1024]{1,0:T(8,128)(2,1)S(1)}, bf16[192,1024]{1,0:T(8,128)(2,1)S(1)}, u32[]{:S(2)}, u32[]{:S(2)}) collective-permute-start(bf16[192,1024]{1,0:T(8,128)(2,1)S(1)} %add_convert_fusion.18), channel_id=1, source_target_pairs={{0,2},{1,3},{2,0},{3,1},{4,6},{5,7},{6,4},{7,5},{8,10},{9,11},{10,... | collective-permute-start | bytes 1179656 | tf_op jit(solution)/shard_map/ppermute | solution.py:127
  291.9 18.7 %collective-permute-start.30 = (bf16[192,1024]{1,0:T(8,128)(2,1)S(1)}, bf16[192,1024]{1,0:T(8,128)(2,1)S(1)}, u32[]{:S(2)}, u32[]{:S(2)}) collective-permute-start(bf16[192,1024]{1,0:T(8,128)(2,1)S(1)} %add_convert_fusion.14), channel_id=1, source_target_pairs={{0,4},{1,5},{2,6},{3,7},{4,0},{5,1},{6,2},{7,3},{8,12},{9,13},{10,... | collective-permute-start | bytes 1179656 | tf_op jit(solution)/shard_map/ppermute | solution.py:127
  300.4 18.1 %collective-permute-start.26 = (bf16[192,1024]{1,0:T(8,128)(2,1)S(1)}, bf16[192,1024]{1,0:T(8,128)(2,1)S(1)}, u32[]{:S(2)}, u32[]{:S(2)}) collective-permute-start(bf16[192,1024]{1,0:T(8,128)(2,1)S(1)} %add_convert_fusion.17), channel_id=1, source_target_pairs={{0,4},{1,5},{2,6},{3,7},{4,0},{5,1},{6,2},{7,3},{8,12},{9,13},{10,... | collective-permute-start | bytes 1179656 | tf_op jit(solution)/shard_map/ppermute | solution.py:127
  310.8 8.8 %collective-permute-start.31 = (bf16[192,1024]{1,0:T(8,128)(2,1)S(1)}, bf16[192,1024]{1,0:T(8,128)(2,1)S(1)}, u32[]{:S(2)}, u32[]{:S(2)}) collective-permute-start(bf16[192,1024]{1,0:T(8,128)(2,1)S(1)} %add_convert_fusion.13), channel_id=1, source_target_pairs={{0,1},{1,0},{2,3},{3,2},{4,5},{5,4},{6,7},{7,6},{8,9},{9,8},{10,11... | collective-permute-start | bytes 1179656 | tf_op jit(solution)/shard_map/ppermute | solution.py:131
  319.4 44.8 %collective-permute-start.27 = (bf16[192,1024]{1,0:T(8,128)(2,1)}, bf16[192,1024]{1,0:T(8,128)(2,1)}, u32[]{:S(2)}, u32[]{:S(2)}) collective-permute-start(bf16[192,1024]{1,0:T(8,128)(2,1)} %add_convert_fusion.16), channel_id=1, source_target_pairs={{0,1},{1,0},{2,3},{3,2},{4,5},{5,4},{6,7},{7,6},{8,9},{9,8},{10,11... | collective-permute-start | bytes 1179656 | tf_op jit(solution)/shard_map/ppermute | solution.py:131
  343.6 222.3 %reduce-scatter.7.cloned.1.call-start = ((), (), s32[]{:S(2)}) async-start(), calls=%async_computation.4 | async-start | bytes 3063808
  344.7 6.7 %collective-permute-start.32 = (bf16[384,128]{1,0:T(8,128)(2,1)S(1)}, bf16[384,128]{1,0:T(8,128)(2,1)S(1)}, u32[]{:S(2)}, u32[]{:S(2)}) collective-permute-start(bf16[384,128]{1,0:T(8,128)(2,1)S(1)} %fusion.130), channel_id=1, source_target_pairs={{0,8},{8,0},{1,9},{9,1},{2,10},{10,2},{3,11},{11,3},{4,12},{12,4},... | collective-permute-start | bytes 294920 | tf_op jit(solution)/shard_map/ppermute | solution.py:141
  347.2 9.0 %collective-permute-start.33 = (bf16[384,128]{0,1:T(8,128)(2,1)S(1)}, bf16[384,128]{0,1:T(8,128)(2,1)S(1)}, u32[]{:S(2)}, u32[]{:S(2)}) collective-permute-start(bf16[384,128]{0,1:T(8,128)(2,1)S(1)} %fusion.132), channel_id=1, source_target_pairs={{0,8},{8,0},{1,9},{9,1},{2,10},{10,2},{3,11},{11,3},{4,12},{12,4},... | collective-permute-start | bytes 294920 | tf_op jit(solution)/shard_map/ppermute | solution.py:141
  362.8 4.5 collective-permute-start.34
  364.1 22.1 %collective-permute-start.59 = (bf16[2,2,1,2,64,512]{5,4,3,2,1,0:T(8,128)(2,1)S(1)}, bf16[2,2,1,2,64,512]{5,4,3,2,1,0:T(8,128)(2,1)S(1)}, u32[]{:S(2)}, u32[]{:S(2)}) collective-permute-start(bf16[2,2,1,2,64,512]{5,4,3,2,1,0:T(8,128)(2,1)S(1)} %constant_dynamic-slice_fusion), channel_id=1, source_target_pairs={{0,16},{16,0},{32,48},{48,32},{64,80},{80,64},{96,112},{112,96},{1... | collective-permute-start | bytes 1572872 | tf_op jit(solution)/shard_map/ppermute | solution.py:194
  367.4 19.8 %collective-permute-start.35 = (bf16[192,1024]{1,0:T(8,128)(2,1)S(1)}, bf16[192,1024]{1,0:T(8,128)(2,1)S(1)}, u32[]{:S(2)}, u32[]{:S(2)}) collective-permute-start(bf16[192,1024]{1,0:T(8,128)(2,1)S(1)} %add_convert_fusion.12), channel_id=1, source_target_pairs={{0,2},{1,3},{2,0},{3,1},{4,6},{5,7},{6,4},{7,5},{8,10},{9,11},{10,... | collective-permute-start | bytes 1179656 | tf_op jit(solution)/shard_map/ppermute | solution.py:127
  386.4 12.2 %collective-permute-start.60 = (bf16[2,1,1,2,64,512]{5,4,3,2,1,0:T(8,128)(2,1)S(1)}, bf16[2,1,1,2,64,512]{5,4,3,2,1,0:T(8,128)(2,1)S(1)}, u32[]{:S(2)}, u32[]{:S(2)}) collective-permute-start(bf16[2,1,1,2,64,512]{5,4,3,2,1,0:T(8,128)(2,1)S(1)} %dynamic-slice_convert_fusion), channel_id=1, source_target_pairs={{0,32},{16,48},{32,0},{48,16},{64,96},{80,112},{96,64},{112,80},{1... | collective-permute-start | bytes 786440 | tf_op jit(solution)/shard_map/ppermute | solution.py:194
  387.4 11.9 %collective-permute-start.36 = (bf16[192,1024]{1,0:T(8,128)(2,1)S(1)}, bf16[192,1024]{1,0:T(8,128)(2,1)S(1)}, u32[]{:S(2)}, u32[]{:S(2)}) collective-permute-start(bf16[192,1024]{1,0:T(8,128)(2,1)S(1)} %add_convert_fusion.11), channel_id=1, source_target_pairs={{0,4},{1,5},{2,6},{3,7},{4,0},{5,1},{6,2},{7,3},{8,12},{9,13},{10,... | collective-permute-start | bytes 1179656 | tf_op jit(solution)/shard_map/ppermute | solution.py:127
  398.7 9.5 %collective-permute-start.61 = (bf16[2,1,1,1,64,512]{5,4,3,2,1,0:T(8,128)(2,1)S(1)}, bf16[2,1,1,1,64,512]{5,4,3,2,1,0:T(8,128)(2,1)S(1)}, u32[]{:S(2)}, u32[]{:S(2)}) collective-permute-start(bf16[2,1,1,1,64,512]{5,4,3,2,1,0:T(8,128)(2,1)S(1)} %dynamic-slice_convert_fusion.2), channel_id=1, source_target_pairs={{0,8},{8,0},{1,9},{9,1},{2,10},{10,2},{3,11},{11,3},{4,12},{12,4},... | collective-permute-start | bytes 393224 | tf_op jit(solution)/shard_map/ppermute | solution.py:194
  399.4 9.8 %collective-permute-start.37 = (bf16[192,1024]{1,0:T(8,128)(2,1)S(1)}, bf16[192,1024]{1,0:T(8,128)(2,1)S(1)}, u32[]{:S(2)}, u32[]{:S(2)}) collective-permute-start(bf16[192,1024]{1,0:T(8,128)(2,1)S(1)} %add_convert_fusion.10), channel_id=1, source_target_pairs={{0,1},{1,0},{2,3},{3,2},{4,5},{5,4},{6,7},{7,6},{8,9},{9,8},{10,11... | collective-permute-start | bytes 1179656 | tf_op jit(solution)/shard_map/ppermute | solution.py:131
  408.2 5.8 %collective-permute-start.62 = (bf16[1,1,1,1,64,512]{5,4,3,2,1,0:T(8,128)(2,1)S(1)}, bf16[1,1,1,1,64,512]{5,4,3,2,1,0:T(8,128)(2,1)S(1)}, u32[]{:S(2)}, u32[]{:S(2)}) collective-permute-start(bf16[1,1,1,1,64,512]{5,4,3,2,1,0:T(8,128)(2,1)S(1)} %dynamic-slice_convert_fusion.12), channel_id=1, source_target_pairs={{0,64},{16,80},{32,96},{48,112},{64,0},{80,16},{96,32},{112,48},{1... | collective-permute-start | bytes 196616 | tf_op jit(solution)/shard_map/ppermute | solution.py:194
  413.7 1.8 collective-permute-start.38
  415.6 11.2 %collective-permute-start.39 = (bf16[192,1024]{1,0:T(8,128)(2,1)S(1)}, bf16[192,1024]{1,0:T(8,128)(2,1)S(1)}, u32[]{:S(2)}, u32[]{:S(2)}) collective-permute-start(bf16[192,1024]{1,0:T(8,128)(2,1)S(1)} %add_convert_fusion.9), channel_id=1, source_target_pairs={{0,2},{1,3},{2,0},{3,1},{4,6},{5,7},{6,4},{7,5},{8,10},{9,11},{10,... | collective-permute-start | bytes 1179656 | tf_op jit(solution)/shard_map/ppermute | solution.py:127
  427.0 12.0 %collective-permute-start.40 = (bf16[192,1024]{1,0:T(8,128)(2,1)S(1)}, bf16[192,1024]{1,0:T(8,128)(2,1)S(1)}, u32[]{:S(2)}, u32[]{:S(2)}) collective-permute-start(bf16[192,1024]{1,0:T(8,128)(2,1)S(1)} %add_convert_fusion.8), channel_id=1, source_target_pairs={{0,4},{1,5},{2,6},{3,7},{4,0},{5,1},{6,2},{7,3},{8,12},{9,13},{10,... | collective-permute-start | bytes 1179656 | tf_op jit(solution)/shard_map/ppermute | solution.py:127
  455.8 15.3 %collective-permute-start.42 = (bf16[384,128]{1,0:T(8,128)(2,1)}, bf16[384,128]{1,0:T(8,128)(2,1)}, u32[]{:S(2)}, u32[]{:S(2)}) collective-permute-start(bf16[384,128]{1,0:T(8,128)(2,1)} %fusion.134), channel_id=1, source_target_pairs={{0,8},{8,0},{1,9},{9,1},{2,10},{10,2},{3,11},{11,3},{4,12},{12,4},... | collective-permute-start | bytes 294920 | tf_op jit(solution)/shard_map/ppermute | solution.py:141
  467.6 10.0 %collective-permute-start.43 = (bf16[384,128]{0,1:T(8,128)(2,1)}, bf16[384,128]{0,1:T(8,128)(2,1)}, u32[]{:S(2)}, u32[]{:S(2)}) collective-permute-start(bf16[384,128]{0,1:T(8,128)(2,1)} %fusion.136), channel_id=1, source_target_pairs={{0,8},{8,0},{1,9},{9,1},{2,10},{10,2},{3,11},{11,3},{4,12},{12,4},... | collective-permute-start | bytes 294920 | tf_op jit(solution)/shard_map/ppermute | solution.py:141
  483.3 22.1 %collective-permute-start.55 = (bf16[2,2,1,2,64,512]{5,4,3,2,1,0:T(8,128)(2,1)S(1)}, bf16[2,2,1,2,64,512]{5,4,3,2,1,0:T(8,128)(2,1)S(1)}, u32[]{:S(2)}, u32[]{:S(2)}) collective-permute-start(bf16[2,2,1,2,64,512]{5,4,3,2,1,0:T(8,128)(2,1)S(1)} %constant_dynamic-slice_fusion.1), channel_id=1, source_target_pairs={{0,16},{16,0},{32,48},{48,32},{64,80},{80,64},{96,112},{112,96},{1... | collective-permute-start | bytes 1572872 | tf_op jit(solution)/shard_map/ppermute | solution.py:194
  486.1 20.7 %collective-permute-start.44 = (bf16[192,1024]{1,0:T(8,128)(2,1)S(1)}, bf16[192,1024]{1,0:T(8,128)(2,1)S(1)}, u32[]{:S(2)}, u32[]{:S(2)}) collective-permute-start(bf16[192,1024]{1,0:T(8,128)(2,1)S(1)} %constant_dynamic-slice_fusion.2), channel_id=1, source_target_pairs={{0,1},{1,0},{2,3},{3,2},{4,5},{5,4},{6,7},{7,6},{8,9},{9,8},{10,11... | collective-permute-start | bytes 1179656 | tf_op jit(solution)/shard_map/ppermute | solution.py:121
  505.6 11.4 %collective-permute-start.56 = (bf16[2,1,1,2,64,512]{5,4,3,2,1,0:T(8,128)(2,1)S(1)}, bf16[2,1,1,2,64,512]{5,4,3,2,1,0:T(8,128)(2,1)S(1)}, u32[]{:S(2)}, u32[]{:S(2)}) collective-permute-start(bf16[2,1,1,2,64,512]{5,4,3,2,1,0:T(8,128)(2,1)S(1)} %dynamic-slice_convert_fusion.1), channel_id=1, source_target_pairs={{0,32},{16,48},{32,0},{48,16},{64,96},{80,112},{96,64},{112,80},{1... | collective-permute-start | bytes 786440 | tf_op jit(solution)/shard_map/ppermute | solution.py:194
  506.9 10.3 %collective-permute-start.45 = (bf16[192,1024]{1,0:T(8,128)(2,1)S(1)}, bf16[192,1024]{1,0:T(8,128)(2,1)S(1)}, u32[]{:S(2)}, u32[]{:S(2)}) collective-permute-start(bf16[192,1024]{1,0:T(8,128)(2,1)S(1)} %add_convert_fusion.6), channel_id=1, source_target_pairs={{0,2},{1,3},{2,0},{3,1},{4,6},{5,7},{6,4},{7,5},{8,10},{9,11},{10,... | collective-permute-start | bytes 1179656 | tf_op jit(solution)/shard_map/ppermute | solution.py:127
  517.1 9.9 %collective-permute-start.57 = (bf16[2,1,1,1,64,512]{5,4,3,2,1,0:T(8,128)(2,1)S(1)}, bf16[2,1,1,1,64,512]{5,4,3,2,1,0:T(8,128)(2,1)S(1)}, u32[]{:S(2)}, u32[]{:S(2)}) collective-permute-start(bf16[2,1,1,1,64,512]{5,4,3,2,1,0:T(8,128)(2,1)S(1)} %dynamic-slice_convert_fusion.3), channel_id=1, source_target_pairs={{0,8},{8,0},{1,9},{9,1},{2,10},{10,2},{3,11},{11,3},{4,12},{12,4},... | collective-permute-start | bytes 393224 | tf_op jit(solution)/shard_map/ppermute | solution.py:194
  517.4 11.8 %collective-permute-start.46 = (bf16[192,1024]{1,0:T(8,128)(2,1)S(1)}, bf16[192,1024]{1,0:T(8,128)(2,1)S(1)}, u32[]{:S(2)}, u32[]{:S(2)}) collective-permute-start(bf16[192,1024]{1,0:T(8,128)(2,1)S(1)} %add_convert_fusion.5), channel_id=1, source_target_pairs={{0,4},{1,5},{2,6},{3,7},{4,0},{5,1},{6,2},{7,3},{8,12},{9,13},{10,... | collective-permute-start | bytes 1179656 | tf_op jit(solution)/shard_map/ppermute | solution.py:127
  527.1 5.8 %collective-permute-start.58 = (bf16[1,1,1,1,64,512]{5,4,3,2,1,0:T(8,128)(2,1)S(1)}, bf16[1,1,1,1,64,512]{5,4,3,2,1,0:T(8,128)(2,1)S(1)}, u32[]{:S(2)}, u32[]{:S(2)}) collective-permute-start(bf16[1,1,1,1,64,512]{5,4,3,2,1,0:T(8,128)(2,1)S(1)} %dynamic-slice_convert_fusion.13), channel_id=1, source_target_pairs={{0,64},{16,80},{32,96},{48,112},{64,0},{80,16},{96,32},{112,48},{1... | collective-permute-start | bytes 196616 | tf_op jit(solution)/shard_map/ppermute | solution.py:194
  529.3 3.7 collective-permute-start.47
  534.7 3.8 collective-permute-start.49
  538.6 5.3 collective-permute-start.50
  544.0 5.5 collective-permute-start.51
  549.5 3.8 collective-permute-start.52
  553.3 3.8 collective-permute-start.53
  557.2 5.3 collective-permute-start.54
  (119 other events, 748.8 us)
Sparse Core Ops, SparseCore 0:
  18.2 85.6 all-gather.2
  147.7 84.2 all-gather.4
  343.7 86.6 reduce-scatter.8
  471.2 87.2 reduce-scatter.6

commit v10 on v7

--- a/solution.py
+++ b/solution.py
@@ -257,6 +257,27 @@
             pieces.append(owned[:, start : start + term.shape[1]].astype(jnp.float32))
             start += term.shape[1]
         return pieces
+
+    def scatter_chain(layer_terms):
+        results = [None] * len(layer_terms)
+        pending = []
+        for layer_index in reversed(range(len(layer_terms))):
+            terms = layer_terms[layer_index]
+            owned = scatter_terms(pending + list(terms[3:]))
+            if pending:
+                results[layer_index + 1] = tuple(owned[:3]) + results[layer_index + 1]
+            results[layer_index] = tuple(owned[len(pending) :])
+            pending = list(terms[:3])
+        joined = shard_scatter(
+            jnp.concatenate([term.astype(jnp.bfloat16) for term in pending], axis=1)
+        )
+        late = []
+        start = 0
+        for term in pending:
+            late.append(joined[:, start : start + term.shape[1]])
+            start += term.shape[1]
+        results[0] = tuple(late) + results[0]
+        return results
 
     def scatter_layer(terms, layer_index):
         if layer_index > 0:
@@ -480,8 +501,9 @@
         gain_terms = (attention_gain_grad, query_gain_grad, key_gain_grad, feed_gain_grad)
         grad_flow, weight_terms, gain_terms = (source_grad, weight_terms, gain_terms)
         grad_query, grad_key, grad_value, grad_output, grad_gate, grad_up, grad_down = weight_terms
-        weight_sums[layer_index] = scatter_layer(weight_terms, layer_index)
+        weight_sums[layer_index] = weight_terms
         gain_parts[layer_index] = gain_terms
+    weight_sums = scatter_chain(weight_sums)
     gain_stacks = [
         jnp.stack([member[which] for member in gain_parts]) for which in range(4)
     ]

time: 573 us -> 579 us (1.010)
    unnamed x5, waiting for transfers between devices: 47.9 us -> 0.07 us
    reduce_scatter x1, waiting for transfers between devices: 0.01 us -> 38.8 us  [scatter_terms(): lax.psum_scatter(joined, ('fsdp', 'ctx'), scatter_dimension=0, tiled=True)]
    ppermute x16, waiting for transfers between devices: 107 us -> 120 us  [tp_sum(): received = lax.ppermute(mine, 'tp', pairs)]
    ppermute x8, waiting for transfers between devices: 13.3 us -> 6.62 us  [swap_halves(): return lax.ppermute(local, axis_name, [(0, 1), (1, 0)])]
    unnamed x342 -> x352, local copies, waits for them, and re-layouts: 31.8 us -> 33.5 us
  transfers between devices with their start and end apart: 59 -> 59, of which waited for: 38 -> 39; matrix products, arithmetic and copies ran while one was open for 24% -> 22% of each run, Pallas kernels for 0% -> 0%
where the time goes in v10:
time: 579 us; the launch traced here: 569 us
  waiting for transfers between devices  306 us (53%)
  starting transfers between devices  69.3 us (12%)
  matrix products  60.6 us (10%)
  local copies, waits for them, and re-layouts  59.2 us (10%)
  other arithmetic  57.3 us (10%)
  between operations  17 us (3%)
    ppermute x16, waiting for transfers between devices, tp_sum(): received = lax.ppermute(mine, 'tp', pairs)  120 us
    reduce_scatter x1, waiting for transfers between devices, scatter_terms(): lax.psum_scatter(joined, ('fsdp', 'ctx'), scatter_dimension=0, tiled=True)  38.8 us
    unnamed x352, local copies, waits for them, and re-layouts  33.5 us
    all_gather x1, waiting for transfers between devices, gather_layer(): full = lax.all_gather(joined, ('fsdp', 'ctx'), axis=0, tiled=True)  31.8 us
    ppermute x4, waiting for transfers between devices, shard_scatter(): received = lax.ppermute(sent.astype(jnp.bfloat16), axis_name, pairs)  31.7 us
    ppermute x16, starting transfers between devices, tp_sum(): received = lax.ppermute(mine, 'tp', pairs)  31.2 us
    ppermute x4, waiting for transfers between devices, shard_gather(): received = lax.ppermute(current, axis_name, pairs)  29.4 us
    all_gather x1, waiting for transfers between devices, gather_layer(): late_full = lax.all_gather(late, ('fsdp', 'ctx'), axis=0, tiled=True)  18.6 us
  transfers between devices with their start and end apart: 59, of which 39 were waited for; matrix products, arithmetic and copies ran while one was open for 22% of the time, Pallas kernels for 0%

profile of v10, /device:TPU:0, one launch (start us, length us, event | category | flops | bytes accessed | tf_op | source)
XLA Modules:
  0.0 568.9 jit_solution(15097377289067339873)
XLA Ops:
  12.1 4.0 collective-permute-start
  23.6 3.1 collective-permute-start.1
  26.8 3.4 collective-permute-done.1
  31.9 8.9 %collective-permute-done.2 = bf16[2,1,1,2,64,512]{5,4,3,2,1,0:T(8,128)(2,1)S(1)} collective-permute-done((bf16[2,1,1,2,64,512]{5,4,3,2,1,0:T(8,128)(2,1)S(1)}, bf16[2,1,1,2,64,512]{5,4,3,2,1,0:T(8,128)(2,1)S(1)}, u32[]{:S(2)}, u32[]{:S(2)}) %collective-permute-start.2) | collective-permute-done | bytes 262176 | tf_op jit(solution)/shard_map/ppermute | solution.py:157
  40.9 1.9 collective-permute-start.3
  44.7 17.1 %collective-permute-done.3 = bf16[2,1,2,2,64,512]{5,4,3,2,1,0:T(8,128)(2,1)S(1)} collective-permute-done((bf16[2,1,2,2,64,512]{5,4,3,2,1,0:T(8,128)(2,1)S(1)}, bf16[2,1,2,2,64,512]{5,4,3,2,1,0:T(8,128)(2,1)S(1)}, u32[]{:S(2)}, u32[]{:S(2)}) %collective-permute-start.3) | collective-permute-done | bytes 524320 | tf_op jit(solution)/shard_map/ppermute | solution.py:157
  67.3 3.6 collective-permute-start.5
  72.0 4.6 collective-permute-done.5
  80.7 18.6 %all-gather.3.cloned.1.call-done = bf16[1024,1408]{1,0:T(8,128)(2,1)} async-done(((bf16[64,1408]{1,0:T(8,128)(2,1)}), bf16[1024,1408]{1,0:T(8,128)(2,1)}) %all-gather.3.cloned.1.call-update) | async-done | bytes 2883600 | tf_op jit(solution)/shard_map/all_gather | solution.py:242
  101.6 1.9 collective-permute-done.6
  103.6 1.9 collective-permute-start.7
  105.5 9.4 %collective-permute-done.7 = bf16[192,1024]{1,0:T(8,128)(2,1)S(1)} collective-permute-done((bf16[192,1024]{1,0:T(8,128)(2,1)S(1)}, bf16[192,1024]{1,0:T(8,128)(2,1)S(1)}, u32[]{:S(2)}, u32[]{:S(2)}) %collective-permute-start.7) | collective-permute-done | bytes 393248 | tf_op jit(solution)/shard_map/ppermute | solution.py:68
  115.1 4.2 collective-permute-start.8
  119.3 8.7 %collective-permute-done.8 = bf16[192,1024]{1,0:T(8,128)(2,1)S(1)} collective-permute-done((bf16[192,1024]{1,0:T(8,128)(2,1)S(1)}, bf16[192,1024]{1,0:T(8,128)(2,1)S(1)}, u32[]{:S(2)}, u32[]{:S(2)}) %collective-permute-start.8) | collective-permute-done | bytes 393248 | tf_op jit(solution)/shard_map/ppermute | solution.py:68
  138.5 10.3 %collective-permute-done.11 = bf16[192,1024]{1,0:T(8,128)(2,1)S(1)} collective-permute-done((bf16[192,1024]{1,0:T(8,128)(2,1)S(1)}, bf16[192,1024]{1,0:T(8,128)(2,1)S(1)}, u32[]{:S(2)}, u32[]{:S(2)}) %collective-permute-start.11) | collective-permute-done | bytes 393248 | tf_op jit(solution)/shard_map/ppermute | solution.py:68
  149.0 3.3 collective-permute-start.12
  152.3 8.7 %collective-permute-done.12 = bf16[192,1024]{1,0:T(8,128)(2,1)S(1)} collective-permute-done((bf16[192,1024]{1,0:T(8,128)(2,1)S(1)}, bf16[192,1024]{1,0:T(8,128)(2,1)S(1)}, u32[]{:S(2)}, u32[]{:S(2)}) %collective-permute-start.12) | collective-permute-done | bytes 393248 | tf_op jit(solution)/shard_map/ppermute | solution.py:68
  165.1 31.8 %all-gather.5.cloned.1.call-done = bf16[1024,1920]{1,0:T(8,128)(2,1)} async-done(((bf16[64,1920]{1,0:T(8,128)(2,1)}), bf16[1024,1920]{1,0:T(8,128)(2,1)}) %all-gather.5.cloned.1.call-update) | async-done | bytes 3932176 | tf_op jit(solution)/shard_map/all_gather | solution.py:237
  196.9 2.0 convolution_convert_fusion.22
  205.7 3.1 collective-permute-start.15
  209.9 2.0 collective-permute-done.15
  212.9 2.4 convolution_convert_fusion.20
  220.0 9.7 %collective-permute-done.17 = bf16[192,1024]{1,0:T(8,128)(2,1)S(1)} collective-permute-done((bf16[192,1024]{1,0:T(8,128)(2,1)S(1)}, bf16[192,1024]{1,0:T(8,128)(2,1)S(1)}, u32[]{:S(2)}, u32[]{:S(2)}) %collective-permute-start.17) | collective-permute-done | bytes 393248 | tf_op jit(solution)/shard_map/ppermute | solution.py:68
  229.8 3.1 collective-permute-start.18
  232.9 8.8 %collective-permute-done.18 = bf16[192,1024]{1,0:T(8,128)(2,1)S(1)} collective-permute-done((bf16[192,1024]{1,0:T(8,128)(2,1)S(1)}, bf16[192,1024]{1,0:T(8,128)(2,1)S(1)}, u32[]{:S(2)}, u32[]{:S(2)}) %collective-permute-start.18) | collective-permute-done | bytes 393248 | tf_op jit(solution)/shard_map/ppermute | solution.py:68
  252.1 9.7 %collective-permute-done.25 = bf16[192,1024]{1,0:T(8,128)(2,1)S(1)} collective-permute-done((bf16[192,1024]{1,0:T(8,128)(2,1)S(1)}, bf16[192,1024]{1,0:T(8,128)(2,1)S(1)}, u32[]{:S(2)}, u32[]{:S(2)}) %collective-permute-start.25) | collective-permute-done | bytes 393248 | tf_op jit(solution)/shard_map/ppermute | solution.py:68
  262.7 3.0 collective-permute-start.26
  267.0 7.9 %collective-permute-done.26 = bf16[192,1024]{1,0:T(8,128)(2,1)} collective-permute-done((bf16[192,1024]{1,0:T(8,128)(2,1)}, bf16[192,1024]{1,0:T(8,128)(2,1)}, u32[]{:S(2)}, u32[]{:S(2)}) %collective-permute-start.26) | collective-permute-done | bytes 393248 | tf_op jit(solution)/shard_map/ppermute | solution.py:68
  277.4 2.7 convolution_convert_fusion.8
  281.7 2.0 multiply_add_fusion.3
  286.7 1.9 fusion.4
  292.9 1.9 copy.158
  295.8 3.0 collective-permute-start.28
  300.5 1.8 fusion.73
  313.8 9.1 %collective-permute-done.31 = bf16[192,1024]{1,0:T(8,128)(2,1)S(1)} collective-permute-done((bf16[192,1024]{1,0:T(8,128)(2,1)S(1)}, bf16[192,1024]{1,0:T(8,128)(2,1)S(1)}, u32[]{:S(2)}, u32[]{:S(2)}) %collective-permute-start.31) | collective-permute-done | bytes 393248 | tf_op jit(solution)/shard_map/ppermute | solution.py:68
  323.0 3.1 collective-permute-start.32
  326.1 5.2 collective-permute-done.21
  331.4 3.1 collective-permute-start.22
  335.2 6.7 %collective-permute-done.32 = bf16[192,1024]{1,0:T(8,128)(2,1)S(1)} collective-permute-done((bf16[192,1024]{1,0:T(8,128)(2,1)S(1)}, bf16[192,1024]{1,0:T(8,128)(2,1)S(1)}, u32[]{:S(2)}, u32[]{:S(2)}) %collective-permute-start.32) | collective-permute-done | bytes 393248 | tf_op jit(solution)/shard_map/ppermute | solution.py:68
  342.1 7.1 %collective-permute-done.22 = bf16[192,1024]{1,0:T(8,128)(2,1)S(1)} collective-permute-done((bf16[192,1024]{1,0:T(8,128)(2,1)S(1)}, bf16[192,1024]{1,0:T(8,128)(2,1)S(1)}, u32[]{:S(2)}, u32[]{:S(2)}) %collective-permute-start.22) | collective-permute-done | bytes 393248 | tf_op jit(solution)/shard_map/ppermute | solution.py:68
  351.7 1.9 copy-done.62
  360.0 4.6 copy.214
  369.7 9.5 %collective-permute-done.35 = bf16[192,1024]{1,0:T(8,128)(2,1)S(1)} collective-permute-done((bf16[192,1024]{1,0:T(8,128)(2,1)S(1)}, bf16[192,1024]{1,0:T(8,128)(2,1)S(1)}, u32[]{:S(2)}, u32[]{:S(2)}) %collective-permute-start.35) | collective-permute-done | bytes 393248 | tf_op jit(solution)/shard_map/ppermute | solution.py:68
  381.0 3.1 convert_add_fusion
  384.1 7.3 %collective-permute-done.36 = bf16[192,1024]{1,0:T(8,128)(2,1)S(1)} collective-permute-done((bf16[192,1024]{1,0:T(8,128)(2,1)S(1)}, bf16[192,1024]{1,0:T(8,128)(2,1)S(1)}, u32[]{:S(2)}, u32[]{:S(2)}) %collective-permute-start.36) | collective-permute-done | bytes 393248 | tf_op jit(solution)/shard_map/ppermute | solution.py:68
  396.6 1.8 fusion
  402.3 1.9 copy.169
  407.2 2.4 collective-permute-start.38
  409.7 2.4 convolution_bitcast_fusion.3
  423.3 6.3 %copy.212 = bf16[1024,1920]{1,0:T(8,128)(2,1)} copy(bf16[1024,1920]{0,1:T(8,128)(2,1)} %fusion.16) | data formatting | bytes 7864320
  437.6 2.4 copy.175
  444.2 11.4 %collective-permute-done.51 = bf16[2,2,1,2,64,512]{5,4,3,2,1,0:T(8,128)(2,1)S(1)} collective-permute-done((bf16[2,2,1,2,64,512]{5,4,3,2,1,0:T(8,128)(2,1)S(1)}, bf16[2,2,1,2,64,512]{5,4,3,2,1,0:T(8,128)(2,1)S(1)}, u32[]{:S(2)}, u32[]{:S(2)}) %collective-permute-start.51) | collective-permute-done | bytes 524320 | tf_op jit(solution)/shard_map/ppermute | solution.py:135
  458.8 6.9 %collective-permute-done.52 = bf16[2,1,1,2,64,512]{5,4,3,2,1,0:T(8,128)(2,1)S(1)} collective-permute-done((bf16[2,1,1,2,64,512]{5,4,3,2,1,0:T(8,128)(2,1)S(1)}, bf16[2,1,1,2,64,512]{5,4,3,2,1,0:T(8,128)(2,1)S(1)}, u32[]{:S(2)}, u32[]{:S(2)}) %collective-permute-start.52) | collective-permute-done | bytes 262176 | tf_op jit(solution)/shard_map/ppermute | solution.py:135
  466.7 1.8 collective-permute-done.42
  468.8 10.1 %collective-permute-done.53 = bf16[2,1,1,1,64,512]{5,4,3,2,1,0:T(8,128)(2,1)S(1)} collective-permute-done((bf16[2,1,1,1,64,512]{5,4,3,2,1,0:T(8,128)(2,1)S(1)}, bf16[2,1,1,1,64,512]{5,4,3,2,1,0:T(8,128)(2,1)S(1)}, u32[]{:S(2)}, u32[]{:S(2)}) %collective-permute-start.53) | collective-permute-done | bytes 131104 | tf_op jit(solution)/shard_map/ppermute | solution.py:135
  482.2 3.3 collective-permute-done.54
  487.0 3.9 collective-permute-done.46
  491.1 6.0 %collective-permute-done.47 = f32[2,2304]{1,0:T(2,128)S(1)} collective-permute-done((f32[2,2304]{1,0:T(2,128)S(1)}, f32[2,2304]{1,0:T(2,128)S(1)}, u32[]{:S(2)}, u32[]{:S(2)}) %collective-permute-start.47) | collective-permute-done | bytes 18464 | tf_op jit(solution)/shard_map/ppermute | solution.py:109
  497.5 3.7 collective-permute-done.48
  501.3 2.7 collective-permute-start.49
  503.9 2.3 collective-permute-done.49
  506.2 1.9 collective-permute-start.50
  509.7 1.9 collective-permute-done.50
  514.9 38.8 %reduce-scatter.7.cloned.1.call-done = bf16[64,1920]{1,0:T(8,128)(2,1)} async-done(((bf16[1024,1920]{1,0:T(8,128)(2,1)}), bf16[64,1920]{1,0:T(8,128)(2,1)}) %reduce-scatter.7.cloned.1.call-update) | async-done | bytes 245776 | tf_op jit(solution)/shard_map/reduce_scatter | solution.py:253
  (647 shorter events, 168.7 us)
Async XLA Ops:
  7.2 92.1 %all-gather.3.cloned.1.call-start = ((), (), s32[]{:S(2)}) async-start(), calls=%async_computation.2 | async-start | bytes 3063808 | tf_op jit(solution)/shard_map/all_gather | solution.py:242
  10.5 186.4 %all-gather.5.cloned.1.call-start = ((), (), s32[]{:S(2)}) async-start(), calls=%async_computation.3 | async-start | bytes 4177920 | tf_op jit(solution)/shard_map/all_gather | solution.py:237
  12.1 11.5 %collective-permute-start = (bf16[1,1,1,1,64,512]{5,4,3,2,1,0:T(8,128)(2,1)S(1)}, bf16[1,1,1,1,64,512]{5,4,3,2,1,0:T(8,128)(2,1)S(1)}, u32[]{:S(2)}, u32[]{:S(2)}) collective-permute-start(bf16[1,1,1,1,64,512]{5,4,3,2,1,0:T(8,128)(2,1)S(1)} %get-tuple-element.123), channel_id=1, source_target_pairs={{0,8},{8,0},{1,9},{9,1},{2,10},{10,2},{3,11},{11,3},{4,12},{12,4},... | collective-permute-start | bytes 196616 | tf_op jit(solution)/shard_map/ppermute | solution.py:157
  21.5 491.3 %reduce-scatter.9.cloned.1.call-start = ((), (), s32[]{:S(2)}) async-start(), calls=%async_computation.5 | async-start | bytes 3063808
  23.1 48.6 %copy-start.34 = (f32[384,64]{1,0:T(8,128)}, f32[384,64]{1,0:T(8,128)S(1)}, u32[]{:S(2)}) copy-start(f32[384,64]{1,0:T(8,128)S(1)} %get-tuple-element.134) | copy-start | bytes 294916
  23.1 48.6 %copy-start.64 = (f32[384,64]{1,0:T(8,128)}, f32[384,64]{1,0:T(8,128)S(1)}, u32[]{:S(2)}) copy-start(f32[384,64]{1,0:T(8,128)S(1)} %get-tuple-element.133) | copy-start | bytes 294916
  23.6 6.6 %collective-permute-start.1 = (bf16[1,1,1,2,64,512]{5,4,3,2,1,0:T(8,128)(2,1)S(1)}, bf16[1,1,1,2,64,512]{5,4,3,2,1,0:T(8,128)(2,1)S(1)}, u32[]{:S(2)}, u32[]{:S(2)}) collective-permute-start(bf16[1,1,1,2,64,512]{5,4,3,2,1,0:T(8,128)(2,1)S(1)} %maximum_select_fusion.17), channel_id=1, source_target_pairs={{0,64},{16,80},{32,96},{48,112},{64,0},{80,16},{96,32},{112,48},{1... | collective-permute-start | bytes 393224 | tf_op jit(solution)/shard_map/ppermute | solution.py:157
  30.2 10.6 %collective-permute-start.2 = (bf16[2,1,1,2,64,512]{5,4,3,2,1,0:T(8,128)(2,1)S(1)}, bf16[2,1,1,2,64,512]{5,4,3,2,1,0:T(8,128)(2,1)S(1)}, u32[]{:S(2)}, u32[]{:S(2)}) collective-permute-start(bf16[2,1,1,2,64,512]{5,4,3,2,1,0:T(8,128)(2,1)S(1)} %maximum_select_fusion.11), channel_id=1, source_target_pairs={{0,16},{16,0},{32,48},{48,32},{64,80},{80,64},{96,112},{112,96},{1... | collective-permute-start | bytes 786440 | tf_op jit(solution)/shard_map/ppermute | solution.py:157
  40.9 20.9 %collective-permute-start.3 = (bf16[2,1,2,2,64,512]{5,4,3,2,1,0:T(8,128)(2,1)S(1)}, bf16[2,1,2,2,64,512]{5,4,3,2,1,0:T(8,128)(2,1)S(1)}, u32[]{:S(2)}, u32[]{:S(2)}) collective-permute-start(bf16[2,1,2,2,64,512]{5,4,3,2,1,0:T(8,128)(2,1)S(1)} %maximum_select_fusion.9), channel_id=1, source_target_pairs={{0,32},{16,48},{32,0},{48,16},{64,96},{80,112},{96,64},{112,80},{1... | collective-permute-start | bytes 1572872 | tf_op jit(solution)/shard_map/ppermute | solution.py:157
  63.8 13.7 %collective-permute-start.4 = (bf16[384,128]{1,0:T(8,128)(2,1)S(1)}, bf16[384,128]{1,0:T(8,128)(2,1)}, u32[]{:S(2)}, u32[]{:S(2)}) collective-permute-start(bf16[384,128]{1,0:T(8,128)(2,1)S(1)} %convolution_convert_fusion.23), channel_id=1, source_target_pairs={{0,8},{8,0},{1,9},{9,1},{2,10},{10,2},{3,11},{11,3},{4,12},{12,4},... | collective-permute-start | bytes 294920 | tf_op jit(solution)/shard_map/ppermute | solution.py:82
  67.3 9.3 %collective-permute-start.5 = (bf16[384,128]{1,0:T(8,128)(2,1)S(1)}, bf16[384,128]{1,0:T(8,128)(2,1)S(1)}, u32[]{:S(2)}, u32[]{:S(2)}) collective-permute-start(bf16[384,128]{1,0:T(8,128)(2,1)S(1)} %pad_maximum_fusion.10), channel_id=1, source_target_pairs={{0,8},{8,0},{1,9},{9,1},{2,10},{10,2},{3,11},{11,3},{4,12},{12,4},... | collective-permute-start | bytes 294920 | tf_op jit(solution)/shard_map/ppermute | solution.py:82
  101.5 1.9 collective-permute-start.6
  103.6 11.3 %collective-permute-start.7 = (bf16[192,1024]{1,0:T(8,128)(2,1)S(1)}, bf16[192,1024]{1,0:T(8,128)(2,1)S(1)}, u32[]{:S(2)}, u32[]{:S(2)}) collective-permute-start(bf16[192,1024]{1,0:T(8,128)(2,1)S(1)} %add_convert_fusion.27), channel_id=1, source_target_pairs={{0,2},{1,3},{2,0},{3,1},{4,6},{5,7},{6,4},{7,5},{8,10},{9,11},{10,... | collective-permute-start | bytes 1179656 | tf_op jit(solution)/shard_map/ppermute | solution.py:68
  115.1 12.9 %collective-permute-start.8 = (bf16[192,1024]{1,0:T(8,128)(2,1)S(1)}, bf16[192,1024]{1,0:T(8,128)(2,1)S(1)}, u32[]{:S(2)}, u32[]{:S(2)}) collective-permute-start(bf16[192,1024]{1,0:T(8,128)(2,1)S(1)} %add_convert_fusion.26), channel_id=1, source_target_pairs={{0,4},{1,5},{2,6},{3,7},{4,0},{5,1},{6,2},{7,3},{8,12},{9,13},{10,... | collective-permute-start | bytes 1179656 | tf_op jit(solution)/shard_map/ppermute | solution.py:68
  128.2 2.0 collective-permute-start.9
  135.6 27.3 %copy-start.29 = (bf16[192,1024]{1,0:T(8,128)(2,1)S(1)}, bf16[192,1024]{1,0:T(8,128)(2,1)}, u32[]{:S(2)}) copy-start(bf16[192,1024]{1,0:T(8,128)(2,1)} %copy-done.28) | copy-start | bytes 1179652
  135.7 1.8 collective-permute-start.10
  137.6 11.2 %collective-permute-start.11 = (bf16[192,1024]{1,0:T(8,128)(2,1)S(1)}, bf16[192,1024]{1,0:T(8,128)(2,1)S(1)}, u32[]{:S(2)}, u32[]{:S(2)}) collective-permute-start(bf16[192,1024]{1,0:T(8,128)(2,1)S(1)} %add_convert_fusion.24), channel_id=1, source_target_pairs={{0,2},{1,3},{2,0},{3,1},{4,6},{5,7},{6,4},{7,5},{8,10},{9,11},{10,... | collective-permute-start | bytes 1179656 | tf_op jit(solution)/shard_map/ppermute | solution.py:68
  149.0 12.0 %collective-permute-start.12 = (bf16[192,1024]{1,0:T(8,128)(2,1)S(1)}, bf16[192,1024]{1,0:T(8,128)(2,1)S(1)}, u32[]{:S(2)}, u32[]{:S(2)}) collective-permute-start(bf16[192,1024]{1,0:T(8,128)(2,1)S(1)} %add_convert_fusion.23), channel_id=1, source_target_pairs={{0,4},{1,5},{2,6},{3,7},{4,0},{5,1},{6,2},{7,3},{8,12},{9,13},{10,... | collective-permute-start | bytes 1179656 | tf_op jit(solution)/shard_map/ppermute | solution.py:68
  161.2 1.8 collective-permute-start.13
  165.1 37.4 %copy-start.13 = (bf16[384,1024]{1,0:T(8,128)(2,1)}, bf16[384,1024]{1,0:T(8,128)(2,1)S(1)}, u32[]{:S(2)}) copy-start(bf16[384,1024]{1,0:T(8,128)(2,1)S(1)} %get-tuple-element.75) | copy-start | bytes 2359300
  198.9 14.0 %collective-permute-start.14 = (bf16[384,128]{1,0:T(8,128)(2,1)}, bf16[384,128]{1,0:T(8,128)(2,1)}, u32[]{:S(2)}, u32[]{:S(2)}) collective-permute-start(bf16[384,128]{1,0:T(8,128)(2,1)} %convolution_convert_fusion.22), channel_id=1, source_target_pairs={{0,8},{8,0},{1,9},{9,1},{2,10},{10,2},{3,11},{11,3},{4,12},{12,4},... | collective-permute-start | bytes 294920 | tf_op jit(solution)/shard_map/ppermute | solution.py:82
  205.7 6.2 %collective-permute-start.15 = (bf16[384,128]{1,0:T(8,128)(2,1)S(1)}, bf16[384,128]{1,0:T(8,128)(2,1)S(1)}, u32[]{:S(2)}, u32[]{:S(2)}) collective-permute-start(bf16[384,128]{1,0:T(8,128)(2,1)S(1)} %pad_maximum_fusion.11), channel_id=1, source_target_pairs={{0,8},{8,0},{1,9},{9,1},{2,10},{10,2},{3,11},{11,3},{4,12},{12,4},... | collective-permute-start | bytes 294920 | tf_op jit(solution)/shard_map/ppermute | solution.py:82
  216.5 1.8 collective-permute-start.16
  218.5 11.2 %collective-permute-start.17 = (bf16[192,1024]{1,0:T(8,128)(2,1)S(1)}, bf16[192,1024]{1,0:T(8,128)(2,1)S(1)}, u32[]{:S(2)}, u32[]{:S(2)}) collective-permute-start(bf16[192,1024]{1,0:T(8,128)(2,1)S(1)} %add_convert_fusion.21), channel_id=1, source_target_pairs={{0,2},{1,3},{2,0},{3,1},{4,6},{5,7},{6,4},{7,5},{8,10},{9,11},{10,... | collective-permute-start | bytes 1179656 | tf_op jit(solution)/shard_map/ppermute | solution.py:68
  229.8 11.9 %collective-permute-start.18 = (bf16[192,1024]{1,0:T(8,128)(2,1)S(1)}, bf16[192,1024]{1,0:T(8,128)(2,1)S(1)}, u32[]{:S(2)}, u32[]{:S(2)}) collective-permute-start(bf16[192,1024]{1,0:T(8,128)(2,1)S(1)} %add_convert_fusion.20), channel_id=1, source_target_pairs={{0,4},{1,5},{2,6},{3,7},{4,0},{5,1},{6,2},{7,3},{8,12},{9,13},{10,... | collective-permute-start | bytes 1179656 | tf_op jit(solution)/shard_map/ppermute | solution.py:68
  241.9 2.2 collective-permute-start.19
  245.1 35.0 %copy-start.6 = (f32[384,1024]{1,0:T(8,128)}, f32[384,1024]{1,0:T(8,128)S(1)}, u32[]{:S(2)}) copy-start(f32[384,1024]{1,0:T(8,128)S(1)} %get-tuple-element.74) | copy-start | bytes 4718596
  248.6 1.8 collective-permute-start.24
  250.5 11.2 %collective-permute-start.25 = (bf16[192,1024]{1,0:T(8,128)(2,1)S(1)}, bf16[192,1024]{1,0:T(8,128)(2,1)S(1)}, u32[]{:S(2)}, u32[]{:S(2)}) collective-permute-start(bf16[192,1024]{1,0:T(8,128)(2,1)S(1)} %add_convert_fusion.15), channel_id=1, source_target_pairs={{0,2},{1,3},{2,0},{3,1},{4,6},{5,7},{6,4},{7,5},{8,10},{9,11},{10,... | collective-permute-start | bytes 1179656 | tf_op jit(solution)/shard_map/ppermute | solution.py:68
  262.7 12.1 %collective-permute-start.26 = (bf16[192,1024]{1,0:T(8,128)(2,1)}, bf16[192,1024]{1,0:T(8,128)(2,1)}, u32[]{:S(2)}, u32[]{:S(2)}) collective-permute-start(bf16[192,1024]{1,0:T(8,128)(2,1)} %add_convert_fusion.14), channel_id=1, source_target_pairs={{0,4},{1,5},{2,6},{3,7},{4,0},{5,1},{6,2},{7,3},{8,12},{9,13},{10,... | collective-permute-start | bytes 1179656 | tf_op jit(solution)/shard_map/ppermute | solution.py:68
  276.1 4.0 collective-permute-start.27
  295.8 8.1 %collective-permute-start.28 = (bf16[384,128]{1,0:T(8,128)(2,1)S(1)}, bf16[384,128]{1,0:T(8,128)(2,1)S(1)}, u32[]{:S(2)}, u32[]{:S(2)}) collective-permute-start(bf16[384,128]{1,0:T(8,128)(2,1)S(1)} %fusion.143), channel_id=1, source_target_pairs={{0,8},{8,0},{1,9},{9,1},{2,10},{10,2},{3,11},{11,3},{4,12},{12,4},... | collective-permute-start | bytes 294920 | tf_op jit(solution)/shard_map/ppermute | solution.py:82
  299.7 7.4 %collective-permute-start.29 = (bf16[384,128]{0,1:T(8,128)(2,1)S(1)}, bf16[384,128]{0,1:T(8,128)(2,1)S(1)}, u32[]{:S(2)}, u32[]{:S(2)}) collective-permute-start(bf16[384,128]{0,1:T(8,128)(2,1)S(1)} %fusion.145), channel_id=1, source_target_pairs={{0,8},{8,0},{1,9},{9,1},{2,10},{10,2},{3,11},{11,3},{4,12},{12,4},... | collective-permute-start | bytes 294920 | tf_op jit(solution)/shard_map/ppermute | solution.py:82
  308.6 2.0 collective-permute-start.30
  308.8 3.6 collective-permute-start.20
  310.8 12.1 %collective-permute-start.31 = (bf16[192,1024]{1,0:T(8,128)(2,1)S(1)}, bf16[192,1024]{1,0:T(8,128)(2,1)S(1)}, u32[]{:S(2)}, u32[]{:S(2)}) collective-permute-start(bf16[192,1024]{1,0:T(8,128)(2,1)S(1)} %add_convert_fusion.12), channel_id=1, source_target_pairs={{0,2},{1,3},{2,0},{3,1},{4,6},{5,7},{6,4},{7,5},{8,10},{9,11},{10,... | collective-permute-start | bytes 1179656 | tf_op jit(solution)/shard_map/ppermute | solution.py:68
  312.5 18.8 %collective-permute-start.21 = (bf16[192,1024]{1,0:T(8,128)(2,1)S(1)}, bf16[192,1024]{1,0:T(8,128)(2,1)S(1)}, u32[]{:S(2)}, u32[]{:S(2)}) collective-permute-start(bf16[192,1024]{1,0:T(8,128)(2,1)S(1)} %add_convert_fusion.18), channel_id=1, source_target_pairs={{0,2},{1,3},{2,0},{3,1},{4,6},{5,7},{6,4},{7,5},{8,10},{9,11},{10,... | collective-permute-start | bytes 1179656 | tf_op jit(solution)/shard_map/ppermute | solution.py:68
  323.0 18.9 %collective-permute-start.32 = (bf16[192,1024]{1,0:T(8,128)(2,1)S(1)}, bf16[192,1024]{1,0:T(8,128)(2,1)S(1)}, u32[]{:S(2)}, u32[]{:S(2)}) collective-permute-start(bf16[192,1024]{1,0:T(8,128)(2,1)S(1)} %add_convert_fusion.11), channel_id=1, source_target_pairs={{0,4},{1,5},{2,6},{3,7},{4,0},{5,1},{6,2},{7,3},{8,12},{9,13},{10,... | collective-permute-start | bytes 1179656 | tf_op jit(solution)/shard_map/ppermute | solution.py:68
  331.4 17.9 %collective-permute-start.22 = (bf16[192,1024]{1,0:T(8,128)(2,1)S(1)}, bf16[192,1024]{1,0:T(8,128)(2,1)S(1)}, u32[]{:S(2)}, u32[]{:S(2)}) collective-permute-start(bf16[192,1024]{1,0:T(8,128)(2,1)S(1)} %add_convert_fusion.17), channel_id=1, source_target_pairs={{0,4},{1,5},{2,6},{3,7},{4,0},{5,1},{6,2},{7,3},{8,12},{9,13},{10,... | collective-permute-start | bytes 1179656 | tf_op jit(solution)/shard_map/ppermute | solution.py:68
  342.0 8.6 %collective-permute-start.33 = (bf16[192,1024]{1,0:T(8,128)(2,1)S(1)}, bf16[192,1024]{1,0:T(8,128)(2,1)S(1)}, u32[]{:S(2)}, u32[]{:S(2)}) collective-permute-start(bf16[192,1024]{1,0:T(8,128)(2,1)S(1)} %add_convert_fusion.10), channel_id=1, source_target_pairs={{0,1},{1,0},{2,3},{3,2},{4,5},{5,4},{6,7},{7,6},{8,9},{9,8},{10,11... | collective-permute-start | bytes 1179656 | tf_op jit(solution)/shard_map/ppermute | solution.py:72
  350.2 30.9 %collective-permute-start.23 = (bf16[192,1024]{1,0:T(8,128)(2,1)}, bf16[192,1024]{1,0:T(8,128)(2,1)}, u32[]{:S(2)}, u32[]{:S(2)}) collective-permute-start(bf16[192,1024]{1,0:T(8,128)(2,1)} %add_convert_fusion.16), channel_id=1, source_target_pairs={{0,1},{1,0},{2,3},{3,2},{4,5},{5,4},{6,7},{7,6},{8,9},{9,8},{10,11... | collective-permute-start | bytes 1179656 | tf_op jit(solution)/shard_map/ppermute | solution.py:72
  357.7 9.3 %collective-permute-start.34 = (bf16[192,1024]{1,0:T(8,128)(2,1)}, bf16[192,1024]{1,0:T(8,128)(2,1)}, u32[]{:S(2)}, u32[]{:S(2)}) collective-permute-start(bf16[192,1024]{1,0:T(8,128)(2,1)} %constant_dynamic-slice_fusion.2), channel_id=1, source_target_pairs={{0,1},{1,0},{2,3},{3,2},{4,5},{5,4},{6,7},{7,6},{8,9},{9,8},{10,11... | collective-permute-start | bytes 1179656 | tf_op jit(solution)/shard_map/ppermute | solution.py:62
  364.6 189.0 %reduce-scatter.7.cloned.1.call-start = ((), (), s32[]{:S(2)}) async-start(), calls=%async_computation.4 | async-start | bytes 4177920 | tf_op jit(solution)/shard_map/reduce_scatter | solution.py:253
  368.1 11.1 %collective-permute-start.35 = (bf16[192,1024]{1,0:T(8,128)(2,1)S(1)}, bf16[192,1024]{1,0:T(8,128)(2,1)S(1)}, u32[]{:S(2)}, u32[]{:S(2)}) collective-permute-start(bf16[192,1024]{1,0:T(8,128)(2,1)S(1)} %add_convert_fusion.9), channel_id=1, source_target_pairs={{0,2},{1,3},{2,0},{3,1},{4,6},{5,7},{6,4},{7,5},{8,10},{9,11},{10,... | collective-permute-start | bytes 1179656 | tf_op jit(solution)/shard_map/ppermute | solution.py:68
  379.4 12.1 %collective-permute-start.36 = (bf16[192,1024]{1,0:T(8,128)(2,1)S(1)}, bf16[192,1024]{1,0:T(8,128)(2,1)S(1)}, u32[]{:S(2)}, u32[]{:S(2)}) collective-permute-start(bf16[192,1024]{1,0:T(8,128)(2,1)S(1)} %add_convert_fusion.8), channel_id=1, source_target_pairs={{0,4},{1,5},{2,6},{3,7},{4,0},{5,1},{6,2},{7,3},{8,12},{9,13},{10,... | collective-permute-start | bytes 1179656 | tf_op jit(solution)/shard_map/ppermute | solution.py:68
  391.6 2.2 collective-permute-start.37
  407.2 22.4 %collective-permute-start.38 = (bf16[384,128]{1,0:T(8,128)(2,1)}, bf16[384,128]{1,0:T(8,128)(2,1)}, u32[]{:S(2)}, u32[]{:S(2)}) collective-permute-start(bf16[384,128]{1,0:T(8,128)(2,1)} %fusion.147), channel_id=1, source_target_pairs={{0,8},{8,0},{1,9},{9,1},{2,10},{10,2},{3,11},{11,3},{4,12},{12,4},... | collective-permute-start | bytes 294920 | tf_op jit(solution)/shard_map/ppermute | solution.py:82
  412.1 22.4 %collective-permute-start.39 = (bf16[384,128]{0,1:T(8,128)(2,1)S(1)}, bf16[384,128]{0,1:T(8,128)(2,1)S(1)}, u32[]{:S(2)}, u32[]{:S(2)}) collective-permute-start(bf16[384,128]{0,1:T(8,128)(2,1)S(1)} %fusion.149), channel_id=1, source_target_pairs={{0,8},{8,0},{1,9},{9,1},{2,10},{10,2},{3,11},{11,3},{4,12},{12,4},... | collective-permute-start | bytes 294920 | tf_op jit(solution)/shard_map/ppermute | solution.py:82
  435.8 6.8 %collective-permute-start.40 = (bf16[192,1024]{1,0:T(8,128)(2,1)}, bf16[192,1024]{1,0:T(8,128)(2,1)}, u32[]{:S(2)}, u32[]{:S(2)}) collective-permute-start(bf16[192,1024]{1,0:T(8,128)(2,1)} %constant_dynamic-slice_fusion.1), channel_id=1, source_target_pairs={{0,1},{1,0},{2,3},{3,2},{4,5},{5,4},{6,7},{7,6},{8,9},{9,8},{10,11... | collective-permute-start | bytes 1179656 | tf_op jit(solution)/shard_map/ppermute | solution.py:62
  441.1 14.6 %collective-permute-start.51 = (bf16[2,2,1,2,64,512]{5,4,3,2,1,0:T(8,128)(2,1)S(1)}, bf16[2,2,1,2,64,512]{5,4,3,2,1,0:T(8,128)(2,1)S(1)}, u32[]{:S(2)}, u32[]{:S(2)}) collective-permute-start(bf16[2,2,1,2,64,512]{5,4,3,2,1,0:T(8,128)(2,1)S(1)} %constant_dynamic-slice_fusion), channel_id=1, source_target_pairs={{0,16},{16,0},{32,48},{48,32},{64,80},{80,64},{96,112},{112,96},{1... | collective-permute-start | bytes 1572872 | tf_op jit(solution)/shard_map/ppermute | solution.py:135
  443.8 12.2 %collective-permute-start.41 = (bf16[192,1024]{1,0:T(8,128)(2,1)S(1)}, bf16[192,1024]{1,0:T(8,128)(2,1)S(1)}, u32[]{:S(2)}, u32[]{:S(2)}) collective-permute-start(bf16[192,1024]{1,0:T(8,128)(2,1)S(1)} %add_convert_fusion.6), channel_id=1, source_target_pairs={{0,2},{1,3},{2,0},{3,1},{4,6},{5,7},{6,4},{7,5},{8,10},{9,11},{10,... | collective-permute-start | bytes 1179656 | tf_op jit(solution)/shard_map/ppermute | solution.py:68
  455.8 9.9 %collective-permute-start.52 = (bf16[2,1,1,2,64,512]{5,4,3,2,1,0:T(8,128)(2,1)S(1)}, bf16[2,1,1,2,64,512]{5,4,3,2,1,0:T(8,128)(2,1)S(1)}, u32[]{:S(2)}, u32[]{:S(2)}) collective-permute-start(bf16[2,1,1,2,64,512]{5,4,3,2,1,0:T(8,128)(2,1)S(1)} %dynamic-slice_convert_fusion), channel_id=1, source_target_pairs={{0,32},{16,48},{32,0},{48,16},{64,96},{80,112},{96,64},{112,80},{1... | collective-permute-start | bytes 786440 | tf_op jit(solution)/shard_map/ppermute | solution.py:135
  456.1 12.4 %collective-permute-start.42 = (bf16[192,1024]{1,0:T(8,128)(2,1)S(1)}, bf16[192,1024]{1,0:T(8,128)(2,1)S(1)}, u32[]{:S(2)}, u32[]{:S(2)}) collective-permute-start(bf16[192,1024]{1,0:T(8,128)(2,1)S(1)} %add_convert_fusion.5), channel_id=1, source_target_pairs={{0,4},{1,5},{2,6},{3,7},{4,0},{5,1},{6,2},{7,3},{8,12},{9,13},{10,... | collective-permute-start | bytes 1179656 | tf_op jit(solution)/shard_map/ppermute | solution.py:68
  465.8 13.1 %collective-permute-start.53 = (bf16[2,1,1,1,64,512]{5,4,3,2,1,0:T(8,128)(2,1)S(1)}, bf16[2,1,1,1,64,512]{5,4,3,2,1,0:T(8,128)(2,1)S(1)}, u32[]{:S(2)}, u32[]{:S(2)}) collective-permute-start(bf16[2,1,1,1,64,512]{5,4,3,2,1,0:T(8,128)(2,1)S(1)} %dynamic-slice_convert_fusion.1), channel_id=1, source_target_pairs={{0,8},{8,0},{1,9},{9,1},{2,10},{10,2},{3,11},{11,3},{4,12},{12,4},... | collective-permute-start | bytes 393224 | tf_op jit(solution)/shard_map/ppermute | solution.py:135
  468.6 10.3 %collective-permute-start.43 = (bf16[192,1024]{1,0:T(8,128)(2,1)S(1)}, bf16[192,1024]{1,0:T(8,128)(2,1)S(1)}, u32[]{:S(2)}, u32[]{:S(2)}) collective-permute-start(bf16[192,1024]{1,0:T(8,128)(2,1)S(1)} %add_convert_fusion.4), channel_id=1, source_target_pairs={{0,1},{1,0},{2,3},{3,2},{4,5},{5,4},{6,7},{7,6},{8,9},{9,8},{10,11... | collective-permute-start | bytes 1179656 | tf_op jit(solution)/shard_map/ppermute | solution.py:72
  479.3 1.7 collective-permute-start.44
  479.5 6.1 %collective-permute-start.54 = (bf16[1,1,1,1,64,512]{5,4,3,2,1,0:T(8,128)(2,1)S(1)}, bf16[1,1,1,1,64,512]{5,4,3,2,1,0:T(8,128)(2,1)S(1)}, u32[]{:S(2)}, u32[]{:S(2)}) collective-permute-start(bf16[1,1,1,1,64,512]{5,4,3,2,1,0:T(8,128)(2,1)S(1)} %dynamic-slice_convert_fusion.10), channel_id=1, source_target_pairs={{0,64},{16,80},{32,96},{48,112},{64,0},{80,16},{96,32},{112,48},{1... | collective-permute-start | bytes 196616 | tf_op jit(solution)/shard_map/ppermute | solution.py:135
  481.1 4.5 collective-permute-start.45
  485.6 5.3 collective-permute-start.46
  491.0 6.1 %collective-permute-start.47 = (f32[2,2304]{1,0:T(2,128)S(1)}, f32[2,2304]{1,0:T(2,128)S(1)}, u32[]{:S(2)}, u32[]{:S(2)}) collective-permute-start(f32[2,2304]{1,0:T(2,128)S(1)} %add.463), channel_id=1, source_target_pairs={{0,8},{8,0},{1,9},{9,1},{2,10},{10,2},{3,11},{11,3},{4,12},{12,4},... | collective-permute-start | bytes 55304 | tf_op jit(solution)/shard_map/ppermute | solution.py:109
  497.0 4.2 collective-permute-start.48
  501.3 4.9 collective-permute-start.49
  506.2 5.3 collective-permute-start.50
  (161 other events, 843.6 us)
Sparse Core Ops, SparseCore 0:
  10.6 88.6 all-gather.2
  100.9 95.9 all-gather.4
  364.7 85.7 reduce-scatter.8
  452.8 100.7 reduce-scatter.6

commit v11 on v6

--- a/solution.py
+++ b/solution.py
@@ -231,9 +231,17 @@
     for width in widths:
         edges.append(edges[-1] + width)
 
+    early_width = edges[3]
+    early_all = shard_gather(
+        jnp.concatenate(
+            [member[layer_index] for layer_index in range(query_weight.shape[0])
+             for member in weight_shards[:3]],
+            axis=1,
+        )
+    )
+
     def gather_layer(layer_index):
-        early = jnp.concatenate([member[layer_index] for member in weight_shards[:3]], axis=1)
-        early_full = shard_gather(early)
+        early_full = early_all[:, layer_index * early_width : (layer_index + 1) * early_width]
         late = jnp.concatenate([member[layer_index] for member in weight_shards[3:]], axis=1)
         late_full = lax.all_gather(late, ("fsdp", "ctx"), axis=0, tiled=True)
         pieces = []

time: 582 us -> 601 us (1.033)
    ppermute x16, waiting for transfers between devices: 86.1 us -> 100 us  [tp_sum(): received = lax.ppermute(mine, 'tp', pairs)]
    ppermute x8 -> x4, waiting for transfers between devices: 68.6 us -> 59 us  [shard_gather(): received = lax.ppermute(current, axis_name, pairs)]
    unnamed x344 -> x333, local copies, waits for them, and re-layouts: 25 us -> 28.6 us
  transfers between devices with their start and end apart: 63 -> 59, of which waited for: 45 -> 41; matrix products, arithmetic and copies ran while one was open for 24% -> 24% of each run, Pallas kernels for 0% -> 0%
where the time goes in v11:
time: 601 us; the launch traced here: 591 us
  waiting for transfers between devices  323 us (54%)
  starting transfers between devices  70.8 us (12%)
  matrix products  63.6 us (11%)
  other arithmetic  61.4 us (10%)
  local copies, waits for them, and re-layouts  55.4 us (9%)
  between operations  16.8 us (3%)
    ppermute x16, waiting for transfers between devices, tp_sum(): received = lax.ppermute(mine, 'tp', pairs)  100 us
    ppermute x4, waiting for transfers between devices, shard_gather(): received = lax.ppermute(current, axis_name, pairs)  59 us
    unnamed x5, waiting for transfers between devices  48.5 us
    all_gather x2, waiting for transfers between devices, gather_layer(): late_full = lax.all_gather(late, ('fsdp', 'ctx'), axis=0, tiled=True)  38.1 us
    ppermute x16, starting transfers between devices, tp_sum(): received = lax.ppermute(mine, 'tp', pairs)  34.4 us
    ppermute x4, waiting for transfers between devices, shard_scatter(): received = lax.ppermute(sent.astype(jnp.bfloat16), axis_name, pairs)  29.8 us
    unnamed x333, local copies, waits for them, and re-layouts  28.6 us
    ppermute x8, waiting for transfers between devices, swap_halves(): return lax.ppermute(local, axis_name, [(0, 1), (1, 0)])  20.1 us
  transfers between devices with their start and end apart: 59, of which 41 were waited for; matrix products, arithmetic and copies ran while one was open for 24% of the time, Pallas kernels for 0%

profile of v11, /device:TPU:0, one launch (start us, length us, event | category | flops | bytes accessed | tf_op | source)
XLA Modules:
  0.0 591.4 jit_solution(13250042425895888481)
XLA Ops:
  11.7 4.0 collective-permute-start
  22.1 3.1 collective-permute-start.1
  25.8 5.6 collective-permute-done.1
  32.9 18.9 %collective-permute-done.2 = bf16[2,1,1,2,64,1024]{5,4,3,2,1,0:T(8,128)(2,1)S(1)} collective-permute-done((bf16[2,1,1,2,64,1024]{5,4,3,2,1,0:T(8,128)(2,1)S(1)}, bf16[2,1,1,2,64,1024]{5,4,3,2,1,0:T(8,128)(2,1)S(1)}, u32[]{:S(2)}, u32[]{:S(2)}) %collective-permute-start.2) | collective-permute-done | bytes 524320 | tf_op jit(solution)/shard_map/ppermute | solution.py:157
  58.1 34.5 %collective-permute-done.3 = bf16[2,1,2,2,64,1024]{5,4,3,2,1,0:T(8,128)(2,1)} collective-permute-done((bf16[2,1,2,2,64,1024]{5,4,3,2,1,0:T(8,128)(2,1)}, bf16[2,1,2,2,64,1024]{5,4,3,2,1,0:T(8,128)(2,1)}, u32[]{:S(2)}, u32[]{:S(2)}) %collective-permute-start.3) | collective-permute-done | bytes 1048608 | tf_op jit(solution)/shard_map/ppermute | solution.py:157
  92.6 2.6 maximum_select_fusion
  99.5 2.1 multiply_reduce_fusion.21
  104.4 3.6 collective-permute-start.5
  108.5 2.1 collective-permute-done.5
  117.1 1.9 collective-permute-done.6
  121.1 9.4 %collective-permute-done.7 = bf16[192,1024]{1,0:T(8,128)(2,1)S(1)} collective-permute-done((bf16[192,1024]{1,0:T(8,128)(2,1)S(1)}, bf16[192,1024]{1,0:T(8,128)(2,1)S(1)}, u32[]{:S(2)}, u32[]{:S(2)}) %collective-permute-start.7) | collective-permute-done | bytes 393248 | tf_op jit(solution)/shard_map/ppermute | solution.py:68
  130.6 3.5 collective-permute-start.8
  134.1 8.6 %collective-permute-done.8 = bf16[192,1024]{1,0:T(8,128)(2,1)S(1)} collective-permute-done((bf16[192,1024]{1,0:T(8,128)(2,1)S(1)}, bf16[192,1024]{1,0:T(8,128)(2,1)S(1)}, u32[]{:S(2)}, u32[]{:S(2)}) %collective-permute-start.8) | collective-permute-done | bytes 393248 | tf_op jit(solution)/shard_map/ppermute | solution.py:68
  155.0 8.8 %collective-permute-done.11 = bf16[192,1024]{1,0:T(8,128)(2,1)S(1)} collective-permute-done((bf16[192,1024]{1,0:T(8,128)(2,1)S(1)}, bf16[192,1024]{1,0:T(8,128)(2,1)S(1)}, u32[]{:S(2)}, u32[]{:S(2)}) %collective-permute-start.11) | collective-permute-done | bytes 393248 | tf_op jit(solution)/shard_map/ppermute | solution.py:68
  163.9 3.3 collective-permute-start.12
  167.2 8.6 %collective-permute-done.12 = bf16[192,1024]{1,0:T(8,128)(2,1)S(1)} collective-permute-done((bf16[192,1024]{1,0:T(8,128)(2,1)S(1)}, bf16[192,1024]{1,0:T(8,128)(2,1)S(1)}, u32[]{:S(2)}, u32[]{:S(2)}) %collective-permute-start.12) | collective-permute-done | bytes 393248 | tf_op jit(solution)/shard_map/ppermute | solution.py:68
  177.7 2.0 multiply_reduce_fusion.5
  181.1 2.2 convolution_convert_fusion.22
  183.3 3.5 collective-permute-start.14
  193.9 7.8 %collective-permute-done.15 = bf16[384,128]{1,0:T(8,128)(2,1)S(1)} collective-permute-done((bf16[384,128]{1,0:T(8,128)(2,1)S(1)}, bf16[384,128]{1,0:T(8,128)(2,1)S(1)}, u32[]{:S(2)}, u32[]{:S(2)}) %collective-permute-start.15) | collective-permute-done | bytes 98336 | tf_op jit(solution)/shard_map/ppermute | solution.py:82
  205.8 38.1 %all-gather.5.cloned.1.call-done = bf16[1024,1408]{1,0:T(8,128)(2,1)} async-done(((bf16[64,1408]{1,0:T(8,128)(2,1)}), bf16[1024,1408]{1,0:T(8,128)(2,1)}) %all-gather.5.cloned.1.call-update) | async-done | bytes 2883600 | tf_op jit(solution)/shard_map/all_gather | solution.py:246
  247.5 2.6 collective-permute-start.17
  250.1 9.4 %collective-permute-done.17 = bf16[192,1024]{1,0:T(8,128)(2,1)S(1)} collective-permute-done((bf16[192,1024]{1,0:T(8,128)(2,1)S(1)}, bf16[192,1024]{1,0:T(8,128)(2,1)S(1)}, u32[]{:S(2)}, u32[]{:S(2)}) %collective-permute-start.17) | collective-permute-done | bytes 393248 | tf_op jit(solution)/shard_map/ppermute | solution.py:68
  259.6 4.5 collective-permute-start.18
  264.1 8.6 %collective-permute-done.18 = bf16[192,1024]{1,0:T(8,128)(2,1)S(1)} collective-permute-done((bf16[192,1024]{1,0:T(8,128)(2,1)S(1)}, bf16[192,1024]{1,0:T(8,128)(2,1)S(1)}, u32[]{:S(2)}, u32[]{:S(2)}) %collective-permute-start.18) | collective-permute-done | bytes 393248 | tf_op jit(solution)/shard_map/ppermute | solution.py:68
  282.5 9.1 %collective-permute-done.25 = bf16[192,1024]{1,0:T(8,128)(2,1)S(1)} collective-permute-done((bf16[192,1024]{1,0:T(8,128)(2,1)S(1)}, bf16[192,1024]{1,0:T(8,128)(2,1)S(1)}, u32[]{:S(2)}, u32[]{:S(2)}) %collective-permute-start.25) | collective-permute-done | bytes 393248 | tf_op jit(solution)/shard_map/ppermute | solution.py:68
  292.5 3.2 collective-permute-start.26
  297.1 9.3 %collective-permute-done.26 = bf16[192,1024]{1,0:T(8,128)(2,1)} collective-permute-done((bf16[192,1024]{1,0:T(8,128)(2,1)}, bf16[192,1024]{1,0:T(8,128)(2,1)}, u32[]{:S(2)}, u32[]{:S(2)}) %collective-permute-start.26) | collective-permute-done | bytes 393248 | tf_op jit(solution)/shard_map/ppermute | solution.py:68
  308.9 3.8 collective-permute-done.21
  315.7 2.0 multiply_add_fusion.3
  327.5 1.9 copy.158
  333.2 3.6 collective-permute-start.29
  336.8 2.5 collective-permute-done.28
  350.8 7.6 %collective-permute-done.31 = bf16[192,1024]{1,0:T(8,128)(2,1)S(1)} collective-permute-done((bf16[192,1024]{1,0:T(8,128)(2,1)S(1)}, bf16[192,1024]{1,0:T(8,128)(2,1)S(1)}, u32[]{:S(2)}, u32[]{:S(2)}) %collective-permute-start.31) | collective-permute-done | bytes 393248 | tf_op jit(solution)/shard_map/ppermute | solution.py:68
  358.6 3.0 collective-permute-start.32
  363.2 7.3 %collective-permute-done.32 = bf16[192,1024]{1,0:T(8,128)(2,1)S(1)} collective-permute-done((bf16[192,1024]{1,0:T(8,128)(2,1)S(1)}, bf16[192,1024]{1,0:T(8,128)(2,1)S(1)}, u32[]{:S(2)}, u32[]{:S(2)}) %collective-permute-start.32) | collective-permute-done | bytes 393248 | tf_op jit(solution)/shard_map/ppermute | solution.py:68
  385.5 6.2 %copy.212 = bf16[1024,1920]{1,0:T(8,128)(2,1)} copy(bf16[1024,1920]{0,1:T(8,128)(2,1)} %fusion.19) | data formatting | bytes 7864320
  392.8 2.5 convolution_convert_fusion.3
  396.6 3.9 collective-permute-start.36
  402.5 7.5 %collective-permute-done.36 = bf16[192,1024]{1,0:T(8,128)(2,1)S(1)} collective-permute-done((bf16[192,1024]{1,0:T(8,128)(2,1)S(1)}, bf16[192,1024]{1,0:T(8,128)(2,1)S(1)}, u32[]{:S(2)}, u32[]{:S(2)}) %collective-permute-start.36) | collective-permute-done | bytes 393248 | tf_op jit(solution)/shard_map/ppermute | solution.py:68
  415.2 2.0 fusion
  420.9 1.9 copy.169
  422.8 2.0 convolution_bitcast_fusion.1
  429.3 2.6 collective-permute-start.39
  431.9 4.8 collective-permute-done.38
  438.4 3.0 collective-permute-done.39
  444.4 2.3 copy.175
  446.7 2.0 constant_dynamic-slice_fusion
  448.7 2.0 add_convert_fusion.6
  450.9 2.8 pad_maximum_fusion
  453.7 4.6 copy.214
  458.4 16.0 %collective-permute-done.51 = bf16[2,2,1,2,64,512]{5,4,3,2,1,0:T(8,128)(2,1)} collective-permute-done((bf16[2,2,1,2,64,512]{5,4,3,2,1,0:T(8,128)(2,1)}, bf16[2,2,1,2,64,512]{5,4,3,2,1,0:T(8,128)(2,1)}, u32[]{:S(2)}, u32[]{:S(2)}) %collective-permute-start.51) | collective-permute-done | bytes 524320 | tf_op jit(solution)/shard_map/ppermute | solution.py:135
  477.1 2.8 collective-permute-start.42
  480.2 6.2 %collective-permute-done.52 = bf16[2,1,1,2,64,512]{5,4,3,2,1,0:T(8,128)(2,1)S(1)} collective-permute-done((bf16[2,1,1,2,64,512]{5,4,3,2,1,0:T(8,128)(2,1)S(1)}, bf16[2,1,1,2,64,512]{5,4,3,2,1,0:T(8,128)(2,1)S(1)}, u32[]{:S(2)}, u32[]{:S(2)}) %collective-permute-start.52) | collective-permute-done | bytes 262176 | tf_op jit(solution)/shard_map/ppermute | solution.py:135
  486.7 2.5 collective-permute-done.42
  489.4 3.7 collective-permute-done.53
  495.8 3.9 collective-permute-done.54
  499.8 3.2 collective-permute-start.46
  503.0 2.1 collective-permute-done.46
  506.6 4.8 collective-permute-done.47
  511.9 3.5 collective-permute-done.48
  515.5 3.7 collective-permute-done.49
  522.3 2.3 collective-permute-done.50
  530.6 48.4 %reduce-scatter.9.cloned.1.call-done = bf16[64,1408]{1,0:T(8,128)(2,1)} async-done(((bf16[1024,1408]{1,0:T(8,128)(2,1)}), bf16[64,1408]{1,0:T(8,128)(2,1)}) %reduce-scatter.9.cloned.1.call-update) | async-done | bytes 180240
  (625 shorter events, 168.8 us)
Async XLA Ops:
  7.2 107.6 %all-gather.3.cloned.1.call-start = ((), (), s32[]{:S(2)}) async-start(), calls=%async_computation.2 | async-start | bytes 3063808 | tf_op jit(solution)/shard_map/all_gather | solution.py:246
  11.7 10.4 %collective-permute-start = (bf16[1,1,1,1,64,1024]{5,4,3,2,1,0:T(8,128)(2,1)S(1)}, bf16[1,1,1,1,64,1024]{5,4,3,2,1,0:T(8,128)(2,1)S(1)}, u32[]{:S(2)}, u32[]{:S(2)}) collective-permute-start(bf16[1,1,1,1,64,1024]{5,4,3,2,1,0:T(8,128)(2,1)S(1)} %bitcast.492), channel_id=1, source_target_pairs={{0,8},{8,0},{1,9},{9,1},{2,10},{10,2},{3,11},{11,3},{4,12},{12,4},... | collective-permute-start | bytes 393224 | tf_op jit(solution)/shard_map/ppermute | solution.py:157
  20.7 223.2 %all-gather.5.cloned.1.call-start = ((), (), s32[]{:S(2)}) async-start(), calls=%async_computation.3 | async-start | bytes 3063808 | tf_op jit(solution)/shard_map/all_gather | solution.py:246
  22.1 9.3 %collective-permute-start.1 = (bf16[1,1,1,2,64,1024]{5,4,3,2,1,0:T(8,128)(2,1)S(1)}, bf16[1,1,1,2,64,1024]{5,4,3,2,1,0:T(8,128)(2,1)S(1)}, u32[]{:S(2)}, u32[]{:S(2)}) collective-permute-start(bf16[1,1,1,2,64,1024]{5,4,3,2,1,0:T(8,128)(2,1)S(1)} %maximum_select_fusion.13), channel_id=1, source_target_pairs={{0,64},{16,80},{32,96},{48,112},{64,0},{80,16},{96,32},{112,48},{1... | collective-permute-start | bytes 786440 | tf_op jit(solution)/shard_map/ppermute | solution.py:157
  25.8 76.9 %copy-start.136 = (f32[128]{0:T(128)}, f32[128]{0:T(128)S(1)}, u32[]{:S(2)}) copy-start(f32[128]{0:T(128)S(1)} %get-tuple-element.144) | copy-start | bytes 1540
  31.5 20.3 %collective-permute-start.2 = (bf16[2,1,1,2,64,1024]{5,4,3,2,1,0:T(8,128)(2,1)S(1)}, bf16[2,1,1,2,64,1024]{5,4,3,2,1,0:T(8,128)(2,1)S(1)}, u32[]{:S(2)}, u32[]{:S(2)}) collective-permute-start(bf16[2,1,1,2,64,1024]{5,4,3,2,1,0:T(8,128)(2,1)S(1)} %maximum_select_fusion.11), channel_id=1, source_target_pairs={{0,16},{16,0},{32,48},{48,32},{64,80},{80,64},{96,112},{112,96},{1... | collective-permute-start | bytes 1572872 | tf_op jit(solution)/shard_map/ppermute | solution.py:157
  53.0 39.6 %collective-permute-start.3 = (bf16[2,1,2,2,64,1024]{5,4,3,2,1,0:T(8,128)(2,1)}, bf16[2,1,2,2,64,1024]{5,4,3,2,1,0:T(8,128)(2,1)}, u32[]{:S(2)}, u32[]{:S(2)}) collective-permute-start(bf16[2,1,2,2,64,1024]{5,4,3,2,1,0:T(8,128)(2,1)} %maximum_select_fusion.1), channel_id=1, source_target_pairs={{0,32},{16,48},{32,0},{48,16},{64,96},{80,112},{96,64},{112,80},{1... | collective-permute-start | bytes 3145736 | tf_op jit(solution)/shard_map/ppermute | solution.py:157
  56.8 51.5 %copy-start.32 = (f32[384,64]{1,0:T(8,128)}, f32[384,64]{1,0:T(8,128)S(1)}, u32[]{:S(2)}) copy-start(f32[384,64]{1,0:T(8,128)S(1)} %get-tuple-element.140) | copy-start | bytes 294916
  56.8 51.5 %copy-start.61 = (f32[384,64]{1,0:T(8,128)}, f32[384,64]{1,0:T(8,128)S(1)}, u32[]{:S(2)}) copy-start(f32[384,64]{1,0:T(8,128)S(1)} %get-tuple-element.139) | copy-start | bytes 294916
  58.1 41.3 %copy-start.1 = (bf16[384,1024]{1,0:T(8,128)(2,1)}, bf16[384,1024]{1,0:T(8,128)(2,1)S(1)}, u32[]{:S(2)}) copy-start(bf16[384,1024]{1,0:T(8,128)(2,1)S(1)} %get-tuple-element.81) | copy-start | bytes 2359300
  96.5 15.1 %collective-permute-start.4 = (bf16[384,128]{1,0:T(8,128)(2,1)}, bf16[384,128]{1,0:T(8,128)(2,1)}, u32[]{:S(2)}, u32[]{:S(2)}) collective-permute-start(bf16[384,128]{1,0:T(8,128)(2,1)} %convolution_convert_fusion.23), channel_id=1, source_target_pairs={{0,8},{8,0},{1,9},{9,1},{2,10},{10,2},{3,11},{11,3},{4,12},{12,4},... | collective-permute-start | bytes 294920 | tf_op jit(solution)/shard_map/ppermute | solution.py:82
  104.4 6.2 %collective-permute-start.5 = (bf16[384,128]{1,0:T(8,128)(2,1)S(1)}, bf16[384,128]{1,0:T(8,128)(2,1)S(1)}, u32[]{:S(2)}, u32[]{:S(2)}) collective-permute-start(bf16[384,128]{1,0:T(8,128)(2,1)S(1)} %pad_maximum_fusion.11), channel_id=1, source_target_pairs={{0,8},{8,0},{1,9},{9,1},{2,10},{10,2},{3,11},{11,3},{4,12},{12,4},... | collective-permute-start | bytes 294920 | tf_op jit(solution)/shard_map/ppermute | solution.py:82
  117.1 1.9 collective-permute-start.6
  119.2 11.3 %collective-permute-start.7 = (bf16[192,1024]{1,0:T(8,128)(2,1)S(1)}, bf16[192,1024]{1,0:T(8,128)(2,1)S(1)}, u32[]{:S(2)}, u32[]{:S(2)}) collective-permute-start(bf16[192,1024]{1,0:T(8,128)(2,1)S(1)} %add_convert_fusion.27), channel_id=1, source_target_pairs={{0,2},{1,3},{2,0},{3,1},{4,6},{5,7},{6,4},{7,5},{8,10},{9,11},{10,... | collective-permute-start | bytes 1179656 | tf_op jit(solution)/shard_map/ppermute | solution.py:68
  130.6 12.0 %collective-permute-start.8 = (bf16[192,1024]{1,0:T(8,128)(2,1)S(1)}, bf16[192,1024]{1,0:T(8,128)(2,1)S(1)}, u32[]{:S(2)}, u32[]{:S(2)}) collective-permute-start(bf16[192,1024]{1,0:T(8,128)(2,1)S(1)} %add_convert_fusion.26), channel_id=1, source_target_pairs={{0,4},{1,5},{2,6},{3,7},{4,0},{5,1},{6,2},{7,3},{8,12},{9,13},{10,... | collective-permute-start | bytes 1179656 | tf_op jit(solution)/shard_map/ppermute | solution.py:68
  142.8 2.3 collective-permute-start.9
  150.6 1.8 collective-permute-start.10
  152.5 11.2 %collective-permute-start.11 = (bf16[192,1024]{1,0:T(8,128)(2,1)S(1)}, bf16[192,1024]{1,0:T(8,128)(2,1)S(1)}, u32[]{:S(2)}, u32[]{:S(2)}) collective-permute-start(bf16[192,1024]{1,0:T(8,128)(2,1)S(1)} %add_convert_fusion.24), channel_id=1, source_target_pairs={{0,2},{1,3},{2,0},{3,1},{4,6},{5,7},{6,4},{7,5},{8,10},{9,11},{10,... | collective-permute-start | bytes 1179656 | tf_op jit(solution)/shard_map/ppermute | solution.py:68
  154.9 370.9 %reduce-scatter.7.cloned.1.call-start = ((), (), s32[]{:S(2)}) async-start(), calls=%async_computation.4 | async-start | bytes 4177920 | tf_op jit(solution)/shard_map/reduce_scatter | solution.py:257
  163.9 11.9 %collective-permute-start.12 = (bf16[192,1024]{1,0:T(8,128)(2,1)S(1)}, bf16[192,1024]{1,0:T(8,128)(2,1)S(1)}, u32[]{:S(2)}, u32[]{:S(2)}) collective-permute-start(bf16[192,1024]{1,0:T(8,128)(2,1)S(1)} %add_convert_fusion.23), channel_id=1, source_target_pairs={{0,4},{1,5},{2,6},{3,7},{4,0},{5,1},{6,2},{7,3},{8,12},{9,13},{10,... | collective-permute-start | bytes 1179656 | tf_op jit(solution)/shard_map/ppermute | solution.py:68
  175.9 1.8 collective-permute-start.13
  183.3 19.4 %collective-permute-start.14 = (bf16[384,128]{1,0:T(8,128)(2,1)}, bf16[384,128]{1,0:T(8,128)(2,1)}, u32[]{:S(2)}, u32[]{:S(2)}) collective-permute-start(bf16[384,128]{1,0:T(8,128)(2,1)} %convolution_convert_fusion.22), channel_id=1, source_target_pairs={{0,8},{8,0},{1,9},{9,1},{2,10},{10,2},{3,11},{11,3},{4,12},{12,4},... | collective-permute-start | bytes 294920 | tf_op jit(solution)/shard_map/ppermute | solution.py:82
  192.7 9.0 %collective-permute-start.15 = (bf16[384,128]{1,0:T(8,128)(2,1)S(1)}, bf16[384,128]{1,0:T(8,128)(2,1)S(1)}, u32[]{:S(2)}, u32[]{:S(2)}) collective-permute-start(bf16[384,128]{1,0:T(8,128)(2,1)S(1)} %pad_maximum_fusion.12), channel_id=1, source_target_pairs={{0,8},{8,0},{1,9},{9,1},{2,10},{10,2},{3,11},{11,3},{4,12},{12,4},... | collective-permute-start | bytes 294920 | tf_op jit(solution)/shard_map/ppermute | solution.py:82
  205.8 41.7 %copy-start.83 = (bf16[128,2,384]{2,0,1:T(8,128)(2,1)}, bf16[128,2,384]{2,0,1:T(8,128)(2,1)S(1)}, u32[]{:S(2)}) copy-start(bf16[128,2,384]{2,0,1:T(8,128)(2,1)S(1)} %convolution_convert_fusion.20) | copy-start | bytes 589828
  245.6 1.8 collective-permute-start.16
  247.5 12.0 %collective-permute-start.17 = (bf16[192,1024]{1,0:T(8,128)(2,1)S(1)}, bf16[192,1024]{1,0:T(8,128)(2,1)S(1)}, u32[]{:S(2)}, u32[]{:S(2)}) collective-permute-start(bf16[192,1024]{1,0:T(8,128)(2,1)S(1)} %add_convert_fusion.21), channel_id=1, source_target_pairs={{0,2},{1,3},{2,0},{3,1},{4,6},{5,7},{6,4},{7,5},{8,10},{9,11},{10,... | collective-permute-start | bytes 1179656 | tf_op jit(solution)/shard_map/ppermute | solution.py:68
  259.6 13.0 %collective-permute-start.18 = (bf16[192,1024]{1,0:T(8,128)(2,1)S(1)}, bf16[192,1024]{1,0:T(8,128)(2,1)S(1)}, u32[]{:S(2)}, u32[]{:S(2)}) collective-permute-start(bf16[192,1024]{1,0:T(8,128)(2,1)S(1)} %add_convert_fusion.20), channel_id=1, source_target_pairs={{0,4},{1,5},{2,6},{3,7},{4,0},{5,1},{6,2},{7,3},{8,12},{9,13},{10,... | collective-permute-start | bytes 1179656 | tf_op jit(solution)/shard_map/ppermute | solution.py:68
  272.8 1.8 collective-permute-start.19
  278.4 1.8 collective-permute-start.24
  280.3 11.2 %collective-permute-start.25 = (bf16[192,1024]{1,0:T(8,128)(2,1)S(1)}, bf16[192,1024]{1,0:T(8,128)(2,1)S(1)}, u32[]{:S(2)}, u32[]{:S(2)}) collective-permute-start(bf16[192,1024]{1,0:T(8,128)(2,1)S(1)} %add_convert_fusion.15), channel_id=1, source_target_pairs={{0,2},{1,3},{2,0},{3,1},{4,6},{5,7},{6,4},{7,5},{8,10},{9,11},{10,... | collective-permute-start | bytes 1179656 | tf_op jit(solution)/shard_map/ppermute | solution.py:68
  282.5 13.2 %collective-permute-start.20 = (bf16[192,1024]{1,0:T(8,128)(2,1)}, bf16[192,1024]{1,0:T(8,128)(2,1)}, u32[]{:S(2)}, u32[]{:S(2)}) collective-permute-start(bf16[192,1024]{1,0:T(8,128)(2,1)} %constant_dynamic-slice_fusion.5), channel_id=1, source_target_pairs={{0,1},{1,0},{2,3},{3,2},{4,5},{5,4},{6,7},{7,6},{8,9},{9,8},{10,11... | collective-permute-start | bytes 1179656 | tf_op jit(solution)/shard_map/ppermute | solution.py:62
  292.5 13.9 %collective-permute-start.26 = (bf16[192,1024]{1,0:T(8,128)(2,1)}, bf16[192,1024]{1,0:T(8,128)(2,1)}, u32[]{:S(2)}, u32[]{:S(2)}) collective-permute-start(bf16[192,1024]{1,0:T(8,128)(2,1)} %add_convert_fusion.14), channel_id=1, source_target_pairs={{0,4},{1,5},{2,6},{3,7},{4,0},{5,1},{6,2},{7,3},{8,12},{9,13},{10,... | collective-permute-start | bytes 1179656 | tf_op jit(solution)/shard_map/ppermute | solution.py:68
  297.0 15.7 %collective-permute-start.21 = (bf16[192,1024]{1,0:T(8,128)(2,1)S(1)}, bf16[192,1024]{1,0:T(8,128)(2,1)S(1)}, u32[]{:S(2)}, u32[]{:S(2)}) collective-permute-start(bf16[192,1024]{1,0:T(8,128)(2,1)S(1)} %add_convert_fusion.18), channel_id=1, source_target_pairs={{0,2},{1,3},{2,0},{3,1},{4,6},{5,7},{6,4},{7,5},{8,10},{9,11},{10,... | collective-permute-start | bytes 1179656 | tf_op jit(solution)/shard_map/ppermute | solution.py:68
  307.6 7.6 %collective-permute-start.27 = (bf16[192,1024]{1,0:T(8,128)(2,1)S(1)}, bf16[192,1024]{1,0:T(8,128)(2,1)S(1)}, u32[]{:S(2)}, u32[]{:S(2)}) collective-permute-start(bf16[192,1024]{1,0:T(8,128)(2,1)S(1)} %add_convert_fusion.13), channel_id=1, source_target_pairs={{0,1},{1,0},{2,3},{3,2},{4,5},{5,4},{6,7},{7,6},{8,9},{9,8},{10,11... | collective-permute-start | bytes 1179656 | tf_op jit(solution)/shard_map/ppermute | solution.py:72
  313.6 30.4 %collective-permute-start.22 = (bf16[192,1024]{1,0:T(8,128)(2,1)}, bf16[192,1024]{1,0:T(8,128)(2,1)}, u32[]{:S(2)}, u32[]{:S(2)}) collective-permute-start(bf16[192,1024]{1,0:T(8,128)(2,1)} %add_convert_fusion.17), channel_id=1, source_target_pairs={{0,4},{1,5},{2,6},{3,7},{4,0},{5,1},{6,2},{7,3},{8,12},{9,13},{10,... | collective-permute-start | bytes 1179656 | tf_op jit(solution)/shard_map/ppermute | solution.py:68
  333.1 6.2 %collective-permute-start.28 = (bf16[384,128]{1,0:T(8,128)(2,1)S(1)}, bf16[384,128]{1,0:T(8,128)(2,1)S(1)}, u32[]{:S(2)}, u32[]{:S(2)}) collective-permute-start(bf16[384,128]{1,0:T(8,128)(2,1)S(1)} %fusion.143), channel_id=1, source_target_pairs={{0,8},{8,0},{1,9},{9,1},{2,10},{10,2},{3,11},{11,3},{4,12},{12,4},... | collective-permute-start | bytes 294920 | tf_op jit(solution)/shard_map/ppermute | solution.py:82
  333.2 9.2 %collective-permute-start.29 = (bf16[384,128]{0,1:T(8,128)(2,1)S(1)}, bf16[384,128]{0,1:T(8,128)(2,1)S(1)}, u32[]{:S(2)}, u32[]{:S(2)}) collective-permute-start(bf16[384,128]{0,1:T(8,128)(2,1)S(1)} %fusion.145), channel_id=1, source_target_pairs={{0,8},{8,0},{1,9},{9,1},{2,10},{10,2},{3,11},{11,3},{4,12},{12,4},... | collective-permute-start | bytes 294920 | tf_op jit(solution)/shard_map/ppermute | solution.py:82
  343.9 3.2 collective-permute-start.30
  345.3 3.8 collective-permute-start.23
  347.2 11.2 %collective-permute-start.31 = (bf16[192,1024]{1,0:T(8,128)(2,1)S(1)}, bf16[192,1024]{1,0:T(8,128)(2,1)S(1)}, u32[]{:S(2)}, u32[]{:S(2)}) collective-permute-start(bf16[192,1024]{1,0:T(8,128)(2,1)S(1)} %add_convert_fusion.12), channel_id=1, source_target_pairs={{0,2},{1,3},{2,0},{3,1},{4,6},{5,7},{6,4},{7,5},{8,10},{9,11},{10,... | collective-permute-start | bytes 1179656 | tf_op jit(solution)/shard_map/ppermute | solution.py:68
  358.6 11.9 %collective-permute-start.32 = (bf16[192,1024]{1,0:T(8,128)(2,1)S(1)}, bf16[192,1024]{1,0:T(8,128)(2,1)S(1)}, u32[]{:S(2)}, u32[]{:S(2)}) collective-permute-start(bf16[192,1024]{1,0:T(8,128)(2,1)S(1)} %add_convert_fusion.11), channel_id=1, source_target_pairs={{0,4},{1,5},{2,6},{3,7},{4,0},{5,1},{6,2},{7,3},{8,12},{9,13},{10,... | collective-permute-start | bytes 1179656 | tf_op jit(solution)/shard_map/ppermute | solution.py:68
  370.6 2.6 collective-permute-start.33
  378.5 3.7 collective-permute-start.34
  383.2 12.2 %collective-permute-start.35 = (bf16[192,1024]{1,0:T(8,128)(2,1)}, bf16[192,1024]{1,0:T(8,128)(2,1)}, u32[]{:S(2)}, u32[]{:S(2)}) collective-permute-start(bf16[192,1024]{1,0:T(8,128)(2,1)} %add_convert_fusion.9), channel_id=1, source_target_pairs={{0,2},{1,3},{2,0},{3,1},{4,6},{5,7},{6,4},{7,5},{8,10},{9,11},{10,... | collective-permute-start | bytes 1179656 | tf_op jit(solution)/shard_map/ppermute | solution.py:68
  391.7 187.3 %reduce-scatter.9.cloned.1.call-start = ((), (), s32[]{:S(2)}) async-start(), calls=%async_computation.5 | async-start | bytes 3063808
  396.6 13.3 %collective-permute-start.36 = (bf16[192,1024]{1,0:T(8,128)(2,1)S(1)}, bf16[192,1024]{1,0:T(8,128)(2,1)S(1)}, u32[]{:S(2)}, u32[]{:S(2)}) collective-permute-start(bf16[192,1024]{1,0:T(8,128)(2,1)S(1)} %add_convert_fusion.8), channel_id=1, source_target_pairs={{0,4},{1,5},{2,6},{3,7},{4,0},{5,1},{6,2},{7,3},{8,12},{9,13},{10,... | collective-permute-start | bytes 1179656 | tf_op jit(solution)/shard_map/ppermute | solution.py:68
  410.2 2.2 collective-permute-start.37
  424.9 11.7 %collective-permute-start.38 = (bf16[384,128]{1,0:T(8,128)(2,1)S(1)}, bf16[384,128]{1,0:T(8,128)(2,1)S(1)}, u32[]{:S(2)}, u32[]{:S(2)}) collective-permute-start(bf16[384,128]{1,0:T(8,128)(2,1)S(1)} %fusion.147), channel_id=1, source_target_pairs={{0,8},{8,0},{1,9},{9,1},{2,10},{10,2},{3,11},{11,3},{4,12},{12,4},... | collective-permute-start | bytes 294920 | tf_op jit(solution)/shard_map/ppermute | solution.py:82
  429.3 12.1 %collective-permute-start.39 = (bf16[384,128]{0,1:T(8,128)(2,1)S(1)}, bf16[384,128]{0,1:T(8,128)(2,1)S(1)}, u32[]{:S(2)}, u32[]{:S(2)}) collective-permute-start(bf16[384,128]{0,1:T(8,128)(2,1)S(1)} %fusion.149), channel_id=1, source_target_pairs={{0,8},{8,0},{1,9},{9,1},{2,10},{10,2},{3,11},{11,3},{4,12},{12,4},... | collective-permute-start | bytes 294920 | tf_op jit(solution)/shard_map/ppermute | solution.py:82
  442.6 6.1 %collective-permute-start.40 = (bf16[192,1024]{1,0:T(8,128)(2,1)}, bf16[192,1024]{1,0:T(8,128)(2,1)}, u32[]{:S(2)}, u32[]{:S(2)}) collective-permute-start(bf16[192,1024]{1,0:T(8,128)(2,1)} %constant_dynamic-slice_fusion.1), channel_id=1, source_target_pairs={{0,1},{1,0},{2,3},{3,2},{4,5},{5,4},{6,7},{7,6},{8,9},{9,8},{10,11... | collective-permute-start | bytes 1179656 | tf_op jit(solution)/shard_map/ppermute | solution.py:62
  448.7 25.6 %collective-permute-start.51 = (bf16[2,2,1,2,64,512]{5,4,3,2,1,0:T(8,128)(2,1)}, bf16[2,2,1,2,64,512]{5,4,3,2,1,0:T(8,128)(2,1)}, u32[]{:S(2)}, u32[]{:S(2)}) collective-permute-start(bf16[2,2,1,2,64,512]{5,4,3,2,1,0:T(8,128)(2,1)} %constant_dynamic-slice_fusion), channel_id=1, source_target_pairs={{0,16},{16,0},{32,48},{48,32},{64,80},{80,64},{96,112},{112,96},{1... | collective-permute-start | bytes 1572872 | tf_op jit(solution)/shard_map/ppermute | solution.py:135
  450.7 25.1 %collective-permute-start.41 = (bf16[192,1024]{1,0:T(8,128)(2,1)}, bf16[192,1024]{1,0:T(8,128)(2,1)}, u32[]{:S(2)}, u32[]{:S(2)}) collective-permute-start(bf16[192,1024]{1,0:T(8,128)(2,1)} %add_convert_fusion.6), channel_id=1, source_target_pairs={{0,2},{1,3},{2,0},{3,1},{4,6},{5,7},{6,4},{7,5},{8,10},{9,11},{10,... | collective-permute-start | bytes 1179656 | tf_op jit(solution)/shard_map/ppermute | solution.py:68
  475.8 10.7 %collective-permute-start.52 = (bf16[2,1,1,2,64,512]{5,4,3,2,1,0:T(8,128)(2,1)S(1)}, bf16[2,1,1,2,64,512]{5,4,3,2,1,0:T(8,128)(2,1)S(1)}, u32[]{:S(2)}, u32[]{:S(2)}) collective-permute-start(bf16[2,1,1,2,64,512]{5,4,3,2,1,0:T(8,128)(2,1)S(1)} %dynamic-slice_convert_fusion), channel_id=1, source_target_pairs={{0,32},{16,48},{32,0},{48,16},{64,96},{80,112},{96,64},{112,80},{1... | collective-permute-start | bytes 786440 | tf_op jit(solution)/shard_map/ppermute | solution.py:135
  477.1 12.0 %collective-permute-start.42 = (bf16[192,1024]{1,0:T(8,128)(2,1)S(1)}, bf16[192,1024]{1,0:T(8,128)(2,1)S(1)}, u32[]{:S(2)}, u32[]{:S(2)}) collective-permute-start(bf16[192,1024]{1,0:T(8,128)(2,1)S(1)} %add_convert_fusion.5), channel_id=1, source_target_pairs={{0,4},{1,5},{2,6},{3,7},{4,0},{5,1},{6,2},{7,3},{8,12},{9,13},{10,... | collective-permute-start | bytes 1179656 | tf_op jit(solution)/shard_map/ppermute | solution.py:68
  486.6 6.6 %collective-permute-start.53 = (bf16[2,1,1,1,64,512]{5,4,3,2,1,0:T(8,128)(2,1)S(1)}, bf16[2,1,1,1,64,512]{5,4,3,2,1,0:T(8,128)(2,1)S(1)}, u32[]{:S(2)}, u32[]{:S(2)}) collective-permute-start(bf16[2,1,1,1,64,512]{5,4,3,2,1,0:T(8,128)(2,1)S(1)} %dynamic-slice_convert_fusion.1), channel_id=1, source_target_pairs={{0,8},{8,0},{1,9},{9,1},{2,10},{10,2},{3,11},{11,3},{4,12},{12,4},... | collective-permute-start | bytes 393224 | tf_op jit(solution)/shard_map/ppermute | solution.py:135
  489.3 3.9 collective-permute-start.43
  493.6 1.3 collective-permute-start.44
  493.7 6.1 %collective-permute-start.54 = (bf16[1,1,1,1,64,512]{5,4,3,2,1,0:T(8,128)(2,1)S(1)}, bf16[1,1,1,1,64,512]{5,4,3,2,1,0:T(8,128)(2,1)S(1)}, u32[]{:S(2)}, u32[]{:S(2)}) collective-permute-start(bf16[1,1,1,1,64,512]{5,4,3,2,1,0:T(8,128)(2,1)S(1)} %dynamic-slice_convert_fusion.10), channel_id=1, source_target_pairs={{0,64},{16,80},{32,96},{48,112},{64,0},{80,16},{96,32},{112,48},{1... | collective-permute-start | bytes 196616 | tf_op jit(solution)/shard_map/ppermute | solution.py:135
  494.9 4.9 collective-permute-start.45
  499.8 5.3 collective-permute-start.46
  505.2 6.2 %collective-permute-start.47 = (f32[2,2304]{1,0:T(2,128)S(1)}, f32[2,2304]{1,0:T(2,128)S(1)}, u32[]{:S(2)}, u32[]{:S(2)}) collective-permute-start(f32[2,2304]{1,0:T(2,128)S(1)} %add.463), channel_id=1, source_target_pairs={{0,8},{8,0},{1,9},{9,1},{2,10},{10,2},{3,11},{11,3},{4,12},{12,4},... | collective-permute-start | bytes 55304 | tf_op jit(solution)/shard_map/ppermute | solution.py:109
  511.4 4.0 collective-permute-start.48
  515.4 3.8 collective-permute-start.49
  519.3 5.3 collective-permute-start.50
  (152 other events, 786.7 us)
Sparse Core Ops, SparseCore 0:
  20.8 83.2 all-gather.2
  155.0 88.8 all-gather.4
  391.8 99.2 reduce-scatter.6
  493.6 85.4 reduce-scatter.8

commit v12 on v7

--- a/solution.py
+++ b/solution.py
@@ -261,13 +261,13 @@
     def scatter_layer(terms, layer_index):
         if layer_index > 0:
             return tuple(scatter_terms(terms))
-        early = scatter_terms(terms[3:])
+        early = scatter_terms(terms[4:])
         joined = shard_scatter(
-            jnp.concatenate([term.astype(jnp.bfloat16) for term in terms[:3]], axis=1)
+            jnp.concatenate([term.astype(jnp.bfloat16) for term in terms[:4]], axis=1)
         )
         late = []
         start = 0
-        for term in terms[:3]:
+        for term in terms[:4]:
             late.append(joined[:, start : start + term.shape[1]])
             start += term.shape[1]
         return tuple(late + early)

time: 573 us -> 560 us (0.977)
  waiting for transfers between devices: 307 us -> 297 us
    unnamed x5, waiting for transfers between devices: 47.9 us -> 0.07 us
    ppermute x4, waiting for transfers between devices: 28.7 us -> 58.4 us  [shard_scatter(): received = lax.ppermute(sent.astype(jnp.bfloat16), axis_name, pairs)]
    ppermute x16, waiting for transfers between devices: 107 us -> 116 us  [tp_sum(): received = lax.ppermute(mine, 'tp', pairs)]
    ppermute x16, starting transfers between devices: 28.3 us -> 35 us  [tp_sum(): received = lax.ppermute(mine, 'tp', pairs)]
    unnamed x342 -> x337, local copies, waits for them, and re-layouts: 31.8 us -> 30.5 us
  transfers between devices with their start and end apart: 59 -> 59, of which waited for: 38 -> 40; matrix products, arithmetic and copies ran while one was open for 24% -> 23% of each run, Pallas kernels for 0% -> 0%
where the time goes in v12:
time: 560 us; the launch traced here: 549 us
  waiting for transfers between devices  297 us (53%)
  starting transfers between devices  69 us (12%)
  matrix products  60.5 us (11%)
  other arithmetic  56.3 us (10%)
  local copies, waits for them, and re-layouts  50 us (9%)
  between operations  16.9 us (3%)
    ppermute x16, waiting for transfers between devices, tp_sum(): received = lax.ppermute(mine, 'tp', pairs)  116 us
    ppermute x4, waiting for transfers between devices, shard_scatter(): received = lax.ppermute(sent.astype(jnp.bfloat16), axis_name, pairs)  58.4 us
    ppermute x16, starting transfers between devices, tp_sum(): received = lax.ppermute(mine, 'tp', pairs)  35 us
    all_gather x1, waiting for transfers between devices, gather_layer(): full = lax.all_gather(joined, ('fsdp', 'ctx'), axis=0, tiled=True)  32.5 us
    unnamed x337, local copies, waits for them, and re-layouts  30.5 us
    ppermute x4, waiting for transfers between devices, shard_gather(): received = lax.ppermute(current, axis_name, pairs)  28.8 us
    all_gather x1, waiting for transfers between devices, gather_layer(): late_full = lax.all_gather(late, ('fsdp', 'ctx'), axis=0, tiled=True)  21.5 us
    ppermute x7, waiting for transfers between devices, all_sum(): total = total + lax.ppermute(total, axis_name, pairs)  19.1 us
  transfers between devices with their start and end apart: 59, of which 40 were waited for; matrix products, arithmetic and copies ran while one was open for 23% of the time, Pallas kernels for 0%

profile of v12, /device:TPU:0, one launch (start us, length us, event | category | flops | bytes accessed | tf_op | source)
XLA Modules:
  0.0 549.4 jit_solution(3257877664239719969)
XLA Ops:
  12.1 4.0 collective-permute-start
  23.6 3.1 collective-permute-start.1
  26.7 3.4 collective-permute-done.1
  31.9 8.7 %collective-permute-done.2 = bf16[2,1,1,2,64,512]{5,4,3,2,1,0:T(8,128)(2,1)S(1)} collective-permute-done((bf16[2,1,1,2,64,512]{5,4,3,2,1,0:T(8,128)(2,1)S(1)}, bf16[2,1,1,2,64,512]{5,4,3,2,1,0:T(8,128)(2,1)S(1)}, u32[]{:S(2)}, u32[]{:S(2)}) %collective-permute-start.2) | collective-permute-done | bytes 262176 | tf_op jit(solution)/shard_map/ppermute | solution.py:157
  40.6 2.3 collective-permute-start.3
  44.8 16.7 %collective-permute-done.3 = bf16[2,1,2,2,64,512]{5,4,3,2,1,0:T(8,128)(2,1)S(1)} collective-permute-done((bf16[2,1,2,2,64,512]{5,4,3,2,1,0:T(8,128)(2,1)S(1)}, bf16[2,1,2,2,64,512]{5,4,3,2,1,0:T(8,128)(2,1)S(1)}, u32[]{:S(2)}, u32[]{:S(2)}) %collective-permute-start.3) | collective-permute-done | bytes 524320 | tf_op jit(solution)/shard_map/ppermute | solution.py:157
  65.3 3.6 collective-permute-start.5
  70.8 3.9 collective-permute-done.5
  74.7 1.8 fusion.13
  78.8 21.5 %all-gather.3.cloned.1.call-done = bf16[1024,1408]{1,0:T(8,128)(2,1)} async-done(((bf16[64,1408]{1,0:T(8,128)(2,1)}), bf16[1024,1408]{1,0:T(8,128)(2,1)}) %all-gather.3.cloned.1.call-update) | async-done | bytes 2883600 | tf_op jit(solution)/shard_map/all_gather | solution.py:242
  102.6 1.9 collective-permute-done.6
  106.1 9.8 %collective-permute-done.7 = bf16[192,1024]{1,0:T(8,128)(2,1)S(1)} collective-permute-done((bf16[192,1024]{1,0:T(8,128)(2,1)S(1)}, bf16[192,1024]{1,0:T(8,128)(2,1)S(1)}, u32[]{:S(2)}, u32[]{:S(2)}) %collective-permute-start.7) | collective-permute-done | bytes 393248 | tf_op jit(solution)/shard_map/ppermute | solution.py:68
  116.0 3.4 collective-permute-start.8
  119.4 8.7 %collective-permute-done.8 = bf16[192,1024]{1,0:T(8,128)(2,1)S(1)} collective-permute-done((bf16[192,1024]{1,0:T(8,128)(2,1)S(1)}, bf16[192,1024]{1,0:T(8,128)(2,1)S(1)}, u32[]{:S(2)}, u32[]{:S(2)}) %collective-permute-start.8) | collective-permute-done | bytes 393248 | tf_op jit(solution)/shard_map/ppermute | solution.py:68
  139.0 9.9 %collective-permute-done.11 = bf16[192,1024]{1,0:T(8,128)(2,1)S(1)} collective-permute-done((bf16[192,1024]{1,0:T(8,128)(2,1)S(1)}, bf16[192,1024]{1,0:T(8,128)(2,1)S(1)}, u32[]{:S(2)}, u32[]{:S(2)}) %collective-permute-start.11) | collective-permute-done | bytes 393248 | tf_op jit(solution)/shard_map/ppermute | solution.py:68
  149.0 3.3 collective-permute-start.12
  152.4 8.7 %collective-permute-done.12 = bf16[192,1024]{1,0:T(8,128)(2,1)S(1)} collective-permute-done((bf16[192,1024]{1,0:T(8,128)(2,1)S(1)}, bf16[192,1024]{1,0:T(8,128)(2,1)S(1)}, u32[]{:S(2)}, u32[]{:S(2)}) %collective-permute-start.12) | collective-permute-done | bytes 393248 | tf_op jit(solution)/shard_map/ppermute | solution.py:68
  161.3 1.7 collective-permute-done.13
  165.1 32.5 %all-gather.5.cloned.1.call-done = bf16[1024,1920]{1,0:T(8,128)(2,1)} async-done(((bf16[64,1920]{1,0:T(8,128)(2,1)}), bf16[1024,1920]{1,0:T(8,128)(2,1)}) %all-gather.5.cloned.1.call-update) | async-done | bytes 3932176 | tf_op jit(solution)/shard_map/all_gather | solution.py:237
  197.6 2.0 convolution_convert_fusion.22
  203.8 3.0 collective-permute-start.15
  210.2 1.9 fusion.9
  212.3 2.4 convolution_convert_fusion.20
  219.3 9.8 %collective-permute-done.17 = bf16[192,1024]{1,0:T(8,128)(2,1)S(1)} collective-permute-done((bf16[192,1024]{1,0:T(8,128)(2,1)S(1)}, bf16[192,1024]{1,0:T(8,128)(2,1)S(1)}, u32[]{:S(2)}, u32[]{:S(2)}) %collective-permute-start.17) | collective-permute-done | bytes 393248 | tf_op jit(solution)/shard_map/ppermute | solution.py:68
  229.2 3.0 collective-permute-start.18
  232.2 9.0 %collective-permute-done.18 = bf16[192,1024]{1,0:T(8,128)(2,1)S(1)} collective-permute-done((bf16[192,1024]{1,0:T(8,128)(2,1)S(1)}, bf16[192,1024]{1,0:T(8,128)(2,1)S(1)}, u32[]{:S(2)}, u32[]{:S(2)}) %collective-permute-start.18) | collective-permute-done | bytes 393248 | tf_op jit(solution)/shard_map/ppermute | solution.py:68
  251.4 9.8 %collective-permute-done.25 = bf16[192,1024]{1,0:T(8,128)(2,1)S(1)} collective-permute-done((bf16[192,1024]{1,0:T(8,128)(2,1)S(1)}, bf16[192,1024]{1,0:T(8,128)(2,1)S(1)}, u32[]{:S(2)}, u32[]{:S(2)}) %collective-permute-start.25) | collective-permute-done | bytes 393248 | tf_op jit(solution)/shard_map/ppermute | solution.py:68
  261.3 3.0 collective-permute-start.26
  264.3 8.9 %collective-permute-done.26 = bf16[192,1024]{1,0:T(8,128)(2,1)S(1)} collective-permute-done((bf16[192,1024]{1,0:T(8,128)(2,1)S(1)}, bf16[192,1024]{1,0:T(8,128)(2,1)S(1)}, u32[]{:S(2)}, u32[]{:S(2)}) %collective-permute-start.26) | collective-permute-done | bytes 393248 | tf_op jit(solution)/shard_map/ppermute | solution.py:68
  276.2 1.7 multiply_reduce_fusion.3
  277.9 2.5 multiply_add_fusion.3
  283.5 2.9 collective-permute-start.29
  286.4 1.8 fusion.4
  295.0 1.9 copy.158
  296.9 1.9 fusion.73
  309.3 9.8 %collective-permute-done.31 = bf16[192,1024]{1,0:T(8,128)(2,1)S(1)} collective-permute-done((bf16[192,1024]{1,0:T(8,128)(2,1)S(1)}, bf16[192,1024]{1,0:T(8,128)(2,1)S(1)}, u32[]{:S(2)}, u32[]{:S(2)}) %collective-permute-start.31) | collective-permute-done | bytes 393248 | tf_op jit(solution)/shard_map/ppermute | solution.py:68
  319.3 2.9 collective-permute-start.32
  322.2 1.7 convolution_convert_fusion.8
  324.1 7.1 %collective-permute-done.32 = bf16[192,1024]{1,0:T(8,128)(2,1)S(1)} collective-permute-done((bf16[192,1024]{1,0:T(8,128)(2,1)S(1)}, bf16[192,1024]{1,0:T(8,128)(2,1)S(1)}, u32[]{:S(2)}, u32[]{:S(2)}) %collective-permute-start.32) | collective-permute-done | bytes 393248 | tf_op jit(solution)/shard_map/ppermute | solution.py:68
  336.8 1.9 multiply_convert_fusion.4
  341.8 4.3 copy.214
  346.2 2.0 add_convert_fusion.17
  348.2 2.7 collective-permute-start.22
  351.5 9.7 %collective-permute-done.22 = bf16[192,1024]{1,0:T(8,128)(2,1)} collective-permute-done((bf16[192,1024]{1,0:T(8,128)(2,1)}, bf16[192,1024]{1,0:T(8,128)(2,1)}, u32[]{:S(2)}, u32[]{:S(2)}) %collective-permute-start.22) | collective-permute-done | bytes 393248 | tf_op jit(solution)/shard_map/ppermute | solution.py:68
  362.7 1.8 fusion.31
  372.7 1.9 fusion.24
  374.6 7.7 %collective-permute-done.35 = bf16[192,1024]{1,0:T(8,128)(2,1)S(1)} collective-permute-done((bf16[192,1024]{1,0:T(8,128)(2,1)S(1)}, bf16[192,1024]{1,0:T(8,128)(2,1)S(1)}, u32[]{:S(2)}, u32[]{:S(2)}) %collective-permute-start.35) | collective-permute-done | bytes 393248 | tf_op jit(solution)/shard_map/ppermute | solution.py:68
  382.4 2.8 collective-permute-start.36
  388.0 6.6 %collective-permute-done.36 = bf16[192,1024]{1,0:T(8,128)(2,1)S(1)} collective-permute-done((bf16[192,1024]{1,0:T(8,128)(2,1)S(1)}, bf16[192,1024]{1,0:T(8,128)(2,1)S(1)}, u32[]{:S(2)}, u32[]{:S(2)}) %collective-permute-start.36) | collective-permute-done | bytes 393248 | tf_op jit(solution)/shard_map/ppermute | solution.py:68
  398.1 6.2 %copy.212 = bf16[1024,1920]{1,0:T(8,128)(2,1)} copy(bf16[1024,1920]{0,1:T(8,128)(2,1)} %fusion.19) | data formatting | bytes 7864320
  406.4 1.9 multiply_add_fusion.1
  422.4 2.4 collective-permute-start.38
  426.1 3.3 collective-permute-done.38
  440.1 29.2 %collective-permute-done.51 = bf16[2,2,1,2,64,768]{5,4,3,2,1,0:T(8,128)(2,1)S(1)} collective-permute-done((bf16[2,2,1,2,64,768]{5,4,3,2,1,0:T(8,128)(2,1)S(1)}, bf16[2,2,1,2,64,768]{5,4,3,2,1,0:T(8,128)(2,1)S(1)}, u32[]{:S(2)}, u32[]{:S(2)}) %collective-permute-start.51) | collective-permute-done | bytes 786464 | tf_op jit(solution)/shard_map/ppermute | solution.py:135
  469.9 3.5 collective-permute-start.42
  474.6 14.0 %collective-permute-done.52 = bf16[2,1,1,2,64,768]{5,4,3,2,1,0:T(8,128)(2,1)S(1)} collective-permute-done((bf16[2,1,1,2,64,768]{5,4,3,2,1,0:T(8,128)(2,1)S(1)}, bf16[2,1,1,2,64,768]{5,4,3,2,1,0:T(8,128)(2,1)S(1)}, u32[]{:S(2)}, u32[]{:S(2)}) %collective-permute-start.52) | collective-permute-done | bytes 393248 | tf_op jit(solution)/shard_map/ppermute | solution.py:135
  489.1 9.7 %collective-permute-done.53 = bf16[2,1,1,1,64,768]{5,4,3,2,1,0:T(8,128)(2,1)S(1)} collective-permute-done((bf16[2,1,1,1,64,768]{5,4,3,2,1,0:T(8,128)(2,1)S(1)}, bf16[2,1,1,1,64,768]{5,4,3,2,1,0:T(8,128)(2,1)S(1)}, u32[]{:S(2)}, u32[]{:S(2)}) %collective-permute-start.53) | collective-permute-done | bytes 196640 | tf_op jit(solution)/shard_map/ppermute | solution.py:135
  500.9 5.5 %collective-permute-done.54 = bf16[1,1,1,1,64,768]{5,4,3,2,1,0:T(8,128)(2,1)S(1)} collective-permute-done((bf16[1,1,1,1,64,768]{5,4,3,2,1,0:T(8,128)(2,1)S(1)}, bf16[1,1,1,1,64,768]{5,4,3,2,1,0:T(8,128)(2,1)S(1)}, u32[]{:S(2)}, u32[]{:S(2)}) %collective-permute-start.54) | collective-permute-done | bytes 98336 | tf_op jit(solution)/shard_map/ppermute | solution.py:135
  506.5 3.2 collective-permute-start.46
  509.7 2.1 collective-permute-done.46
  511.9 6.1 %collective-permute-done.47 = f32[2,2304]{1,0:T(2,128)S(1)} collective-permute-done((f32[2,2304]{1,0:T(2,128)S(1)}, f32[2,2304]{1,0:T(2,128)S(1)}, u32[]{:S(2)}, u32[]{:S(2)}) %collective-permute-start.47) | collective-permute-done | bytes 18464 | tf_op jit(solution)/shard_map/ppermute | solution.py:109
  518.6 4.1 collective-permute-done.48
  523.0 3.6 collective-permute-done.49
  529.5 2.5 collective-permute-done.50
  (631 shorter events, 157.6 us)
Async XLA Ops:
  7.2 93.1 %all-gather.3.cloned.1.call-start = ((), (), s32[]{:S(2)}) async-start(), calls=%async_computation.2 | async-start | bytes 3063808 | tf_op jit(solution)/shard_map/all_gather | solution.py:242
  10.5 187.1 %all-gather.5.cloned.1.call-start = ((), (), s32[]{:S(2)}) async-start(), calls=%async_computation.3 | async-start | bytes 4177920 | tf_op jit(solution)/shard_map/all_gather | solution.py:237
  12.1 11.5 %collective-permute-start = (bf16[1,1,1,1,64,512]{5,4,3,2,1,0:T(8,128)(2,1)S(1)}, bf16[1,1,1,1,64,512]{5,4,3,2,1,0:T(8,128)(2,1)S(1)}, u32[]{:S(2)}, u32[]{:S(2)}) collective-permute-start(bf16[1,1,1,1,64,512]{5,4,3,2,1,0:T(8,128)(2,1)S(1)} %get-tuple-element.125), channel_id=1, source_target_pairs={{0,8},{8,0},{1,9},{9,1},{2,10},{10,2},{3,11},{11,3},{4,12},{12,4},... | collective-permute-start | bytes 196616 | tf_op jit(solution)/shard_map/ppermute | solution.py:157
  21.4 511.7 %reduce-scatter.9.cloned.1.call-start = ((), (), s32[]{:S(2)}) async-start(), calls=%async_computation.5 | async-start | bytes 2506752
  21.5 42.8 %copy-start.137 = (f32[64]{0:T(128)}, f32[64]{0:T(128)S(1)}, u32[]{:S(2)}) copy-start(f32[64]{0:T(128)S(1)} %multiply_power_fusion) | copy-start | bytes 772
  23.1 47.4 %copy-start.34 = (f32[384,64]{1,0:T(8,128)}, f32[384,64]{1,0:T(8,128)S(1)}, u32[]{:S(2)}) copy-start(f32[384,64]{1,0:T(8,128)S(1)} %get-tuple-element.136) | copy-start | bytes 294916
  23.1 47.5 %copy-start.57 = (f32[384,64]{1,0:T(8,128)}, f32[384,64]{1,0:T(8,128)S(1)}, u32[]{:S(2)}) copy-start(f32[384,64]{1,0:T(8,128)S(1)} %get-tuple-element.135) | copy-start | bytes 294916
  23.6 6.6 %collective-permute-start.1 = (bf16[1,1,1,2,64,512]{5,4,3,2,1,0:T(8,128)(2,1)S(1)}, bf16[1,1,1,2,64,512]{5,4,3,2,1,0:T(8,128)(2,1)S(1)}, u32[]{:S(2)}, u32[]{:S(2)}) collective-permute-start(bf16[1,1,1,2,64,512]{5,4,3,2,1,0:T(8,128)(2,1)S(1)} %maximum_select_fusion.17), channel_id=1, source_target_pairs={{0,64},{16,80},{32,96},{48,112},{64,0},{80,16},{96,32},{112,48},{1... | collective-permute-start | bytes 393224 | tf_op jit(solution)/shard_map/ppermute | solution.py:157
  30.2 10.4 %collective-permute-start.2 = (bf16[2,1,1,2,64,512]{5,4,3,2,1,0:T(8,128)(2,1)S(1)}, bf16[2,1,1,2,64,512]{5,4,3,2,1,0:T(8,128)(2,1)S(1)}, u32[]{:S(2)}, u32[]{:S(2)}) collective-permute-start(bf16[2,1,1,2,64,512]{5,4,3,2,1,0:T(8,128)(2,1)S(1)} %maximum_select_fusion.11), channel_id=1, source_target_pairs={{0,16},{16,0},{32,48},{48,32},{64,80},{80,64},{96,112},{112,96},{1... | collective-permute-start | bytes 786440 | tf_op jit(solution)/shard_map/ppermute | solution.py:157
  40.6 20.9 %collective-permute-start.3 = (bf16[2,1,2,2,64,512]{5,4,3,2,1,0:T(8,128)(2,1)S(1)}, bf16[2,1,2,2,64,512]{5,4,3,2,1,0:T(8,128)(2,1)S(1)}, u32[]{:S(2)}, u32[]{:S(2)}) collective-permute-start(bf16[2,1,2,2,64,512]{5,4,3,2,1,0:T(8,128)(2,1)S(1)} %maximum_select_fusion.9), channel_id=1, source_target_pairs={{0,32},{16,48},{32,0},{48,16},{64,96},{80,112},{96,64},{112,80},{1... | collective-permute-start | bytes 1572872 | tf_op jit(solution)/shard_map/ppermute | solution.py:157
  63.6 13.1 %collective-permute-start.4 = (bf16[384,128]{1,0:T(8,128)(2,1)S(1)}, bf16[384,128]{1,0:T(8,128)(2,1)S(1)}, u32[]{:S(2)}, u32[]{:S(2)}) collective-permute-start(bf16[384,128]{1,0:T(8,128)(2,1)S(1)} %convolution_convert_fusion.23), channel_id=1, source_target_pairs={{0,8},{8,0},{1,9},{9,1},{2,10},{10,2},{3,11},{11,3},{4,12},{12,4},... | collective-permute-start | bytes 294920 | tf_op jit(solution)/shard_map/ppermute | solution.py:82
  65.3 9.4 %collective-permute-start.5 = (bf16[384,128]{1,0:T(8,128)(2,1)S(1)}, bf16[384,128]{1,0:T(8,128)(2,1)}, u32[]{:S(2)}, u32[]{:S(2)}) collective-permute-start(bf16[384,128]{1,0:T(8,128)(2,1)S(1)} %pad_maximum_fusion.11), channel_id=1, source_target_pairs={{0,8},{8,0},{1,9},{9,1},{2,10},{10,2},{3,11},{11,3},{4,12},{12,4},... | collective-permute-start | bytes 294920 | tf_op jit(solution)/shard_map/ppermute | solution.py:82
  102.6 1.9 collective-permute-start.6
  104.7 11.2 %collective-permute-start.7 = (bf16[192,1024]{1,0:T(8,128)(2,1)S(1)}, bf16[192,1024]{1,0:T(8,128)(2,1)S(1)}, u32[]{:S(2)}, u32[]{:S(2)}) collective-permute-start(bf16[192,1024]{1,0:T(8,128)(2,1)S(1)} %add_convert_fusion.27), channel_id=1, source_target_pairs={{0,2},{1,3},{2,0},{3,1},{4,6},{5,7},{6,4},{7,5},{8,10},{9,11},{10,... | collective-permute-start | bytes 1179656 | tf_op jit(solution)/shard_map/ppermute | solution.py:68
  116.0 12.0 %collective-permute-start.8 = (bf16[192,1024]{1,0:T(8,128)(2,1)S(1)}, bf16[192,1024]{1,0:T(8,128)(2,1)S(1)}, u32[]{:S(2)}, u32[]{:S(2)}) collective-permute-start(bf16[192,1024]{1,0:T(8,128)(2,1)S(1)} %add_convert_fusion.26), channel_id=1, source_target_pairs={{0,4},{1,5},{2,6},{3,7},{4,0},{5,1},{6,2},{7,3},{8,12},{9,13},{10,... | collective-permute-start | bytes 1179656 | tf_op jit(solution)/shard_map/ppermute | solution.py:68
  128.2 2.0 collective-permute-start.9
  135.7 1.8 collective-permute-start.10
  137.7 11.2 %collective-permute-start.11 = (bf16[192,1024]{1,0:T(8,128)(2,1)S(1)}, bf16[192,1024]{1,0:T(8,128)(2,1)S(1)}, u32[]{:S(2)}, u32[]{:S(2)}) collective-permute-start(bf16[192,1024]{1,0:T(8,128)(2,1)S(1)} %add_convert_fusion.24), channel_id=1, source_target_pairs={{0,2},{1,3},{2,0},{3,1},{4,6},{5,7},{6,4},{7,5},{8,10},{9,11},{10,... | collective-permute-start | bytes 1179656 | tf_op jit(solution)/shard_map/ppermute | solution.py:68
  149.0 12.0 %collective-permute-start.12 = (bf16[192,1024]{1,0:T(8,128)(2,1)S(1)}, bf16[192,1024]{1,0:T(8,128)(2,1)S(1)}, u32[]{:S(2)}, u32[]{:S(2)}) collective-permute-start(bf16[192,1024]{1,0:T(8,128)(2,1)S(1)} %add_convert_fusion.23), channel_id=1, source_target_pairs={{0,4},{1,5},{2,6},{3,7},{4,0},{5,1},{6,2},{7,3},{8,12},{9,13},{10,... | collective-permute-start | bytes 1179656 | tf_op jit(solution)/shard_map/ppermute | solution.py:68
  161.2 1.8 collective-permute-start.13
  165.1 41.7 %copy-start.12 = (bf16[384,1024]{1,0:T(8,128)(2,1)}, bf16[384,1024]{1,0:T(8,128)(2,1)S(1)}, u32[]{:S(2)}) copy-start(bf16[384,1024]{1,0:T(8,128)(2,1)S(1)} %get-tuple-element.75) | copy-start | bytes 2359300
  165.1 36.9 %copy-start.144 = (f32[128]{0:T(128)S(1)}, f32[128]{0:T(128)}, u32[]{:S(2)}) copy-start(f32[128]{0:T(128)} %get-tuple-element.139) | copy-start | bytes 1540
  199.6 12.7 %collective-permute-start.14 = (bf16[384,128]{1,0:T(8,128)(2,1)}, bf16[384,128]{1,0:T(8,128)(2,1)}, u32[]{:S(2)}, u32[]{:S(2)}) collective-permute-start(bf16[384,128]{1,0:T(8,128)(2,1)} %convolution_convert_fusion.22), channel_id=1, source_target_pairs={{0,8},{8,0},{1,9},{9,1},{2,10},{10,2},{3,11},{11,3},{4,12},{12,4},... | collective-permute-start | bytes 294920 | tf_op jit(solution)/shard_map/ppermute | solution.py:82
  203.8 6.5 %collective-permute-start.15 = (bf16[384,128]{1,0:T(8,128)(2,1)}, bf16[384,128]{1,0:T(8,128)(2,1)}, u32[]{:S(2)}, u32[]{:S(2)}) collective-permute-start(bf16[384,128]{1,0:T(8,128)(2,1)} %pad_maximum_fusion.12), channel_id=1, source_target_pairs={{0,8},{8,0},{1,9},{9,1},{2,10},{10,2},{3,11},{11,3},{4,12},{12,4},... | collective-permute-start | bytes 294920 | tf_op jit(solution)/shard_map/ppermute | solution.py:82
  215.9 1.8 collective-permute-start.16
  217.8 11.2 %collective-permute-start.17 = (bf16[192,1024]{1,0:T(8,128)(2,1)S(1)}, bf16[192,1024]{1,0:T(8,128)(2,1)S(1)}, u32[]{:S(2)}, u32[]{:S(2)}) collective-permute-start(bf16[192,1024]{1,0:T(8,128)(2,1)S(1)} %add_convert_fusion.21), channel_id=1, source_target_pairs={{0,2},{1,3},{2,0},{3,1},{4,6},{5,7},{6,4},{7,5},{8,10},{9,11},{10,... | collective-permute-start | bytes 1179656 | tf_op jit(solution)/shard_map/ppermute | solution.py:68
  229.2 11.9 %collective-permute-start.18 = (bf16[192,1024]{1,0:T(8,128)(2,1)S(1)}, bf16[192,1024]{1,0:T(8,128)(2,1)S(1)}, u32[]{:S(2)}, u32[]{:S(2)}) collective-permute-start(bf16[192,1024]{1,0:T(8,128)(2,1)S(1)} %add_convert_fusion.20), channel_id=1, source_target_pairs={{0,4},{1,5},{2,6},{3,7},{4,0},{5,1},{6,2},{7,3},{8,12},{9,13},{10,... | collective-permute-start | bytes 1179656 | tf_op jit(solution)/shard_map/ppermute | solution.py:68
  241.3 2.2 collective-permute-start.19
  248.0 1.8 collective-permute-start.24
  249.9 11.2 %collective-permute-start.25 = (bf16[192,1024]{1,0:T(8,128)(2,1)S(1)}, bf16[192,1024]{1,0:T(8,128)(2,1)S(1)}, u32[]{:S(2)}, u32[]{:S(2)}) collective-permute-start(bf16[192,1024]{1,0:T(8,128)(2,1)S(1)} %add_convert_fusion.15), channel_id=1, source_target_pairs={{0,2},{1,3},{2,0},{3,1},{4,6},{5,7},{6,4},{7,5},{8,10},{9,11},{10,... | collective-permute-start | bytes 1179656 | tf_op jit(solution)/shard_map/ppermute | solution.py:68
  261.3 11.9 %collective-permute-start.26 = (bf16[192,1024]{1,0:T(8,128)(2,1)S(1)}, bf16[192,1024]{1,0:T(8,128)(2,1)S(1)}, u32[]{:S(2)}, u32[]{:S(2)}) collective-permute-start(bf16[192,1024]{1,0:T(8,128)(2,1)S(1)} %add_convert_fusion.14), channel_id=1, source_target_pairs={{0,4},{1,5},{2,6},{3,7},{4,0},{5,1},{6,2},{7,3},{8,12},{9,13},{10,... | collective-permute-start | bytes 1179656 | tf_op jit(solution)/shard_map/ppermute | solution.py:68
  274.1 2.1 collective-permute-start.27
  283.5 21.0 %collective-permute-start.29 = (bf16[384,128]{0,1:T(8,128)(2,1)}, bf16[384,128]{0,1:T(8,128)(2,1)}, u32[]{:S(2)}, u32[]{:S(2)}) collective-permute-start(bf16[384,128]{0,1:T(8,128)(2,1)} %fusion.145), channel_id=1, source_target_pairs={{0,8},{8,0},{1,9},{9,1},{2,10},{10,2},{3,11},{11,3},{4,12},{12,4},... | collective-permute-start | bytes 294920 | tf_op jit(solution)/shard_map/ppermute | solution.py:82
  291.1 9.2 %collective-permute-start.28 = (bf16[384,128]{1,0:T(8,128)(2,1)}, bf16[384,128]{1,0:T(8,128)(2,1)}, u32[]{:S(2)}, u32[]{:S(2)}) collective-permute-start(bf16[384,128]{1,0:T(8,128)(2,1)} %fusion.143), channel_id=1, source_target_pairs={{0,8},{8,0},{1,9},{9,1},{2,10},{10,2},{3,11},{11,3},{4,12},{12,4},... | collective-permute-start | bytes 294920 | tf_op jit(solution)/shard_map/ppermute | solution.py:82
  305.9 1.8 collective-permute-start.30
  307.9 11.2 %collective-permute-start.31 = (bf16[192,1024]{1,0:T(8,128)(2,1)S(1)}, bf16[192,1024]{1,0:T(8,128)(2,1)S(1)}, u32[]{:S(2)}, u32[]{:S(2)}) collective-permute-start(bf16[192,1024]{1,0:T(8,128)(2,1)S(1)} %add_convert_fusion.12), channel_id=1, source_target_pairs={{0,2},{1,3},{2,0},{3,1},{4,6},{5,7},{6,4},{7,5},{8,10},{9,11},{10,... | collective-permute-start | bytes 1179656 | tf_op jit(solution)/shard_map/ppermute | solution.py:68
  319.3 11.9 %collective-permute-start.32 = (bf16[192,1024]{1,0:T(8,128)(2,1)S(1)}, bf16[192,1024]{1,0:T(8,128)(2,1)S(1)}, u32[]{:S(2)}, u32[]{:S(2)}) collective-permute-start(bf16[192,1024]{1,0:T(8,128)(2,1)S(1)} %add_convert_fusion.11), channel_id=1, source_target_pairs={{0,4},{1,5},{2,6},{3,7},{4,0},{5,1},{6,2},{7,3},{8,12},{9,13},{10,... | collective-permute-start | bytes 1179656 | tf_op jit(solution)/shard_map/ppermute | solution.py:68
  324.0 7.4 %collective-permute-start.20 = (bf16[192,1024]{1,0:T(8,128)(2,1)S(1)}, bf16[192,1024]{1,0:T(8,128)(2,1)S(1)}, u32[]{:S(2)}, u32[]{:S(2)}) collective-permute-start(bf16[192,1024]{1,0:T(8,128)(2,1)S(1)} %constant_dynamic-slice_fusion.5), channel_id=1, source_target_pairs={{0,1},{1,0},{2,3},{3,2},{4,5},{5,4},{6,7},{7,6},{8,9},{9,8},{10,11... | collective-permute-start | bytes 1179656 | tf_op jit(solution)/shard_map/ppermute | solution.py:62
  331.3 2.3 collective-permute-start.33
  332.3 13.9 %collective-permute-start.21 = (bf16[192,1024]{1,0:T(8,128)(2,1)}, bf16[192,1024]{1,0:T(8,128)(2,1)}, u32[]{:S(2)}, u32[]{:S(2)}) collective-permute-start(bf16[192,1024]{1,0:T(8,128)(2,1)} %add_convert_fusion.18), channel_id=1, source_target_pairs={{0,2},{1,3},{2,0},{3,1},{4,6},{5,7},{6,4},{7,5},{8,10},{9,11},{10,... | collective-permute-start | bytes 1179656 | tf_op jit(solution)/shard_map/ppermute | solution.py:68
  346.2 188.3 %reduce-scatter.7.cloned.1.call-start = ((), (), s32[]{:S(2)}) async-start(), calls=%async_computation.4 | async-start | bytes 4177920 | tf_op jit(solution)/shard_map/reduce_scatter | solution.py:253
  348.2 13.1 %collective-permute-start.22 = (bf16[192,1024]{1,0:T(8,128)(2,1)}, bf16[192,1024]{1,0:T(8,128)(2,1)}, u32[]{:S(2)}, u32[]{:S(2)}) collective-permute-start(bf16[192,1024]{1,0:T(8,128)(2,1)} %add_convert_fusion.17), channel_id=1, source_target_pairs={{0,4},{1,5},{2,6},{3,7},{4,0},{5,1},{6,2},{7,3},{8,12},{9,13},{10,... | collective-permute-start | bytes 1179656 | tf_op jit(solution)/shard_map/ppermute | solution.py:68
  362.6 6.4 %collective-permute-start.23 = (bf16[192,1024]{1,0:T(8,128)(2,1)S(1)}, bf16[192,1024]{1,0:T(8,128)(2,1)S(1)}, u32[]{:S(2)}, u32[]{:S(2)}) collective-permute-start(bf16[192,1024]{1,0:T(8,128)(2,1)S(1)} %add_convert_fusion.16), channel_id=1, source_target_pairs={{0,1},{1,0},{2,3},{3,2},{4,5},{5,4},{6,7},{7,6},{8,9},{9,8},{10,11... | collective-permute-start | bytes 1179656 | tf_op jit(solution)/shard_map/ppermute | solution.py:72
  368.4 2.3 collective-permute-start.34
  370.8 11.4 %collective-permute-start.35 = (bf16[192,1024]{1,0:T(8,128)(2,1)S(1)}, bf16[192,1024]{1,0:T(8,128)(2,1)S(1)}, u32[]{:S(2)}, u32[]{:S(2)}) collective-permute-start(bf16[192,1024]{1,0:T(8,128)(2,1)S(1)} %add_convert_fusion.9), channel_id=1, source_target_pairs={{0,2},{1,3},{2,0},{3,1},{4,6},{5,7},{6,4},{7,5},{8,10},{9,11},{10,... | collective-permute-start | bytes 1179656 | tf_op jit(solution)/shard_map/ppermute | solution.py:68
  382.4 12.3 %collective-permute-start.36 = (bf16[192,1024]{1,0:T(8,128)(2,1)S(1)}, bf16[192,1024]{1,0:T(8,128)(2,1)S(1)}, u32[]{:S(2)}, u32[]{:S(2)}) collective-permute-start(bf16[192,1024]{1,0:T(8,128)(2,1)S(1)} %add_convert_fusion.8), channel_id=1, source_target_pairs={{0,4},{1,5},{2,6},{3,7},{4,0},{5,1},{6,2},{7,3},{8,12},{9,13},{10,... | collective-permute-start | bytes 1179656 | tf_op jit(solution)/shard_map/ppermute | solution.py:68
  394.8 9.6 %collective-permute-start.37 = (bf16[192,1024]{1,0:T(8,128)(2,1)S(1)}, bf16[192,1024]{1,0:T(8,128)(2,1)S(1)}, u32[]{:S(2)}, u32[]{:S(2)}) collective-permute-start(bf16[192,1024]{1,0:T(8,128)(2,1)S(1)} %add_convert_fusion.7), channel_id=1, source_target_pairs={{0,1},{1,0},{2,3},{3,2},{4,5},{5,4},{6,7},{7,6},{8,9},{9,8},{10,11... | collective-permute-start | bytes 1179656 | tf_op jit(solution)/shard_map/ppermute | solution.py:72
  422.4 7.0 %collective-permute-start.38 = (bf16[384,128]{1,0:T(8,128)(2,1)S(1)}, bf16[384,128]{1,0:T(8,128)(2,1)S(1)}, u32[]{:S(2)}, u32[]{:S(2)}) collective-permute-start(bf16[384,128]{1,0:T(8,128)(2,1)S(1)} %fusion.147), channel_id=1, source_target_pairs={{0,8},{8,0},{1,9},{9,1},{2,10},{10,2},{3,11},{11,3},{4,12},{12,4},... | collective-permute-start | bytes 294920 | tf_op jit(solution)/shard_map/ppermute | solution.py:82
  424.8 6.6 %collective-permute-start.39 = (bf16[384,128]{0,1:T(8,128)(2,1)S(1)}, bf16[384,128]{0,1:T(8,128)(2,1)S(1)}, u32[]{:S(2)}, u32[]{:S(2)}) collective-permute-start(bf16[384,128]{0,1:T(8,128)(2,1)S(1)} %fusion.149), channel_id=1, source_target_pairs={{0,8},{8,0},{1,9},{9,1},{2,10},{10,2},{3,11},{11,3},{4,12},{12,4},... | collective-permute-start | bytes 294920 | tf_op jit(solution)/shard_map/ppermute | solution.py:82
  435.6 33.8 %collective-permute-start.51 = (bf16[2,2,1,2,64,768]{5,4,3,2,1,0:T(8,128)(2,1)S(1)}, bf16[2,2,1,2,64,768]{5,4,3,2,1,0:T(8,128)(2,1)S(1)}, u32[]{:S(2)}, u32[]{:S(2)}) collective-permute-start(bf16[2,2,1,2,64,768]{5,4,3,2,1,0:T(8,128)(2,1)S(1)} %constant_dynamic-slice_fusion), channel_id=1, source_target_pairs={{0,16},{16,0},{32,48},{48,32},{64,80},{80,64},{96,112},{112,96},{1... | collective-permute-start | bytes 2359304 | tf_op jit(solution)/shard_map/ppermute | solution.py:135
  436.7 2.1 collective-permute-start.40
  439.0 30.7 %collective-permute-start.41 = (bf16[192,1024]{1,0:T(8,128)(2,1)S(1)}, bf16[192,1024]{1,0:T(8,128)(2,1)S(1)}, u32[]{:S(2)}, u32[]{:S(2)}) collective-permute-start(bf16[192,1024]{1,0:T(8,128)(2,1)S(1)} %add_convert_fusion.6), channel_id=1, source_target_pairs={{0,2},{1,3},{2,0},{3,1},{4,6},{5,7},{6,4},{7,5},{8,10},{9,11},{10,... | collective-permute-start | bytes 1179656 | tf_op jit(solution)/shard_map/ppermute | solution.py:68
  469.6 19.0 %collective-permute-start.52 = (bf16[2,1,1,2,64,768]{5,4,3,2,1,0:T(8,128)(2,1)S(1)}, bf16[2,1,1,2,64,768]{5,4,3,2,1,0:T(8,128)(2,1)S(1)}, u32[]{:S(2)}, u32[]{:S(2)}) collective-permute-start(bf16[2,1,1,2,64,768]{5,4,3,2,1,0:T(8,128)(2,1)S(1)} %dynamic-slice_convert_fusion), channel_id=1, source_target_pairs={{0,32},{16,48},{32,0},{48,16},{64,96},{80,112},{96,64},{112,80},{1... | collective-permute-start | bytes 1179656 | tf_op jit(solution)/shard_map/ppermute | solution.py:135
  469.9 19.0 %collective-permute-start.42 = (bf16[192,1024]{1,0:T(8,128)(2,1)S(1)}, bf16[192,1024]{1,0:T(8,128)(2,1)S(1)}, u32[]{:S(2)}, u32[]{:S(2)}) collective-permute-start(bf16[192,1024]{1,0:T(8,128)(2,1)S(1)} %add_convert_fusion.5), channel_id=1, source_target_pairs={{0,4},{1,5},{2,6},{3,7},{4,0},{5,1},{6,2},{7,3},{8,12},{9,13},{10,... | collective-permute-start | bytes 1179656 | tf_op jit(solution)/shard_map/ppermute | solution.py:68
  488.7 10.1 %collective-permute-start.53 = (bf16[2,1,1,1,64,768]{5,4,3,2,1,0:T(8,128)(2,1)S(1)}, bf16[2,1,1,1,64,768]{5,4,3,2,1,0:T(8,128)(2,1)S(1)}, u32[]{:S(2)}, u32[]{:S(2)}) collective-permute-start(bf16[2,1,1,1,64,768]{5,4,3,2,1,0:T(8,128)(2,1)S(1)} %dynamic-slice_convert_fusion.1), channel_id=1, source_target_pairs={{0,8},{8,0},{1,9},{9,1},{2,10},{10,2},{3,11},{11,3},{4,12},{12,4},... | collective-permute-start | bytes 589832 | tf_op jit(solution)/shard_map/ppermute | solution.py:135
  489.0 9.9 %collective-permute-start.43 = (bf16[192,1024]{1,0:T(8,128)(2,1)S(1)}, bf16[192,1024]{1,0:T(8,128)(2,1)S(1)}, u32[]{:S(2)}, u32[]{:S(2)}) collective-permute-start(bf16[192,1024]{1,0:T(8,128)(2,1)S(1)} %add_convert_fusion.4), channel_id=1, source_target_pairs={{0,1},{1,0},{2,3},{3,2},{4,5},{5,4},{6,7},{7,6},{8,9},{9,8},{10,11... | collective-permute-start | bytes 1179656 | tf_op jit(solution)/shard_map/ppermute | solution.py:72
  499.5 1.3 collective-permute-start.44
  499.6 6.8 %collective-permute-start.54 = (bf16[1,1,1,1,64,768]{5,4,3,2,1,0:T(8,128)(2,1)S(1)}, bf16[1,1,1,1,64,768]{5,4,3,2,1,0:T(8,128)(2,1)S(1)}, u32[]{:S(2)}, u32[]{:S(2)}) collective-permute-start(bf16[1,1,1,1,64,768]{5,4,3,2,1,0:T(8,128)(2,1)S(1)} %dynamic-slice_convert_fusion.2), channel_id=1, source_target_pairs={{0,64},{16,80},{32,96},{48,112},{64,0},{80,16},{96,32},{112,48},{1... | collective-permute-start | bytes 294920 | tf_op jit(solution)/shard_map/ppermute | solution.py:135
  500.8 5.6 %collective-permute-start.45 = (f32[2,2304]{1,0:T(2,128)S(1)}, f32[2,2304]{1,0:T(2,128)S(1)}, u32[]{:S(2)}, u32[]{:S(2)}) collective-permute-start(f32[2,2304]{1,0:T(2,128)S(1)} %fusion.247), channel_id=1, source_target_pairs={{0,2},{1,3},{2,0},{3,1},{4,6},{5,7},{6,4},{7,5},{8,10},{9,11},{10,... | collective-permute-start | bytes 55304 | tf_op jit(solution)/shard_map/ppermute | solution.py:109
  506.5 5.3 collective-permute-start.46
  511.8 6.2 %collective-permute-start.47 = (f32[2,2304]{1,0:T(2,128)S(1)}, f32[2,2304]{1,0:T(2,128)S(1)}, u32[]{:S(2)}, u32[]{:S(2)}) collective-permute-start(f32[2,2304]{1,0:T(2,128)S(1)} %add.463), channel_id=1, source_target_pairs={{0,8},{8,0},{1,9},{9,1},{2,10},{10,2},{3,11},{11,3},{4,12},{12,4},... | collective-permute-start | bytes 55304 | tf_op jit(solution)/shard_map/ppermute | solution.py:109
  518.1 4.6 collective-permute-start.48
  522.7 3.9 collective-permute-start.49
  526.6 5.3 collective-permute-start.50
  (155 other events, 824.2 us)
Sparse Core Ops, SparseCore 0:
  10.6 89.6 all-gather.2
  102.0 95.5 all-gather.4
  346.3 82.8 reduce-scatter.8
  431.5 98.2 reduce-scatter.6

commit v13 on v12

--- a/solution.py
+++ b/solution.py
@@ -261,16 +261,16 @@
     def scatter_layer(terms, layer_index):
         if layer_index > 0:
             return tuple(scatter_terms(terms))
-        early = scatter_terms(terms[4:])
+        early = scatter_terms(terms[4:6])
         joined = shard_scatter(
-            jnp.concatenate([term.astype(jnp.bfloat16) for term in terms[:4]], axis=1)
+            jnp.concatenate([term.astype(jnp.bfloat16) for term in terms[:4] + terms[6:]], axis=1)
         )
         late = []
         start = 0
-        for term in terms[:4]:
+        for term in terms[:4] + terms[6:]:
             late.append(joined[:, start : start + term.shape[1]])
             start += term.shape[1]
-        return tuple(late + early)
+        return tuple(late[:4] + early + late[4:])
 
     kept_weights = []
     stored_layers = []

time: 560 us -> 583 us (1.041)
  other arithmetic: 56.3 us -> 68.5 us
  matrix products: 60.5 us -> 67.7 us
    ppermute x16, waiting for transfers between devices: 116 us -> 132 us  [tp_sum(): received = lax.ppermute(mine, 'tp', pairs)]
    unnamed x337 -> x348, local copies, waits for them, and re-layouts: 30.5 us -> 26.3 us
  transfers between devices with their start and end apart: 59 -> 59, of which waited for: 40 -> 38; matrix products, arithmetic and copies ran while one was open for 23% -> 27% of each run, Pallas kernels for 0% -> 0%
where the time goes in v13:
time: 583 us; the launch traced here: 573 us
  waiting for transfers between devices  302 us (52%)
  other arithmetic  68.5 us (12%)
  matrix products  67.7 us (12%)
  starting transfers between devices  66.4 us (11%)
  local copies, waits for them, and re-layouts  51.7 us (9%)
  between operations  17 us (3%)
    ppermute x16, waiting for transfers between devices, tp_sum(): received = lax.ppermute(mine, 'tp', pairs)  132 us
    ppermute x4, waiting for transfers between devices, shard_scatter(): received = lax.ppermute(sent.astype(jnp.bfloat16), axis_name, pairs)  56.5 us
    all_gather x1, waiting for transfers between devices, gather_layer(): full = lax.all_gather(joined, ('fsdp', 'ctx'), axis=0, tiled=True)  32.7 us
    ppermute x16, starting transfers between devices, tp_sum(): received = lax.ppermute(mine, 'tp', pairs)  31.2 us
    ppermute x4, waiting for transfers between devices, shard_gather(): received = lax.ppermute(current, axis_name, pairs)  29.5 us
    unnamed x348, local copies, waits for them, and re-layouts  26.3 us
    dot_general x14, matrix products, contract_first(): lax.dot_general(left_side, right_side, (((0,), (0,)), ((), ())), preferre...  17.3 us
    all_gather x1, waiting for transfers between devices, gather_layer(): late_full = lax.all_gather(late, ('fsdp', 'ctx'), axis=0, tiled=True)  16.2 us
  transfers between devices with their start and end apart: 59, of which 38 were waited for; matrix products, arithmetic and copies ran while one was open for 27% of the time, Pallas kernels for 0%

profile of v13, /device:TPU:0, one launch (start us, length us, event | category | flops | bytes accessed | tf_op | source)
XLA Modules:
  0.0 573.2 jit_solution(581800801684039395)
XLA Ops:
  12.1 4.0 collective-permute-start
  23.6 3.1 collective-permute-start.1
  26.8 3.4 collective-permute-done.1
  31.8 9.0 %collective-permute-done.2 = bf16[2,1,1,2,64,512]{5,4,3,2,1,0:T(8,128)(2,1)S(1)} collective-permute-done((bf16[2,1,1,2,64,512]{5,4,3,2,1,0:T(8,128)(2,1)S(1)}, bf16[2,1,1,2,64,512]{5,4,3,2,1,0:T(8,128)(2,1)S(1)}, u32[]{:S(2)}, u32[]{:S(2)}) %collective-permute-start.2) | collective-permute-done | bytes 262176 | tf_op jit(solution)/shard_map/ppermute | solution.py:157
  40.9 1.9 collective-permute-start.3
  44.7 17.1 %collective-permute-done.3 = bf16[2,1,2,2,64,512]{5,4,3,2,1,0:T(8,128)(2,1)S(1)} collective-permute-done((bf16[2,1,2,2,64,512]{5,4,3,2,1,0:T(8,128)(2,1)S(1)}, bf16[2,1,2,2,64,512]{5,4,3,2,1,0:T(8,128)(2,1)S(1)}, u32[]{:S(2)}, u32[]{:S(2)}) %collective-permute-start.3) | collective-permute-done | bytes 524320 | tf_op jit(solution)/shard_map/ppermute | solution.py:157
  66.5 3.5 collective-permute-start.5
  71.7 6.5 %collective-permute-done.5 = bf16[384,128]{1,0:T(8,128)(2,1)} collective-permute-done((bf16[384,128]{1,0:T(8,128)(2,1)}, bf16[384,128]{1,0:T(8,128)(2,1)}, u32[]{:S(2)}, u32[]{:S(2)}) %collective-permute-start.5) | collective-permute-done | bytes 98336 | tf_op jit(solution)/shard_map/ppermute | solution.py:82
  83.3 16.2 %all-gather.3.cloned.1.call-done = bf16[1024,1408]{1,0:T(8,128)(2,1)} async-done(((bf16[64,1408]{1,0:T(8,128)(2,1)}), bf16[1024,1408]{1,0:T(8,128)(2,1)}) %all-gather.3.cloned.1.call-update) | async-done | bytes 2883600 | tf_op jit(solution)/shard_map/all_gather | solution.py:242
  101.8 1.9 collective-permute-done.6
  103.8 2.5 collective-permute-start.7
  106.4 9.4 %collective-permute-done.7 = bf16[192,1024]{1,0:T(8,128)(2,1)S(1)} collective-permute-done((bf16[192,1024]{1,0:T(8,128)(2,1)S(1)}, bf16[192,1024]{1,0:T(8,128)(2,1)S(1)}, u32[]{:S(2)}, u32[]{:S(2)}) %collective-permute-start.7) | collective-permute-done | bytes 393248 | tf_op jit(solution)/shard_map/ppermute | solution.py:68
  115.9 3.3 collective-permute-start.8
  119.2 9.1 %collective-permute-done.8 = bf16[192,1024]{1,0:T(8,128)(2,1)S(1)} collective-permute-done((bf16[192,1024]{1,0:T(8,128)(2,1)S(1)}, bf16[192,1024]{1,0:T(8,128)(2,1)S(1)}, u32[]{:S(2)}, u32[]{:S(2)}) %collective-permute-start.8) | collective-permute-done | bytes 393248 | tf_op jit(solution)/shard_map/ppermute | solution.py:68
  139.3 9.8 %collective-permute-done.11 = bf16[192,1024]{1,0:T(8,128)(2,1)S(1)} collective-permute-done((bf16[192,1024]{1,0:T(8,128)(2,1)S(1)}, bf16[192,1024]{1,0:T(8,128)(2,1)S(1)}, u32[]{:S(2)}, u32[]{:S(2)}) %collective-permute-start.11) | collective-permute-done | bytes 393248 | tf_op jit(solution)/shard_map/ppermute | solution.py:68
  149.2 2.9 collective-permute-start.12
  152.2 9.1 %collective-permute-done.12 = bf16[192,1024]{1,0:T(8,128)(2,1)S(1)} collective-permute-done((bf16[192,1024]{1,0:T(8,128)(2,1)S(1)}, bf16[192,1024]{1,0:T(8,128)(2,1)S(1)}, u32[]{:S(2)}, u32[]{:S(2)}) %collective-permute-start.12) | collective-permute-done | bytes 393248 | tf_op jit(solution)/shard_map/ppermute | solution.py:68
  165.3 32.7 %all-gather.5.cloned.1.call-done = bf16[1024,1920]{1,0:T(8,128)(2,1)} async-done(((bf16[64,1920]{1,0:T(8,128)(2,1)}), bf16[1024,1920]{1,0:T(8,128)(2,1)}) %all-gather.5.cloned.1.call-update) | async-done | bytes 3932176 | tf_op jit(solution)/shard_map/all_gather | solution.py:237
  198.0 2.0 convolution_convert_fusion.22
  204.9 2.4 collective-permute-start.15
  213.3 2.4 convolution_convert_fusion.20
  220.4 9.7 %collective-permute-done.17 = bf16[192,1024]{1,0:T(8,128)(2,1)S(1)} collective-permute-done((bf16[192,1024]{1,0:T(8,128)(2,1)S(1)}, bf16[192,1024]{1,0:T(8,128)(2,1)S(1)}, u32[]{:S(2)}, u32[]{:S(2)}) %collective-permute-start.17) | collective-permute-done | bytes 393248 | tf_op jit(solution)/shard_map/ppermute | solution.py:68
  230.2 3.1 collective-permute-start.18
  233.3 8.8 %collective-permute-done.18 = bf16[192,1024]{1,0:T(8,128)(2,1)S(1)} collective-permute-done((bf16[192,1024]{1,0:T(8,128)(2,1)S(1)}, bf16[192,1024]{1,0:T(8,128)(2,1)S(1)}, u32[]{:S(2)}, u32[]{:S(2)}) %collective-permute-start.18) | collective-permute-done | bytes 393248 | tf_op jit(solution)/shard_map/ppermute | solution.py:68
  252.5 9.7 %collective-permute-done.25 = bf16[192,1024]{1,0:T(8,128)(2,1)S(1)} collective-permute-done((bf16[192,1024]{1,0:T(8,128)(2,1)S(1)}, bf16[192,1024]{1,0:T(8,128)(2,1)S(1)}, u32[]{:S(2)}, u32[]{:S(2)}) %collective-permute-start.25) | collective-permute-done | bytes 393248 | tf_op jit(solution)/shard_map/ppermute | solution.py:68
  263.1 3.0 collective-permute-start.26
  267.3 7.9 %collective-permute-done.26 = bf16[192,1024]{1,0:T(8,128)(2,1)} collective-permute-done((bf16[192,1024]{1,0:T(8,128)(2,1)}, bf16[192,1024]{1,0:T(8,128)(2,1)}, u32[]{:S(2)}, u32[]{:S(2)}) %collective-permute-start.26) | collective-permute-done | bytes 393248 | tf_op jit(solution)/shard_map/ppermute | solution.py:68
  276.6 1.9 convolution_convert_fusion.8
  280.3 2.0 multiply_add_fusion.3
  285.4 2.4 collective-permute-start.29
  296.8 1.9 copy.158
  298.7 1.9 fusion.78
  308.0 1.9 add_convert_fusion.18
  312.8 9.3 %collective-permute-done.21 = bf16[192,1024]{1,0:T(8,128)(2,1)} collective-permute-done((bf16[192,1024]{1,0:T(8,128)(2,1)}, bf16[192,1024]{1,0:T(8,128)(2,1)}, u32[]{:S(2)}, u32[]{:S(2)}) %collective-permute-start.21) | collective-permute-done | bytes 393248 | tf_op jit(solution)/shard_map/ppermute | solution.py:68
  323.4 3.1 collective-permute-start.22
  326.4 4.1 collective-permute-done.31
  331.8 3.1 collective-permute-start.32
  335.4 5.6 collective-permute-done.22
  341.9 7.1 %collective-permute-done.32 = bf16[192,1024]{1,0:T(8,128)(2,1)S(1)} collective-permute-done((bf16[192,1024]{1,0:T(8,128)(2,1)S(1)}, bf16[192,1024]{1,0:T(8,128)(2,1)S(1)}, u32[]{:S(2)}, u32[]{:S(2)}) %collective-permute-start.32) | collective-permute-done | bytes 393248 | tf_op jit(solution)/shard_map/ppermute | solution.py:68
  354.3 1.9 multiply_convert_fusion.4
  359.0 2.6 copy.214
  361.7 1.9 fusion.55
  368.3 1.9 fusion.27
  371.4 7.8 %collective-permute-done.35 = bf16[192,1024]{1,0:T(8,128)(2,1)S(1)} collective-permute-done((bf16[192,1024]{1,0:T(8,128)(2,1)S(1)}, bf16[192,1024]{1,0:T(8,128)(2,1)S(1)}, u32[]{:S(2)}, u32[]{:S(2)}) %collective-permute-start.35) | collective-permute-done | bytes 393248 | tf_op jit(solution)/shard_map/ppermute | solution.py:68
  383.2 8.0 %collective-permute-done.36 = bf16[192,1024]{1,0:T(8,128)(2,1)S(1)} collective-permute-done((bf16[192,1024]{1,0:T(8,128)(2,1)S(1)}, bf16[192,1024]{1,0:T(8,128)(2,1)S(1)}, u32[]{:S(2)}, u32[]{:S(2)}) %collective-permute-start.36) | collective-permute-done | bytes 393248 | tf_op jit(solution)/shard_map/ppermute | solution.py:68
  393.0 6.3 %copy.212 = bf16[1024,1920]{1,0:T(8,128)(2,1)} copy(bf16[1024,1920]{0,1:T(8,128)(2,1)} %fusion.20) | data formatting | bytes 7864320
  402.6 2.0 multiply_add_fusion.1
  407.6 2.5 collective-permute-start.39
  410.2 1.9 fusion
  418.4 1.9 copy.169
  423.2 2.1 collective-permute-done.38
  434.6 8.6 %collective-permute-done.41 = bf16[192,1024]{1,0:T(8,128)(2,1)S(1)} collective-permute-done((bf16[192,1024]{1,0:T(8,128)(2,1)S(1)}, bf16[192,1024]{1,0:T(8,128)(2,1)S(1)}, u32[]{:S(2)}, u32[]{:S(2)}) %collective-permute-start.41) | collective-permute-done | bytes 393248 | tf_op jit(solution)/shard_map/ppermute | solution.py:68
  447.0 8.1 %collective-permute-done.42 = bf16[192,1024]{1,0:T(8,128)(2,1)S(1)} collective-permute-done((bf16[192,1024]{1,0:T(8,128)(2,1)S(1)}, bf16[192,1024]{1,0:T(8,128)(2,1)S(1)}, u32[]{:S(2)}, u32[]{:S(2)}) %collective-permute-start.42) | collective-permute-done | bytes 393248 | tf_op jit(solution)/shard_map/ppermute | solution.py:68
  457.5 4.4 copy.175
  466.8 3.2 convert_add_fusion.1
  471.0 45.3 %collective-permute-done.51 = bf16[2,2,1,2,64,1152]{5,4,3,2,1,0:T(8,128)(2,1)S(1)} collective-permute-done((bf16[2,2,1,2,64,1152]{5,4,3,2,1,0:T(8,128)(2,1)S(1)}, bf16[2,2,1,2,64,1152]{5,4,3,2,1,0:T(8,128)(2,1)S(1)}, u32[]{:S(2)}, u32[]{:S(2)}) %collective-permute-start.51) | collective-permute-done | bytes 1179680 | tf_op jit(solution)/shard_map/ppermute | solution.py:135
  519.2 2.7 collective-permute-done.46
  524.3 4.7 collective-permute-done.47
  530.9 2.0 collective-permute-done.48
  533.0 5.2 collective-permute-done.49
  538.2 2.0 collective-permute-start.50
  541.6 2.9 multiply_add_fusion
  545.2 6.4 %collective-permute-done.53 = bf16[2,1,1,1,64,1152]{5,4,3,2,1,0:T(8,128)(2,1)S(1)} collective-permute-done((bf16[2,1,1,1,64,1152]{5,4,3,2,1,0:T(8,128)(2,1)S(1)}, bf16[2,1,1,1,64,1152]{5,4,3,2,1,0:T(8,128)(2,1)S(1)}, u32[]{:S(2)}, u32[]{:S(2)}) %collective-permute-start.53) | collective-permute-done | bytes 294944 | tf_op jit(solution)/shard_map/ppermute | solution.py:135
  553.6 4.8 collective-permute-done.54
  (642 shorter events, 176.8 us)
Async XLA Ops:
  7.2 92.3 %all-gather.3.cloned.1.call-start = ((), (), s32[]{:S(2)}) async-start(), calls=%async_computation.2 | async-start | bytes 3063808 | tf_op jit(solution)/shard_map/all_gather | solution.py:242
  10.5 187.5 %all-gather.5.cloned.1.call-start = ((), (), s32[]{:S(2)}) async-start(), calls=%async_computation.3 | async-start | bytes 4177920 | tf_op jit(solution)/shard_map/all_gather | solution.py:237
  12.1 11.5 %collective-permute-start = (bf16[1,1,1,1,64,512]{5,4,3,2,1,0:T(8,128)(2,1)S(1)}, bf16[1,1,1,1,64,512]{5,4,3,2,1,0:T(8,128)(2,1)S(1)}, u32[]{:S(2)}, u32[]{:S(2)}) collective-permute-start(bf16[1,1,1,1,64,512]{5,4,3,2,1,0:T(8,128)(2,1)S(1)} %get-tuple-element.124), channel_id=1, source_target_pairs={{0,8},{8,0},{1,9},{9,1},{2,10},{10,2},{3,11},{11,3},{4,12},{12,4},... | collective-permute-start | bytes 196616 | tf_op jit(solution)/shard_map/ppermute | solution.py:157
  21.5 501.2 %reduce-scatter.9.cloned.1.call-start = ((), (), s32[]{:S(2)}) async-start(), calls=%async_computation.5 | async-start | bytes 1671168
  23.1 48.4 %copy-start.38 = (f32[384,64]{1,0:T(8,128)}, f32[384,64]{1,0:T(8,128)S(1)}, u32[]{:S(2)}) copy-start(f32[384,64]{1,0:T(8,128)S(1)} %get-tuple-element.135) | copy-start | bytes 294916
  23.1 48.4 %copy-start.61 = (f32[384,64]{1,0:T(8,128)}, f32[384,64]{1,0:T(8,128)S(1)}, u32[]{:S(2)}) copy-start(f32[384,64]{1,0:T(8,128)S(1)} %get-tuple-element.134) | copy-start | bytes 294916
  23.6 6.6 %collective-permute-start.1 = (bf16[1,1,1,2,64,512]{5,4,3,2,1,0:T(8,128)(2,1)S(1)}, bf16[1,1,1,2,64,512]{5,4,3,2,1,0:T(8,128)(2,1)S(1)}, u32[]{:S(2)}, u32[]{:S(2)}) collective-permute-start(bf16[1,1,1,2,64,512]{5,4,3,2,1,0:T(8,128)(2,1)S(1)} %maximum_select_fusion.17), channel_id=1, source_target_pairs={{0,64},{16,80},{32,96},{48,112},{64,0},{80,16},{96,32},{112,48},{1... | collective-permute-start | bytes 393224 | tf_op jit(solution)/shard_map/ppermute | solution.py:157
  30.2 10.6 %collective-permute-start.2 = (bf16[2,1,1,2,64,512]{5,4,3,2,1,0:T(8,128)(2,1)S(1)}, bf16[2,1,1,2,64,512]{5,4,3,2,1,0:T(8,128)(2,1)S(1)}, u32[]{:S(2)}, u32[]{:S(2)}) collective-permute-start(bf16[2,1,1,2,64,512]{5,4,3,2,1,0:T(8,128)(2,1)S(1)} %maximum_select_fusion.11), channel_id=1, source_target_pairs={{0,16},{16,0},{32,48},{48,32},{64,80},{80,64},{96,112},{112,96},{1... | collective-permute-start | bytes 786440 | tf_op jit(solution)/shard_map/ppermute | solution.py:157
  31.8 39.5 %copy-start.154 = (f32[128]{0:T(128)}, f32[128]{0:T(128)S(1)}, u32[]{:S(2)}) copy-start(f32[128]{0:T(128)S(1)} %get-tuple-element.137) | copy-start | bytes 1540
  40.9 20.9 %collective-permute-start.3 = (bf16[2,1,2,2,64,512]{5,4,3,2,1,0:T(8,128)(2,1)S(1)}, bf16[2,1,2,2,64,512]{5,4,3,2,1,0:T(8,128)(2,1)S(1)}, u32[]{:S(2)}, u32[]{:S(2)}) collective-permute-start(bf16[2,1,2,2,64,512]{5,4,3,2,1,0:T(8,128)(2,1)S(1)} %maximum_select_fusion.9), channel_id=1, source_target_pairs={{0,32},{16,48},{32,0},{48,16},{64,96},{80,112},{96,64},{112,80},{1... | collective-permute-start | bytes 1572872 | tf_op jit(solution)/shard_map/ppermute | solution.py:157
  64.6 15.5 %collective-permute-start.4 = (bf16[384,128]{1,0:T(8,128)(2,1)}, bf16[384,128]{1,0:T(8,128)(2,1)}, u32[]{:S(2)}, u32[]{:S(2)}) collective-permute-start(bf16[384,128]{1,0:T(8,128)(2,1)} %convolution_convert_fusion.23), channel_id=1, source_target_pairs={{0,8},{8,0},{1,9},{9,1},{2,10},{10,2},{3,11},{11,3},{4,12},{12,4},... | collective-permute-start | bytes 294920 | tf_op jit(solution)/shard_map/ppermute | solution.py:82
  66.5 11.6 %collective-permute-start.5 = (bf16[384,128]{1,0:T(8,128)(2,1)}, bf16[384,128]{1,0:T(8,128)(2,1)}, u32[]{:S(2)}, u32[]{:S(2)}) collective-permute-start(bf16[384,128]{1,0:T(8,128)(2,1)} %pad_maximum_fusion.11), channel_id=1, source_target_pairs={{0,8},{8,0},{1,9},{9,1},{2,10},{10,2},{3,11},{11,3},{4,12},{12,4},... | collective-permute-start | bytes 294920 | tf_op jit(solution)/shard_map/ppermute | solution.py:82
  101.8 1.9 collective-permute-start.6
  103.8 11.9 %collective-permute-start.7 = (bf16[192,1024]{1,0:T(8,128)(2,1)S(1)}, bf16[192,1024]{1,0:T(8,128)(2,1)S(1)}, u32[]{:S(2)}, u32[]{:S(2)}) collective-permute-start(bf16[192,1024]{1,0:T(8,128)(2,1)S(1)} %add_convert_fusion.27), channel_id=1, source_target_pairs={{0,2},{1,3},{2,0},{3,1},{4,6},{5,7},{6,4},{7,5},{8,10},{9,11},{10,... | collective-permute-start | bytes 1179656 | tf_op jit(solution)/shard_map/ppermute | solution.py:68
  115.9 12.3 %collective-permute-start.8 = (bf16[192,1024]{1,0:T(8,128)(2,1)S(1)}, bf16[192,1024]{1,0:T(8,128)(2,1)S(1)}, u32[]{:S(2)}, u32[]{:S(2)}) collective-permute-start(bf16[192,1024]{1,0:T(8,128)(2,1)S(1)} %add_convert_fusion.26), channel_id=1, source_target_pairs={{0,4},{1,5},{2,6},{3,7},{4,0},{5,1},{6,2},{7,3},{8,12},{9,13},{10,... | collective-permute-start | bytes 1179656 | tf_op jit(solution)/shard_map/ppermute | solution.py:68
  128.4 2.0 collective-permute-start.9
  135.9 1.8 collective-permute-start.10
  137.9 11.2 %collective-permute-start.11 = (bf16[192,1024]{1,0:T(8,128)(2,1)S(1)}, bf16[192,1024]{1,0:T(8,128)(2,1)S(1)}, u32[]{:S(2)}, u32[]{:S(2)}) collective-permute-start(bf16[192,1024]{1,0:T(8,128)(2,1)S(1)} %add_convert_fusion.24), channel_id=1, source_target_pairs={{0,2},{1,3},{2,0},{3,1},{4,6},{5,7},{6,4},{7,5},{8,10},{9,11},{10,... | collective-permute-start | bytes 1179656 | tf_op jit(solution)/shard_map/ppermute | solution.py:68
  149.2 12.0 %collective-permute-start.12 = (bf16[192,1024]{1,0:T(8,128)(2,1)S(1)}, bf16[192,1024]{1,0:T(8,128)(2,1)S(1)}, u32[]{:S(2)}, u32[]{:S(2)}) collective-permute-start(bf16[192,1024]{1,0:T(8,128)(2,1)S(1)} %add_convert_fusion.23), channel_id=1, source_target_pairs={{0,4},{1,5},{2,6},{3,7},{4,0},{5,1},{6,2},{7,3},{8,12},{9,13},{10,... | collective-permute-start | bytes 1179656 | tf_op jit(solution)/shard_map/ppermute | solution.py:68
  161.4 1.8 collective-permute-start.13
  165.3 42.1 %copy-start.13 = (bf16[384,1024]{1,0:T(8,128)(2,1)}, bf16[384,1024]{1,0:T(8,128)(2,1)S(1)}, u32[]{:S(2)}) copy-start(bf16[384,1024]{1,0:T(8,128)(2,1)S(1)} %get-tuple-element.75) | copy-start | bytes 2359300
  199.9 13.3 %collective-permute-start.14 = (bf16[384,128]{1,0:T(8,128)(2,1)}, bf16[384,128]{1,0:T(8,128)(2,1)}, u32[]{:S(2)}, u32[]{:S(2)}) collective-permute-start(bf16[384,128]{1,0:T(8,128)(2,1)} %convolution_convert_fusion.22), channel_id=1, source_target_pairs={{0,8},{8,0},{1,9},{9,1},{2,10},{10,2},{3,11},{11,3},{4,12},{12,4},... | collective-permute-start | bytes 294920 | tf_op jit(solution)/shard_map/ppermute | solution.py:82
  204.9 6.4 %collective-permute-start.15 = (bf16[384,128]{1,0:T(8,128)(2,1)}, bf16[384,128]{1,0:T(8,128)(2,1)}, u32[]{:S(2)}, u32[]{:S(2)}) collective-permute-start(bf16[384,128]{1,0:T(8,128)(2,1)} %pad_maximum_fusion.12), channel_id=1, source_target_pairs={{0,8},{8,0},{1,9},{9,1},{2,10},{10,2},{3,11},{11,3},{4,12},{12,4},... | collective-permute-start | bytes 294920 | tf_op jit(solution)/shard_map/ppermute | solution.py:82
  216.9 1.8 collective-permute-start.16
  218.8 11.2 %collective-permute-start.17 = (bf16[192,1024]{1,0:T(8,128)(2,1)S(1)}, bf16[192,1024]{1,0:T(8,128)(2,1)S(1)}, u32[]{:S(2)}, u32[]{:S(2)}) collective-permute-start(bf16[192,1024]{1,0:T(8,128)(2,1)S(1)} %add_convert_fusion.21), channel_id=1, source_target_pairs={{0,2},{1,3},{2,0},{3,1},{4,6},{5,7},{6,4},{7,5},{8,10},{9,11},{10,... | collective-permute-start | bytes 1179656 | tf_op jit(solution)/shard_map/ppermute | solution.py:68
  230.2 11.9 %collective-permute-start.18 = (bf16[192,1024]{1,0:T(8,128)(2,1)S(1)}, bf16[192,1024]{1,0:T(8,128)(2,1)S(1)}, u32[]{:S(2)}, u32[]{:S(2)}) collective-permute-start(bf16[192,1024]{1,0:T(8,128)(2,1)S(1)} %add_convert_fusion.20), channel_id=1, source_target_pairs={{0,4},{1,5},{2,6},{3,7},{4,0},{5,1},{6,2},{7,3},{8,12},{9,13},{10,... | collective-permute-start | bytes 1179656 | tf_op jit(solution)/shard_map/ppermute | solution.py:68
  242.3 2.2 collective-permute-start.19
  249.0 1.8 collective-permute-start.24
  250.9 11.2 %collective-permute-start.25 = (bf16[192,1024]{1,0:T(8,128)(2,1)S(1)}, bf16[192,1024]{1,0:T(8,128)(2,1)S(1)}, u32[]{:S(2)}, u32[]{:S(2)}) collective-permute-start(bf16[192,1024]{1,0:T(8,128)(2,1)S(1)} %add_convert_fusion.15), channel_id=1, source_target_pairs={{0,2},{1,3},{2,0},{3,1},{4,6},{5,7},{6,4},{7,5},{8,10},{9,11},{10,... | collective-permute-start | bytes 1179656 | tf_op jit(solution)/shard_map/ppermute | solution.py:68
  263.1 12.1 %collective-permute-start.26 = (bf16[192,1024]{1,0:T(8,128)(2,1)}, bf16[192,1024]{1,0:T(8,128)(2,1)}, u32[]{:S(2)}, u32[]{:S(2)}) collective-permute-start(bf16[192,1024]{1,0:T(8,128)(2,1)} %add_convert_fusion.14), channel_id=1, source_target_pairs={{0,4},{1,5},{2,6},{3,7},{4,0},{5,1},{6,2},{7,3},{8,12},{9,13},{10,... | collective-permute-start | bytes 1179656 | tf_op jit(solution)/shard_map/ppermute | solution.py:68
  276.5 3.2 collective-permute-start.27
  279.3 28.7 %collective-permute-start.20 = (bf16[192,1024]{1,0:T(8,128)(2,1)}, bf16[192,1024]{1,0:T(8,128)(2,1)}, u32[]{:S(2)}, u32[]{:S(2)}) collective-permute-start(bf16[192,1024]{1,0:T(8,128)(2,1)} %constant_dynamic-slice_fusion.5), channel_id=1, source_target_pairs={{0,1},{1,0},{2,3},{3,2},{4,5},{5,4},{6,7},{7,6},{8,9},{9,8},{10,11... | collective-permute-start | bytes 1179656 | tf_op jit(solution)/shard_map/ppermute | solution.py:62
  285.4 20.9 %collective-permute-start.29 = (bf16[384,128]{0,1:T(8,128)(2,1)}, bf16[384,128]{0,1:T(8,128)(2,1)}, u32[]{:S(2)}, u32[]{:S(2)}) collective-permute-start(bf16[384,128]{0,1:T(8,128)(2,1)} %fusion.150), channel_id=1, source_target_pairs={{0,8},{8,0},{1,9},{9,1},{2,10},{10,2},{3,11},{11,3},{4,12},{12,4},... | collective-permute-start | bytes 294920 | tf_op jit(solution)/shard_map/ppermute | solution.py:82
  292.6 9.6 %collective-permute-start.28 = (bf16[384,128]{1,0:T(8,128)(2,1)}, bf16[384,128]{1,0:T(8,128)(2,1)}, u32[]{:S(2)}, u32[]{:S(2)}) collective-permute-start(bf16[384,128]{1,0:T(8,128)(2,1)} %fusion.148), channel_id=1, source_target_pairs={{0,8},{8,0},{1,9},{9,1},{2,10},{10,2},{3,11},{11,3},{4,12},{12,4},... | collective-permute-start | bytes 294920 | tf_op jit(solution)/shard_map/ppermute | solution.py:82
  307.9 3.5 collective-permute-start.30
  309.9 12.2 %collective-permute-start.21 = (bf16[192,1024]{1,0:T(8,128)(2,1)}, bf16[192,1024]{1,0:T(8,128)(2,1)}, u32[]{:S(2)}, u32[]{:S(2)}) collective-permute-start(bf16[192,1024]{1,0:T(8,128)(2,1)} %add_convert_fusion.18), channel_id=1, source_target_pairs={{0,2},{1,3},{2,0},{3,1},{4,6},{5,7},{6,4},{7,5},{8,10},{9,11},{10,... | collective-permute-start | bytes 1179656 | tf_op jit(solution)/shard_map/ppermute | solution.py:68
  312.2 18.3 %collective-permute-start.31 = (bf16[192,1024]{1,0:T(8,128)(2,1)}, bf16[192,1024]{1,0:T(8,128)(2,1)}, u32[]{:S(2)}, u32[]{:S(2)}) collective-permute-start(bf16[192,1024]{1,0:T(8,128)(2,1)} %add_convert_fusion.12), channel_id=1, source_target_pairs={{0,2},{1,3},{2,0},{3,1},{4,6},{5,7},{6,4},{7,5},{8,10},{9,11},{10,... | collective-permute-start | bytes 1179656 | tf_op jit(solution)/shard_map/ppermute | solution.py:68
  323.4 17.6 %collective-permute-start.22 = (bf16[192,1024]{1,0:T(8,128)(2,1)S(1)}, bf16[192,1024]{1,0:T(8,128)(2,1)S(1)}, u32[]{:S(2)}, u32[]{:S(2)}) collective-permute-start(bf16[192,1024]{1,0:T(8,128)(2,1)S(1)} %add_convert_fusion.17), channel_id=1, source_target_pairs={{0,4},{1,5},{2,6},{3,7},{4,0},{5,1},{6,2},{7,3},{8,12},{9,13},{10,... | collective-permute-start | bytes 1179656 | tf_op jit(solution)/shard_map/ppermute | solution.py:68
  331.8 17.2 %collective-permute-start.32 = (bf16[192,1024]{1,0:T(8,128)(2,1)S(1)}, bf16[192,1024]{1,0:T(8,128)(2,1)S(1)}, u32[]{:S(2)}, u32[]{:S(2)}) collective-permute-start(bf16[192,1024]{1,0:T(8,128)(2,1)S(1)} %add_convert_fusion.11), channel_id=1, source_target_pairs={{0,4},{1,5},{2,6},{3,7},{4,0},{5,1},{6,2},{7,3},{8,12},{9,13},{10,... | collective-permute-start | bytes 1179656 | tf_op jit(solution)/shard_map/ppermute | solution.py:68
  341.9 124.9 %collective-permute-start.23 = (bf16[192,1024]{1,0:T(8,128)(2,1)}, bf16[192,1024]{1,0:T(8,128)(2,1)}, u32[]{:S(2)}, u32[]{:S(2)}) collective-permute-start(bf16[192,1024]{1,0:T(8,128)(2,1)} %add_convert_fusion.16), channel_id=1, source_target_pairs={{0,1},{1,0},{2,3},{3,2},{4,5},{5,4},{6,7},{7,6},{8,9},{9,8},{10,11... | collective-permute-start | bytes 1179656 | tf_op jit(solution)/shard_map/ppermute | solution.py:72
  349.2 3.2 collective-permute-start.33
  361.6 196.9 %reduce-scatter.7.cloned.1.call-start = ((), (), s32[]{:S(2)}) async-start(), calls=%async_computation.4 | async-start | bytes 4177920 | tf_op jit(solution)/shard_map/reduce_scatter | solution.py:253
  365.5 2.1 collective-permute-start.34
  367.8 11.4 %collective-permute-start.35 = (bf16[192,1024]{1,0:T(8,128)(2,1)S(1)}, bf16[192,1024]{1,0:T(8,128)(2,1)S(1)}, u32[]{:S(2)}, u32[]{:S(2)}) collective-permute-start(bf16[192,1024]{1,0:T(8,128)(2,1)S(1)} %add_convert_fusion.9), channel_id=1, source_target_pairs={{0,2},{1,3},{2,0},{3,1},{4,6},{5,7},{6,4},{7,5},{8,10},{9,11},{10,... | collective-permute-start | bytes 1179656 | tf_op jit(solution)/shard_map/ppermute | solution.py:68
  379.3 11.9 %collective-permute-start.36 = (bf16[192,1024]{1,0:T(8,128)(2,1)S(1)}, bf16[192,1024]{1,0:T(8,128)(2,1)S(1)}, u32[]{:S(2)}, u32[]{:S(2)}) collective-permute-start(bf16[192,1024]{1,0:T(8,128)(2,1)S(1)} %add_convert_fusion.8), channel_id=1, source_target_pairs={{0,4},{1,5},{2,6},{3,7},{4,0},{5,1},{6,2},{7,3},{8,12},{9,13},{10,... | collective-permute-start | bytes 1179656 | tf_op jit(solution)/shard_map/ppermute | solution.py:68
  391.4 10.5 %collective-permute-start.37 = (bf16[192,1024]{1,0:T(8,128)(2,1)S(1)}, bf16[192,1024]{1,0:T(8,128)(2,1)S(1)}, u32[]{:S(2)}, u32[]{:S(2)}) collective-permute-start(bf16[192,1024]{1,0:T(8,128)(2,1)S(1)} %add_convert_fusion.7), channel_id=1, source_target_pairs={{0,1},{1,0},{2,3},{3,2},{4,5},{5,4},{6,7},{7,6},{8,9},{9,8},{10,11... | collective-permute-start | bytes 1179656 | tf_op jit(solution)/shard_map/ppermute | solution.py:72
  407.6 20.8 %collective-permute-start.39 = (bf16[384,128]{0,1:T(8,128)(2,1)}, bf16[384,128]{0,1:T(8,128)(2,1)S(1)}, u32[]{:S(2)}, u32[]{:S(2)}) collective-permute-start(bf16[384,128]{0,1:T(8,128)(2,1)} %fusion.154), channel_id=1, source_target_pairs={{0,8},{8,0},{1,9},{9,1},{2,10},{10,2},{3,11},{11,3},{4,12},{12,4},... | collective-permute-start | bytes 294920 | tf_op jit(solution)/shard_map/ppermute | solution.py:82
  417.1 8.2 %collective-permute-start.38 = (bf16[384,128]{1,0:T(8,128)(2,1)S(1)}, bf16[384,128]{1,0:T(8,128)(2,1)}, u32[]{:S(2)}, u32[]{:S(2)}) collective-permute-start(bf16[384,128]{1,0:T(8,128)(2,1)S(1)} %fusion.152), channel_id=1, source_target_pairs={{0,8},{8,0},{1,9},{9,1},{2,10},{10,2},{3,11},{11,3},{4,12},{12,4},... | collective-permute-start | bytes 294920 | tf_op jit(solution)/shard_map/ppermute | solution.py:82
  428.9 3.1 collective-permute-start.40
  432.2 11.1 %collective-permute-start.41 = (bf16[192,1024]{1,0:T(8,128)(2,1)S(1)}, bf16[192,1024]{1,0:T(8,128)(2,1)S(1)}, u32[]{:S(2)}, u32[]{:S(2)}) collective-permute-start(bf16[192,1024]{1,0:T(8,128)(2,1)S(1)} %add_convert_fusion.6), channel_id=1, source_target_pairs={{0,2},{1,3},{2,0},{3,1},{4,6},{5,7},{6,4},{7,5},{8,10},{9,11},{10,... | collective-permute-start | bytes 1179656 | tf_op jit(solution)/shard_map/ppermute | solution.py:68
  443.4 11.7 %collective-permute-start.42 = (bf16[192,1024]{1,0:T(8,128)(2,1)S(1)}, bf16[192,1024]{1,0:T(8,128)(2,1)S(1)}, u32[]{:S(2)}, u32[]{:S(2)}) collective-permute-start(bf16[192,1024]{1,0:T(8,128)(2,1)S(1)} %add_convert_fusion.5), channel_id=1, source_target_pairs={{0,4},{1,5},{2,6},{3,7},{4,0},{5,1},{6,2},{7,3},{8,12},{9,13},{10,... | collective-permute-start | bytes 1179656 | tf_op jit(solution)/shard_map/ppermute | solution.py:68
  456.0 7.4 %collective-permute-start.43 = (bf16[192,1024]{1,0:T(8,128)(2,1)}, bf16[192,1024]{1,0:T(8,128)(2,1)}, u32[]{:S(2)}, u32[]{:S(2)}) collective-permute-start(bf16[192,1024]{1,0:T(8,128)(2,1)} %add_convert_fusion.4), channel_id=1, source_target_pairs={{0,1},{1,0},{2,3},{3,2},{4,5},{5,4},{6,7},{7,6},{8,9},{9,8},{10,11... | collective-permute-start | bytes 1179656 | tf_op jit(solution)/shard_map/ppermute | solution.py:72
  463.3 53.0 %collective-permute-start.51 = (bf16[2,2,1,2,64,1152]{5,4,3,2,1,0:T(8,128)(2,1)S(1)}, bf16[2,2,1,2,64,1152]{5,4,3,2,1,0:T(8,128)(2,1)S(1)}, u32[]{:S(2)}, u32[]{:S(2)}) collective-permute-start(bf16[2,2,1,2,64,1152]{5,4,3,2,1,0:T(8,128)(2,1)S(1)} %constant_dynamic-slice_fusion), channel_id=1, source_target_pairs={{0,16},{16,0},{32,48},{48,32},{64,80},{80,64},{96,112},{112,96},{1... | collective-permute-start | bytes 3538952 | tf_op jit(solution)/shard_map/ppermute | solution.py:135
  466.2 50.1 %copy-start.20 = (bf16[1024,1152]{1,0:T(8,128)(2,1)S(1)}, bf16[1024,1152]{1,0:T(8,128)(2,1)}, u32[]{:S(2)}) copy-start(bf16[1024,1152]{1,0:T(8,128)(2,1)} %copy.175) | copy-start | bytes 7077892
  466.2 3.8 collective-permute-start.44
  470.1 46.5 %collective-permute-start.45 = (f32[2,2304]{1,0:T(2,128)S(1)}, f32[2,2304]{1,0:T(2,128)S(1)}, u32[]{:S(2)}, u32[]{:S(2)}) collective-permute-start(f32[2,2304]{1,0:T(2,128)S(1)} %fusion.252), channel_id=1, source_target_pairs={{0,2},{1,3},{2,0},{3,1},{4,6},{5,7},{6,4},{7,5},{8,10},{9,11},{10,... | collective-permute-start | bytes 55304 | tf_op jit(solution)/shard_map/ppermute | solution.py:109
  516.6 5.3 collective-permute-start.46
  519.2 21.0 %collective-permute-start.52 = (bf16[2,1,1,2,64,1152]{5,4,3,2,1,0:T(8,128)(2,1)}, bf16[2,1,1,2,64,1152]{5,4,3,2,1,0:T(8,128)(2,1)}, u32[]{:S(2)}, u32[]{:S(2)}) collective-permute-start(bf16[2,1,1,2,64,1152]{5,4,3,2,1,0:T(8,128)(2,1)} %dynamic-slice_convert_fusion), channel_id=1, source_target_pairs={{0,32},{16,48},{32,0},{48,16},{64,96},{80,112},{96,64},{112,80},{1... | collective-permute-start | bytes 1769480 | tf_op jit(solution)/shard_map/ppermute | solution.py:135
  521.9 7.1 %collective-permute-start.47 = (f32[2,2304]{1,0:T(2,128)S(1)}, f32[2,2304]{1,0:T(2,128)S(1)}, u32[]{:S(2)}, u32[]{:S(2)}) collective-permute-start(f32[2,2304]{1,0:T(2,128)S(1)} %add.463), channel_id=1, source_target_pairs={{0,8},{8,0},{1,9},{9,1},{2,10},{10,2},{3,11},{11,3},{4,12},{12,4},... | collective-permute-start | bytes 55304 | tf_op jit(solution)/shard_map/ppermute | solution.py:109
  529.0 3.8 collective-permute-start.48
  532.9 5.3 collective-permute-start.49
  538.2 6.3 %collective-permute-start.50 = (f32[2,2304]{1,0:T(2,128)S(1)}, f32[2,2304]{1,0:T(2,128)S(1)}, u32[]{:S(2)}, u32[]{:S(2)}) collective-permute-start(f32[2,2304]{1,0:T(2,128)S(1)} %add.466), channel_id=1, source_target_pairs={{0,64},{16,80},{32,96},{48,112},{64,0},{80,16},{96,32},{112,48},{1... | collective-permute-start | bytes 55304 | tf_op jit(solution)/shard_map/ppermute | solution.py:109
  541.5 10.1 %collective-permute-start.53 = (bf16[2,1,1,1,64,1152]{5,4,3,2,1,0:T(8,128)(2,1)S(1)}, bf16[2,1,1,1,64,1152]{5,4,3,2,1,0:T(8,128)(2,1)S(1)}, u32[]{:S(2)}, u32[]{:S(2)}) collective-permute-start(bf16[2,1,1,1,64,1152]{5,4,3,2,1,0:T(8,128)(2,1)S(1)} %dynamic-slice_convert_fusion.1), channel_id=1, source_target_pairs={{0,8},{8,0},{1,9},{9,1},{2,10},{10,2},{3,11},{11,3},{4,12},{12,4},... | collective-permute-start | bytes 884744 | tf_op jit(solution)/shard_map/ppermute | solution.py:135
  551.7 6.7 %collective-permute-start.54 = (bf16[1,1,1,1,64,1152]{5,4,3,2,1,0:T(8,128)(2,1)S(1)}, bf16[1,1,1,1,64,1152]{5,4,3,2,1,0:T(8,128)(2,1)S(1)}, u32[]{:S(2)}, u32[]{:S(2)}) collective-permute-start(bf16[1,1,1,1,64,1152]{5,4,3,2,1,0:T(8,128)(2,1)S(1)} %dynamic-slice_convert_fusion.2), channel_id=1, source_target_pairs={{0,64},{16,80},{32,96},{48,112},{64,0},{80,16},{96,32},{112,48},{1... | collective-permute-start | bytes 442376 | tf_op jit(solution)/shard_map/ppermute | solution.py:135
  (162 other events, 928.1 us)
Sparse Core Ops, SparseCore 0:
  10.6 88.8 all-gather.2
  101.2 96.7 all-gather.4
  361.7 78.6 reduce-scatter.8
  442.8 92.0 reduce-scatter.6

commit v14 on v13

--- a/solution.py
+++ b/solution.py
@@ -261,16 +261,19 @@
     def scatter_layer(terms, layer_index):
         if layer_index > 0:
             return tuple(scatter_terms(terms))
-        early = scatter_terms(terms[4:6])
+        split = terms[6].shape[1] // 3
+        early = scatter_terms(list(terms[4:6]) + [terms[6][:, split:]])
+        moved = list(terms[:4]) + [terms[6][:, :split]]
         joined = shard_scatter(
-            jnp.concatenate([term.astype(jnp.bfloat16) for term in terms[:4] + terms[6:]], axis=1)
+            jnp.concatenate([term.astype(jnp.bfloat16) for term in moved], axis=1)
         )
         late = []
         start = 0
-        for term in terms[:4] + terms[6:]:
+        for term in moved:
             late.append(joined[:, start : start + term.shape[1]])
             start += term.shape[1]
-        return tuple(late[:4] + early + late[4:])
+        down_owned = jnp.concatenate([late[4], early[2]], axis=1)
+        return tuple(late[:4] + early[:2] + [down_owned])
 
     kept_weights = []
     stored_layers = []

time: 583 us -> 563 us (0.966)
  waiting for transfers between devices: 302 us -> 290 us
  other arithmetic: 68.5 us -> 59.6 us
    ppermute x4, waiting for transfers between devices: 56.5 us -> 43.2 us  [shard_scatter(): received = lax.ppermute(sent.astype(jnp.bfloat16), axis_name, pairs)]
    ppermute x16, waiting for transfers between devices: 132 us -> 124 us  [tp_sum(): received = lax.ppermute(mine, 'tp', pairs)]
    unnamed x348 -> x329, local copies, waits for them, and re-layouts: 26.3 us -> 30.7 us
  transfers between devices with their start and end apart: 59 -> 59, of which waited for: 38 -> 41; matrix products, arithmetic and copies ran while one was open for 27% -> 25% of each run, Pallas kernels for 0% -> 0%
where the time goes in v14:
time: 563 us; the launch traced here: 552 us
  waiting for transfers between devices  290 us (52%)
  starting transfers between devices  66.8 us (12%)
  matrix products  62.6 us (11%)
  other arithmetic  59.6 us (11%)
  local copies, waits for them, and re-layouts  56.6 us (10%)
  between operations  16.9 us (3%)
    ppermute x16, waiting for transfers between devices, tp_sum(): received = lax.ppermute(mine, 'tp', pairs)  124 us
    ppermute x4, waiting for transfers between devices, shard_scatter(): received = lax.ppermute(sent.astype(jnp.bfloat16), axis_name, pairs)  43.2 us
    all_gather x1, waiting for transfers between devices, gather_layer(): full = lax.all_gather(joined, ('fsdp', 'ctx'), axis=0, tiled=True)  31 us
    unnamed x329, local copies, waits for them, and re-layouts  30.7 us
    ppermute x16, starting transfers between devices, tp_sum(): received = lax.ppermute(mine, 'tp', pairs)  29.4 us
    ppermute x4, waiting for transfers between devices, shard_gather(): received = lax.ppermute(current, axis_name, pairs)  29.2 us
    all_gather x1, waiting for transfers between devices, gather_layer(): late_full = lax.all_gather(late, ('fsdp', 'ctx'), axis=0, tiled=True)  21.3 us
    ppermute x7, waiting for transfers between devices, all_sum(): total = total + lax.ppermute(total, axis_name, pairs)  17.1 us
  transfers between devices with their start and end apart: 59, of which 41 were waited for; matrix products, arithmetic and copies ran while one was open for 25% of the time, Pallas kernels for 0%

profile of v14, /device:TPU:0, one launch (start us, length us, event | category | flops | bytes accessed | tf_op | source)
XLA Modules:
  0.0 552.3 jit_solution(11399029478722725882)
XLA Ops:
  12.1 4.0 collective-permute-start
  23.6 3.1 collective-permute-start.1
  26.7 3.4 collective-permute-done.1
  31.9 9.0 %collective-permute-done.2 = bf16[2,1,1,2,64,512]{5,4,3,2,1,0:T(8,128)(2,1)S(1)} collective-permute-done((bf16[2,1,1,2,64,512]{5,4,3,2,1,0:T(8,128)(2,1)S(1)}, bf16[2,1,1,2,64,512]{5,4,3,2,1,0:T(8,128)(2,1)S(1)}, u32[]{:S(2)}, u32[]{:S(2)}) %collective-permute-start.2) | collective-permute-done | bytes 262176 | tf_op jit(solution)/shard_map/ppermute | solution.py:157
  40.9 1.9 collective-permute-start.3
  44.7 16.8 %collective-permute-done.3 = bf16[2,1,2,2,64,512]{5,4,3,2,1,0:T(8,128)(2,1)S(1)} collective-permute-done((bf16[2,1,2,2,64,512]{5,4,3,2,1,0:T(8,128)(2,1)S(1)}, bf16[2,1,2,2,64,512]{5,4,3,2,1,0:T(8,128)(2,1)S(1)}, u32[]{:S(2)}, u32[]{:S(2)}) %collective-permute-start.3) | collective-permute-done | bytes 524320 | tf_op jit(solution)/shard_map/ppermute | solution.py:157
  65.3 3.6 collective-permute-start.5
  70.9 4.6 collective-permute-done.5
  75.4 1.8 fusion.13
  79.5 21.3 %all-gather.3.cloned.1.call-done = bf16[1024,1408]{1,0:T(8,128)(2,1)} async-done(((bf16[64,1408]{1,0:T(8,128)(2,1)}), bf16[1024,1408]{1,0:T(8,128)(2,1)}) %all-gather.3.cloned.1.call-update) | async-done | bytes 2883600 | tf_op jit(solution)/shard_map/all_gather | solution.py:242
  103.0 1.9 collective-permute-done.6
  105.9 10.4 %collective-permute-done.7 = bf16[192,1024]{1,0:T(8,128)(2,1)S(1)} collective-permute-done((bf16[192,1024]{1,0:T(8,128)(2,1)S(1)}, bf16[192,1024]{1,0:T(8,128)(2,1)S(1)}, u32[]{:S(2)}, u32[]{:S(2)}) %collective-permute-start.7) | collective-permute-done | bytes 393248 | tf_op jit(solution)/shard_map/ppermute | solution.py:68
  116.5 3.2 collective-permute-start.8
  119.6 8.9 %collective-permute-done.8 = bf16[192,1024]{1,0:T(8,128)(2,1)S(1)} collective-permute-done((bf16[192,1024]{1,0:T(8,128)(2,1)S(1)}, bf16[192,1024]{1,0:T(8,128)(2,1)S(1)}, u32[]{:S(2)}, u32[]{:S(2)}) %collective-permute-start.8) | collective-permute-done | bytes 393248 | tf_op jit(solution)/shard_map/ppermute | solution.py:68
  138.9 10.4 %collective-permute-done.11 = bf16[192,1024]{1,0:T(8,128)(2,1)S(1)} collective-permute-done((bf16[192,1024]{1,0:T(8,128)(2,1)S(1)}, bf16[192,1024]{1,0:T(8,128)(2,1)S(1)}, u32[]{:S(2)}, u32[]{:S(2)}) %collective-permute-start.11) | collective-permute-done | bytes 393248 | tf_op jit(solution)/shard_map/ppermute | solution.py:68
  149.5 3.1 collective-permute-start.12
  152.6 8.9 %collective-permute-done.12 = bf16[192,1024]{1,0:T(8,128)(2,1)S(1)} collective-permute-done((bf16[192,1024]{1,0:T(8,128)(2,1)S(1)}, bf16[192,1024]{1,0:T(8,128)(2,1)S(1)}, u32[]{:S(2)}, u32[]{:S(2)}) %collective-permute-start.12) | collective-permute-done | bytes 393248 | tf_op jit(solution)/shard_map/ppermute | solution.py:68
  165.6 31.0 %all-gather.5.cloned.1.call-done = bf16[1024,1920]{1,0:T(8,128)(2,1)} async-done(((bf16[64,1920]{1,0:T(8,128)(2,1)}), bf16[1024,1920]{1,0:T(8,128)(2,1)}) %all-gather.5.cloned.1.call-update) | async-done | bytes 3932176 | tf_op jit(solution)/shard_map/all_gather | solution.py:237
  196.6 2.0 convolution_convert_fusion.22
  203.2 2.6 collective-permute-start.15
  209.7 1.8 fusion.9
  211.6 2.4 convolution_convert_fusion.20
  218.7 9.7 %collective-permute-done.17 = bf16[192,1024]{1,0:T(8,128)(2,1)S(1)} collective-permute-done((bf16[192,1024]{1,0:T(8,128)(2,1)S(1)}, bf16[192,1024]{1,0:T(8,128)(2,1)S(1)}, u32[]{:S(2)}, u32[]{:S(2)}) %collective-permute-start.17) | collective-permute-done | bytes 393248 | tf_op jit(solution)/shard_map/ppermute | solution.py:68
  228.5 3.1 collective-permute-start.18
  231.6 8.8 %collective-permute-done.18 = bf16[192,1024]{1,0:T(8,128)(2,1)S(1)} collective-permute-done((bf16[192,1024]{1,0:T(8,128)(2,1)S(1)}, bf16[192,1024]{1,0:T(8,128)(2,1)S(1)}, u32[]{:S(2)}, u32[]{:S(2)}) %collective-permute-start.18) | collective-permute-done | bytes 393248 | tf_op jit(solution)/shard_map/ppermute | solution.py:68
  250.9 9.7 %collective-permute-done.25 = bf16[192,1024]{1,0:T(8,128)(2,1)S(1)} collective-permute-done((bf16[192,1024]{1,0:T(8,128)(2,1)S(1)}, bf16[192,1024]{1,0:T(8,128)(2,1)S(1)}, u32[]{:S(2)}, u32[]{:S(2)}) %collective-permute-start.25) | collective-permute-done | bytes 393248 | tf_op jit(solution)/shard_map/ppermute | solution.py:68
  260.7 3.1 collective-permute-start.26
  263.8 8.8 %collective-permute-done.26 = bf16[192,1024]{1,0:T(8,128)(2,1)S(1)} collective-permute-done((bf16[192,1024]{1,0:T(8,128)(2,1)S(1)}, bf16[192,1024]{1,0:T(8,128)(2,1)S(1)}, u32[]{:S(2)}, u32[]{:S(2)}) %collective-permute-start.26) | collective-permute-done | bytes 393248 | tf_op jit(solution)/shard_map/ppermute | solution.py:68
  275.6 1.7 multiply_reduce_fusion.3
  277.4 2.5 multiply_add_fusion.3
  282.9 2.6 collective-permute-start.29
  285.5 1.9 fusion.4
  294.4 2.0 copy.159
  296.4 1.9 fusion.77
  308.9 1.7 convolution_convert_fusion.8
  311.5 7.1 %collective-permute-done.31 = bf16[192,1024]{1,0:T(8,128)(2,1)S(1)} collective-permute-done((bf16[192,1024]{1,0:T(8,128)(2,1)S(1)}, bf16[192,1024]{1,0:T(8,128)(2,1)S(1)}, u32[]{:S(2)}, u32[]{:S(2)}) %collective-permute-start.31) | collective-permute-done | bytes 393248 | tf_op jit(solution)/shard_map/ppermute | solution.py:68
  319.5 3.0 collective-permute-start.32
  324.5 8.8 %collective-permute-done.32 = bf16[192,1024]{1,0:T(8,128)(2,1)} collective-permute-done((bf16[192,1024]{1,0:T(8,128)(2,1)}, bf16[192,1024]{1,0:T(8,128)(2,1)}, u32[]{:S(2)}, u32[]{:S(2)}) %collective-permute-start.32) | collective-permute-done | bytes 393248 | tf_op jit(solution)/shard_map/ppermute | solution.py:68
  336.0 4.1 collective-permute-done.21
  340.9 2.0 collective-permute-start.22
  346.4 1.9 multiply_convert_fusion.4
  351.3 3.9 copy.216
  367.1 1.9 fusion.26
  370.2 8.0 %collective-permute-done.35 = bf16[192,1024]{1,0:T(8,128)(2,1)S(1)} collective-permute-done((bf16[192,1024]{1,0:T(8,128)(2,1)S(1)}, bf16[192,1024]{1,0:T(8,128)(2,1)S(1)}, u32[]{:S(2)}, u32[]{:S(2)}) %collective-permute-start.35) | collective-permute-done | bytes 393248 | tf_op jit(solution)/shard_map/ppermute | solution.py:68
  378.4 1.9 collective-permute-start.36
  383.4 7.0 %collective-permute-done.36 = bf16[192,1024]{1,0:T(8,128)(2,1)S(1)} collective-permute-done((bf16[192,1024]{1,0:T(8,128)(2,1)S(1)}, bf16[192,1024]{1,0:T(8,128)(2,1)S(1)}, u32[]{:S(2)}, u32[]{:S(2)}) %collective-permute-start.36) | collective-permute-done | bytes 393248 | tf_op jit(solution)/shard_map/ppermute | solution.py:68
  392.3 6.3 %copy.214 = bf16[1024,1920]{1,0:T(8,128)(2,1)} copy(bf16[1024,1920]{0,1:T(8,128)(2,1)} %fusion.19) | data formatting | bytes 7864320
  402.0 2.0 multiply_add_fusion.1
  413.1 1.9 copy.170
  419.3 2.5 collective-permute-start.38
  423.0 5.6 %collective-permute-done.38 = bf16[384,128]{1,0:T(8,128)(2,1)S(1)} collective-permute-done((bf16[384,128]{1,0:T(8,128)(2,1)S(1)}, bf16[384,128]{1,0:T(8,128)(2,1)S(1)}, u32[]{:S(2)}, u32[]{:S(2)}) %collective-permute-start.38) | collective-permute-done | bytes 98336 | tf_op jit(solution)/shard_map/ppermute | solution.py:82
  436.8 3.8 copy.176
  442.3 3.7 collective-permute-done.41
  447.2 2.4 collective-permute-start.42
  450.0 9.6 %collective-permute-done.42 = bf16[192,1024]{1,0:T(8,128)(2,1)S(1)} collective-permute-done((bf16[192,1024]{1,0:T(8,128)(2,1)S(1)}, bf16[192,1024]{1,0:T(8,128)(2,1)S(1)}, u32[]{:S(2)}, u32[]{:S(2)}) %collective-permute-start.42) | collective-permute-done | bytes 393248 | tf_op jit(solution)/shard_map/ppermute | solution.py:68
  459.8 22.7 %collective-permute-done.51 = bf16[2,2,1,2,64,896]{5,4,3,2,1,0:T(8,128)(2,1)S(1)} collective-permute-done((bf16[2,2,1,2,64,896]{5,4,3,2,1,0:T(8,128)(2,1)S(1)}, bf16[2,2,1,2,64,896]{5,4,3,2,1,0:T(8,128)(2,1)S(1)}, u32[]{:S(2)}, u32[]{:S(2)}) %collective-permute-start.51) | collective-permute-done | bytes 917536 | tf_op jit(solution)/shard_map/ppermute | solution.py:135
  484.4 20.5 %collective-permute-done.52 = bf16[2,1,1,2,64,896]{5,4,3,2,1,0:T(8,128)(2,1)S(1)} collective-permute-done((bf16[2,1,1,2,64,896]{5,4,3,2,1,0:T(8,128)(2,1)S(1)}, bf16[2,1,1,2,64,896]{5,4,3,2,1,0:T(8,128)(2,1)S(1)}, u32[]{:S(2)}, u32[]{:S(2)}) %collective-permute-start.52) | collective-permute-done | bytes 458784 | tf_op jit(solution)/shard_map/ppermute | solution.py:135
  506.4 2.4 collective-permute-done.45
  508.8 3.0 collective-permute-start.46
  512.2 2.0 collective-permute-done.46
  515.4 5.2 collective-permute-done.47
  522.3 2.2 collective-permute-done.48
  524.8 3.7 collective-permute-done.49
  528.6 3.6 collective-permute-start.54
  (630 shorter events, 169.3 us)
Async XLA Ops:
  7.2 93.5 %all-gather.3.cloned.1.call-start = ((), (), s32[]{:S(2)}) async-start(), calls=%async_computation.2 | async-start | bytes 3063808 | tf_op jit(solution)/shard_map/all_gather | solution.py:242
  10.5 186.1 %all-gather.5.cloned.1.call-start = ((), (), s32[]{:S(2)}) async-start(), calls=%async_computation.3 | async-start | bytes 4177920 | tf_op jit(solution)/shard_map/all_gather | solution.py:237
  12.1 11.5 %collective-permute-start = (bf16[1,1,1,1,64,512]{5,4,3,2,1,0:T(8,128)(2,1)S(1)}, bf16[1,1,1,1,64,512]{5,4,3,2,1,0:T(8,128)(2,1)S(1)}, u32[]{:S(2)}, u32[]{:S(2)}) collective-permute-start(bf16[1,1,1,1,64,512]{5,4,3,2,1,0:T(8,128)(2,1)S(1)} %get-tuple-element.125), channel_id=1, source_target_pairs={{0,8},{8,0},{1,9},{9,1},{2,10},{10,2},{3,11},{11,3},{4,12},{12,4},... | collective-permute-start | bytes 196616 | tf_op jit(solution)/shard_map/ppermute | solution.py:157
  21.4 513.8 %reduce-scatter.9.cloned.1.call-start = ((), (), s32[]{:S(2)}) async-start(), calls=%async_computation.5 | async-start | bytes 2228224
  21.5 42.8 %copy-start.133 = (f32[64]{0:T(128)}, f32[64]{0:T(128)S(1)}, u32[]{:S(2)}) copy-start(f32[64]{0:T(128)S(1)} %multiply_power_fusion) | copy-start | bytes 772
  23.1 47.5 %copy-start.32 = (f32[384,64]{1,0:T(8,128)}, f32[384,64]{1,0:T(8,128)S(1)}, u32[]{:S(2)}) copy-start(f32[384,64]{1,0:T(8,128)S(1)} %get-tuple-element.136) | copy-start | bytes 294916
  23.1 47.5 %copy-start.56 = (f32[384,64]{1,0:T(8,128)}, f32[384,64]{1,0:T(8,128)S(1)}, u32[]{:S(2)}) copy-start(f32[384,64]{1,0:T(8,128)S(1)} %get-tuple-element.135) | copy-start | bytes 294916
  23.6 6.6 %collective-permute-start.1 = (bf16[1,1,1,2,64,512]{5,4,3,2,1,0:T(8,128)(2,1)S(1)}, bf16[1,1,1,2,64,512]{5,4,3,2,1,0:T(8,128)(2,1)S(1)}, u32[]{:S(2)}, u32[]{:S(2)}) collective-permute-start(bf16[1,1,1,2,64,512]{5,4,3,2,1,0:T(8,128)(2,1)S(1)} %maximum_select_fusion.17), channel_id=1, source_target_pairs={{0,64},{16,80},{32,96},{48,112},{64,0},{80,16},{96,32},{112,48},{1... | collective-permute-start | bytes 393224 | tf_op jit(solution)/shard_map/ppermute | solution.py:157
  30.2 10.7 %collective-permute-start.2 = (bf16[2,1,1,2,64,512]{5,4,3,2,1,0:T(8,128)(2,1)S(1)}, bf16[2,1,1,2,64,512]{5,4,3,2,1,0:T(8,128)(2,1)S(1)}, u32[]{:S(2)}, u32[]{:S(2)}) collective-permute-start(bf16[2,1,1,2,64,512]{5,4,3,2,1,0:T(8,128)(2,1)S(1)} %maximum_select_fusion.11), channel_id=1, source_target_pairs={{0,16},{16,0},{32,48},{48,32},{64,80},{80,64},{96,112},{112,96},{1... | collective-permute-start | bytes 786440 | tf_op jit(solution)/shard_map/ppermute | solution.py:157
  40.9 20.6 %collective-permute-start.3 = (bf16[2,1,2,2,64,512]{5,4,3,2,1,0:T(8,128)(2,1)S(1)}, bf16[2,1,2,2,64,512]{5,4,3,2,1,0:T(8,128)(2,1)S(1)}, u32[]{:S(2)}, u32[]{:S(2)}) collective-permute-start(bf16[2,1,2,2,64,512]{5,4,3,2,1,0:T(8,128)(2,1)S(1)} %maximum_select_fusion.9), channel_id=1, source_target_pairs={{0,32},{16,48},{32,0},{48,16},{64,96},{80,112},{96,64},{112,80},{1... | collective-permute-start | bytes 1572872 | tf_op jit(solution)/shard_map/ppermute | solution.py:157
  63.6 13.8 %collective-permute-start.4 = (bf16[384,128]{1,0:T(8,128)(2,1)S(1)}, bf16[384,128]{1,0:T(8,128)(2,1)S(1)}, u32[]{:S(2)}, u32[]{:S(2)}) collective-permute-start(bf16[384,128]{1,0:T(8,128)(2,1)S(1)} %convolution_convert_fusion.23), channel_id=1, source_target_pairs={{0,8},{8,0},{1,9},{9,1},{2,10},{10,2},{3,11},{11,3},{4,12},{12,4},... | collective-permute-start | bytes 294920 | tf_op jit(solution)/shard_map/ppermute | solution.py:82
  65.3 10.1 %collective-permute-start.5 = (bf16[384,128]{1,0:T(8,128)(2,1)S(1)}, bf16[384,128]{1,0:T(8,128)(2,1)}, u32[]{:S(2)}, u32[]{:S(2)}) collective-permute-start(bf16[384,128]{1,0:T(8,128)(2,1)S(1)} %pad_maximum_fusion.11), channel_id=1, source_target_pairs={{0,8},{8,0},{1,9},{9,1},{2,10},{10,2},{3,11},{11,3},{4,12},{12,4},... | collective-permute-start | bytes 294920 | tf_op jit(solution)/shard_map/ppermute | solution.py:82
  103.0 1.9 collective-permute-start.6
  105.1 11.2 %collective-permute-start.7 = (bf16[192,1024]{1,0:T(8,128)(2,1)S(1)}, bf16[192,1024]{1,0:T(8,128)(2,1)S(1)}, u32[]{:S(2)}, u32[]{:S(2)}) collective-permute-start(bf16[192,1024]{1,0:T(8,128)(2,1)S(1)} %add_convert_fusion.27), channel_id=1, source_target_pairs={{0,2},{1,3},{2,0},{3,1},{4,6},{5,7},{6,4},{7,5},{8,10},{9,11},{10,... | collective-permute-start | bytes 1179656 | tf_op jit(solution)/shard_map/ppermute | solution.py:68
  116.5 12.0 %collective-permute-start.8 = (bf16[192,1024]{1,0:T(8,128)(2,1)S(1)}, bf16[192,1024]{1,0:T(8,128)(2,1)S(1)}, u32[]{:S(2)}, u32[]{:S(2)}) collective-permute-start(bf16[192,1024]{1,0:T(8,128)(2,1)S(1)} %add_convert_fusion.26), channel_id=1, source_target_pairs={{0,4},{1,5},{2,6},{3,7},{4,0},{5,1},{6,2},{7,3},{8,12},{9,13},{10,... | collective-permute-start | bytes 1179656 | tf_op jit(solution)/shard_map/ppermute | solution.py:68
  128.6 2.0 collective-permute-start.9
  136.1 1.8 collective-permute-start.10
  138.1 11.3 %collective-permute-start.11 = (bf16[192,1024]{1,0:T(8,128)(2,1)S(1)}, bf16[192,1024]{1,0:T(8,128)(2,1)S(1)}, u32[]{:S(2)}, u32[]{:S(2)}) collective-permute-start(bf16[192,1024]{1,0:T(8,128)(2,1)S(1)} %add_convert_fusion.24), channel_id=1, source_target_pairs={{0,2},{1,3},{2,0},{3,1},{4,6},{5,7},{6,4},{7,5},{8,10},{9,11},{10,... | collective-permute-start | bytes 1179656 | tf_op jit(solution)/shard_map/ppermute | solution.py:68
  149.5 12.0 %collective-permute-start.12 = (bf16[192,1024]{1,0:T(8,128)(2,1)S(1)}, bf16[192,1024]{1,0:T(8,128)(2,1)S(1)}, u32[]{:S(2)}, u32[]{:S(2)}) collective-permute-start(bf16[192,1024]{1,0:T(8,128)(2,1)S(1)} %add_convert_fusion.23), channel_id=1, source_target_pairs={{0,4},{1,5},{2,6},{3,7},{4,0},{5,1},{6,2},{7,3},{8,12},{9,13},{10,... | collective-permute-start | bytes 1179656 | tf_op jit(solution)/shard_map/ppermute | solution.py:68
  161.7 1.8 collective-permute-start.13
  165.6 40.2 %copy-start.12 = (bf16[384,1024]{1,0:T(8,128)(2,1)}, bf16[384,1024]{1,0:T(8,128)(2,1)S(1)}, u32[]{:S(2)}) copy-start(bf16[384,1024]{1,0:T(8,128)(2,1)S(1)} %get-tuple-element.75) | copy-start | bytes 2359300
  165.6 35.9 %copy-start.140 = (f32[128]{0:T(128)S(1)}, f32[128]{0:T(128)}, u32[]{:S(2)}) copy-start(f32[128]{0:T(128)} %get-tuple-element.139) | copy-start | bytes 1540
  198.6 13.0 %collective-permute-start.14 = (bf16[384,128]{1,0:T(8,128)(2,1)}, bf16[384,128]{1,0:T(8,128)(2,1)}, u32[]{:S(2)}, u32[]{:S(2)}) collective-permute-start(bf16[384,128]{1,0:T(8,128)(2,1)} %convolution_convert_fusion.22), channel_id=1, source_target_pairs={{0,8},{8,0},{1,9},{9,1},{2,10},{10,2},{3,11},{11,3},{4,12},{12,4},... | collective-permute-start | bytes 294920 | tf_op jit(solution)/shard_map/ppermute | solution.py:82
  203.2 6.4 %collective-permute-start.15 = (bf16[384,128]{1,0:T(8,128)(2,1)}, bf16[384,128]{1,0:T(8,128)(2,1)}, u32[]{:S(2)}, u32[]{:S(2)}) collective-permute-start(bf16[384,128]{1,0:T(8,128)(2,1)} %pad_maximum_fusion.12), channel_id=1, source_target_pairs={{0,8},{8,0},{1,9},{9,1},{2,10},{10,2},{3,11},{11,3},{4,12},{12,4},... | collective-permute-start | bytes 294920 | tf_op jit(solution)/shard_map/ppermute | solution.py:82
  215.2 1.8 collective-permute-start.16
  217.1 11.2 %collective-permute-start.17 = (bf16[192,1024]{1,0:T(8,128)(2,1)S(1)}, bf16[192,1024]{1,0:T(8,128)(2,1)S(1)}, u32[]{:S(2)}, u32[]{:S(2)}) collective-permute-start(bf16[192,1024]{1,0:T(8,128)(2,1)S(1)} %add_convert_fusion.21), channel_id=1, source_target_pairs={{0,2},{1,3},{2,0},{3,1},{4,6},{5,7},{6,4},{7,5},{8,10},{9,11},{10,... | collective-permute-start | bytes 1179656 | tf_op jit(solution)/shard_map/ppermute | solution.py:68
  228.5 11.9 %collective-permute-start.18 = (bf16[192,1024]{1,0:T(8,128)(2,1)S(1)}, bf16[192,1024]{1,0:T(8,128)(2,1)S(1)}, u32[]{:S(2)}, u32[]{:S(2)}) collective-permute-start(bf16[192,1024]{1,0:T(8,128)(2,1)S(1)} %add_convert_fusion.20), channel_id=1, source_target_pairs={{0,4},{1,5},{2,6},{3,7},{4,0},{5,1},{6,2},{7,3},{8,12},{9,13},{10,... | collective-permute-start | bytes 1179656 | tf_op jit(solution)/shard_map/ppermute | solution.py:68
  240.6 2.3 collective-permute-start.19
  247.4 1.8 collective-permute-start.24
  249.3 11.2 %collective-permute-start.25 = (bf16[192,1024]{1,0:T(8,128)(2,1)S(1)}, bf16[192,1024]{1,0:T(8,128)(2,1)S(1)}, u32[]{:S(2)}, u32[]{:S(2)}) collective-permute-start(bf16[192,1024]{1,0:T(8,128)(2,1)S(1)} %add_convert_fusion.15), channel_id=1, source_target_pairs={{0,2},{1,3},{2,0},{3,1},{4,6},{5,7},{6,4},{7,5},{8,10},{9,11},{10,... | collective-permute-start | bytes 1179656 | tf_op jit(solution)/shard_map/ppermute | solution.py:68
  260.7 11.9 %collective-permute-start.26 = (bf16[192,1024]{1,0:T(8,128)(2,1)S(1)}, bf16[192,1024]{1,0:T(8,128)(2,1)S(1)}, u32[]{:S(2)}, u32[]{:S(2)}) collective-permute-start(bf16[192,1024]{1,0:T(8,128)(2,1)S(1)} %add_convert_fusion.14), channel_id=1, source_target_pairs={{0,4},{1,5},{2,6},{3,7},{4,0},{5,1},{6,2},{7,3},{8,12},{9,13},{10,... | collective-permute-start | bytes 1179656 | tf_op jit(solution)/shard_map/ppermute | solution.py:68
  273.5 2.1 collective-permute-start.27
  282.9 21.0 %collective-permute-start.29 = (bf16[384,128]{0,1:T(8,128)(2,1)}, bf16[384,128]{0,1:T(8,128)(2,1)}, u32[]{:S(2)}, u32[]{:S(2)}) collective-permute-start(bf16[384,128]{0,1:T(8,128)(2,1)} %fusion.149), channel_id=1, source_target_pairs={{0,8},{8,0},{1,9},{9,1},{2,10},{10,2},{3,11},{11,3},{4,12},{12,4},... | collective-permute-start | bytes 294920 | tf_op jit(solution)/shard_map/ppermute | solution.py:82
  290.3 9.5 %collective-permute-start.28 = (bf16[384,128]{1,0:T(8,128)(2,1)}, bf16[384,128]{1,0:T(8,128)(2,1)}, u32[]{:S(2)}, u32[]{:S(2)}) collective-permute-start(bf16[384,128]{1,0:T(8,128)(2,1)} %fusion.147), channel_id=1, source_target_pairs={{0,8},{8,0},{1,9},{9,1},{2,10},{10,2},{3,11},{11,3},{4,12},{12,4},... | collective-permute-start | bytes 294920 | tf_op jit(solution)/shard_map/ppermute | solution.py:82
  305.4 1.8 collective-permute-start.30
  307.4 11.2 %collective-permute-start.31 = (bf16[192,1024]{1,0:T(8,128)(2,1)S(1)}, bf16[192,1024]{1,0:T(8,128)(2,1)S(1)}, u32[]{:S(2)}, u32[]{:S(2)}) collective-permute-start(bf16[192,1024]{1,0:T(8,128)(2,1)S(1)} %add_convert_fusion.12), channel_id=1, source_target_pairs={{0,2},{1,3},{2,0},{3,1},{4,6},{5,7},{6,4},{7,5},{8,10},{9,11},{10,... | collective-permute-start | bytes 1179656 | tf_op jit(solution)/shard_map/ppermute | solution.py:68
  311.5 11.0 %collective-permute-start.20 = (bf16[192,1024]{1,0:T(8,128)(2,1)}, bf16[192,1024]{1,0:T(8,128)(2,1)}, u32[]{:S(2)}, u32[]{:S(2)}) collective-permute-start(bf16[192,1024]{1,0:T(8,128)(2,1)} %constant_dynamic-slice_fusion.5), channel_id=1, source_target_pairs={{0,1},{1,0},{2,3},{3,2},{4,5},{5,4},{6,7},{7,6},{8,9},{9,8},{10,11... | collective-permute-start | bytes 1179656 | tf_op jit(solution)/shard_map/ppermute | solution.py:62
  319.5 13.9 %collective-permute-start.32 = (bf16[192,1024]{1,0:T(8,128)(2,1)}, bf16[192,1024]{1,0:T(8,128)(2,1)}, u32[]{:S(2)}, u32[]{:S(2)}) collective-permute-start(bf16[192,1024]{1,0:T(8,128)(2,1)} %add_convert_fusion.11), channel_id=1, source_target_pairs={{0,4},{1,5},{2,6},{3,7},{4,0},{5,1},{6,2},{7,3},{8,12},{9,13},{10,... | collective-permute-start | bytes 1179656 | tf_op jit(solution)/shard_map/ppermute | solution.py:68
  323.8 16.2 %collective-permute-start.21 = (bf16[192,1024]{1,0:T(8,128)(2,1)S(1)}, bf16[192,1024]{1,0:T(8,128)(2,1)S(1)}, u32[]{:S(2)}, u32[]{:S(2)}) collective-permute-start(bf16[192,1024]{1,0:T(8,128)(2,1)S(1)} %add_convert_fusion.18), channel_id=1, source_target_pairs={{0,2},{1,3},{2,0},{3,1},{4,6},{5,7},{6,4},{7,5},{8,10},{9,11},{10,... | collective-permute-start | bytes 1179656 | tf_op jit(solution)/shard_map/ppermute | solution.py:68
  334.6 8.3 %collective-permute-start.33 = (bf16[192,1024]{1,0:T(8,128)(2,1)S(1)}, bf16[192,1024]{1,0:T(8,128)(2,1)S(1)}, u32[]{:S(2)}, u32[]{:S(2)}) collective-permute-start(bf16[192,1024]{1,0:T(8,128)(2,1)S(1)} %add_convert_fusion.10), channel_id=1, source_target_pairs={{0,1},{1,0},{2,3},{3,2},{4,5},{5,4},{6,7},{7,6},{8,9},{9,8},{10,11... | collective-permute-start | bytes 1179656 | tf_op jit(solution)/shard_map/ppermute | solution.py:72
  340.9 14.3 %collective-permute-start.22 = (bf16[192,1024]{1,0:T(8,128)(2,1)}, bf16[192,1024]{1,0:T(8,128)(2,1)}, u32[]{:S(2)}, u32[]{:S(2)}) collective-permute-start(bf16[192,1024]{1,0:T(8,128)(2,1)} %add_convert_fusion.17), channel_id=1, source_target_pairs={{0,4},{1,5},{2,6},{3,7},{4,0},{5,1},{6,2},{7,3},{8,12},{9,13},{10,... | collective-permute-start | bytes 1179656 | tf_op jit(solution)/shard_map/ppermute | solution.py:68
  355.2 182.0 %reduce-scatter.7.cloned.1.call-start = ((), (), s32[]{:S(2)}) async-start(), calls=%async_computation.4 | async-start | bytes 4177920 | tf_op jit(solution)/shard_map/reduce_scatter | solution.py:253
  356.6 4.1 collective-permute-start.23
  364.7 2.1 collective-permute-start.34
  367.0 11.2 %collective-permute-start.35 = (bf16[192,1024]{1,0:T(8,128)(2,1)S(1)}, bf16[192,1024]{1,0:T(8,128)(2,1)S(1)}, u32[]{:S(2)}, u32[]{:S(2)}) collective-permute-start(bf16[192,1024]{1,0:T(8,128)(2,1)S(1)} %add_convert_fusion.9), channel_id=1, source_target_pairs={{0,2},{1,3},{2,0},{3,1},{4,6},{5,7},{6,4},{7,5},{8,10},{9,11},{10,... | collective-permute-start | bytes 1179656 | tf_op jit(solution)/shard_map/ppermute | solution.py:68
  378.4 12.0 %collective-permute-start.36 = (bf16[192,1024]{1,0:T(8,128)(2,1)S(1)}, bf16[192,1024]{1,0:T(8,128)(2,1)S(1)}, u32[]{:S(2)}, u32[]{:S(2)}) collective-permute-start(bf16[192,1024]{1,0:T(8,128)(2,1)S(1)} %add_convert_fusion.8), channel_id=1, source_target_pairs={{0,4},{1,5},{2,6},{3,7},{4,0},{5,1},{6,2},{7,3},{8,12},{9,13},{10,... | collective-permute-start | bytes 1179656 | tf_op jit(solution)/shard_map/ppermute | solution.py:68
  390.5 10.7 %collective-permute-start.37 = (bf16[192,1024]{1,0:T(8,128)(2,1)S(1)}, bf16[192,1024]{1,0:T(8,128)(2,1)S(1)}, u32[]{:S(2)}, u32[]{:S(2)}) collective-permute-start(bf16[192,1024]{1,0:T(8,128)(2,1)S(1)} %add_convert_fusion.7), channel_id=1, source_target_pairs={{0,1},{1,0},{2,3},{3,2},{4,5},{5,4},{6,7},{7,6},{8,9},{9,8},{10,11... | collective-permute-start | bytes 1179656 | tf_op jit(solution)/shard_map/ppermute | solution.py:72
  419.3 9.3 %collective-permute-start.38 = (bf16[384,128]{1,0:T(8,128)(2,1)S(1)}, bf16[384,128]{1,0:T(8,128)(2,1)S(1)}, u32[]{:S(2)}, u32[]{:S(2)}) collective-permute-start(bf16[384,128]{1,0:T(8,128)(2,1)S(1)} %fusion.151), channel_id=1, source_target_pairs={{0,8},{8,0},{1,9},{9,1},{2,10},{10,2},{3,11},{11,3},{4,12},{12,4},... | collective-permute-start | bytes 294920 | tf_op jit(solution)/shard_map/ppermute | solution.py:82
  421.8 8.9 %collective-permute-start.39 = (bf16[384,128]{0,1:T(8,128)(2,1)S(1)}, bf16[384,128]{0,1:T(8,128)(2,1)S(1)}, u32[]{:S(2)}, u32[]{:S(2)}) collective-permute-start(bf16[384,128]{0,1:T(8,128)(2,1)S(1)} %fusion.153), channel_id=1, source_target_pairs={{0,8},{8,0},{1,9},{9,1},{2,10},{10,2},{3,11},{11,3},{4,12},{12,4},... | collective-permute-start | bytes 294920 | tf_op jit(solution)/shard_map/ppermute | solution.py:82
  431.1 2.2 collective-permute-start.40
  434.2 11.8 %collective-permute-start.41 = (bf16[192,1024]{1,0:T(8,128)(2,1)}, bf16[192,1024]{1,0:T(8,128)(2,1)}, u32[]{:S(2)}, u32[]{:S(2)}) collective-permute-start(bf16[192,1024]{1,0:T(8,128)(2,1)} %add_convert_fusion.6), channel_id=1, source_target_pairs={{0,2},{1,3},{2,0},{3,1},{4,6},{5,7},{6,4},{7,5},{8,10},{9,11},{10,... | collective-permute-start | bytes 1179656 | tf_op jit(solution)/shard_map/ppermute | solution.py:68
  442.0 40.5 %collective-permute-start.51 = (bf16[2,2,1,2,64,896]{5,4,3,2,1,0:T(8,128)(2,1)S(1)}, bf16[2,2,1,2,64,896]{5,4,3,2,1,0:T(8,128)(2,1)S(1)}, u32[]{:S(2)}, u32[]{:S(2)}) collective-permute-start(bf16[2,2,1,2,64,896]{5,4,3,2,1,0:T(8,128)(2,1)S(1)} %constant_dynamic-slice_fusion), channel_id=1, source_target_pairs={{0,16},{16,0},{32,48},{48,32},{64,80},{80,64},{96,112},{112,96},{1... | collective-permute-start | bytes 2752520 | tf_op jit(solution)/shard_map/ppermute | solution.py:135
  447.2 12.3 %collective-permute-start.42 = (bf16[192,1024]{1,0:T(8,128)(2,1)S(1)}, bf16[192,1024]{1,0:T(8,128)(2,1)S(1)}, u32[]{:S(2)}, u32[]{:S(2)}) collective-permute-start(bf16[192,1024]{1,0:T(8,128)(2,1)S(1)} %add_convert_fusion.5), channel_id=1, source_target_pairs={{0,4},{1,5},{2,6},{3,7},{4,0},{5,1},{6,2},{7,3},{8,12},{9,13},{10,... | collective-permute-start | bytes 1179656 | tf_op jit(solution)/shard_map/ppermute | solution.py:68
  459.7 23.2 %collective-permute-start.43 = (bf16[192,1024]{1,0:T(8,128)(2,1)S(1)}, bf16[192,1024]{1,0:T(8,128)(2,1)S(1)}, u32[]{:S(2)}, u32[]{:S(2)}) collective-permute-start(bf16[192,1024]{1,0:T(8,128)(2,1)S(1)} %add_convert_fusion.4), channel_id=1, source_target_pairs={{0,1},{1,0},{2,3},{3,2},{4,5},{5,4},{6,7},{7,6},{8,9},{9,8},{10,11... | collective-permute-start | bytes 1179656 | tf_op jit(solution)/shard_map/ppermute | solution.py:72
  482.8 22.0 %collective-permute-start.52 = (bf16[2,1,1,2,64,896]{5,4,3,2,1,0:T(8,128)(2,1)S(1)}, bf16[2,1,1,2,64,896]{5,4,3,2,1,0:T(8,128)(2,1)S(1)}, u32[]{:S(2)}, u32[]{:S(2)}) collective-permute-start(bf16[2,1,1,2,64,896]{5,4,3,2,1,0:T(8,128)(2,1)S(1)} %dynamic-slice_convert_fusion), channel_id=1, source_target_pairs={{0,32},{16,48},{32,0},{48,16},{64,96},{80,112},{96,64},{112,80},{1... | collective-permute-start | bytes 1376264 | tf_op jit(solution)/shard_map/ppermute | solution.py:135
  484.3 20.7 %collective-permute-start.44 = (f32[2,2304]{1,0:T(2,128)S(1)}, f32[2,2304]{1,0:T(2,128)S(1)}, u32[]{:S(2)}, u32[]{:S(2)}) collective-permute-start(f32[2,2304]{1,0:T(2,128)S(1)} %maximum_maximum_fusion), channel_id=1, source_target_pairs={{0,1},{1,0},{2,3},{3,2},{4,5},{5,4},{6,7},{7,6},{8,9},{9,8},{10,11... | collective-permute-start | bytes 55304 | tf_op jit(solution)/shard_map/ppermute | solution.py:109
  505.0 3.8 collective-permute-start.45
  506.3 18.4 %collective-permute-start.53 = (bf16[2,1,1,1,64,896]{5,4,3,2,1,0:T(8,128)(2,1)S(1)}, bf16[2,1,1,1,64,896]{5,4,3,2,1,0:T(8,128)(2,1)S(1)}, u32[]{:S(2)}, u32[]{:S(2)}) collective-permute-start(bf16[2,1,1,1,64,896]{5,4,3,2,1,0:T(8,128)(2,1)S(1)} %dynamic-slice_convert_fusion.1), channel_id=1, source_target_pairs={{0,8},{8,0},{1,9},{9,1},{2,10},{10,2},{3,11},{11,3},{4,12},{12,4},... | collective-permute-start | bytes 688136 | tf_op jit(solution)/shard_map/ppermute | solution.py:135
  508.8 5.3 collective-permute-start.46
  514.2 6.4 %collective-permute-start.47 = (f32[2,2304]{1,0:T(2,128)S(1)}, f32[2,2304]{1,0:T(2,128)S(1)}, u32[]{:S(2)}, u32[]{:S(2)}) collective-permute-start(f32[2,2304]{1,0:T(2,128)S(1)} %add.463), channel_id=1, source_target_pairs={{0,8},{8,0},{1,9},{9,1},{2,10},{10,2},{3,11},{11,3},{4,12},{12,4},... | collective-permute-start | bytes 55304 | tf_op jit(solution)/shard_map/ppermute | solution.py:109
  520.6 4.0 collective-permute-start.48
  524.6 3.8 collective-permute-start.49
  528.5 5.3 collective-permute-start.50
  528.6 6.4 %collective-permute-start.54 = (bf16[1,1,1,1,64,896]{5,4,3,2,1,0:T(8,128)(2,1)S(1)}, bf16[1,1,1,1,64,896]{5,4,3,2,1,0:T(8,128)(2,1)S(1)}, u32[]{:S(2)}, u32[]{:S(2)}) collective-permute-start(bf16[1,1,1,1,64,896]{5,4,3,2,1,0:T(8,128)(2,1)S(1)} %dynamic-slice_convert_fusion.2), channel_id=1, source_target_pairs={{0,64},{16,80},{32,96},{48,112},{64,0},{80,16},{96,32},{112,48},{1... | collective-permute-start | bytes 344072 | tf_op jit(solution)/shard_map/ppermute | solution.py:135
  (152 other events, 855.0 us)
Sparse Core Ops, SparseCore 0:
  10.6 90.0 all-gather.2
  102.4 94.1 all-gather.4
  355.3 81.6 reduce-scatter.8
  439.3 97.8 reduce-scatter.6
